TPU v7x, 256 devices: a whole 4x4x8 slice. The times are simulated.
256 devices in a mesh: dom: 32 (over y, x, core), tp: 8 (over z).
Axes of the slice: x: 4, y: 4, z: 8, core: 2. Of those that a mesh axis runs over, the one named last changes fastest.
Arguments:
- activations: bfloat16 [4, 512, 4096], P(None, 'dom', 'tp'), may hold values from -6 to 6
- norm_gain: float32 [4096], replicated, may hold values from 0.5 to 1.5
- w_query: bfloat16 [4096, 4096], P(None, 'tp'), may hold values from -0.09375 to 0.09375
- w_key: bfloat16 [4096, 1024], P(None, 'tp'), may hold values from -0.09375 to 0.09375
- value_weight: bfloat16 [4096, 1024], P(None, 'tp'), may hold values from -0.5 to 0.5
- w_output: bfloat16 [4096, 4096], P('tp'), may hold values from -0.09375 to 0.09375
- cache_keys: bfloat16 [512, 128, 1024], P('dom', None, 'tp'), may hold values from -740 to 740
- cache_values: bfloat16 [512, 128, 1024], P('dom', None, 'tp'), may hold values from -48 to 48
- tokens: int32 [4, 512], P(None, 'dom'), may hold values from 0 to 128255
- twisting_table: bfloat16 [128256], replicated, may hold values from -6 to 6
- twist_vec: float32 [4096], P('tp'), may hold values from -0.09375 to 0.09375
- previous_log_weights: float32 [512], P('dom'), may hold values from -300 to 0
- copy_counts: int32 [512], P('dom'), may hold values from 0 to 4, as said below
Outputs:
- attn_out: bfloat16 [4, 512, 4096], P(None, 'dom', 'tp')
- new_keys: bfloat16 [512, 132, 1024], P('dom', None, 'tp')
- new_values: bfloat16 [512, 132, 1024], P('dom', None, 'tp')
- out_logw: float32 [512], P('dom')
Inputs may be any that keep to these rules, and one draw needn't show every extreme that they name: copy_counts sum to 512; the particles of one index of dom have together at most 64 copies, and one index has exactly that many.
All inputs are finite; a program needn't handle non-finite values.
Results may differ from a plain program's by a relative error of at most 0.012.
The roundings to bfloat16 on the way count: a program that leaves them out, or rounds other values in their place, can miss the bound.
Values may be sent and summed in bfloat16 or wider, within the bound.
No kernel may reach another device: no remote copies, remote signals or barrier semaphores. Data moves between devices by JAX's collectives and lax.ppermute only.
A program may use at most 64 MiB of HBM per device.

v0:
```python
import jax
import jax.numpy as jnp
from jax import lax
from jax.sharding import PartitionSpec as P

D = 4096
HD = 128


def copy_for_each(value, axis):
    length = lax.axis_size(axis)
    return lax.all_to_all(
        jnp.broadcast_to(value[None], (length, *value.shape)), axis, 0, 0, tiled=True
    )


def folded_in_pairs(pieces, combine):
    while len(jax.tree.leaves(pieces)[0]) > 1:
        pieces = jax.vmap(combine)(
            *(jax.tree.map(lambda part: part[side::2], pieces) for side in (0, 1))
        )
    return jax.tree.map(lambda part: part[0], pieces)


def prefix(value, axis, combine, identity):
    length, position = (lax.axis_size(axis), lax.axis_index(axis))
    passed = jnp.arange(length) < position

    def kept(part, zero, own):
        part = jnp.where(
            passed.reshape(-1, *(1 for _ in own.shape)), part, jnp.asarray(zero, own.dtype)
        )
        return part

    pieces = copy_for_each(value, axis)
    return folded_in_pairs(kept(pieces, identity, value), combine)


def joined_along(pieces, dim):
    pieces = jnp.moveaxis(pieces, 0, dim)
    lengths = pieces.shape
    return pieces.reshape(*lengths[:dim], lengths[dim] * lengths[dim + 1], *lengths[dim + 2 :])


def collect(value, axis, dim):
    return joined_along(copy_for_each(value, axis), dim)


def in_blocks(value, dim, length):
    before, after = (value.shape[:dim], value.shape[dim + 1 :])
    return jnp.moveaxis(value.reshape(*before, length, -1, *after), dim, 0)


def summed_on_arrival(value, axis, dim):
    length = lax.axis_size(axis)
    pieces = lax.all_to_all(in_blocks(value, dim, length), axis, 0, 0, tiled=True)
    return jnp.sum(pieces, axis=0)


def over_copies(value, axis):
    everything = copy_for_each(value, axis)
    return jnp.sum(everything, axis=0)


def in_one(arrays, axis):
    vector, at, finished = (jnp.concatenate([a.reshape(-1) for a in arrays]), 0, [])
    so_far = over_copies(vector, axis)
    for a in arrays:
        finished.append(so_far[at : at + a.size].reshape(a.shape))
        at += a.size
    return tuple(finished)


def collected_together(value, axis):
    leaves = jax.tree.leaves(value)
    order = sorted(range(len(leaves)), key=lambda k: -leaves[k].size)
    width = (1, *leaves[order[0]].shape)[-1]
    lines = [
        jnp.pad(leaves[k].reshape(-1), (0, -leaves[k].size % width)).reshape(-1, width)
        for k in order
    ]
    both, at, found = (copy_for_each(jnp.concatenate(lines), axis), 0, {})
    for k, line in zip(order, lines):
        section = both[:, at : at + len(line)].reshape(len(both), -1)
        found[k] = section[:, : leaves[k].size].reshape(-1, *leaves[k].shape)
        at += len(line)
    numbers = iter(range(len(leaves)))
    return jax.tree.map(lambda _: found[next(numbers)], value)


def joined_all(value, axis, combine):
    pieces = collected_together(value, axis)
    return folded_in_pairs(pieces, combine)


def rotate(tensor, positions):
    middle = tensor.shape[-1] // 2
    frequency = 500000.0 ** (-2.0 * jnp.arange(middle, dtype=jnp.float32) / tensor.shape[-1])
    angles = positions[:, None] * frequency[None, :]
    cosine = jnp.cos(angles)[:, None, None, :]
    sine_part = jnp.sin(angles)[:, None, None, :]
    lower_half = tensor[..., :middle]
    upper_half = tensor[..., middle:]
    return jnp.concatenate(
        [
            lower_half * cosine - upper_half * sine_part,
            upper_half * cosine + lower_half * sine_part,
        ],
        -1,
    )


def add_counts(former, latter):
    return former + latter


def join_mass(former, latter):
    largest = jnp.maximum(former[0], latter[0])
    return (
        largest,
        former[1] * jnp.exp(former[0] - largest) + latter[1] * jnp.exp(latter[0] - largest),
    )


def local(
    activations,
    norm_gain,
    w_query,
    w_key,
    value_weight,
    w_output,
    cache_keys,
    cache_values,
    tokens,
    twisting_table,
    twist_vec,
    previous_log_weights,
    copy_counts,
):
    step_count = activations.shape[0]
    particle_count = activations.shape[1]
    span_old = cache_keys.shape[1]
    dom_size = lax.axis_size("dom")
    kv_local = w_key.shape[1] // HD
    q_local = w_query.shape[1] // HD
    group_size = q_local // kv_local
    capacity = 4 * particle_count // dom_size
    total_copies = jnp.sum(copy_counts)
    offset = prefix(total_copies, "dom", add_counts, jnp.int32(0))
    starts = jnp.cumsum(copy_counts) - copy_counts
    position = jnp.arange(dom_size * capacity, dtype=jnp.int32)
    target = position // capacity
    copy_rank = position % capacity * dom_size + (target - offset) % dom_size
    is_live = copy_rank < total_copies
    source = jnp.sum((starts[None, :] <= copy_rank[:, None]).astype(jnp.int32), 1) - 1
    arrival = jnp.where(is_live, (offset + copy_rank) // dom_size, particle_count).astype(
        jnp.bfloat16
    )

    def pack_rows(tensor):
        return jnp.where(is_live[:, None, None], tensor[source], jnp.zeros((), tensor.dtype))

    def place_rows(tensor, slot_index):
        blank = jnp.zeros((particle_count,) + tensor.shape[1:], tensor.dtype)
        return blank.at[slot_index].set(tensor, mode="drop")

    gathered = collect(activations, "tp", 2)
    inputs = gathered.astype(jnp.float32)
    normed = (
        inputs * lax.rsqrt(jnp.mean(inputs * inputs, -1, keepdims=True) + 1e-05) * norm_gain
    ).astype(jnp.bfloat16)
    flat_rows = normed.reshape(step_count * particle_count, D)
    positions = (span_old + jnp.arange(step_count, dtype=jnp.int32)).astype(jnp.float32)
    queries = jnp.dot(flat_rows, w_query, preferred_element_type=jnp.float32).reshape(
        step_count, particle_count, q_local, HD
    )
    queries = rotate(queries, positions).astype(jnp.bfloat16)
    fresh_keys = jnp.dot(flat_rows, w_key, preferred_element_type=jnp.float32).reshape(
        step_count, particle_count, kv_local, HD
    )
    fresh_keys = (
        rotate(fresh_keys, positions)
        .astype(jnp.bfloat16)
        .reshape(step_count, particle_count, kv_local * HD)
    )
    fresh_values = jnp.dot(flat_rows, value_weight, preferred_element_type=jnp.float32).astype(
        jnp.bfloat16
    )
    fresh_values = fresh_values.reshape(step_count, particle_count, kv_local * HD)
    fresh_keys = jnp.transpose(fresh_keys, (1, 0, 2))
    fresh_values = jnp.transpose(fresh_values, (1, 0, 2))
    key_rows = jnp.concatenate([cache_keys, fresh_keys], 1)
    value_rows = jnp.concatenate([cache_values, fresh_values], 1)
    key_span = span_old + step_count
    query_heads = queries.reshape(step_count, particle_count, kv_local, group_size, HD)
    key_heads = key_rows.reshape(particle_count, key_span, kv_local, HD)
    value_heads = value_rows.reshape(particle_count, key_span, kv_local, HD)
    scores = (
        jnp.einsum("snkgd,nlkd->snkgl", query_heads, key_heads, preferred_element_type=jnp.float32)
        / HD**0.5
    )
    allowed = (
        jnp.arange(key_span, dtype=jnp.int32)[None, :]
        <= (span_old + jnp.arange(step_count, dtype=jnp.int32))[:, None]
    )
    allowed = allowed[:, None, None, None, :]
    masked = jnp.where(allowed, scores, -jnp.inf)
    highest = jnp.max(masked, -1, keepdims=True)
    exponent = jnp.exp(masked - highest)
    weights = (exponent / jnp.sum(exponent, -1, keepdims=True)).astype(jnp.bfloat16)
    context = jnp.einsum(
        "snkgl,nlkd->snkgd", weights, value_heads, preferred_element_type=jnp.float32
    ).astype(jnp.bfloat16)
    context = context.reshape(step_count * particle_count, q_local * HD)
    partial_value = jnp.dot(context, w_output, preferred_element_type=jnp.float32).reshape(
        step_count, particle_count, D
    )
    head_mix = summed_on_arrival(partial_value, "tp", 2)
    attn_out = head_mix.astype(jnp.bfloat16)
    summed = activations.astype(jnp.float32) + head_mix
    aligned, energy = in_one((jnp.sum(summed * twist_vec, -1), jnp.sum(summed * summed, -1)), "tp")
    twisting_score = aligned / jnp.sqrt(energy / D + 1e-06)
    token_reward = twisting_table[tokens].astype(jnp.float32)
    particle_log_weight = previous_log_weights + jnp.sum(token_reward + twisting_score, 0)
    local_top = jnp.max(particle_log_weight)
    local_mass = jnp.sum(jnp.exp(particle_log_weight - local_top))
    largest, mass_total = joined_all((local_top, local_mass), "dom", join_mass)
    out_logw = particle_log_weight - (largest + jnp.log(mass_total))
    moved_keys, moved_values, arrived = (
        lax.all_to_all(pack_rows(key_rows), "dom", split_axis=0, concat_axis=0, tiled=True),
        lax.all_to_all(pack_rows(value_rows), "dom", split_axis=0, concat_axis=0, tiled=True),
        lax.all_to_all(arrival, "dom", split_axis=0, concat_axis=0, tiled=True),
    )
    slot_index = arrived.astype(jnp.int32)
    new_keys = place_rows(moved_keys, slot_index)
    new_values = place_rows(moved_values, slot_index)
    return (attn_out, new_keys, new_values, out_logw)


def solution(mesh):
    return jax.shard_map(
        local,
        mesh=mesh,
        in_specs=(
            P(None, "dom", "tp"),
            P(),
            P(None, "tp"),
            P(None, "tp"),
            P(None, "tp"),
            P("tp", None),
            P("dom", None, "tp"),
            P("dom", None, "tp"),
            P(None, "dom"),
            P(),
            P("tp"),
            P("dom"),
            P("dom"),
        ),
        out_specs=(P(None, "dom", "tp"), P("dom", None, "tp"), P("dom", None, "tp"), P("dom")),
        check_vma=False,
    )
```

profile of v0, /device:TPU:1, one launch (start us, length us, event | category | flops | bytes accessed | tf_op | source)
XLA Modules:
  0.0 203.3 jit_solution(14204163190005590366)
XLA Ops:
  0.6 1.8 broadcast_in_dim.46
  2.4 9.0 %all-to-all-start = ((bf16[8,4,16,512]{3,2,1,0:T(8,128)(2,1)}), bf16[8,4,16,512]{3,2,1,0:T(8,128)(2,1)S(1)}, u32[]{:S(2)}, u32[]{:S(2)}) async-start(bf16[8,4,16,512]{3,2,1,0:T(8,128)(2,1)} %broadcast_in_dim.46), calls=%async_computation | async-start | bytes 1048576 | tf_op jit(solution)/shard_map/all_to_all | solution.py:12
  12.2 6.5 %copy.100 = bf16[512,4096]{1,0:T(8,128)(2,1)} copy(bf16[512,4096]{0,1:T(8,128)(2,1)} %bitcast.89) | data formatting | bytes 8388608 | tf_op jit(solution)/shard_map/dot_general | solution.py:174
  18.6 6.5 %copy.103 = bf16[4096,512]{1,0:T(8,128)(2,1)} copy(bf16[4096,512]{0,1:T(8,128)(2,1)} %bitcast.90) | data formatting | bytes 8388608 | tf_op jit(solution)/shard_map/dot_general | solution.py:215
  26.3 3.1 %all-to-all-done = bf16[8,4,16,512]{3,2,1,0:T(8,128)(2,1)S(1)} async-done(((bf16[8,4,16,512]{3,2,1,0:T(8,128)(2,1)}), bf16[8,4,16,512]{3,2,1,0:T(8,128)(2,1)S(1)}, u32[]{:S(2)}, u32[]{:S(2)}) %all-to-all-start) | async-done | bytes 524320 | tf_op jit(solution)/shard_map/all_to_all | solution.py:12
  30.7 7.6 %all-to-all-start.2 = ((s32[32,1,1]{2,1,0:T(1,128)}), s32[32,1,1]{2,1,0:T(1,128)S(1)}, u32[]{:S(2)}, u32[]{:S(2)}) async-start(s32[32,1,1]{2,1,0:T(1,128)} %broadcast_in_dim.49), calls=%async_computation.2 | async-start | bytes 32768 | tf_op jit(solution)/shard_map/all_to_all | solution.py:12
  41.9 3.8 %fusion.10 = f32[4,16,4,128]{3,1,2,0:T(8,128)S(1)} fusion(bf16[4,128,4096,1]{2,1,0,3:T(8,128)(2,1)} %bitcast.92, bf16[4,16,4096,1]{2,1,0,3:T(8,128)(2,1)} %reshape.622), kind=kOutput, calls=%fused_computation.29 | convolution fusion | flops 268435456 | bytes 4849664 | tf_op jit(solution)/shard_map/dot_general | solution.py:174
  49.0 3.6 %convolution_bitcast_fusion = f32[8,4,16,512]{3,2,0,1:T(8,128)S(1)} fusion(bf16[8,512,512,1]{2,1,0,3:T(8,128)(2,1)} %bitcast.91, bf16[4,16,512,1]{2,0,1,3:T(4,128)(2,1)S(1)} %bitcast.97), kind=kOutput, calls=%fused_computation.11 | convolution fusion | flops 268435456 | bytes 5308416 | tf_op jit(solution)/shard_map/dot_general | solution.py:215
  53.6 4.4 %all-to-all-start.1 = ((f32[8,4,16,512]{3,2,1,0:T(8,128)}), f32[8,4,16,512]{3,2,1,0:T(8,128)S(1)}, u32[]{:S(2)}, u32[]{:S(2)}) async-start(f32[8,4,16,512]{3,2,1,0:T(8,128)} %copy.91), calls=%async_computation.1 | async-start | bytes 2097152 | tf_op jit(solution)/shard_map/all_to_all | solution.py:56
  64.6 22.7 %all-to-all-done.1 = f32[8,4,16,512]{3,2,1,0:T(8,128)S(1)} async-done(((f32[8,4,16,512]{3,2,1,0:T(8,128)}), f32[8,4,16,512]{3,2,1,0:T(8,128)S(1)}, u32[]{:S(2)}, u32[]{:S(2)}) %all-to-all-start.1) | async-done | bytes 1048608 | tf_op jit(solution)/shard_map/all_to_all | solution.py:56
  88.9 3.3 %all-to-all-start.6 = ((f32[8,1,128]{2,1,0:T(1,128)}), f32[8,1,128]{2,1,0:T(1,128)S(1)}, u32[]{:S(2)}, u32[]{:S(2)}) async-start(f32[8,1,128]{2,1,0:T(1,128)} %broadcast_in_dim.60), calls=%async_computation.6 | async-start | bytes 8192 | tf_op jit(solution)/shard_map/all_to_all | solution.py:12
  92.3 2.2 %gather_fusion = bf16[64,132,128]{2,1,0:T(8,128)(2,1)} fusion(bf16[16,132,128]{2,1,0:T(8,128)(2,1)S(1)} %copy_dynamic-update-slice_fusion, s32[1024]{0:T(1024)S(1)} %pad_clamp_fusion.1), kind=kCustom, calls=%fused_computation | custom fusion | bytes 4325632 | tf_op jit(solution)/shard_map/gather | solution.py:161
  94.5 2.2 %gather_fusion.1 = bf16[64,132,128]{2,1,0:T(8,128)(2,1)} fusion(bf16[16,132,128]{2,1,0:T(8,128)(2,1)S(1)} %pad_maximum_fusion, s32[1024]{0:T(1024)S(1)} %pad_clamp_fusion.1), kind=kCustom, calls=%fused_computation.1 | custom fusion | bytes 4325632 | tf_op jit(solution)/shard_map/gather | solution.py:161
  96.8 1.9 all-to-all-done.6
  98.6 8.7 %all-to-all-start.3 = ((bf16[32,2,1]{1,2,0:T(2,128)(2,1)}), bf16[32,2,1]{1,2,0:T(2,128)(2,1)S(1)}, u32[]{:S(2)}, u32[]{:S(2)}) async-start(bf16[32,2,1]{1,2,0:T(2,128)(2,1)} %fusion.25), calls=%async_computation.3 | async-start | bytes 32768 | tf_op jit(solution)/shard_map/all_to_all | solution.py:232
  110.7 3.4 %all-to-all-done.3 = bf16[32,2,1]{1,2,0:T(2,128)(2,1)S(1)} async-done(((bf16[32,2,1]{1,2,0:T(2,128)(2,1)}), bf16[32,2,1]{1,2,0:T(2,128)(2,1)S(1)}, u32[]{:S(2)}, u32[]{:S(2)}) %all-to-all-start.3) | async-done | bytes 160 | tf_op jit(solution)/shard_map/all_to_all | solution.py:232
  114.8 4.1 %all-to-all-start.7 = ((f32[32,2,1]{1,2,0:T(1,128)}), f32[32,2,1]{1,2,0:T(1,128)S(1)}, u32[]{:S(2)}, u32[]{:S(2)}) async-start(f32[32,2,1]{1,2,0:T(1,128)} %broadcast_in_dim.103), calls=%async_computation.7 | async-start | bytes 32768 | tf_op jit(solution)/shard_map/all_to_all | solution.py:12
  118.9 4.7 %broadcast_select_fusion = (bf16[64,132,128]{2,1,0:T(8,128)(2,1)}, bf16[64,132,128]{2,1,0:T(8,128)(2,1)}) fusion(bf16[64,132,128]{2,1,0:T(8,128)(2,1)} %gather_fusion.1, pred[64]{0:T(512)(128)(4,1)S(1)} %broadcast_compare_fusion, bf16[64,132,128]{2,1,0:T(8,128)(2,1)} %gather_fusion), kind=kLoop, calls=%fused_computation.5 | loop fusion | flops 2162688 | bytes 8650816 | tf_op jit(solution)/shard_map/jit(_where)/select_n | solution.py:161
  123.6 2.3 %all-to-all-done.7 = f32[32,2,1]{1,2,0:T(1,128)S(1)} async-done(((f32[32,2,1]{1,2,0:T(1,128)}), f32[32,2,1]{1,2,0:T(1,128)S(1)}, u32[]{:S(2)}, u32[]{:S(2)}) %all-to-all-start.7) | async-done | bytes 288 | tf_op jit(solution)/shard_map/all_to_all | solution.py:12
  125.9 35.5 %all_to_all.46 = bf16[64,132,128]{2,1,0:T(8,128)(2,1)} all-to-all(bf16[64,132,128]{2,1,0:T(8,128)(2,1)} %get-tuple-element.55), channel_id=1, replica_groups=mesh['dom'=32,'tp'=8] {'dom'}, dimensions={0} | all-to-all | bytes 4325376 | tf_op jit(solution)/shard_map/all_to_all | solution.py:231
  161.4 4.8 %all-to-all-start.4 = ((bf16[64,132,128]{2,1,0:T(8,128)(2,1)}), bf16[64,132,128]{2,1,0:T(8,128)(2,1)}, u32[]{:S(2)}, u32[]{:S(2)}) async-start(bf16[64,132,128]{2,1,0:T(8,128)(2,1)} %get-tuple-element.56), calls=%async_computation.4 | async-start | bytes 4456448 | tf_op jit(solution)/shard_map/all_to_all | solution.py:230
  173.9 6.8 %scatter_fusion.1 = bf16[16,132,128]{2,1,0:T(8,128)(2,1)S(1)} fusion(bf16[16,132,128]{2,1,0:T(8,128)(2,1)S(1)} %broadcast.540.clone.1, s32[64]{0:T(128)S(1)} %fusion.31, bf16[64,132,128]{2,1,0:T(8,128)(2,1)} %all_to_all.46), kind=kCustom, calls=%fused_computation.4 | custom fusion | bytes 6488320 | tf_op jit(solution)/shard_map/scatter | solution.py:165
  181.5 14.0 %all-to-all-done.4 = bf16[64,132,128]{2,1,0:T(8,128)(2,1)} async-done(((bf16[64,132,128]{2,1,0:T(8,128)(2,1)}), bf16[64,132,128]{2,1,0:T(8,128)(2,1)}, u32[]{:S(2)}, u32[]{:S(2)}) %all-to-all-start.4) | async-done | bytes 2162720 | tf_op jit(solution)/shard_map/all_to_all | solution.py:230
  195.6 6.8 %scatter_fusion = bf16[16,132,128]{2,1,0:T(8,128)(2,1)S(1)} fusion(bf16[16,132,128]{2,1,0:T(8,128)(2,1)S(1)} %broadcast.540.clone, s32[64]{0:T(128)S(1)} %fusion.31, bf16[64,132,128]{2,1,0:T(8,128)(2,1)} %all-to-all-done.4), kind=kCustom, calls=%fused_computation.3 | custom fusion | bytes 6488320 | tf_op jit(solution)/shard_map/scatter | solution.py:165
  (130 shorter events, 27.3 us)
Async XLA Ops:
  0.6 40.9 %copy-start = (bf16[4096,128]{1,0:T(8,128)(2,1)S(1)}, bf16[4096,128]{1,0:T(8,128)(2,1)}, u32[]{:S(2)}) copy-start(bf16[4096,128]{1,0:T(8,128)(2,1)} %param.16) | copy-start | bytes 3145732
  2.4 27.0 %all-to-all-start = ((bf16[8,4,16,512]{3,2,1,0:T(8,128)(2,1)}), bf16[8,4,16,512]{3,2,1,0:T(8,128)(2,1)S(1)}, u32[]{:S(2)}, u32[]{:S(2)}) async-start(bf16[8,4,16,512]{3,2,1,0:T(8,128)(2,1)} %broadcast_in_dim.46), calls=%async_computation | async-start | bytes 1048576 | tf_op jit(solution)/shard_map/all_to_all | solution.py:12
  18.6 6.5 %copy-start.10 = (s32[16]{0:T(128)S(1)}, s32[16]{0:T(128)}, u32[]{:S(2)}) copy-start(s32[16]{0:T(128)} %param.25) | copy-start | bytes 196
  18.6 6.8 %copy-start.4 = (bf16[16,128,128]{2,1,0:T(8,128)(2,1)S(1)}, bf16[16,128,128]{2,1,0:T(8,128)(2,1)}, u32[]{:S(2)}) copy-start(bf16[16,128,128]{2,1,0:T(8,128)(2,1)} %param.19) | copy-start | bytes 1572868
  30.7 23.0 %all-to-all-start.2 = ((s32[32,1,1]{2,1,0:T(1,128)}), s32[32,1,1]{2,1,0:T(1,128)S(1)}, u32[]{:S(2)}, u32[]{:S(2)}) async-start(s32[32,1,1]{2,1,0:T(1,128)} %broadcast_in_dim.49), calls=%async_computation.2 | async-start | bytes 32768 | tf_op jit(solution)/shard_map/all_to_all | solution.py:12
  39.8 1.7 copy-start.7
  41.9 4.1 %copy-start.2 = (f32[4,16,8,512]{3,1,0,2:T(8,128)S(1)}, f32[4,16,8,512]{3,1,0,2:T(8,128)}, u32[]{:S(2)}) copy-start(f32[4,16,8,512]{3,1,0,2:T(8,128)} %get-tuple-element.42) | copy-start | bytes 3145732
  45.8 1.4 copy-start.3
  47.2 1.5 copy-start.5
  52.5 5.5 %copy-start.9 = (s32[4,16]{1,0:T(4,128)S(1)}, s32[4,16]{1,0:T(4,128)}, u32[]{:S(2)}) copy-start(s32[4,16]{1,0:T(4,128)} %param.21) | copy-start | bytes 772
  52.6 5.6 %copy-start.1 = (bf16[128256]{0:T(1024)(128)(2,1)S(1)}, bf16[128256]{0:T(1024)(128)(2,1)}, u32[]{:S(2)}) copy-start(bf16[128256]{0:T(1024)(128)(2,1)} %param.22) | copy-start | bytes 769540
  53.6 33.8 %copy-start.6 = (bf16[4,16,512]{2,1,0:T(8,128)(2,1)S(1)}, bf16[4,16,512]{2,1,0:T(8,128)(2,1)}, u32[]{:S(2)}) copy-start(bf16[4,16,512]{2,1,0:T(8,128)(2,1)} %param.13) | copy-start | bytes 196612
  53.6 33.8 %copy-start.8 = (f32[512]{0:T(512)S(1)}, f32[512]{0:T(512)}, u32[]{:S(2)}) copy-start(f32[512]{0:T(512)} %param.23) | copy-start | bytes 6148
  53.6 33.7 %all-to-all-start.1 = ((f32[8,4,16,512]{3,2,1,0:T(8,128)}), f32[8,4,16,512]{3,2,1,0:T(8,128)S(1)}, u32[]{:S(2)}, u32[]{:S(2)}) async-start(f32[8,4,16,512]{3,2,1,0:T(8,128)} %copy.91), calls=%async_computation.1 | async-start | bytes 2097152 | tf_op jit(solution)/shard_map/all_to_all | solution.py:56
  88.9 9.7 %all-to-all-start.6 = ((f32[8,1,128]{2,1,0:T(1,128)}), f32[8,1,128]{2,1,0:T(1,128)S(1)}, u32[]{:S(2)}, u32[]{:S(2)}) async-start(f32[8,1,128]{2,1,0:T(1,128)} %broadcast_in_dim.60), calls=%async_computation.6 | async-start | bytes 8192 | tf_op jit(solution)/shard_map/all_to_all | solution.py:12
  94.5 13.0 %copy-start.11 = (f32[16]{0:T(128)S(1)}, f32[16]{0:T(128)}, u32[]{:S(2)}) copy-start(f32[16]{0:T(128)} %param.24) | copy-start | bytes 196
  98.6 15.5 %all-to-all-start.3 = ((bf16[32,2,1]{1,2,0:T(2,128)(2,1)}), bf16[32,2,1]{1,2,0:T(2,128)(2,1)S(1)}, u32[]{:S(2)}, u32[]{:S(2)}) async-start(bf16[32,2,1]{1,2,0:T(2,128)(2,1)} %fusion.25), calls=%async_computation.3 | async-start | bytes 32768 | tf_op jit(solution)/shard_map/all_to_all | solution.py:232
  114.8 11.1 %all-to-all-start.7 = ((f32[32,2,1]{1,2,0:T(1,128)}), f32[32,2,1]{1,2,0:T(1,128)S(1)}, u32[]{:S(2)}, u32[]{:S(2)}) async-start(f32[32,2,1]{1,2,0:T(1,128)} %broadcast_in_dim.103), calls=%async_computation.7 | async-start | bytes 32768 | tf_op jit(solution)/shard_map/all_to_all | solution.py:12
  161.4 34.2 %all-to-all-start.4 = ((bf16[64,132,128]{2,1,0:T(8,128)(2,1)}), bf16[64,132,128]{2,1,0:T(8,128)(2,1)}, u32[]{:S(2)}, u32[]{:S(2)}) async-start(bf16[64,132,128]{2,1,0:T(8,128)(2,1)} %get-tuple-element.56), calls=%async_computation.4 | async-start | bytes 4456448 | tf_op jit(solution)/shard_map/all_to_all | solution.py:230
where the time goes:
time: 205 us; the launch traced here: 203 us
  waiting for transfers between devices  47.4 us (23%)
  local copies, waits for them, and re-layouts  47.3 us (23%)
  starting transfers between devices  41.9 us (20%)
  blocking collectives  35.5 us (17%)
  other arithmetic  15.8 us (8%)
  matrix products  8.98 us (4%)
  between operations  6.42 us (3%)
    all_to_all x1, blocking collectives, local(): lax.all_to_all(pack_rows(value_rows), 'dom', split_axis=0, concat_axis=0,...  35.5 us
    all_to_all x4, starting transfers between devices, copy_for_each(): lax.all_to_all(jnp.broadcast_to(value[None], (length, *value.shape)), axi...  24 us
    all_to_all x1, waiting for transfers between devices, summed_on_arrival(): lax.all_to_all(in_blocks(value, dim, length), axis, 0, 0, tiled=True)  22.7 us
    all_to_all x1, waiting for transfers between devices, local(): lax.all_to_all(pack_rows(key_rows), 'dom', split_axis=0, concat_axis=0, t...  14 us
    scatter x2, local copies, waits for them, and re-layouts, place_rows(): return blank.at[slot_index].set(tensor, mode='drop')  13.5 us
    all_to_all x1, starting transfers between devices, local(): lax.all_to_all(arrival, 'dom', split_axis=0, concat_axis=0, tiled=True)  8.65 us
    all_to_all x4, waiting for transfers between devices, copy_for_each(): lax.all_to_all(jnp.broadcast_to(value[None], (length, *value.shape)), axi...  7.24 us
    dot_general x2, local copies, waits for them, and re-layouts, local(): jnp.dot(context, w_output, preferred_element_type=jnp.float32)  6.56 us
  transfers between devices with their start and end apart: 7, of which 6 were waited for; matrix products, arithmetic and copies ran while one was open for 29% of the time, Pallas kernels for 0%

commit v1 on v0

v1 whole, which is shorter than its diff:
```python
import jax
import jax.numpy as jnp
import numpy as np
from jax import lax
from jax.experimental import pallas as pl
from jax.experimental.pallas import tpu as pltpu
from jax.sharding import PartitionSpec as P

D = 4096
HD = 128
STEPS = 4
NP = 16
ROWS = STEPS * NP
SPAN = 128
TP = 8
DB = D // TP
NDOM = 32
NCHIP = 16
SLOTS = 3
BF = jnp.bfloat16
F32 = jnp.float32
ANY = pl.ANY
VM = pltpu.VMEM
SM = pltpu.SMEM


def spec(space):
    return pl.BlockSpec(memory_space=space)


def nt(a, b):
    return lax.dot_general(a, b, (((1,), (1,)), ((), ())), preferred_element_type=F32)


def mm(a, b):
    return jnp.dot(a, b, preferred_element_type=F32)


def layer_body(blk, *refs):
    acts = refs[:TP]
    gain, wq, wk, wv, wo, kc, vc, table = refs[TP : TP + 8]
    outs = refs[TP + 8 : 2 * TP + 8]
    fresh = refs[2 * TP + 8]
    wq_s, wk_s, wv_s, wo_s, q_s, qa_s, s1_s, ctx_s, kf_s, vf_s, sems = refs[2 * TP + 9 :]

    def loads(s):
        src = pl.multiple_of(blk[s] * DB, DB)
        dst = pl.multiple_of(blk[TP + s] * DB, DB)
        return (
            pltpu.make_async_copy(wq.at[pl.ds(src, DB), :], wq_s.at[s], sems.at[0, s]),
            pltpu.make_async_copy(wk.at[pl.ds(src, DB), :], wk_s.at[s], sems.at[1, s]),
            pltpu.make_async_copy(wv.at[pl.ds(src, DB), :], wv_s.at[s], sems.at[2, s]),
            pltpu.make_async_copy(wo.at[:, pl.ds(dst, DB)], wo_s.at[s], sems.at[3, s]),
        )

    copies = [loads(s) for s in range(TP)]
    for s in range(TP):
        for c in copies[s][:3]:
            c.start()
    for s in range(TP):
        copies[s][3].start()

    square = jnp.zeros((ROWS, 1), F32)
    for s in range(TP):
        x = acts[s][...].astype(F32)
        square = square + jnp.sum(x * x, -1, keepdims=True)
    inv = lax.rsqrt(square / D + 1e-05)
    q = jnp.zeros((ROWS, DB), F32)
    k = jnp.zeros((ROWS, HD), F32)
    v = jnp.zeros((ROWS, HD), F32)
    for s in range(TP):
        x = acts[s][...].astype(F32)
        normed = (x * inv * gain[pl.ds(blk[s], 1), :]).astype(BF)
        for c in copies[s][:3]:
            c.wait()
        q = q + mm(normed, wq_s[s])
        k = k + mm(normed, wk_s[s])
        v = v + mm(normed, wv_s[s])
    cosine = table[0]
    sine = table[1]

    def turned(u):
        return (u * cosine + pltpu.roll(u, HD // 2, 1) * sine).astype(BF)

    heads = DB // HD
    for g in range(heads):
        q_s[g] = turned(q[:, g * HD : (g + 1) * HD]).astype(F32)
    kf = turned(k)
    vf = v.astype(BF)
    kf_s[...] = kf.astype(F32)
    vf_s[...] = vf.astype(F32)
    group = heads * STEPS
    for n in range(NP):
        mine = pl.ds(n, STEPS, stride=NP)
        fresh[n] = jnp.concatenate([kf_s[mine, :], vf_s[mine, :]], 0).astype(BF)
        qn = jnp.concatenate(
            [q_s[g, mine, :] for g in range(heads)], 0
        ).astype(BF)
        qa_s[n * group : (n + 1) * group, :] = qn
        s1_s[n * group : (n + 1) * group, :] = nt(qn, kc[n])
    scale = 1.0 / HD**0.5
    s1 = s1_s[...] * scale
    s2 = nt(qa_s[...], kf) * scale
    row = lax.broadcasted_iota(jnp.int32, (NP * group, ROWS), 0)
    col = lax.broadcasted_iota(jnp.int32, (NP * group, ROWS), 1)
    seen = ((row // group) == (col % NP)) & ((col // NP) <= (row % STEPS))
    s2 = jnp.where(seen, s2, -jnp.inf)
    top = jnp.maximum(jnp.max(s1, -1, keepdims=True), jnp.max(s2, -1, keepdims=True))
    e1 = jnp.exp(s1 - top)
    e2 = jnp.exp(s2 - top)
    total = jnp.sum(e1, -1, keepdims=True) + jnp.sum(e2, -1, keepdims=True)
    w1 = (e1 / total).astype(BF)
    w2 = (e2 / total).astype(BF)
    c2 = mm(w2, vf)
    for n in range(NP):
        span = slice(n * group, (n + 1) * group)
        cn = (mm(w1[span], vc[n]) + c2[span]).astype(BF).astype(F32)
        for g in range(heads):
            ctx_s[g, pl.ds(n, STEPS, stride=NP), :] = cn[
                g * STEPS : (g + 1) * STEPS
            ]
    ctx = jnp.concatenate([ctx_s[g] for g in range(heads)], 1).astype(BF)
    for s in range(TP):
        copies[s][3].wait()
        outs[s][...] = mm(ctx, wo_s[s]).astype(BF)


def layer(blk, acts, gain, wq, wk, wv, wo, kc, vc, table):
    sd = jax.ShapeDtypeStruct
    return pl.pallas_call(
        layer_body,
        in_specs=[spec(SM)] + [spec(VM)] * TP + [spec(VM)] + [spec(ANY)] * 4 + [spec(VM)] * 3,
        out_specs=[spec(VM)] * (TP + 1),
        out_shape=[sd((ROWS, DB), BF)] * TP + [sd((NP, 2 * STEPS, HD), BF)],
        scratch_shapes=[
            VM((TP, DB, DB), BF),
            VM((TP, DB, HD), BF),
            VM((TP, DB, HD), BF),
            VM((TP, DB, DB), BF),
            VM((DB // HD, ROWS, HD), F32),
            VM((NP * 16, HD), BF),
            VM((NP * 16, SPAN), F32),
            VM((DB // HD, ROWS, HD), F32),
            VM((ROWS, HD), F32),
            VM((ROWS, HD), F32),
            pltpu.SemaphoreType.DMA((4, TP)),
        ],
        compiler_params=pltpu.CompilerParams(vmem_limit_bytes=40 * 2**20),
        cost_estimate=pl.CostEstimate(
            flops=2 * ROWS * D * 1280, bytes_accessed=12 * 2**20, transcendentals=NP * 16 * 192
        ),
        name="layer",
    )(blk, *acts, gain, wq, wk, wv, wo, kc, vc, table)


def mix_body(*refs):
    parts = refs[:TP]
    act, twist, attn, sums = refs[TP:]
    mix = parts[0][...].astype(F32)
    for s in range(1, TP):
        mix = mix + parts[s][...].astype(F32)
    attn[...] = mix.astype(BF)
    summed = act[...].astype(F32) + mix
    aligned = jnp.sum(summed * twist[...], -1, keepdims=True)
    energy = jnp.sum(summed * summed, -1, keepdims=True)
    lane = lax.broadcasted_iota(jnp.int32, (ROWS, HD), 1)
    sums[...] = jnp.where(lane == 0, aligned, energy)


def mix(parts, act, twist):
    sd = jax.ShapeDtypeStruct
    return pl.pallas_call(
        mix_body,
        in_specs=[spec(VM)] * (TP + 2),
        out_specs=[spec(VM)] * 2,
        out_shape=[sd((ROWS, DB), BF), sd((ROWS, HD), F32)],
        name="mix",
    )(*parts, act, twist)


def weigh_body(*refs):
    parts = refs[:TP]
    reward, previous, out = refs[TP:]
    sums = parts[0][...]
    for s in range(1, TP):
        sums = sums + parts[s][...]
    score = sums[:, 0:1] / jnp.sqrt(sums[:, 1:2] / D + 1e-06) + reward[...]
    gain = score[0:NP]
    for t in range(1, STEPS):
        gain = gain + score[t * NP : (t + 1) * NP]
    out[...] = jnp.broadcast_to(previous[...] + gain, (NP, HD))


def weigh(parts, reward, previous):
    return pl.pallas_call(
        weigh_body,
        in_specs=[spec(VM)] * (TP + 2),
        out_specs=spec(VM),
        out_shape=jax.ShapeDtypeStruct((NP, HD), F32),
        name="weigh",
    )(*parts, reward, previous)


def plan_body(me_ref, counts_ref, out):
    me = me_ref[0]
    counts = counts_ref[...].astype(F32)
    r16 = lax.broadcasted_iota(jnp.int32, (NP, NP), 0)
    c16 = lax.broadcasted_iota(jnp.int32, (NP, NP), 1)
    within = mm(counts, (r16 <= c16).astype(F32))
    r32 = lax.broadcasted_iota(jnp.int32, (NDOM, NDOM), 0)
    c32 = lax.broadcasted_iota(jnp.int32, (NDOM, NDOM), 1)
    before = jnp.sum(mm((c32 < r32).astype(F32), counts), -1, keepdims=True)
    ends = (within + before).astype(jnp.int32)
    before = before.astype(jnp.int32)
    device = lax.broadcasted_iota(jnp.int32, (NDOM, 1), 0)
    chip_end = jnp.where(device % 2 == 1, ends[:, NP - 1 : NP], -1)
    chip = me // 2
    first = jnp.sum(jnp.where(device == 2 * chip, before, 0))
    lane = lax.broadcasted_iota(jnp.int32, (1, HD), 1)
    dest = 2 * (lane // 4) + me % 2
    sent = first + ((dest - first) & (NDOM - 1)) + NDOM * (lane % 4)
    kept = NDOM * (lane - 64) + me
    found = jnp.zeros((NDOM, HD), jnp.int32)
    for j in range(NP):
        found = found + (ends[:, j : j + 1] <= sent).astype(jnp.int32)
    particle = jnp.sum(found, 0, keepdims=True) - 2 * NP * chip
    particle = jnp.clip(particle, 0, 2 * NP - 1)
    passed = (chip_end >= 0) & (chip_end <= kept)
    source = jnp.sum(passed.astype(jnp.int32), 0, keepdims=True)
    base = jnp.max(jnp.where(passed, chip_end, 0), 0, keepdims=True)
    slot = jnp.clip((kept - base) // NDOM, 0, 3)
    arrived = 4 * jnp.clip(source, 0, NCHIP - 1) + slot
    owned = jnp.sum(counts, -1, keepdims=True).astype(jnp.int32)
    pair = lax.broadcasted_iota(jnp.int32, (NDOM, HD), 1)
    most = jnp.max(jnp.sum(jnp.where(pair == device // 2, owned, 0), 0, keepdims=True))
    line = jnp.where(lane < 64, particle, jnp.where(lane < 80, arrived, most))
    out[...] = jnp.broadcast_to(line, (8, HD))


def plan(me, counts):
    return pl.pallas_call(
        plan_body,
        in_specs=[spec(SM), spec(VM)],
        out_specs=spec(VM),
        out_shape=jax.ShapeDtypeStruct((8, HD), jnp.int32),
        name="plan",
    )(me, counts)


def pack_body(me_ref, idx, *refs):
    half = (len(refs) - 3) // 2
    own, partner = (refs[:half], refs[half : 2 * half])
    out, rows, sems = refs[2 * half :]
    core = me_ref[0] % 2
    loads, at = ([], 0)
    for n in range(half):
        length = own[n].shape[1]
        for side, ref in ((core, own[n]), (1 - core, partner[n])):
            there = rows.at[pl.ds(side * NP, NP), pl.ds(at, length), :]
            loads.append(pltpu.make_async_copy(ref, there, sems.at[len(loads) + 1]))
        at += length
    for c in loads:
        c.start()
    for c in loads:
        c.wait()
    for q in range(NCHIP):
        for s in range(SLOTS):
            pltpu.make_async_copy(rows.at[idx[0, 4 * q + s]], out.at[q, s], sems.at[0]).start()
    pltpu.make_async_copy(out, out, sems.at[0]).wait()


def pack(me, idx, own, partner):
    length = sum(a.shape[1] for a in own)
    return pl.pallas_call(
        pack_body,
        in_specs=[spec(SM), spec(SM)] + [spec(ANY)] * (2 * len(own)),
        out_specs=spec(ANY),
        out_shape=jax.ShapeDtypeStruct((NCHIP, SLOTS, length, HD), BF),
        scratch_shapes=[
            VM((2 * NP, length, HD), BF),
            pltpu.SemaphoreType.DMA((1 + 2 * len(own),)),
        ],
        name="pack",
    )(me, idx, *own, *partner)


def place_body(slots, idx, first, second, keys, values, k_s, v_s, sems):
    copies = []
    for k in range(NP):
        code = idx[0, 64 + k]
        chip = code // 4
        slot = jnp.minimum(code % 4, slots - 1)
        copies.append(pltpu.make_async_copy(first.at[chip, slot], k_s.at[k], sems.at[0, k]))
        copies.append(pltpu.make_async_copy(second.at[chip, slot], v_s.at[k], sems.at[1, k]))
    for c in copies:
        c.start()
    for k in range(NP):
        copies[2 * k].wait()
        copies[2 * k + 1].wait()
        keys[k, 0:SPAN, :] = k_s[k]
        values[k, 0:SPAN, :] = v_s[k, 0:SPAN, :]
        tail = v_s[k, SPAN : SPAN + 2 * STEPS, :].astype(F32)
        keys[k, SPAN : SPAN + STEPS, :] = tail[0:STEPS].astype(BF)
        values[k, SPAN : SPAN + STEPS, :] = tail[STEPS : 2 * STEPS].astype(BF)


def place(idx, first, second):
    out = jax.ShapeDtypeStruct((NP, SPAN + STEPS, HD), BF)
    slots = first.shape[1]
    return pl.pallas_call(
        lambda *refs: place_body(slots, *refs),
        in_specs=[spec(SM), spec(ANY), spec(ANY)],
        out_specs=[spec(VM)] * 2,
        out_shape=[out] * 2,
        scratch_shapes=[
            VM((NP, SPAN, HD), BF),
            VM((NP, SPAN + 2 * STEPS, HD), BF),
            pltpu.SemaphoreType.DMA((2, NP)),
        ],
        name="place",
    )(idx, first, second)


def shifted(value, shift):
    return lax.ppermute(value, "tp", [(i, (i + shift) % TP) for i in range(TP)])


def swapped(value):
    return lax.ppermute(value, "dom", [(i, i ^ 1) for i in range(NDOM)])


SAME_CORE = [list(range(c, NDOM, 2)) for c in range(2)]


def exchanged(rows):
    return lax.all_to_all(rows, "dom", 0, 0, tiled=True, axis_index_groups=SAME_CORE)


def copy_for_each(value):
    sent = jnp.broadcast_to(value[None], (NDOM, *value.shape))
    return lax.all_to_all(sent, "dom", 0, 0, tiled=True)


def rotation_table():
    frequency = np.float32(500000.0) ** (-2.0 * np.arange(HD // 2, dtype=np.float32) / HD)
    angles = (SPAN + np.arange(STEPS, dtype=np.float32))[:, None] * frequency.astype(np.float32)
    cosine = np.concatenate([np.cos(angles), np.cos(angles)], 1)
    sine = np.concatenate([-np.sin(angles), np.sin(angles)], 1)
    return np.stack([np.repeat(cosine, NP, 0), np.repeat(sine, NP, 0)]).astype(np.float32)


def local(
    activations,
    norm_gain,
    w_query,
    w_key,
    value_weight,
    w_output,
    cache_keys,
    cache_values,
    tokens,
    twisting_table,
    twist_vec,
    previous_log_weights,
    copy_counts,
):
    dom = lax.axis_index("dom")
    tp = lax.axis_index("tp")
    me = dom.reshape(1)
    ring = np.arange(TP)
    blk = jnp.concatenate([(tp - ring) % TP, (tp + ring) % TP]).astype(jnp.int32)

    counts = copy_for_each(copy_counts)
    act = activations.reshape(ROWS, DB)
    acts = [act] + [shifted(act, s) for s in range(1, TP)]
    partner_keys = swapped(cache_keys)
    partner_values = swapped(cache_values)

    idx = plan(me, counts)
    first = exchanged(pack(me, idx, [cache_keys], [partner_keys]))

    outs = layer(
        blk,
        acts,
        norm_gain.reshape(TP, DB),
        w_query,
        w_key,
        value_weight,
        w_output,
        cache_keys,
        cache_values,
        rotation_table(),
    )
    partials, fresh = (outs[:TP], outs[TP])
    partner_fresh = swapped(fresh)
    second = exchanged(
        pack(me, idx, [cache_values, fresh], [partner_values, partner_fresh])
    )

    parts = [partials[0]] + [shifted(partials[s], s) for s in range(1, TP)]
    attn, sums = mix(parts, act, twist_vec.reshape(1, DB))
    all_sums = [sums] + [shifted(sums, s) for s in range(1, TP)]
    reward = twisting_table[tokens.reshape(ROWS)].astype(F32).reshape(ROWS, 1)
    logw = weigh(all_sums, reward, previous_log_weights.reshape(NP, 1))[:, 0]
    every = copy_for_each(logw)
    largest = jnp.max(every)
    out_logw = logw - (largest + jnp.log(jnp.sum(jnp.exp(every - largest))))

    def usual(first, second, *_):
        return tuple(place(idx, first, second))

    def crowded(first, second, partner_keys, partner_values, partner_fresh, fresh, idx):
        even = dom % 2 == 0
        mine = jnp.concatenate([cache_keys, cache_values, fresh], 1)
        other = jnp.concatenate([partner_keys, partner_values, partner_fresh], 1)
        chip_rows = jnp.concatenate(
            [jnp.where(even, mine, other), jnp.where(even, other, mine)], 0
        )
        more = exchanged(chip_rows[idx[0, 3:64:4]][:, None])
        return tuple(
            place(
                idx,
                jnp.concatenate([first, more[:, :, :SPAN]], 1),
                jnp.concatenate([second, more[:, :, SPAN:]], 1),
            )
        )

    new_keys, new_values = lax.cond(
        idx[0, 127] > SLOTS * NDOM,
        crowded,
        usual,
        first,
        second,
        partner_keys,
        partner_values,
        partner_fresh,
        fresh,
        idx,
    )
    return (attn.reshape(STEPS, NP, DB), new_keys, new_values, out_logw)


def solution(mesh):
    return jax.shard_map(
        local,
        mesh=mesh,
        in_specs=(
            P(None, "dom", "tp"),
            P(),
            P(None, "tp"),
            P(None, "tp"),
            P(None, "tp"),
            P("tp", None),
            P("dom", None, "tp"),
            P("dom", None, "tp"),
            P(None, "dom"),
            P(),
            P("tp"),
            P("dom"),
            P("dom"),
        ),
        out_specs=(P(None, "dom", "tp"), P("dom", None, "tp"), P("dom", None, "tp"), P("dom")),
        check_vma=False,
    )
```

time: 205 us -> 178 us (0.87)
  blocking collectives: 35.5 us -> 0 us
  local copies, waits for them, and re-layouts: 47.3 us -> 19.7 us
  starting transfers between devices: 41.9 us -> 68.7 us
  Pallas kernels: 0 us -> 22.1 us
  other arithmetic: 15.8 us -> 3.8 us
  waiting for transfers between devices: 47.4 us -> 59.3 us
  matrix products: 8.98 us -> 0 us
  between operations: 6.42 us -> 2.89 us
    ppermute x0 -> x24, starting transfers between devices: none -> 43.5 us  [the longest x21 40.8 us: shifted(): return lax.ppermute(value, 'tp', [(i, (i + shift) % TP) for i in range(TP)])]
    all_to_all x1 -> x0, blocking collectives: 35.5 us -> none  [local(): lax.all_to_all(pack_rows(value_rows), 'dom', split_axis=0, concat_axis=0,...]
    pallas_call x0 -> x7, Pallas kernels: none -> 22.1 us  [the longest x1 10 us: layer(): pl.pallas_call(layer_body, in_specs=[spec(SM)] + [spec(VM)] * TP + [spec(...]
    ppermute x0 -> x24, waiting for transfers between devices: none -> 20.5 us  [the longest x21 19 us: shifted(): return lax.ppermute(value, 'tp', [(i, (i + shift) % TP) for i in range(TP)])]
    all_to_all x7 -> x4, starting transfers between devices: 41.9 us -> 25.3 us  [the longest x2 17.3 us: copy_for_each(): return lax.all_to_all(sent, 'dom', 0, 0, tiled=True)]
    scatter x2 -> x0, local copies, waits for them, and re-layouts: 13.5 us -> none  [place_rows(): return blank.at[slot_index].set(tensor, mode='drop')]
    dot_general x3 -> x0, local copies, waits for them, and re-layouts: 13 us -> none  [the longest x2 6.56 us: local(): jnp.dot(context, w_output, preferred_element_type=jnp.float32)]
    unnamed x28 -> x68, local copies, waits for them, and re-layouts: 2.44 us -> 12.2 us
  transfers between devices with their start and end apart: 7 -> 28, of which waited for: 6 -> 12; matrix products, arithmetic and copies ran while one was open for 29% -> 6% of each run, Pallas kernels for 0% -> 5%
where the time goes in v1:
time: 178 us; the launch traced here: 177 us
  starting transfers between devices  68.7 us (39%)
  waiting for transfers between devices  59.3 us (33%)
  Pallas kernels  22.1 us (12%)
  local copies, waits for them, and re-layouts  19.7 us (11%)
  other arithmetic  3.8 us (2%)
  between operations  2.89 us (2%)
    ppermute x21, starting transfers between devices, shifted(): return lax.ppermute(value, 'tp', [(i, (i + shift) % TP) for i in range(TP)])  40.8 us
    all_to_all x2, waiting for transfers between devices, exchanged(): lax.all_to_all(rows, 'dom', 0, 0, tiled=True, axis_index_groups=SAME_CORE)  35.8 us
    ppermute x21, waiting for transfers between devices, shifted(): return lax.ppermute(value, 'tp', [(i, (i + shift) % TP) for i in range(TP)])  19 us
    all_to_all x2, starting transfers between devices, copy_for_each(): return lax.all_to_all(sent, 'dom', 0, 0, tiled=True)  17.3 us
    unnamed x68, local copies, waits for them, and re-layouts  12.2 us
    pallas_call x1, Pallas kernels, layer(): pl.pallas_call(layer_body, in_specs=[spec(SM)] + [spec(VM)] * TP + [spec(...  10 us
    all_to_all x2, starting transfers between devices, exchanged(): lax.all_to_all(rows, 'dom', 0, 0, tiled=True, axis_index_groups=SAME_CORE)  7.92 us
    pallas_call x2, Pallas kernels, pack(): pl.pallas_call(pack_body, in_specs=[spec(SM), spec(SM)] + [spec(ANY)] * (...  3.81 us
  transfers between devices with their start and end apart: 28, of which 12 were waited for; matrix products, arithmetic and copies ran while one was open for 6% of the time, Pallas kernels for 5%

profile of v1, /device:TPU:1, one launch (start us, length us, event | category | flops | bytes accessed | tf_op | source)
XLA Modules:
  0.0 176.6 jit_solution(10562306834066116962)
XLA Ops:
  0.6 6.5 %collective-permute-start.6 = (bf16[64,512]{1,0:T(8,128)(2,1)}, bf16[64,512]{1,0:T(8,128)(2,1)S(1)}, u32[]{:S(2)}, u32[]{:S(2)}) collective-permute-start(bf16[64,512]{1,0:T(8,128)(2,1)} %bitcast.17), channel_id=1, source_target_pairs={{0,7},{1,0},{2,1},{3,2},{4,3},{5,4},{6,5},{7,6},{8,15},{9,8},{10,9... | collective-permute-start | bytes 196616 | tf_op jit(solution)/shard_map/ppermute | solution.py:325
  8.7 4.5 %collective-permute-start.3 = (bf16[64,512]{1,0:T(8,128)(2,1)}, bf16[64,512]{1,0:T(8,128)(2,1)S(1)}, u32[]{:S(2)}, u32[]{:S(2)}) collective-permute-start(bf16[64,512]{1,0:T(8,128)(2,1)} %bitcast.20), channel_id=1, source_target_pairs={{0,4},{1,5},{2,6},{3,7},{4,0},{5,1},{6,2},{7,3},{8,12},{9,13},{10,... | collective-permute-start | bytes 196616 | tf_op jit(solution)/shard_map/ppermute | solution.py:325
  14.0 2.2 %collective-permute-start.1 = (bf16[64,512]{1,0:T(8,128)(2,1)}, bf16[64,512]{1,0:T(8,128)(2,1)S(1)}, u32[]{:S(2)}, u32[]{:S(2)}) collective-permute-start(bf16[64,512]{1,0:T(8,128)(2,1)} %bitcast.22), channel_id=1, source_target_pairs={{0,2},{1,3},{2,4},{3,5},{4,6},{5,7},{6,0},{7,1},{8,10},{9,11},{10,... | collective-permute-start | bytes 196616 | tf_op jit(solution)/shard_map/ppermute | solution.py:325
  17.7 2.2 %collective-permute-done.2.refs_3_ = bf16[64,512]{1,0:T(8,128)(2,1)S(1)} collective-permute-done((bf16[64,512]{1,0:T(8,128)(2,1)}, bf16[64,512]{1,0:T(8,128)(2,1)S(1)}, u32[]{:S(2)}, u32[]{:S(2)}) %collective-permute-start.2) | collective-permute-done | bytes 65568 | tf_op jit(solution)/shard_map/ppermute | solution.py:325
  19.9 4.9 %collective-permute-done.1.refs_2_ = bf16[64,512]{1,0:T(8,128)(2,1)S(1)} collective-permute-done((bf16[64,512]{1,0:T(8,128)(2,1)}, bf16[64,512]{1,0:T(8,128)(2,1)S(1)}, u32[]{:S(2)}, u32[]{:S(2)}) %collective-permute-start.1) | collective-permute-done | bytes 65568 | tf_op jit(solution)/shard_map/ppermute | solution.py:325
  26.1 2.2 %copy-done.1 = bf16[4096,512]{1,0:T(8,128)(2,1)S(1)} copy-done((bf16[4096,512]{1,0:T(8,128)(2,1)S(1)}, bf16[4096,512]{1,0:T(8,128)(2,1)}, u32[]{:S(2)}) %copy-start.1) | copy-done | bytes 4194328
  28.3 2.2 %copy-done.2 = bf16[512,4096]{1,0:T(8,128)(2,1)S(1)} copy-done((bf16[512,4096]{1,0:T(8,128)(2,1)S(1)}, bf16[512,4096]{1,0:T(8,128)(2,1)}, u32[]{:S(2)}) %copy-start.2) | copy-done | bytes 4194328
  34.6 10.0 %layer.1 = (bf16[64,512]{1,0:T(8,128)(2,1)S(1)}, bf16[64,512]{1,0:T(8,128)(2,1)S(1)}, bf16[64,512]{1,0:T(8,128)(2,1)S(1)}, bf16[64,512]{1,0:T(8,128)(2,1)S(1)}, ...) custom-call(s32[16]{0:T(128)S(1)} %pad_add_fusion.blk, ...), custom_call_target="tpu_custom_call" | custom-call | flops 671088640 | bytes 12582912 | tf_op jit(solution)/shard_map/layer/pallas_call | solution.py:130
  50.9 7.2 %all-to-all-start.1 = ((s32[32,1,16]{2,1,0:T(1,128)}), s32[32,1,16]{2,1,0:T(1,128)S(1)}, u32[]{:S(2)}, u32[]{:S(2)}) async-start(s32[32,1,16]{2,1,0:T(1,128)} %broadcast_in_dim.6), calls=%async_computation.1 | async-start | bytes 32768 | tf_op jit(solution)/shard_map/all_to_all | solution.py:341
  58.2 4.2 %collective-permute-start.10 = (bf16[64,512]{1,0:T(8,128)(2,1)S(1)}, bf16[64,512]{1,0:T(8,128)(2,1)S(1)}, u32[]{:S(2)}, u32[]{:S(2)}) collective-permute-start(bf16[64,512]{1,0:T(8,128)(2,1)S(1)} %get-tuple-element.60), channel_id=1, source_target_pairs={{0,4},{1,5},{2,6},{3,7},{4,0},{5,1},{6,2},{7,3},{8,12},{9,13},{10,... | collective-permute-start | bytes 196616 | tf_op jit(solution)/shard_map/ppermute | solution.py:325
  64.1 2.4 %collective-permute-start.12 = (bf16[64,512]{1,0:T(8,128)(2,1)S(1)}, bf16[64,512]{1,0:T(8,128)(2,1)S(1)}, u32[]{:S(2)}, u32[]{:S(2)}) collective-permute-start(bf16[64,512]{1,0:T(8,128)(2,1)S(1)} %get-tuple-element.62), channel_id=1, source_target_pairs={{0,6},{1,7},{2,0},{3,1},{4,2},{5,3},{6,4},{7,5},{8,14},{9,15},{10,... | collective-permute-start | bytes 196616 | tf_op jit(solution)/shard_map/ppermute | solution.py:325
  68.0 3.1 %collective-permute-done.11.refs_5_ = bf16[64,512]{1,0:T(8,128)(2,1)S(1)} collective-permute-done((bf16[64,512]{1,0:T(8,128)(2,1)S(1)}, bf16[64,512]{1,0:T(8,128)(2,1)S(1)}, u32[]{:S(2)}, u32[]{:S(2)}) %collective-permute-start.11) | collective-permute-done | bytes 65568 | tf_op jit(solution)/shard_map/ppermute | solution.py:325
  71.0 4.0 %collective-permute-done.12.refs_6_ = bf16[64,512]{1,0:T(8,128)(2,1)S(1)} collective-permute-done((bf16[64,512]{1,0:T(8,128)(2,1)S(1)}, bf16[64,512]{1,0:T(8,128)(2,1)S(1)}, u32[]{:S(2)}, u32[]{:S(2)}) %collective-permute-start.12) | collective-permute-done | bytes 65568 | tf_op jit(solution)/shard_map/ppermute | solution.py:325
  77.6 2.3 %collective-permute-start.23 = (f32[64,128]{1,0:T(8,128)}, f32[64,128]{1,0:T(8,128)S(1)}, u32[]{:S(2)}, u32[]{:S(2)}) collective-permute-start(f32[64,128]{1,0:T(8,128)} %get-tuple-element.68.refs_0_), channel_id=1, source_target_pairs={{0,7},{1,0},{2,1},{3,2},{4,3},{5,4},{6,5},{7,6},{8,15},{9,8},{10,9... | collective-permute-start | bytes 98312 | tf_op jit(solution)/shard_map/ppermute | solution.py:325
  83.2 3.0 %collective-permute-start.20 = (f32[64,128]{1,0:T(8,128)}, f32[64,128]{1,0:T(8,128)S(1)}, u32[]{:S(2)}, u32[]{:S(2)}) collective-permute-start(f32[64,128]{1,0:T(8,128)} %get-tuple-element.68.refs_0_), channel_id=1, source_target_pairs={{0,4},{1,5},{2,6},{3,7},{4,0},{5,1},{6,2},{7,3},{8,12},{9,13},{10,... | collective-permute-start | bytes 98312 | tf_op jit(solution)/shard_map/ppermute | solution.py:325
  87.9 2.2 %collective-permute-start.18 = (f32[64,128]{1,0:T(8,128)}, f32[64,128]{1,0:T(8,128)S(1)}, u32[]{:S(2)}, u32[]{:S(2)}) collective-permute-start(f32[64,128]{1,0:T(8,128)} %get-tuple-element.68.refs_0_), channel_id=1, source_target_pairs={{0,2},{1,3},{2,4},{3,5},{4,6},{5,7},{6,0},{7,1},{8,10},{9,11},{10,... | collective-permute-start | bytes 98312 | tf_op jit(solution)/shard_map/ppermute | solution.py:325
  98.8 10.1 %all-to-all-start.4 = ((f32[32,1,16]{2,1,0:T(1,128)}), f32[32,1,16]{2,1,0:T(1,128)S(1)}, u32[]{:S(2)}, u32[]{:S(2)}) async-start(f32[32,1,16]{2,1,0:T(1,128)} %broadcast_in_dim.7), calls=%async_computation.4 | async-start | bytes 32768 | tf_op jit(solution)/shard_map/all_to_all | solution.py:341
  112.8 3.0 %all-to-all-done.4 = f32[32,1,16]{2,1,0:T(1,128)S(1)} async-done(((f32[32,1,16]{2,1,0:T(1,128)}), f32[32,1,16]{2,1,0:T(1,128)S(1)}, u32[]{:S(2)}, u32[]{:S(2)}) %all-to-all-start.4) | async-done | bytes 2080 | tf_op jit(solution)/shard_map/all_to_all | solution.py:341
  115.8 3.8 %all-to-all-start.2 = ((bf16[16,3,128,128]{3,2,1,0:T(8,128)(2,1)}), bf16[16,3,128,128]{3,2,1,0:T(8,128)(2,1)S(1)}, u32[]{:S(2)}, u32[]{:S(2)}) async-start(bf16[16,3,128,128]{3,2,1,0:T(8,128)(2,1)} %pack.2), calls=%async_computation.2 | async-start | bytes 3145728 | tf_op jit(solution)/shard_map/all_to_all | solution.py:336
  123.9 19.7 %all-to-all-done.2 = bf16[16,3,128,128]{3,2,1,0:T(8,128)(2,1)S(1)} async-done(((bf16[16,3,128,128]{3,2,1,0:T(8,128)(2,1)}), bf16[16,3,128,128]{3,2,1,0:T(8,128)(2,1)S(1)}, u32[]{:S(2)}, u32[]{:S(2)}) %all-to-all-start.2) | async-done | bytes 1572896 | tf_op jit(solution)/shard_map/all_to_all | solution.py:336
  143.6 4.1 %all-to-all-start.3 = ((bf16[16,3,136,128]{3,2,1,0:T(8,128)(2,1)}), bf16[16,3,136,128]{3,2,1,0:T(8,128)(2,1)S(1)}, u32[]{:S(2)}, u32[]{:S(2)}) async-start(bf16[16,3,136,128]{3,2,1,0:T(8,128)(2,1)} %pack.3), calls=%async_computation.3 | async-start | bytes 3342336 | tf_op jit(solution)/shard_map/all_to_all | solution.py:336
  154.6 16.1 %all-to-all-done.3 = bf16[16,3,136,128]{3,2,1,0:T(8,128)(2,1)S(1)} async-done(((bf16[16,3,136,128]{3,2,1,0:T(8,128)(2,1)}), bf16[16,3,136,128]{3,2,1,0:T(8,128)(2,1)S(1)}, u32[]{:S(2)}, u32[]{:S(2)}) %all-to-all-start.3) | async-done | bytes 1671200 | tf_op jit(solution)/shard_map/all_to_all | solution.py:336
  170.7 4.9 %conditional.1 = (bf16[16,132,128]{2,0,1:T(8,128)(2,1)S(1)}, bf16[16,132,128]{2,0,1:T(8,128)(2,1)S(1)}) conditional(s32[]{:T(128)} %bitcast.8, (s32[8,128]{1,0:T(8,128)S(1)}, bf16[16,3,128,128]{3,2,1,0:T(8,128)(2,1)S(1)}, bf16[16,3,136,128]{3,2,1,0:T(8,128)(2,1)S(1)}) %tuple.14, (s32[]{:T(128)}, bf16[16,128,128]{2,1,0:T(8,128)(2,1)}, ...), branch_computations={%region_0.1_spmd, %region_1.2_spmd} | conditional | flops 4326460 | bytes 38867604 | solution.py:428
  170.7 3.6 %place.2 = (bf16[16,132,128]{2,1,0:T(8,128)(2,1)}, bf16[16,132,128]{2,1,0:T(8,128)(2,1)}) custom-call(s32[8,128]{1,0:T(8,128)S(1)} %get-tuple-element.26.refs_0_, bf16[16,3,128,128]{3,2,1,0:T(8,128)(2,1)S(1)} %get-tuple-element.27.refs_1_, bf16[16,3,136,128]{3,2,1,0:T(8,128)(2,1)S(1)} %get-tuple-element.28.refs_2_), custom_call_target="tpu_custom_call" | custom-call | tf_op jit(solution)/shard_map/cond/branch_0_fun/place/pallas_call | solution.py:310
  (130 shorter events, 50.0 us)
Async XLA Ops:
  0.6 13.3 %collective-permute-start.6 = (bf16[64,512]{1,0:T(8,128)(2,1)}, bf16[64,512]{1,0:T(8,128)(2,1)S(1)}, u32[]{:S(2)}, u32[]{:S(2)}) collective-permute-start(bf16[64,512]{1,0:T(8,128)(2,1)} %bitcast.17), channel_id=1, source_target_pairs={{0,7},{1,0},{2,1},{3,2},{4,3},{5,4},{6,5},{7,6},{8,15},{9,8},{10,9... | collective-permute-start | bytes 196616 | tf_op jit(solution)/shard_map/ppermute | solution.py:325
  7.1 9.1 %collective-permute-start.5 = (bf16[64,512]{1,0:T(8,128)(2,1)}, bf16[64,512]{1,0:T(8,128)(2,1)S(1)}, u32[]{:S(2)}, u32[]{:S(2)}) collective-permute-start(bf16[64,512]{1,0:T(8,128)(2,1)} %bitcast.18), channel_id=1, source_target_pairs={{0,6},{1,7},{2,0},{3,1},{4,2},{5,3},{6,4},{7,5},{8,14},{9,15},{10,... | collective-permute-start | bytes 196616 | tf_op jit(solution)/shard_map/ppermute | solution.py:325
  8.3 9.4 %collective-permute-start.4 = (bf16[64,512]{1,0:T(8,128)(2,1)}, bf16[64,512]{1,0:T(8,128)(2,1)S(1)}, u32[]{:S(2)}, u32[]{:S(2)}) collective-permute-start(bf16[64,512]{1,0:T(8,128)(2,1)} %bitcast.19), channel_id=1, source_target_pairs={{0,5},{1,6},{2,7},{3,0},{4,1},{5,2},{6,3},{7,4},{8,13},{9,14},{10,... | collective-permute-start | bytes 196616 | tf_op jit(solution)/shard_map/ppermute | solution.py:325
  8.7 8.9 %collective-permute-start.3 = (bf16[64,512]{1,0:T(8,128)(2,1)}, bf16[64,512]{1,0:T(8,128)(2,1)S(1)}, u32[]{:S(2)}, u32[]{:S(2)}) collective-permute-start(bf16[64,512]{1,0:T(8,128)(2,1)} %bitcast.20), channel_id=1, source_target_pairs={{0,4},{1,5},{2,6},{3,7},{4,0},{5,1},{6,2},{7,3},{8,12},{9,13},{10,... | collective-permute-start | bytes 196616 | tf_op jit(solution)/shard_map/ppermute | solution.py:325
  13.2 6.7 %collective-permute-start.2 = (bf16[64,512]{1,0:T(8,128)(2,1)}, bf16[64,512]{1,0:T(8,128)(2,1)S(1)}, u32[]{:S(2)}, u32[]{:S(2)}) collective-permute-start(bf16[64,512]{1,0:T(8,128)(2,1)} %bitcast.21), channel_id=1, source_target_pairs={{0,3},{1,4},{2,5},{3,6},{4,7},{5,0},{6,1},{7,2},{8,11},{9,12},{10,... | collective-permute-start | bytes 196616 | tf_op jit(solution)/shard_map/ppermute | solution.py:325
  14.0 10.8 %collective-permute-start.1 = (bf16[64,512]{1,0:T(8,128)(2,1)}, bf16[64,512]{1,0:T(8,128)(2,1)S(1)}, u32[]{:S(2)}, u32[]{:S(2)}) collective-permute-start(bf16[64,512]{1,0:T(8,128)(2,1)} %bitcast.22), channel_id=1, source_target_pairs={{0,2},{1,3},{2,4},{3,5},{4,6},{5,7},{6,0},{7,1},{8,10},{9,11},{10,... | collective-permute-start | bytes 196616 | tf_op jit(solution)/shard_map/ppermute | solution.py:325
  16.2 9.9 %collective-permute-start = (bf16[64,512]{1,0:T(8,128)(2,1)}, bf16[64,512]{1,0:T(8,128)(2,1)S(1)}, u32[]{:S(2)}, u32[]{:S(2)}) collective-permute-start(bf16[64,512]{1,0:T(8,128)(2,1)} %bitcast.23), channel_id=1, source_target_pairs={{0,1},{1,2},{2,3},{3,4},{4,5},{5,6},{6,7},{7,0},{8,9},{9,10},{10,1... | collective-permute-start | bytes 196616 | tf_op jit(solution)/shard_map/ppermute | solution.py:325
  45.3 17.2 %collective-permute-start.7 = (bf16[64,512]{1,0:T(8,128)(2,1)S(1)}, bf16[64,512]{1,0:T(8,128)(2,1)S(1)}, u32[]{:S(2)}, u32[]{:S(2)}) collective-permute-start(bf16[64,512]{1,0:T(8,128)(2,1)S(1)} %get-tuple-element.57), channel_id=1, source_target_pairs={{0,1},{1,2},{2,3},{3,4},{4,5},{5,6},{6,7},{7,0},{8,9},{9,10},{10,1... | collective-permute-start | bytes 196616 | tf_op jit(solution)/shard_map/ppermute | solution.py:325
  45.6 18.6 %collective-permute-start.8 = (bf16[64,512]{1,0:T(8,128)(2,1)S(1)}, bf16[64,512]{1,0:T(8,128)(2,1)S(1)}, u32[]{:S(2)}, u32[]{:S(2)}) collective-permute-start(bf16[64,512]{1,0:T(8,128)(2,1)S(1)} %get-tuple-element.58), channel_id=1, source_target_pairs={{0,2},{1,3},{2,4},{3,5},{4,6},{5,7},{6,0},{7,1},{8,10},{9,11},{10,... | collective-permute-start | bytes 196616 | tf_op jit(solution)/shard_map/ppermute | solution.py:325
  47.4 19.1 %collective-permute-start.9 = (bf16[64,512]{1,0:T(8,128)(2,1)S(1)}, bf16[64,512]{1,0:T(8,128)(2,1)S(1)}, u32[]{:S(2)}, u32[]{:S(2)}) collective-permute-start(bf16[64,512]{1,0:T(8,128)(2,1)S(1)} %get-tuple-element.59), channel_id=1, source_target_pairs={{0,3},{1,4},{2,5},{3,6},{4,7},{5,0},{6,1},{7,2},{8,11},{9,12},{10,... | collective-permute-start | bytes 196616 | tf_op jit(solution)/shard_map/ppermute | solution.py:325
  48.5 61.6 %collective-permute-start.14 = (bf16[16,128,128]{2,1,0:T(8,128)(2,1)S(1)}, bf16[16,128,128]{2,1,0:T(8,128)(2,1)S(1)}, u32[]{:S(2)}, u32[]{:S(2)}) collective-permute-start(bf16[16,128,128]{2,1,0:T(8,128)(2,1)S(1)} %copy-done.8), channel_id=1, source_target_pairs={{0,8},{8,0},{16,24},{24,16},{32,40},{40,32},{48,56},{56,48},{64,72... | collective-permute-start | bytes 1572872 | tf_op jit(solution)/shard_map/ppermute | solution.py:329
  50.9 47.2 %all-to-all-start.1 = ((s32[32,1,16]{2,1,0:T(1,128)}), s32[32,1,16]{2,1,0:T(1,128)S(1)}, u32[]{:S(2)}, u32[]{:S(2)}) async-start(s32[32,1,16]{2,1,0:T(1,128)} %broadcast_in_dim.6), calls=%async_computation.1 | async-start | bytes 32768 | tf_op jit(solution)/shard_map/all_to_all | solution.py:341
  58.2 9.7 %collective-permute-start.10 = (bf16[64,512]{1,0:T(8,128)(2,1)S(1)}, bf16[64,512]{1,0:T(8,128)(2,1)S(1)}, u32[]{:S(2)}, u32[]{:S(2)}) collective-permute-start(bf16[64,512]{1,0:T(8,128)(2,1)S(1)} %get-tuple-element.60), channel_id=1, source_target_pairs={{0,4},{1,5},{2,6},{3,7},{4,0},{5,1},{6,2},{7,3},{8,12},{9,13},{10,... | collective-permute-start | bytes 196616 | tf_op jit(solution)/shard_map/ppermute | solution.py:325
  62.5 8.6 %collective-permute-start.11 = (bf16[64,512]{1,0:T(8,128)(2,1)S(1)}, bf16[64,512]{1,0:T(8,128)(2,1)S(1)}, u32[]{:S(2)}, u32[]{:S(2)}) collective-permute-start(bf16[64,512]{1,0:T(8,128)(2,1)S(1)} %get-tuple-element.61), channel_id=1, source_target_pairs={{0,5},{1,6},{2,7},{3,0},{4,1},{5,2},{6,3},{7,4},{8,13},{9,14},{10,... | collective-permute-start | bytes 196616 | tf_op jit(solution)/shard_map/ppermute | solution.py:325
  64.1 11.0 %collective-permute-start.12 = (bf16[64,512]{1,0:T(8,128)(2,1)S(1)}, bf16[64,512]{1,0:T(8,128)(2,1)S(1)}, u32[]{:S(2)}, u32[]{:S(2)}) collective-permute-start(bf16[64,512]{1,0:T(8,128)(2,1)S(1)} %get-tuple-element.62), channel_id=1, source_target_pairs={{0,6},{1,7},{2,0},{3,1},{4,2},{5,3},{6,4},{7,5},{8,14},{9,15},{10,... | collective-permute-start | bytes 196616 | tf_op jit(solution)/shard_map/ppermute | solution.py:325
  66.5 8.6 %collective-permute-start.13 = (bf16[64,512]{1,0:T(8,128)(2,1)S(1)}, bf16[64,512]{1,0:T(8,128)(2,1)S(1)}, u32[]{:S(2)}, u32[]{:S(2)}) collective-permute-start(bf16[64,512]{1,0:T(8,128)(2,1)S(1)} %get-tuple-element.63), channel_id=1, source_target_pairs={{0,7},{1,0},{2,1},{3,2},{4,3},{5,4},{6,5},{7,6},{8,15},{9,8},{10,9... | collective-permute-start | bytes 196616 | tf_op jit(solution)/shard_map/ppermute | solution.py:325
  77.6 8.6 %collective-permute-start.23 = (f32[64,128]{1,0:T(8,128)}, f32[64,128]{1,0:T(8,128)S(1)}, u32[]{:S(2)}, u32[]{:S(2)}) collective-permute-start(f32[64,128]{1,0:T(8,128)} %get-tuple-element.68.refs_0_), channel_id=1, source_target_pairs={{0,7},{1,0},{2,1},{3,2},{4,3},{5,4},{6,5},{7,6},{8,15},{9,8},{10,9... | collective-permute-start | bytes 98312 | tf_op jit(solution)/shard_map/ppermute | solution.py:325
  79.9 8.0 %collective-permute-start.22 = (f32[64,128]{1,0:T(8,128)}, f32[64,128]{1,0:T(8,128)S(1)}, u32[]{:S(2)}, u32[]{:S(2)}) collective-permute-start(f32[64,128]{1,0:T(8,128)} %get-tuple-element.68.refs_0_), channel_id=1, source_target_pairs={{0,6},{1,7},{2,0},{3,1},{4,2},{5,3},{6,4},{7,5},{8,14},{9,15},{10,... | collective-permute-start | bytes 98312 | tf_op jit(solution)/shard_map/ppermute | solution.py:325
  81.3 8.9 %collective-permute-start.21 = (f32[64,128]{1,0:T(8,128)}, f32[64,128]{1,0:T(8,128)S(1)}, u32[]{:S(2)}, u32[]{:S(2)}) collective-permute-start(f32[64,128]{1,0:T(8,128)} %get-tuple-element.68.refs_0_), channel_id=1, source_target_pairs={{0,5},{1,6},{2,7},{3,0},{4,1},{5,2},{6,3},{7,4},{8,13},{9,14},{10,... | collective-permute-start | bytes 98312 | tf_op jit(solution)/shard_map/ppermute | solution.py:325
  83.2 8.3 %collective-permute-start.20 = (f32[64,128]{1,0:T(8,128)}, f32[64,128]{1,0:T(8,128)S(1)}, u32[]{:S(2)}, u32[]{:S(2)}) collective-permute-start(f32[64,128]{1,0:T(8,128)} %get-tuple-element.68.refs_0_), channel_id=1, source_target_pairs={{0,4},{1,5},{2,6},{3,7},{4,0},{5,1},{6,2},{7,3},{8,12},{9,13},{10,... | collective-permute-start | bytes 98312 | tf_op jit(solution)/shard_map/ppermute | solution.py:325
  86.2 6.8 %collective-permute-start.19 = (f32[64,128]{1,0:T(8,128)}, f32[64,128]{1,0:T(8,128)S(1)}, u32[]{:S(2)}, u32[]{:S(2)}) collective-permute-start(f32[64,128]{1,0:T(8,128)} %get-tuple-element.68.refs_0_), channel_id=1, source_target_pairs={{0,3},{1,4},{2,5},{3,6},{4,7},{5,0},{6,1},{7,2},{8,11},{9,12},{10,... | collective-permute-start | bytes 98312 | tf_op jit(solution)/shard_map/ppermute | solution.py:325
  98.8 17.0 %all-to-all-start.4 = ((f32[32,1,16]{2,1,0:T(1,128)}), f32[32,1,16]{2,1,0:T(1,128)S(1)}, u32[]{:S(2)}, u32[]{:S(2)}) async-start(f32[32,1,16]{2,1,0:T(1,128)} %broadcast_in_dim.7), calls=%async_computation.4 | async-start | bytes 32768 | tf_op jit(solution)/shard_map/all_to_all | solution.py:341
  115.8 27.8 %all-to-all-start.2 = ((bf16[16,3,128,128]{3,2,1,0:T(8,128)(2,1)}), bf16[16,3,128,128]{3,2,1,0:T(8,128)(2,1)S(1)}, u32[]{:S(2)}, u32[]{:S(2)}) async-start(bf16[16,3,128,128]{3,2,1,0:T(8,128)(2,1)} %pack.2), calls=%async_computation.2 | async-start | bytes 3145728 | tf_op jit(solution)/shard_map/all_to_all | solution.py:336
  143.6 27.1 %all-to-all-start.3 = ((bf16[16,3,136,128]{3,2,1,0:T(8,128)(2,1)}), bf16[16,3,136,128]{3,2,1,0:T(8,128)(2,1)S(1)}, u32[]{:S(2)}, u32[]{:S(2)}) async-start(bf16[16,3,136,128]{3,2,1,0:T(8,128)(2,1)} %pack.3), calls=%async_computation.3 | async-start | bytes 3342336 | tf_op jit(solution)/shard_map/all_to_all | solution.py:336
  (39 other events, 350.4 us)

commit v2 on v1

v2 whole, which is shorter than its diff:
```python
import jax
import jax.numpy as jnp
import numpy as np
from jax import lax
from jax.experimental import pallas as pl
from jax.experimental.pallas import tpu as pltpu
from jax.sharding import PartitionSpec as P

D = 4096
HD = 128
STEPS = 4
NP = 16
ROWS = STEPS * NP
SPAN = 128
TP = 8
DB = D // TP
HEADS = DB // HD
GROUP = HEADS * STEPS
NDOM = 32
NCHIP = 16
SLOTS = 3
BF = jnp.bfloat16
F32 = jnp.float32
ANY = pl.ANY
VM = pltpu.VMEM
SM = pltpu.SMEM


def spec(space):
    return pl.BlockSpec(memory_space=space)


def limit(mib):
    return pltpu.CompilerParams(vmem_limit_bytes=mib * 2**20)


def nt(a, b):
    return lax.dot_general(a, b, (((1,), (1,)), ((), ())), preferred_element_type=F32)


def mm(a, b):
    return jnp.dot(a, b, preferred_element_type=F32)


def project_body(acts, gain, wq, wk, wv, table, qa, kf, vf, fresh, *scratch):
    wq_s, wk_s, wv_s, q_s, kf_s, vf_s, sems = scratch
    copies = []
    for s in range(TP):
        part = pl.ds(s * DB, DB)
        copies.append(
            [
                pltpu.make_async_copy(w.at[part, :], w_s.at[s], sems.at[n, s])
                for n, (w, w_s) in enumerate(((wq, wq_s), (wk, wk_s), (wv, wv_s)))
            ]
        )
    for group in copies:
        for c in group:
            c.start()
    square = jnp.zeros((ROWS, 1), F32)
    for s in range(TP):
        x = acts[s].astype(F32)
        square = square + jnp.sum(x * x, -1, keepdims=True)
    inv = lax.rsqrt(square / D + 1e-05)
    q = jnp.zeros((ROWS, DB), F32)
    k = jnp.zeros((ROWS, HD), F32)
    v = jnp.zeros((ROWS, HD), F32)
    for s in range(TP):
        x = acts[s].astype(F32)
        normed = (x * inv * gain[s : s + 1, :]).astype(BF)
        for c in copies[s]:
            c.wait()
        q = q + mm(normed, wq_s[s])
        k = k + mm(normed, wk_s[s])
        v = v + mm(normed, wv_s[s])
    cosine = table[0]
    sine = table[1]

    def turned(u):
        return (u * cosine + pltpu.roll(u, HD // 2, 1) * sine).astype(BF)

    for g in range(HEADS):
        q_s[g] = turned(q[:, g * HD : (g + 1) * HD]).astype(F32)
    k = turned(k)
    v = v.astype(BF)
    kf[...] = k
    vf[...] = v
    kf_s[...] = k.astype(F32)
    vf_s[...] = v.astype(F32)
    for n in range(NP):
        mine = pl.ds(n, STEPS, stride=NP)
        fresh[n] = jnp.concatenate([kf_s[mine, :], vf_s[mine, :]], 0).astype(BF)
        qa[n * GROUP : (n + 1) * GROUP, :] = jnp.concatenate(
            [q_s[g, mine, :] for g in range(HEADS)], 0
        ).astype(BF)


def project(acts, gain, wq, wk, wv, table):
    sd = jax.ShapeDtypeStruct
    return pl.pallas_call(
        project_body,
        in_specs=[spec(VM)] * 2 + [spec(ANY)] * 3 + [spec(VM)],
        out_specs=[spec(VM)] * 4,
        out_shape=[
            sd((NP * GROUP, HD), BF),
            sd((ROWS, HD), BF),
            sd((ROWS, HD), BF),
            sd((NP, 2 * STEPS, HD), BF),
        ],
        scratch_shapes=[
            VM((TP, DB, DB), BF),
            VM((TP, DB, HD), BF),
            VM((TP, DB, HD), BF),
            VM((HEADS, ROWS, HD), F32),
            VM((ROWS, HD), F32),
            VM((ROWS, HD), F32),
            pltpu.SemaphoreType.DMA((3, TP)),
        ],
        compiler_params=limit(55),
        cost_estimate=pl.CostEstimate(
            flops=2 * ROWS * D * 768, bytes_accessed=7 * 2**20, transcendentals=0
        ),
        name="project",
    )(acts, gain, wq, wk, wv, table)


def attend_body(blk, qa, kf, vf, kc, vc, wo, *refs):
    outs = refs[:TP]
    s1_s, ctx_s, wo_s, sems = refs[TP:]
    copies = []
    for s in range(TP):
        there = pl.ds(pl.multiple_of(blk[s] * DB, DB), DB)
        copies.append(pltpu.make_async_copy(wo.at[:, there], wo_s.at[s], sems.at[s]))
    for c in copies:
        c.start()
    for n in range(NP):
        span = slice(n * GROUP, (n + 1) * GROUP)
        s1_s[span, :] = nt(qa[span, :], kc[n])
    scale = 1.0 / HD**0.5
    s1 = s1_s[...] * scale
    s2 = nt(qa[...], kf[...]) * scale
    row = lax.broadcasted_iota(jnp.int32, (NP * GROUP, ROWS), 0)
    col = lax.broadcasted_iota(jnp.int32, (NP * GROUP, ROWS), 1)
    seen = ((row // GROUP) == (col % NP)) & ((col // NP) <= (row % STEPS))
    s2 = jnp.where(seen, s2, -jnp.inf)
    top = jnp.maximum(jnp.max(s1, -1, keepdims=True), jnp.max(s2, -1, keepdims=True))
    e1 = jnp.exp(s1 - top)
    e2 = jnp.exp(s2 - top)
    total = jnp.sum(e1, -1, keepdims=True) + jnp.sum(e2, -1, keepdims=True)
    w1 = (e1 / total).astype(BF)
    w2 = (e2 / total).astype(BF)
    c2 = mm(w2, vf[...])
    for n in range(NP):
        span = slice(n * GROUP, (n + 1) * GROUP)
        cn = (mm(w1[span], vc[n]) + c2[span]).astype(BF).astype(F32)
        for g in range(HEADS):
            ctx_s[g, pl.ds(n, STEPS, stride=NP), :] = cn[g * STEPS : (g + 1) * STEPS]
    ctx = jnp.concatenate([ctx_s[g] for g in range(HEADS)], 1).astype(BF)
    for s in range(TP):
        copies[s].wait()
        outs[s][...] = mm(ctx, wo_s[s]).astype(BF)


def attend(blk, qa, kf, vf, kc, vc, wo):
    return pl.pallas_call(
        attend_body,
        in_specs=[spec(SM)] + [spec(VM)] * 5 + [spec(ANY)],
        out_specs=[spec(VM)] * TP,
        out_shape=[jax.ShapeDtypeStruct((ROWS, DB), BF)] * TP,
        scratch_shapes=[
            VM((NP * GROUP, SPAN), F32),
            VM((HEADS, ROWS, HD), F32),
            VM((TP, DB, DB), BF),
            pltpu.SemaphoreType.DMA((TP,)),
        ],
        compiler_params=limit(55),
        cost_estimate=pl.CostEstimate(
            flops=2 * ROWS * D * 640, bytes_accessed=6 * 2**20, transcendentals=NP * 16 * 192
        ),
        name="attend",
    )(blk, qa, kf, vf, kc, vc, wo)


def mix_body(*refs):
    parts = refs[:TP]
    act, twist, attn, sums = refs[TP:]
    mix = parts[0][...].astype(F32)
    for s in range(1, TP):
        mix = mix + parts[s][...].astype(F32)
    attn[...] = mix.astype(BF)
    summed = act[...].astype(F32) + mix
    aligned = jnp.sum(summed * twist[...], -1, keepdims=True)
    energy = jnp.sum(summed * summed, -1, keepdims=True)
    lane = lax.broadcasted_iota(jnp.int32, (ROWS, HD), 1)
    sums[...] = jnp.where(lane == 0, aligned, energy)


def mix(parts, act, twist):
    sd = jax.ShapeDtypeStruct
    return pl.pallas_call(
        mix_body,
        in_specs=[spec(VM)] * (TP + 2),
        out_specs=[spec(VM)] * 2,
        out_shape=[sd((ROWS, DB), BF), sd((ROWS, HD), F32)],
        compiler_params=limit(8),
        name="mix",
    )(*parts, act, twist)


def weigh_body(*refs):
    parts = refs[:TP]
    reward, previous, out = refs[TP:]
    sums = parts[0][...]
    for s in range(1, TP):
        sums = sums + parts[s][...]
    score = sums[:, 0:1] / jnp.sqrt(sums[:, 1:2] / D + 1e-06) + reward[...]
    gain = score[0:NP]
    for t in range(1, STEPS):
        gain = gain + score[t * NP : (t + 1) * NP]
    column = jnp.broadcast_to(previous[...] + gain, (NP, HD))
    row = lax.broadcasted_iota(jnp.int32, (NP, HD), 0)
    lane = lax.broadcasted_iota(jnp.int32, (NP, HD), 1)
    line = jnp.sum(jnp.where(row == lane, column, 0.0), 0, keepdims=True)
    out[...] = jnp.broadcast_to(line[None], (NDOM, 1, HD))


def weigh(parts, reward, previous):
    return pl.pallas_call(
        weigh_body,
        in_specs=[spec(VM)] * (TP + 2),
        out_specs=spec(VM),
        out_shape=jax.ShapeDtypeStruct((NDOM, 1, HD), F32),
        compiler_params=limit(8),
        name="weigh",
    )(*parts, reward, previous)


def finish_body(mine, every, out):
    lane = lax.broadcasted_iota(jnp.int32, (NDOM, HD), 1)
    all_w = jnp.where(lane < NP, every[:, 0, :], -jnp.inf)
    largest = jnp.max(all_w, keepdims=True)
    mass = jnp.sum(jnp.exp(all_w - largest), keepdims=True)
    out[...] = (mine[0] - (largest + jnp.log(mass)))[:, 0:NP]


def finish(mine, every):
    return pl.pallas_call(
        finish_body,
        in_specs=[spec(VM)] * 2,
        out_specs=spec(VM),
        out_shape=jax.ShapeDtypeStruct((1, NP), F32),
        compiler_params=limit(8),
        name="finish",
    )(mine, every)


def plan_body(me_ref, *refs):
    out = refs[-1]
    me = me_ref[0]
    blocks = jnp.concatenate([r[...] for r in refs[:-1]], 0).astype(F32)
    rel = lax.broadcasted_iota(jnp.int32, (NDOM, NDOM), 1)
    back_y = (me // 8 - rel // 8) & 3
    back_x = (me // 2 - rel // 2) & 3
    holder = 8 * back_y + 2 * back_x + ((me + rel) & 1)
    sorted_rows = lax.broadcasted_iota(jnp.int32, (NDOM, NDOM), 0) == holder
    counts = mm(sorted_rows.astype(F32), blocks)
    r16 = lax.broadcasted_iota(jnp.int32, (NP, NP), 0)
    c16 = lax.broadcasted_iota(jnp.int32, (NP, NP), 1)
    within = mm(counts, (r16 <= c16).astype(F32))
    r32 = lax.broadcasted_iota(jnp.int32, (NDOM, NDOM), 0)
    c32 = lax.broadcasted_iota(jnp.int32, (NDOM, NDOM), 1)
    before = jnp.sum(mm((c32 < r32).astype(F32), counts), -1, keepdims=True)
    ends = (within + before).astype(jnp.int32)
    before = before.astype(jnp.int32)
    device = lax.broadcasted_iota(jnp.int32, (NDOM, 1), 0)
    chip_end = jnp.where(device % 2 == 1, ends[:, NP - 1 : NP], -1)
    chip = me // 2
    first = jnp.sum(jnp.where(device == 2 * chip, before, 0))
    lane = lax.broadcasted_iota(jnp.int32, (1, HD), 1)
    dest = 2 * (lane // 4) + me % 2
    sent = first + ((dest - first) & (NDOM - 1)) + NDOM * (lane % 4)
    kept = NDOM * (lane - 64) + me
    found = jnp.zeros((NDOM, HD), jnp.int32)
    for j in range(NP):
        found = found + (ends[:, j : j + 1] <= sent).astype(jnp.int32)
    particle = jnp.sum(found, 0, keepdims=True) - 2 * NP * chip
    particle = jnp.clip(particle, 0, 2 * NP - 1)
    passed = (chip_end >= 0) & (chip_end <= kept)
    source = jnp.sum(passed.astype(jnp.int32), 0, keepdims=True)
    base = jnp.max(jnp.where(passed, chip_end, 0), 0, keepdims=True)
    slot = jnp.clip((kept - base) // NDOM, 0, 3)
    arrived = 4 * jnp.clip(source, 0, NCHIP - 1) + slot
    owned = jnp.sum(counts, -1, keepdims=True).astype(jnp.int32)
    pair = lax.broadcasted_iota(jnp.int32, (NDOM, HD), 1)
    most = jnp.max(jnp.sum(jnp.where(pair == device // 2, owned, 0), 0, keepdims=True))
    line = jnp.where(lane < 64, particle, jnp.where(lane < 80, arrived, most))
    out[...] = jnp.broadcast_to(line, (8, HD))


def plan(me, blocks):
    return pl.pallas_call(
        plan_body,
        in_specs=[spec(SM)] + [spec(VM)] * len(blocks),
        out_specs=spec(VM),
        out_shape=jax.ShapeDtypeStruct((8, HD), jnp.int32),
        compiler_params=limit(8),
        name="plan",
    )(me, *blocks)


def pack_body(me_ref, idx, *refs):
    half = (len(refs) - 3) // 2
    own, partner = (refs[:half], refs[half : 2 * half])
    out, rows, sems = refs[2 * half :]
    core = me_ref[0] % 2
    loads, at = ([], 0)
    for n in range(half):
        length = own[n].shape[1]
        for side, ref in ((core, own[n]), (1 - core, partner[n])):
            there = rows.at[pl.ds(side * NP, NP), pl.ds(at, length), :]
            loads.append(pltpu.make_async_copy(ref, there, sems.at[len(loads) + 1]))
        at += length
    for c in loads:
        c.start()
    for c in loads:
        c.wait()
    for q in range(NCHIP):
        for s in range(SLOTS):
            pltpu.make_async_copy(rows.at[idx[0, 4 * q + s]], out.at[q, s], sems.at[0]).start()
    pltpu.make_async_copy(out, out, sems.at[0]).wait()


def pack(me, idx, own, partner):
    length = sum(a.shape[1] for a in own)
    return pl.pallas_call(
        pack_body,
        in_specs=[spec(SM), spec(SM)] + [spec(ANY)] * (2 * len(own)),
        out_specs=spec(ANY),
        out_shape=jax.ShapeDtypeStruct((NCHIP, SLOTS, length, HD), BF),
        scratch_shapes=[
            VM((2 * NP, length, HD), BF),
            pltpu.SemaphoreType.DMA((1 + 2 * len(own),)),
        ],
        compiler_params=limit(16),
        name="pack",
    )(me, idx, *own, *partner)


def place_body(slots, idx, rows, keys, values, r_s, sems):
    copies = []
    for k in range(NP):
        code = idx[0, 64 + k]
        slot = jnp.minimum(code % 4, slots - 1)
        copies.append(
            pltpu.make_async_copy(rows.at[code // 4, slot], r_s.at[k], sems.at[k])
        )
    for c in copies:
        c.start()
    for k in range(NP):
        copies[k].wait()
        keys[k, 0:SPAN, :] = r_s[k, 0:SPAN, :]
        values[k, 0:SPAN, :] = r_s[k, SPAN : 2 * SPAN, :]
        tail = r_s[k, 2 * SPAN : 2 * SPAN + 2 * STEPS, :].astype(F32)
        keys[k, SPAN : SPAN + STEPS, :] = tail[0:STEPS].astype(BF)
        values[k, SPAN : SPAN + STEPS, :] = tail[STEPS : 2 * STEPS].astype(BF)


def place(idx, rows):
    out = jax.ShapeDtypeStruct((NP, SPAN + STEPS, HD), BF)
    slots = rows.shape[1]
    return pl.pallas_call(
        lambda *refs: place_body(slots, *refs),
        in_specs=[spec(SM), spec(ANY)],
        out_specs=[spec(VM)] * 2,
        out_shape=[out] * 2,
        scratch_shapes=[
            VM((NP, 2 * SPAN + 2 * STEPS, HD), BF),
            pltpu.SemaphoreType.DMA((NP,)),
        ],
        compiler_params=limit(16),
        name="place",
    )(idx, rows)


def shifted(value, shift):
    return lax.ppermute(value, "tp", [(i, (i + shift) % TP) for i in range(TP)])


def swapped(value):
    return lax.ppermute(value, "dom", [(i, i ^ 1) for i in range(NDOM)])


def next_chip(value):
    return lax.ppermute(value, "dom", [(i, (i + 2) % NDOM) for i in range(NDOM)])


SAME_CORE = [list(range(c, NDOM, 2)) for c in range(2)]


def exchanged(rows):
    return lax.all_to_all(rows, "dom", 0, 0, tiled=True, axis_index_groups=SAME_CORE)


def moved(value, axis_stride, shift):
    def to(i):
        at = i // axis_stride % 4
        return i + ((at + shift) % 4 - at) * axis_stride

    return lax.ppermute(value, "dom", [(i, to(i)) for i in range(NDOM)])


def spread_counts(copy_counts):
    own = copy_counts.reshape(1, NP)
    chip = jnp.concatenate([own, swapped(own)], 0)
    row = jnp.concatenate([chip] + [moved(chip, 2, s) for s in range(1, 4)], 0)
    return [row] + [moved(row, 8, s) for s in range(1, 4)]


def rotation_table():
    frequency = np.float32(500000.0) ** (-2.0 * np.arange(HD // 2, dtype=np.float32) / HD)
    angles = (SPAN + np.arange(STEPS, dtype=np.float32))[:, None] * frequency.astype(np.float32)
    cosine = np.concatenate([np.cos(angles), np.cos(angles)], 1)
    sine = np.concatenate([-np.sin(angles), np.sin(angles)], 1)
    return np.stack([np.repeat(cosine, NP, 0), np.repeat(sine, NP, 0)]).astype(np.float32)


def local(
    activations,
    norm_gain,
    w_query,
    w_key,
    value_weight,
    w_output,
    cache_keys,
    cache_values,
    tokens,
    twisting_table,
    twist_vec,
    previous_log_weights,
    copy_counts,
):
    dom = lax.axis_index("dom")
    tp = lax.axis_index("tp")
    me = dom.reshape(1)
    blk = ((tp + np.arange(TP)) % TP).astype(jnp.int32)
    act = activations.reshape(ROWS, DB)

    gathered = lax.all_to_all(
        jnp.broadcast_to(act[None], (TP, ROWS, DB)), "tp", 0, 0, tiled=True
    )
    idx = plan(me, spread_counts(copy_counts))
    partner_keys = swapped(cache_keys)
    partner_values = swapped(cache_values)
    reward = twisting_table[tokens.reshape(ROWS)].astype(F32).reshape(ROWS, 1)

    gathered, idx, partner_keys, partner_values, reward = lax.optimization_barrier(
        (gathered, idx, partner_keys, partner_values, reward)
    )
    qa, kf, vf, fresh = project(
        gathered, norm_gain.reshape(TP, DB), w_query, w_key, value_weight, rotation_table()
    )
    partner_fresh = swapped(fresh)
    packed = pack(
        me,
        idx,
        [cache_keys, cache_values, fresh],
        [partner_keys, partner_values, partner_fresh],
    )
    packed, qa = lax.optimization_barrier((packed, qa))
    rows = exchanged(packed)
    partials = attend(blk, qa, kf, vf, cache_keys, cache_values, w_output)

    parts = [partials[0]] + [shifted(partials[s], s) for s in range(1, TP)]
    attn, sums = mix(parts, act, twist_vec.reshape(1, DB))
    all_sums = [sums] + [shifted(sums, s) for s in range(1, TP)]
    logw = weigh(all_sums, reward, previous_log_weights.reshape(NP, 1))
    logw, rows = lax.optimization_barrier((logw, rows))
    every = lax.all_to_all(logw, "dom", 0, 0, tiled=True)
    out_logw = finish(logw, every).reshape(NP)

    def usual(rows, *_):
        return tuple(place(idx, rows))

    def crowded(rows, partner_keys, partner_values, partner_fresh, fresh, idx):
        even = dom % 2 == 0
        mine = jnp.concatenate([cache_keys, cache_values, fresh], 1)
        other = jnp.concatenate([partner_keys, partner_values, partner_fresh], 1)
        chip_rows = jnp.concatenate(
            [jnp.where(even, mine, other), jnp.where(even, other, mine)], 0
        )
        chosen = chip_rows[idx[0, 3:64:4]]
        chip = dom // 2

        def turn(step, state):
            passing, more = state
            passing = next_chip(passing)
            return passing, more.at[(chip - step) % NCHIP].set(passing[chip])

        start = (chosen, chosen)
        more = lax.fori_loop(1, NCHIP, turn, start)[1].at[chip].set(chosen[chip])
        return tuple(place(idx, jnp.concatenate([rows, more[:, None]], 1)))

    new_keys, new_values = lax.cond(
        idx[0, 127] > SLOTS * NDOM,
        crowded,
        usual,
        rows,
        partner_keys,
        partner_values,
        partner_fresh,
        fresh,
        idx,
    )
    return (attn.reshape(STEPS, NP, DB), new_keys, new_values, out_logw)


def solution(mesh):
    return jax.shard_map(
        local,
        mesh=mesh,
        in_specs=(
            P(None, "dom", "tp"),
            P(),
            P(None, "tp"),
            P(None, "tp"),
            P(None, "tp"),
            P("tp", None),
            P("dom", None, "tp"),
            P("dom", None, "tp"),
            P(None, "dom"),
            P(),
            P("tp"),
            P("dom"),
            P("dom"),
        ),
        out_specs=(P(None, "dom", "tp"), P("dom", None, "tp"), P("dom", None, "tp"), P("dom")),
        check_vma=False,
    )
```

time: 178 us -> 111 us (0.62)
  waiting for transfers between devices: 59.3 us -> 20.8 us
  local copies, waits for them, and re-layouts: 19.7 us -> 7.46 us
  starting transfers between devices: 68.7 us -> 61.6 us
  Pallas kernels: 22.1 us -> 18.6 us
  other arithmetic: 3.8 us -> 0.55 us
    all_to_all x2 -> x1, waiting for transfers between devices: 35.8 us -> 3.06 us  [exchanged(): lax.all_to_all(rows, 'dom', 0, 0, tiled=True, axis_index_groups=SAME_CORE)]
    ppermute x21 -> x14, starting transfers between devices: 40.8 us -> 27.1 us  [shifted(): return lax.ppermute(value, 'tp', [(i, (i + shift) % TP) for i in range(TP)])]
    unnamed x68 -> x22, local copies, waits for them, and re-layouts: 12.2 us -> 1.67 us
    ppermute x0 -> x6, starting transfers between devices: none -> 9.98 us  [moved(): return lax.ppermute(value, 'dom', [(i, to(i)) for i in range(NDOM)])]
    ppermute x21 -> x14, waiting for transfers between devices: 19 us -> 10.8 us  [shifted(): return lax.ppermute(value, 'tp', [(i, (i + shift) % TP) for i in range(TP)])]
    ppermute x0 -> x6, waiting for transfers between devices: none -> 2.63 us  [moved(): return lax.ppermute(value, 'dom', [(i, to(i)) for i in range(NDOM)])]
    reduce_sum x1 -> x0, other arithmetic: 1.95 us -> none  [local(): out_logw = logw - (largest + jnp.log(jnp.sum(jnp.exp(every - largest))))]
    all_to_all x2 -> x1, starting transfers between devices: 7.92 us -> 5.99 us  [exchanged(): lax.all_to_all(rows, 'dom', 0, 0, tiled=True, axis_index_groups=SAME_CORE)]
  transfers between devices with their start and end apart: 28 -> 27, of which waited for: 12 -> 11; matrix products, arithmetic and copies ran while one was open for 6% -> 4% of each run, Pallas kernels for 5% -> 8%
where the time goes in v2:
time: 111 us
  starting transfers between devices  61.6 us (55%)
  waiting for transfers between devices  20.8 us (19%)
  Pallas kernels  18.6 us (17%)
  local copies, waits for them, and re-layouts  7.46 us (7%)
  between operations  1.47 us (1%)
    ppermute x14, starting transfers between devices, shifted(): return lax.ppermute(value, 'tp', [(i, (i + shift) % TP) for i in range(TP)])  27.1 us
    ppermute x14, waiting for transfers between devices, shifted(): return lax.ppermute(value, 'tp', [(i, (i + shift) % TP) for i in range(TP)])  10.8 us
    ppermute x6, starting transfers between devices, moved(): return lax.ppermute(value, 'dom', [(i, to(i)) for i in range(NDOM)])  9.98 us
    all_to_all x1, starting transfers between devices, local(): lax.all_to_all(jnp.broadcast_to(act[None], (TP, ROWS, DB)), 'tp', 0, 0, t...  9.01 us
    all_to_all x1, starting transfers between devices, local(): every = lax.all_to_all(logw, 'dom', 0, 0, tiled=True)  6.53 us
    all_to_all x1, starting transfers between devices, exchanged(): lax.all_to_all(rows, 'dom', 0, 0, tiled=True, axis_index_groups=SAME_CORE)  5.99 us
    pallas_call x1, Pallas kernels, project(): pl.pallas_call(project_body, in_specs=[spec(VM)] * 2 + [spec(ANY)] * 3 +...  5.35 us
    pallas_call x1, Pallas kernels, attend(): pl.pallas_call(attend_body, in_specs=[spec(SM)] + [spec(VM)] * 5 + [spec(...  5.08 us
  transfers between devices with their start and end apart: 27, of which 11 were waited for; matrix products, arithmetic and copies ran while one was open for 4% of the time, Pallas kernels for 8%

profile of v2, /device:TPU:1, one launch (start us, length us, event | category | flops | bytes accessed | tf_op | source)
XLA Modules:
  0.0 110.5 jit_solution(11134266616140206996)
XLA Ops:
  0.7 1.8 %broadcast_in_dim.19 = bf16[8,64,512]{2,1,0:T(8,128)(2,1)} broadcast(bf16[64,512]{1,0:T(8,128)(2,1)} %bitcast.24), dimensions={1,2} | broadcast | bytes 589824 | tf_op jit(solution)/shard_map/broadcast_in_dim | solution.py:448
  2.5 9.0 %all-to-all-start = ((bf16[8,64,512]{2,1,0:T(8,128)(2,1)}), bf16[8,64,512]{2,1,0:T(8,128)(2,1)S(1)}, u32[]{:S(2)}, u32[]{:S(2)}) async-start(bf16[8,64,512]{2,1,0:T(8,128)(2,1)} %broadcast_in_dim.19), calls=%async_computation | async-start | bytes 1048576 | tf_op jit(solution)/shard_map/all_to_all | solution.py:447
  15.3 2.4 %collective-permute-start.3 = (s32[2,16]{1,0:T(2,128)S(1)}, s32[2,16]{1,0:T(2,128)S(1)}, u32[]{:S(2)}, u32[]{:S(2)}) collective-permute-start(s32[2,16]{1,0:T(2,128)S(1)} %pad_add_fusion), channel_id=1, source_target_pairs={{0,32},{8,40},{16,48},{24,56},{32,0},{40,8},{48,16},{56,24},{64,96... | collective-permute-start | bytes 392 | tf_op jit(solution)/shard_map/ppermute | solution.py:408
  21.9 2.6 %collective-permute-start.6 = (s32[8,16]{1,0:T(8,128)S(1)}, s32[8,16]{1,0:T(8,128)S(1)}, u32[]{:S(2)}, u32[]{:S(2)}) collective-permute-start(s32[8,16]{1,0:T(8,128)S(1)} %concatenate.35.refs_0_), channel_id=1, source_target_pairs={{0,128},{8,136},{16,144},{24,152},{32,160},{40,168},{48,176},{56,1... | collective-permute-start | bytes 1544 | tf_op jit(solution)/shard_map/ppermute | solution.py:408
  30.2 5.4 %project.1 = (bf16[256,128]{1,0:T(8,128)(2,1)}, bf16[64,128]{1,0:T(8,128)(2,1)}, bf16[64,128]{1,0:T(8,128)(2,1)}, bf16[16,8,128]{2,1,0:T(8,128)(2,1)S(1)}) custom-call(bf16[8,64,512]{2,1,0:T(8,128)(2,1)} %copy-done.6, f32[8,512]{1,0:T(8,128)} %reshape.200.gain, bf16[4096,512]{1,0:T(8,128)(2,1)} %wq.1, bf16[4096,128]{1,0:T(8,128)(2,1)} %wk.1, ...), custom_call_target="tpu_custom_call" | custom-call | flops 402653184 | bytes 7340032 | tf_op jit(solution)/shard_map/project/pallas_call | solution.py:99
  37.9 2.5 %pack.1 = bf16[16,3,264,128]{3,2,1,0:T(8,128)(2,1)} custom-call(s32[1]{0:T(128)} %bitcast.6.me_ref, s32[8,128]{1,0:T(8,128)S(1)} %plan.1.idx, bf16[16,128,128]{2,1,0:T(8,128)(2,1)S(1)} %copy-done.4, bf16[16,128,128]{2,1,0:T(8,128)(2,1)S(1)} %copy-done.5, bf16[16,8,128]{2,1,0:T(8,128)(2,1)S(1)} %get-tuple-element.217.refs_2_, ...), custom_call_target="tpu_custom_call" | custom-call | tf_op jit(solution)/shard_map/pack/pallas_call | solution.py:334
  40.4 6.0 %all-to-all-start.1 = ((bf16[16,3,264,128]{3,2,1,0:T(8,128)(2,1)}), bf16[16,3,264,128]{3,2,1,0:T(8,128)(2,1)}, u32[]{:S(2)}, u32[]{:S(2)}) async-start(bf16[16,3,264,128]{3,2,1,0:T(8,128)(2,1)} %pack.1), calls=%async_computation.1 | async-start | bytes 6488064 | tf_op jit(solution)/shard_map/all_to_all | solution.py:400
  46.9 5.1 %attend.1 = (bf16[64,512]{1,0:T(8,128)(2,1)}, bf16[64,512]{1,0:T(8,128)(2,1)}, bf16[64,512]{1,0:T(8,128)(2,1)}, bf16[64,512]{1,0:T(8,128)(2,1)}, bf16[64,512]{1,...) custom-call(s32[8]{0:T(128)} %and_select_fusion.blk, ...), custom_call_target="tpu_custom_call" | custom-call | flops 335544320 | bytes 6291456 | tf_op jit(solution)/shard_map/attend/pallas_call | solution.py:164
  53.5 2.1 %collective-permute-start.12 = (bf16[64,512]{1,0:T(8,128)(2,1)}, bf16[64,512]{1,0:T(8,128)(2,1)S(1)}, u32[]{:S(2)}, u32[]{:S(2)}) collective-permute-start(bf16[64,512]{1,0:T(8,128)(2,1)} %get-tuple-element.226), channel_id=1, source_target_pairs={{0,2},{1,3},{2,4},{3,5},{4,6},{5,7},{6,0},{7,1},{8,10},{9,11},{10,... | collective-permute-start | bytes 196616 | tf_op jit(solution)/shard_map/ppermute | solution.py:385
  55.6 2.4 %collective-permute-start.13 = (bf16[64,512]{1,0:T(8,128)(2,1)}, bf16[64,512]{1,0:T(8,128)(2,1)S(1)}, u32[]{:S(2)}, u32[]{:S(2)}) collective-permute-start(bf16[64,512]{1,0:T(8,128)(2,1)} %get-tuple-element.227), channel_id=1, source_target_pairs={{0,3},{1,4},{2,5},{3,6},{4,7},{5,0},{6,1},{7,2},{8,11},{9,12},{10,... | collective-permute-start | bytes 196616 | tf_op jit(solution)/shard_map/ppermute | solution.py:385
  58.0 2.1 %collective-permute-start.14 = (bf16[64,512]{1,0:T(8,128)(2,1)}, bf16[64,512]{1,0:T(8,128)(2,1)S(1)}, u32[]{:S(2)}, u32[]{:S(2)}) collective-permute-start(bf16[64,512]{1,0:T(8,128)(2,1)} %get-tuple-element.228), channel_id=1, source_target_pairs={{0,4},{1,5},{2,6},{3,7},{4,0},{5,1},{6,2},{7,3},{8,12},{9,13},{10,... | collective-permute-start | bytes 196616 | tf_op jit(solution)/shard_map/ppermute | solution.py:385
  60.1 2.4 %collective-permute-start.15 = (bf16[64,512]{1,0:T(8,128)(2,1)}, bf16[64,512]{1,0:T(8,128)(2,1)S(1)}, u32[]{:S(2)}, u32[]{:S(2)}) collective-permute-start(bf16[64,512]{1,0:T(8,128)(2,1)} %get-tuple-element.229), channel_id=1, source_target_pairs={{0,5},{1,6},{2,7},{3,0},{4,1},{5,2},{6,3},{7,4},{8,13},{9,14},{10,... | collective-permute-start | bytes 196616 | tf_op jit(solution)/shard_map/ppermute | solution.py:385
  62.5 3.3 %collective-permute-start.16 = (bf16[64,512]{1,0:T(8,128)(2,1)}, bf16[64,512]{1,0:T(8,128)(2,1)S(1)}, u32[]{:S(2)}, u32[]{:S(2)}) collective-permute-start(bf16[64,512]{1,0:T(8,128)(2,1)} %get-tuple-element.230), channel_id=1, source_target_pairs={{0,6},{1,7},{2,0},{3,1},{4,2},{5,3},{6,4},{7,5},{8,14},{9,15},{10,... | collective-permute-start | bytes 196616 | tf_op jit(solution)/shard_map/ppermute | solution.py:385
  68.7 5.3 %collective-permute-done.16.refs_6_ = bf16[64,512]{1,0:T(8,128)(2,1)S(1)} collective-permute-done((bf16[64,512]{1,0:T(8,128)(2,1)}, bf16[64,512]{1,0:T(8,128)(2,1)S(1)}, u32[]{:S(2)}, u32[]{:S(2)}) %collective-permute-start.16) | collective-permute-done | bytes 65568 | tf_op jit(solution)/shard_map/ppermute | solution.py:385
  75.6 2.4 %collective-permute-start.18 = (f32[64,128]{1,0:T(8,128)S(1)}, f32[64,128]{1,0:T(8,128)S(1)}, u32[]{:S(2)}, u32[]{:S(2)}) collective-permute-start(f32[64,128]{1,0:T(8,128)S(1)} %get-tuple-element.233.refs_0_), channel_id=1, source_target_pairs={{0,1},{1,2},{2,3},{3,4},{4,5},{5,6},{6,7},{7,0},{8,9},{9,10},{10,1... | collective-permute-start | bytes 98312 | tf_op jit(solution)/shard_map/ppermute | solution.py:385
  77.9 2.2 %collective-permute-start.20 = (f32[64,128]{1,0:T(8,128)S(1)}, f32[64,128]{1,0:T(8,128)S(1)}, u32[]{:S(2)}, u32[]{:S(2)}) collective-permute-start(f32[64,128]{1,0:T(8,128)S(1)} %get-tuple-element.233.refs_0_), channel_id=1, source_target_pairs={{0,3},{1,4},{2,5},{3,6},{4,7},{5,0},{6,1},{7,2},{8,11},{9,12},{10,... | collective-permute-start | bytes 98312 | tf_op jit(solution)/shard_map/ppermute | solution.py:385
  80.1 3.2 %collective-permute-start.21 = (f32[64,128]{1,0:T(8,128)S(1)}, f32[64,128]{1,0:T(8,128)S(1)}, u32[]{:S(2)}, u32[]{:S(2)}) collective-permute-start(f32[64,128]{1,0:T(8,128)S(1)} %get-tuple-element.233.refs_0_), channel_id=1, source_target_pairs={{0,4},{1,5},{2,6},{3,7},{4,0},{5,1},{6,2},{7,3},{8,12},{9,13},{10,... | collective-permute-start | bytes 98312 | tf_op jit(solution)/shard_map/ppermute | solution.py:385
  83.3 2.9 %collective-permute-start.22 = (f32[64,128]{1,0:T(8,128)S(1)}, f32[64,128]{1,0:T(8,128)S(1)}, u32[]{:S(2)}, u32[]{:S(2)}) collective-permute-start(f32[64,128]{1,0:T(8,128)S(1)} %get-tuple-element.233.refs_0_), channel_id=1, source_target_pairs={{0,5},{1,6},{2,7},{3,0},{4,1},{5,2},{6,3},{7,4},{8,13},{9,14},{10,... | collective-permute-start | bytes 98312 | tf_op jit(solution)/shard_map/ppermute | solution.py:385
  88.0 2.9 %collective-permute-done.23.refs_6_ = f32[64,128]{1,0:T(8,128)S(1)} collective-permute-done((f32[64,128]{1,0:T(8,128)S(1)}, f32[64,128]{1,0:T(8,128)S(1)}, u32[]{:S(2)}, u32[]{:S(2)}) %collective-permute-start.23) | collective-permute-done | bytes 32800 | tf_op jit(solution)/shard_map/ppermute | solution.py:385
  92.5 3.1 %all-to-all-done.1 = bf16[16,3,264,128]{3,2,1,0:T(8,128)(2,1)} async-done(((bf16[16,3,264,128]{3,2,1,0:T(8,128)(2,1)}), bf16[16,3,264,128]{3,2,1,0:T(8,128)(2,1)}, u32[]{:S(2)}, u32[]{:S(2)}) %all-to-all-start.1) | async-done | bytes 3244064 | tf_op jit(solution)/shard_map/all_to_all | solution.py:400
  95.5 6.5 %all-to-all-start.2 = ((f32[32,1,128]{2,1,0:T(1,128)}), f32[32,1,128]{2,1,0:T(1,128)S(1)}, u32[]{:S(2)}, u32[]{:S(2)}) async-start(f32[32,1,128]{2,1,0:T(1,128)} %weigh.1.mine), calls=%async_computation.2 | async-start | bytes 32768 | tf_op jit(solution)/shard_map/all_to_all | solution.py:477
  103.3 3.8 %conditional.1 = (bf16[16,132,128]{2,0,1:T(8,128)(2,1)}, bf16[16,132,128]{2,0,1:T(8,128)(2,1)}) conditional(s32[]{:T(128)} %bitcast.13, (s32[8,128]{1,0:T(8,128)S(1)}, bf16[16,3,264,128]{3,2,1,0:T(8,128)(2,1)}) %tuple.54, (s32[]{:T(128)}, bf16[16,128,128]{2,1,0:T(8,128)(2,1)S(1)}, bf16[16,128,128]{2,1,0:T(8,128)(2,1)S(1)}, ...), branch_computations={%region_0.1_spmd, %region_1.6_spmd} | conditional | flops 4394106 | bytes 39339144 | solution.py:502
  103.3 2.1 %place.2 = (bf16[16,132,128]{2,1,0:T(8,128)(2,1)S(1)}, bf16[16,132,128]{2,1,0:T(8,128)(2,1)S(1)}) custom-call(s32[8,128]{1,0:T(8,128)S(1)} %get-tuple-element.168.refs_0_, bf16[16,3,264,128]{3,2,1,0:T(8,128)(2,1)} %get-tuple-element.169.refs_1_), custom_call_target="tpu_custom_call" | custom-call | tf_op jit(solution)/shard_map/cond/branch_0_fun/place/pallas_call | solution.py:370
  107.1 1.9 %all-to-all-done.2.every = f32[32,1,128]{2,1,0:T(1,128)S(1)} async-done(((f32[32,1,128]{2,1,0:T(1,128)}), f32[32,1,128]{2,1,0:T(1,128)S(1)}, u32[]{:S(2)}, u32[]{:S(2)}) %all-to-all-start.2) | async-done | bytes 16416 | tf_op jit(solution)/shard_map/all_to_all | solution.py:477
  (76 shorter events, 29.6 us)
Async XLA Ops:
  2.5 27.0 %all-to-all-start = ((bf16[8,64,512]{2,1,0:T(8,128)(2,1)}), bf16[8,64,512]{2,1,0:T(8,128)(2,1)S(1)}, u32[]{:S(2)}, u32[]{:S(2)}) async-start(bf16[8,64,512]{2,1,0:T(8,128)(2,1)} %broadcast_in_dim.19), calls=%async_computation | async-start | bytes 1048576 | tf_op jit(solution)/shard_map/all_to_all | solution.py:447
  12.5 15.3 %collective-permute-start.8 = (bf16[16,128,128]{2,1,0:T(8,128)(2,1)S(1)}, bf16[16,128,128]{2,1,0:T(8,128)(2,1)S(1)}, u32[]{:S(2)}, u32[]{:S(2)}) collective-permute-start(bf16[16,128,128]{2,1,0:T(8,128)(2,1)S(1)} %copy-done.4), channel_id=1, source_target_pairs={{0,8},{8,0},{16,24},{24,16},{32,40},{40,32},{48,56},{56,48},{64,72... | collective-permute-start | bytes 1572872 | tf_op jit(solution)/shard_map/ppermute | solution.py:389
  12.6 15.2 %collective-permute-start.9 = (bf16[16,128,128]{2,1,0:T(8,128)(2,1)S(1)}, bf16[16,128,128]{2,1,0:T(8,128)(2,1)S(1)}, u32[]{:S(2)}, u32[]{:S(2)}) collective-permute-start(bf16[16,128,128]{2,1,0:T(8,128)(2,1)S(1)} %copy-done.5), channel_id=1, source_target_pairs={{0,8},{8,0},{16,24},{24,16},{32,40},{40,32},{48,56},{56,48},{64,72... | collective-permute-start | bytes 1572872 | tf_op jit(solution)/shard_map/ppermute | solution.py:389
  14.0 4.9 %collective-permute-start.2 = (s32[2,16]{1,0:T(2,128)S(1)}, s32[2,16]{1,0:T(2,128)S(1)}, u32[]{:S(2)}, u32[]{:S(2)}) collective-permute-start(s32[2,16]{1,0:T(2,128)S(1)} %pad_add_fusion), channel_id=1, source_target_pairs={{0,16},{8,24},{16,32},{24,40},{32,48},{40,56},{48,0},{56,8},{64,80... | collective-permute-start | bytes 392 | tf_op jit(solution)/shard_map/ppermute | solution.py:408
  15.3 4.2 %collective-permute-start.3 = (s32[2,16]{1,0:T(2,128)S(1)}, s32[2,16]{1,0:T(2,128)S(1)}, u32[]{:S(2)}, u32[]{:S(2)}) collective-permute-start(s32[2,16]{1,0:T(2,128)S(1)} %pad_add_fusion), channel_id=1, source_target_pairs={{0,32},{8,40},{16,48},{24,56},{32,0},{40,8},{48,16},{56,24},{64,96... | collective-permute-start | bytes 392 | tf_op jit(solution)/shard_map/ppermute | solution.py:408
  20.5 5.7 %collective-permute-start.5 = (s32[8,16]{1,0:T(8,128)S(1)}, s32[8,16]{1,0:T(8,128)S(1)}, u32[]{:S(2)}, u32[]{:S(2)}) collective-permute-start(s32[8,16]{1,0:T(8,128)S(1)} %concatenate.35.refs_0_), channel_id=1, source_target_pairs={{0,64},{8,72},{16,80},{24,88},{32,96},{40,104},{48,112},{56,120},{... | collective-permute-start | bytes 1544 | tf_op jit(solution)/shard_map/ppermute | solution.py:408
  21.9 4.3 %collective-permute-start.6 = (s32[8,16]{1,0:T(8,128)S(1)}, s32[8,16]{1,0:T(8,128)S(1)}, u32[]{:S(2)}, u32[]{:S(2)}) collective-permute-start(s32[8,16]{1,0:T(8,128)S(1)} %concatenate.35.refs_0_), channel_id=1, source_target_pairs={{0,128},{8,136},{16,144},{24,152},{32,160},{40,168},{48,176},{56,1... | collective-permute-start | bytes 1544 | tf_op jit(solution)/shard_map/ppermute | solution.py:408
  24.5 2.8 %collective-permute-start.7 = (s32[8,16]{1,0:T(8,128)S(1)}, s32[8,16]{1,0:T(8,128)S(1)}, u32[]{:S(2)}, u32[]{:S(2)}) collective-permute-start(s32[8,16]{1,0:T(8,128)S(1)} %concatenate.35.refs_0_), channel_id=1, source_target_pairs={{0,192},{8,200},{16,208},{24,216},{32,224},{40,232},{48,240},{56,2... | collective-permute-start | bytes 1544 | tf_op jit(solution)/shard_map/ppermute | solution.py:408
  40.4 55.1 %all-to-all-start.1 = ((bf16[16,3,264,128]{3,2,1,0:T(8,128)(2,1)}), bf16[16,3,264,128]{3,2,1,0:T(8,128)(2,1)}, u32[]{:S(2)}, u32[]{:S(2)}) async-start(bf16[16,3,264,128]{3,2,1,0:T(8,128)(2,1)} %pack.1), calls=%async_computation.1 | async-start | bytes 6488064 | tf_op jit(solution)/shard_map/all_to_all | solution.py:400
  52.0 10.5 %collective-permute-start.11 = (bf16[64,512]{1,0:T(8,128)(2,1)}, bf16[64,512]{1,0:T(8,128)(2,1)S(1)}, u32[]{:S(2)}, u32[]{:S(2)}) collective-permute-start(bf16[64,512]{1,0:T(8,128)(2,1)} %get-tuple-element.225), channel_id=1, source_target_pairs={{0,1},{1,2},{2,3},{3,4},{4,5},{5,6},{6,7},{7,0},{8,9},{9,10},{10,1... | collective-permute-start | bytes 196616 | tf_op jit(solution)/shard_map/ppermute | solution.py:385
  53.5 12.3 %collective-permute-start.12 = (bf16[64,512]{1,0:T(8,128)(2,1)}, bf16[64,512]{1,0:T(8,128)(2,1)S(1)}, u32[]{:S(2)}, u32[]{:S(2)}) collective-permute-start(bf16[64,512]{1,0:T(8,128)(2,1)} %get-tuple-element.226), channel_id=1, source_target_pairs={{0,2},{1,3},{2,4},{3,5},{4,6},{5,7},{6,0},{7,1},{8,10},{9,11},{10,... | collective-permute-start | bytes 196616 | tf_op jit(solution)/shard_map/ppermute | solution.py:385
  55.6 11.4 %collective-permute-start.13 = (bf16[64,512]{1,0:T(8,128)(2,1)}, bf16[64,512]{1,0:T(8,128)(2,1)S(1)}, u32[]{:S(2)}, u32[]{:S(2)}) collective-permute-start(bf16[64,512]{1,0:T(8,128)(2,1)} %get-tuple-element.227), channel_id=1, source_target_pairs={{0,3},{1,4},{2,5},{3,6},{4,7},{5,0},{6,1},{7,2},{8,11},{9,12},{10,... | collective-permute-start | bytes 196616 | tf_op jit(solution)/shard_map/ppermute | solution.py:385
  58.0 9.0 %collective-permute-start.14 = (bf16[64,512]{1,0:T(8,128)(2,1)}, bf16[64,512]{1,0:T(8,128)(2,1)S(1)}, u32[]{:S(2)}, u32[]{:S(2)}) collective-permute-start(bf16[64,512]{1,0:T(8,128)(2,1)} %get-tuple-element.228), channel_id=1, source_target_pairs={{0,4},{1,5},{2,6},{3,7},{4,0},{5,1},{6,2},{7,3},{8,12},{9,13},{10,... | collective-permute-start | bytes 196616 | tf_op jit(solution)/shard_map/ppermute | solution.py:385
  60.1 8.6 %collective-permute-start.15 = (bf16[64,512]{1,0:T(8,128)(2,1)}, bf16[64,512]{1,0:T(8,128)(2,1)S(1)}, u32[]{:S(2)}, u32[]{:S(2)}) collective-permute-start(bf16[64,512]{1,0:T(8,128)(2,1)} %get-tuple-element.229), channel_id=1, source_target_pairs={{0,5},{1,6},{2,7},{3,0},{4,1},{5,2},{6,3},{7,4},{8,13},{9,14},{10,... | collective-permute-start | bytes 196616 | tf_op jit(solution)/shard_map/ppermute | solution.py:385
  62.5 11.5 %collective-permute-start.16 = (bf16[64,512]{1,0:T(8,128)(2,1)}, bf16[64,512]{1,0:T(8,128)(2,1)S(1)}, u32[]{:S(2)}, u32[]{:S(2)}) collective-permute-start(bf16[64,512]{1,0:T(8,128)(2,1)} %get-tuple-element.230), channel_id=1, source_target_pairs={{0,6},{1,7},{2,0},{3,1},{4,2},{5,3},{6,4},{7,5},{8,14},{9,15},{10,... | collective-permute-start | bytes 196616 | tf_op jit(solution)/shard_map/ppermute | solution.py:385
  65.8 8.2 %collective-permute-start.17 = (bf16[64,512]{1,0:T(8,128)(2,1)}, bf16[64,512]{1,0:T(8,128)(2,1)S(1)}, u32[]{:S(2)}, u32[]{:S(2)}) collective-permute-start(bf16[64,512]{1,0:T(8,128)(2,1)} %get-tuple-element.231), channel_id=1, source_target_pairs={{0,7},{1,0},{2,1},{3,2},{4,3},{5,4},{6,5},{7,6},{8,15},{9,8},{10,9... | collective-permute-start | bytes 196616 | tf_op jit(solution)/shard_map/ppermute | solution.py:385
  75.6 10.6 %collective-permute-start.18 = (f32[64,128]{1,0:T(8,128)S(1)}, f32[64,128]{1,0:T(8,128)S(1)}, u32[]{:S(2)}, u32[]{:S(2)}) collective-permute-start(f32[64,128]{1,0:T(8,128)S(1)} %get-tuple-element.233.refs_0_), channel_id=1, source_target_pairs={{0,1},{1,2},{2,3},{3,4},{4,5},{5,6},{6,7},{7,0},{8,9},{9,10},{10,1... | collective-permute-start | bytes 98312 | tf_op jit(solution)/shard_map/ppermute | solution.py:385
  77.9 9.8 %collective-permute-start.19 = (f32[64,128]{1,0:T(8,128)S(1)}, f32[64,128]{1,0:T(8,128)S(1)}, u32[]{:S(2)}, u32[]{:S(2)}) collective-permute-start(f32[64,128]{1,0:T(8,128)S(1)} %get-tuple-element.233.refs_0_), channel_id=1, source_target_pairs={{0,2},{1,3},{2,4},{3,5},{4,6},{5,7},{6,0},{7,1},{8,10},{9,11},{10,... | collective-permute-start | bytes 98312 | tf_op jit(solution)/shard_map/ppermute | solution.py:385
  77.9 10.0 %collective-permute-start.20 = (f32[64,128]{1,0:T(8,128)S(1)}, f32[64,128]{1,0:T(8,128)S(1)}, u32[]{:S(2)}, u32[]{:S(2)}) collective-permute-start(f32[64,128]{1,0:T(8,128)S(1)} %get-tuple-element.233.refs_0_), channel_id=1, source_target_pairs={{0,3},{1,4},{2,5},{3,6},{4,7},{5,0},{6,1},{7,2},{8,11},{9,12},{10,... | collective-permute-start | bytes 98312 | tf_op jit(solution)/shard_map/ppermute | solution.py:385
  80.1 7.8 %collective-permute-start.21 = (f32[64,128]{1,0:T(8,128)S(1)}, f32[64,128]{1,0:T(8,128)S(1)}, u32[]{:S(2)}, u32[]{:S(2)}) collective-permute-start(f32[64,128]{1,0:T(8,128)S(1)} %get-tuple-element.233.refs_0_), channel_id=1, source_target_pairs={{0,4},{1,5},{2,6},{3,7},{4,0},{5,1},{6,2},{7,3},{8,12},{9,13},{10,... | collective-permute-start | bytes 98312 | tf_op jit(solution)/shard_map/ppermute | solution.py:385
  83.3 4.7 %collective-permute-start.22 = (f32[64,128]{1,0:T(8,128)S(1)}, f32[64,128]{1,0:T(8,128)S(1)}, u32[]{:S(2)}, u32[]{:S(2)}) collective-permute-start(f32[64,128]{1,0:T(8,128)S(1)} %get-tuple-element.233.refs_0_), channel_id=1, source_target_pairs={{0,5},{1,6},{2,7},{3,0},{4,1},{5,2},{6,3},{7,4},{8,13},{9,14},{10,... | collective-permute-start | bytes 98312 | tf_op jit(solution)/shard_map/ppermute | solution.py:385
  86.2 4.6 %collective-permute-start.23 = (f32[64,128]{1,0:T(8,128)S(1)}, f32[64,128]{1,0:T(8,128)S(1)}, u32[]{:S(2)}, u32[]{:S(2)}) collective-permute-start(f32[64,128]{1,0:T(8,128)S(1)} %get-tuple-element.233.refs_0_), channel_id=1, source_target_pairs={{0,6},{1,7},{2,0},{3,1},{4,2},{5,3},{6,4},{7,5},{8,14},{9,15},{10,... | collective-permute-start | bytes 98312 | tf_op jit(solution)/shard_map/ppermute | solution.py:385
  87.8 3.9 %collective-permute-start.24 = (f32[64,128]{1,0:T(8,128)S(1)}, f32[64,128]{1,0:T(8,128)S(1)}, u32[]{:S(2)}, u32[]{:S(2)}) collective-permute-start(f32[64,128]{1,0:T(8,128)S(1)} %get-tuple-element.233.refs_0_), channel_id=1, source_target_pairs={{0,7},{1,0},{2,1},{3,2},{4,3},{5,4},{6,5},{7,6},{8,15},{9,8},{10,9... | collective-permute-start | bytes 98312 | tf_op jit(solution)/shard_map/ppermute | solution.py:385
  95.5 13.5 %all-to-all-start.2 = ((f32[32,1,128]{2,1,0:T(1,128)}), f32[32,1,128]{2,1,0:T(1,128)S(1)}, u32[]{:S(2)}, u32[]{:S(2)}) async-start(f32[32,1,128]{2,1,0:T(1,128)} %weigh.1.mine), calls=%async_computation.2 | async-start | bytes 32768 | tf_op jit(solution)/shard_map/all_to_all | solution.py:477
  (14 other events, 188.6 us)

commit v3 on v2

--- a/solution.py
+++ b/solution.py
@@ -42,11 +42,13 @@
     return jnp.dot(a, b, preferred_element_type=F32)
 
 
-def project_body(acts, gain, wq, wk, wv, table, qa, kf, vf, fresh, *scratch):
-    wq_s, wk_s, wv_s, q_s, kf_s, vf_s, sems = scratch
+def project_body(blk, *refs):
+    acts = refs[:TP]
+    gain, wq, wk, wv, table, qa, kf, vf, fresh = refs[TP : TP + 9]
+    wq_s, wk_s, wv_s, q_s, kf_s, vf_s, sems = refs[TP + 9 :]
     copies = []
     for s in range(TP):
-        part = pl.ds(s * DB, DB)
+        part = pl.ds(pl.multiple_of(blk[s] * DB, DB), DB)
         copies.append(
             [
                 pltpu.make_async_copy(w.at[part, :], w_s.at[s], sems.at[n, s])
@@ -58,15 +60,15 @@
             c.start()
     square = jnp.zeros((ROWS, 1), F32)
     for s in range(TP):
-        x = acts[s].astype(F32)
+        x = acts[s][...].astype(F32)
         square = square + jnp.sum(x * x, -1, keepdims=True)
     inv = lax.rsqrt(square / D + 1e-05)
     q = jnp.zeros((ROWS, DB), F32)
     k = jnp.zeros((ROWS, HD), F32)
     v = jnp.zeros((ROWS, HD), F32)
     for s in range(TP):
-        x = acts[s].astype(F32)
-        normed = (x * inv * gain[s : s + 1, :]).astype(BF)
+        x = acts[s][...].astype(F32)
+        normed = (x * inv * gain[pl.ds(blk[s], 1), :]).astype(BF)
         for c in copies[s]:
             c.wait()
         q = q + mm(normed, wq_s[s])
@@ -94,11 +96,11 @@
         ).astype(BF)
 
 
-def project(acts, gain, wq, wk, wv, table):
+def project(blk, acts, gain, wq, wk, wv, table):
     sd = jax.ShapeDtypeStruct
     return pl.pallas_call(
         project_body,
-        in_specs=[spec(VM)] * 2 + [spec(ANY)] * 3 + [spec(VM)],
+        in_specs=[spec(SM)] + [spec(VM)] * (TP + 1) + [spec(ANY)] * 3 + [spec(VM)],
         out_specs=[spec(VM)] * 4,
         out_shape=[
             sd((NP * GROUP, HD), BF),
@@ -120,7 +122,7 @@
             flops=2 * ROWS * D * 768, bytes_accessed=7 * 2**20, transcendentals=0
         ),
         name="project",
-    )(acts, gain, wq, wk, wv, table)
+    )(blk, *acts, gain, wq, wk, wv, table)
 
 
 def attend_body(blk, qa, kf, vf, kc, vc, wo, *refs):
@@ -128,7 +130,7 @@
     s1_s, ctx_s, wo_s, sems = refs[TP:]
     copies = []
     for s in range(TP):
-        there = pl.ds(pl.multiple_of(blk[s] * DB, DB), DB)
+        there = pl.ds(pl.multiple_of(blk[TP + s] * DB, DB), DB)
         copies.append(pltpu.make_async_copy(wo.at[:, there], wo_s.at[s], sems.at[s]))
     for c in copies:
         c.start()
@@ -190,8 +192,10 @@
     summed = act[...].astype(F32) + mix
     aligned = jnp.sum(summed * twist[...], -1, keepdims=True)
     energy = jnp.sum(summed * summed, -1, keepdims=True)
+    row = lax.broadcasted_iota(jnp.int32, (ROWS, HD), 0)
     lane = lax.broadcasted_iota(jnp.int32, (ROWS, HD), 1)
-    sums[...] = jnp.where(lane == 0, aligned, energy)
+    both = jnp.where(lane == row, aligned, 0.0) + jnp.where(lane == row + ROWS, energy, 0.0)
+    sums[...] = jnp.broadcast_to(jnp.sum(both, 0, keepdims=True)[None], (TP, 1, HD))
 
 
 def mix(parts, act, twist):
@@ -200,69 +204,95 @@
         mix_body,
         in_specs=[spec(VM)] * (TP + 2),
         out_specs=[spec(VM)] * 2,
-        out_shape=[sd((ROWS, DB), BF), sd((ROWS, HD), F32)],
+        out_shape=[sd((ROWS, DB), BF), sd((TP, 1, HD), F32)],
         compiler_params=limit(8),
         name="mix",
     )(*parts, act, twist)
 
 
-def weigh_body(*refs):
-    parts = refs[:TP]
-    reward, previous, out = refs[TP:]
-    sums = parts[0][...]
-    for s in range(1, TP):
-        sums = sums + parts[s][...]
-    score = sums[:, 0:1] / jnp.sqrt(sums[:, 1:2] / D + 1e-06) + reward[...]
-    gain = score[0:NP]
+def weigh_body(idx, sums, reward, previous, fresh, line, sent):
+    total = sums[0]
+    for t in range(1, TP):
+        total = total + sums[t]
+    energy = pltpu.roll(total, ROWS, 1)
+    score = total / jnp.sqrt(energy / D + 1e-06) + reward[...]
+    gain = score
     for t in range(1, STEPS):
-        gain = gain + score[t * NP : (t + 1) * NP]
-    column = jnp.broadcast_to(previous[...] + gain, (NP, HD))
-    row = lax.broadcasted_iota(jnp.int32, (NP, HD), 0)
-    lane = lax.broadcasted_iota(jnp.int32, (NP, HD), 1)
-    line = jnp.sum(jnp.where(row == lane, column, 0.0), 0, keepdims=True)
-    out[...] = jnp.broadcast_to(line[None], (NDOM, 1, HD))
-
-
-def weigh(parts, reward, previous):
+        gain = gain + pltpu.roll(score, HD - NP * t, 1)
+    logw = previous[...] + gain
+    line[...] = logw
+    high = logw.astype(BF).astype(F32)
+    middle = (logw - high).astype(BF).astype(F32)
+    low = logw - high - middle
+    row = lax.broadcasted_iota(jnp.int32, (8, HD), 0)
+    parts = jnp.where(row == 0, high, jnp.where(row == 1, middle, jnp.where(row == 2, low, 0.0)))
+    parts = parts.astype(BF)
+    for d in range(NDOM):
+        sent[d, 0] = fresh[idx[1, 2 * d]]
+        sent[d, 1] = fresh[idx[1, 2 * d + 1]]
+        sent[d, 2] = parts
+
+
+def weigh(idx, sums, reward, previous, fresh):
+    sd = jax.ShapeDtypeStruct
     return pl.pallas_call(
         weigh_body,
-        in_specs=[spec(VM)] * (TP + 2),
-        out_specs=spec(VM),
-        out_shape=jax.ShapeDtypeStruct((NDOM, 1, HD), F32),
+        in_specs=[spec(SM)] + [spec(VM)] * 4,
+        out_specs=[spec(VM)] * 2,
+        out_shape=[sd((1, HD), F32), sd((NDOM, 3, 8, HD), BF)],
         compiler_params=limit(8),
         name="weigh",
-    )(*parts, reward, previous)
-
-
-def finish_body(mine, every, out):
+    )(idx, sums, reward, previous, fresh)
+
+
+def finish_body(idx, line, got, keys_in, values_in, logw, keys, values, all_s, f_s, k_s, v_s, sems):
+    for k in range(NP):
+        code = idx[1, 64 + k]
+        f_s[pl.ds(k, 2 * STEPS, stride=NP), :] = got[code // 2, code % 2].astype(F32)
+    half = STEPS * NP
+    k_s[...] = f_s[0:half, :].reshape(STEPS, NP, HD).astype(BF)
+    v_s[...] = f_s[half : 2 * half, :].reshape(STEPS, NP, HD).astype(BF)
+    tail = pl.ds(SPAN, STEPS)
+    copies = [
+        pltpu.make_async_copy(k_s, keys.at[tail], sems.at[0]),
+        pltpu.make_async_copy(v_s, values.at[tail], sems.at[1]),
+    ]
+    for c in copies:
+        c.start()
+    for d in range(NDOM):
+        all_s[d : d + 1, :] = jnp.sum(got[d, 2].astype(F32), 0, keepdims=True)
     lane = lax.broadcasted_iota(jnp.int32, (NDOM, HD), 1)
-    all_w = jnp.where(lane < NP, every[:, 0, :], -jnp.inf)
+    all_w = jnp.where(lane < NP, all_s[...], -jnp.inf)
     largest = jnp.max(all_w, keepdims=True)
     mass = jnp.sum(jnp.exp(all_w - largest), keepdims=True)
-    out[...] = (mine[0] - (largest + jnp.log(mass)))[:, 0:NP]
-
-
-def finish(mine, every):
+    logw[...] = (line[...] - (largest + jnp.log(mass)))[:, 0:NP]
+    for c in copies:
+        c.wait()
+
+
+def finish(idx, line, got, keys, values):
+    sd = jax.ShapeDtypeStruct
     return pl.pallas_call(
         finish_body,
-        in_specs=[spec(VM)] * 2,
-        out_specs=spec(VM),
-        out_shape=jax.ShapeDtypeStruct((1, NP), F32),
+        in_specs=[spec(SM)] + [spec(VM)] * 2 + [spec(ANY)] * 2,
+        out_specs=[spec(VM)] + [spec(ANY)] * 2,
+        out_shape=[sd((1, NP), F32), sd(keys.shape, BF), sd(values.shape, BF)],
+        scratch_shapes=[
+            VM((NDOM, HD), F32),
+            VM((2 * STEPS * NP, HD), F32),
+            VM((STEPS, NP, HD), BF),
+            VM((STEPS, NP, HD), BF),
+            pltpu.SemaphoreType.DMA((2,)),
+        ],
+        input_output_aliases={3: 1, 4: 2},
         compiler_params=limit(8),
         name="finish",
-    )(mine, every)
-
-
-def plan_body(me_ref, *refs):
-    out = refs[-1]
+    )(idx, line, got, keys, values)
+
+
+def plan_body(me_ref, counts_ref, out):
     me = me_ref[0]
-    blocks = jnp.concatenate([r[...] for r in refs[:-1]], 0).astype(F32)
-    rel = lax.broadcasted_iota(jnp.int32, (NDOM, NDOM), 1)
-    back_y = (me // 8 - rel // 8) & 3
-    back_x = (me // 2 - rel // 2) & 3
-    holder = 8 * back_y + 2 * back_x + ((me + rel) & 1)
-    sorted_rows = lax.broadcasted_iota(jnp.int32, (NDOM, NDOM), 0) == holder
-    counts = mm(sorted_rows.astype(F32), blocks)
+    counts = counts_ref[:, 0, 0:NP].astype(F32)
     r16 = lax.broadcasted_iota(jnp.int32, (NP, NP), 0)
     c16 = lax.broadcasted_iota(jnp.int32, (NP, NP), 1)
     within = mm(counts, (r16 <= c16).astype(F32))
@@ -293,18 +323,33 @@
     pair = lax.broadcasted_iota(jnp.int32, (NDOM, HD), 1)
     most = jnp.max(jnp.sum(jnp.where(pair == device // 2, owned, 0), 0, keepdims=True))
     line = jnp.where(lane < 64, particle, jnp.where(lane < 80, arrived, most))
-    out[...] = jnp.broadcast_to(line, (8, HD))
-
-
-def plan(me, blocks):
+
+    own = jnp.sum(jnp.where(device == me, before, 0))
+    sent = own + ((lane // 2 - own) & (NDOM - 1)) + NDOM * (lane % 2)
+    found = jnp.zeros((NDOM, HD), jnp.int32)
+    for j in range(NP):
+        found = found + (ends[:, j : j + 1] <= sent).astype(jnp.int32)
+    particle = jnp.sum(found, 0, keepdims=True) - NP * me
+    particle = jnp.clip(particle, 0, NP - 1)
+    passed = ends[:, NP - 1 : NP] <= kept
+    source = jnp.sum(passed.astype(jnp.int32), 0, keepdims=True)
+    base = jnp.max(jnp.where(passed, ends[:, NP - 1 : NP], 0), 0, keepdims=True)
+    slot = jnp.clip((kept - base) // NDOM, 0, 1)
+    arrived = 2 * jnp.clip(source, 0, NDOM - 1) + slot
+    second = jnp.where(lane < 64, particle, arrived)
+    row = lax.broadcasted_iota(jnp.int32, (8, HD), 0)
+    out[...] = jnp.where(row == 0, line, second)
+
+
+def plan(me, counts):
     return pl.pallas_call(
         plan_body,
-        in_specs=[spec(SM)] + [spec(VM)] * len(blocks),
+        in_specs=[spec(SM), spec(VM)],
         out_specs=spec(VM),
         out_shape=jax.ShapeDtypeStruct((8, HD), jnp.int32),
         compiler_params=limit(8),
         name="plan",
-    )(me, *blocks)
+    )(me, counts)
 
 
 def pack_body(me_ref, idx, *refs):
@@ -345,37 +390,28 @@
     )(me, idx, *own, *partner)
 
 
-def place_body(slots, idx, rows, keys, values, r_s, sems):
+def place_body(slots, idx, rows, keys, values, sems):
     copies = []
     for k in range(NP):
         code = idx[0, 64 + k]
         slot = jnp.minimum(code % 4, slots - 1)
-        copies.append(
-            pltpu.make_async_copy(rows.at[code // 4, slot], r_s.at[k], sems.at[k])
-        )
+        for n, out in enumerate((keys, values)):
+            part = rows.at[code // 4, slot, pl.ds(n * SPAN, SPAN), :]
+            copies.append(pltpu.make_async_copy(part, out.at[k], sems.at[n, k]))
     for c in copies:
         c.start()
-    for k in range(NP):
-        copies[k].wait()
-        keys[k, 0:SPAN, :] = r_s[k, 0:SPAN, :]
-        values[k, 0:SPAN, :] = r_s[k, SPAN : 2 * SPAN, :]
-        tail = r_s[k, 2 * SPAN : 2 * SPAN + 2 * STEPS, :].astype(F32)
-        keys[k, SPAN : SPAN + STEPS, :] = tail[0:STEPS].astype(BF)
-        values[k, SPAN : SPAN + STEPS, :] = tail[STEPS : 2 * STEPS].astype(BF)
+    for c in copies:
+        c.wait()
 
 
 def place(idx, rows):
-    out = jax.ShapeDtypeStruct((NP, SPAN + STEPS, HD), BF)
     slots = rows.shape[1]
     return pl.pallas_call(
         lambda *refs: place_body(slots, *refs),
         in_specs=[spec(SM), spec(ANY)],
         out_specs=[spec(VM)] * 2,
-        out_shape=[out] * 2,
-        scratch_shapes=[
-            VM((NP, 2 * SPAN + 2 * STEPS, HD), BF),
-            pltpu.SemaphoreType.DMA((NP,)),
-        ],
+        out_shape=[jax.ShapeDtypeStruct((NP, SPAN, HD), BF)] * 2,
+        scratch_shapes=[pltpu.SemaphoreType.DMA((2, NP))],
         compiler_params=limit(16),
         name="place",
     )(idx, rows)
@@ -400,19 +436,10 @@
     return lax.all_to_all(rows, "dom", 0, 0, tiled=True, axis_index_groups=SAME_CORE)
 
 
-def moved(value, axis_stride, shift):
-    def to(i):
-        at = i // axis_stride % 4
-        return i + ((at + shift) % 4 - at) * axis_stride
-
-    return lax.ppermute(value, "dom", [(i, to(i)) for i in range(NDOM)])
-
-
-def spread_counts(copy_counts):
-    own = copy_counts.reshape(1, NP)
-    chip = jnp.concatenate([own, swapped(own)], 0)
-    row = jnp.concatenate([chip] + [moved(chip, 2, s) for s in range(1, 4)], 0)
-    return [row] + [moved(row, 8, s) for s in range(1, 4)]
+def counts_of_all(counts):
+    line = jnp.pad(counts, (0, HD - NP))
+    sent = jnp.broadcast_to(line[None, None], (NDOM, 8, HD))
+    return lax.all_to_all(sent, "dom", 0, 0, tiled=True)
 
 
 def rotation_table():
@@ -441,49 +468,41 @@
     dom = lax.axis_index("dom")
     tp = lax.axis_index("tp")
     me = dom.reshape(1)
-    blk = ((tp + np.arange(TP)) % TP).astype(jnp.int32)
+    ring = np.arange(TP)
+    blk = (jnp.concatenate([tp - ring, tp + ring]) % TP).astype(jnp.int32)
     act = activations.reshape(ROWS, DB)
 
-    gathered = lax.all_to_all(
-        jnp.broadcast_to(act[None], (TP, ROWS, DB)), "tp", 0, 0, tiled=True
-    )
-    idx = plan(me, spread_counts(copy_counts))
+    counts = counts_of_all(copy_counts)
+    acts = [act] + [shifted(act, s) for s in range(1, TP)]
+    counts, *acts[2:6] = lax.optimization_barrier((counts, *acts[2:6]))
     partner_keys = swapped(cache_keys)
     partner_values = swapped(cache_values)
-    reward = twisting_table[tokens.reshape(ROWS)].astype(F32).reshape(ROWS, 1)
-
-    gathered, idx, partner_keys, partner_values, reward = lax.optimization_barrier(
-        (gathered, idx, partner_keys, partner_values, reward)
+    idx = plan(me, counts)
+    packed = pack(me, idx, [cache_keys, cache_values], [partner_keys, partner_values])
+    rows = exchanged(packed)
+    reward = twisting_table[tokens.reshape(ROWS)].astype(F32)
+    reward = jnp.pad(reward, (0, HD - ROWS)).reshape(1, HD)
+    previous = jnp.pad(previous_log_weights, (0, HD - NP)).reshape(1, HD)
+
+    packed, *acts = lax.optimization_barrier((packed, *acts))
+    qa, kf, vf, fresh = project(
+        blk, acts, norm_gain.reshape(TP, DB), w_query, w_key, value_weight, rotation_table()
     )
-    qa, kf, vf, fresh = project(
-        gathered, norm_gain.reshape(TP, DB), w_query, w_key, value_weight, rotation_table()
-    )
-    partner_fresh = swapped(fresh)
-    packed = pack(
-        me,
-        idx,
-        [cache_keys, cache_values, fresh],
-        [partner_keys, partner_values, partner_fresh],
-    )
-    packed, qa = lax.optimization_barrier((packed, qa))
-    rows = exchanged(packed)
     partials = attend(blk, qa, kf, vf, cache_keys, cache_values, w_output)
-
     parts = [partials[0]] + [shifted(partials[s], s) for s in range(1, TP)]
     attn, sums = mix(parts, act, twist_vec.reshape(1, DB))
-    all_sums = [sums] + [shifted(sums, s) for s in range(1, TP)]
-    logw = weigh(all_sums, reward, previous_log_weights.reshape(NP, 1))
-    logw, rows = lax.optimization_barrier((logw, rows))
-    every = lax.all_to_all(logw, "dom", 0, 0, tiled=True)
-    out_logw = finish(logw, every).reshape(NP)
+    sums, rows, reward, previous = lax.optimization_barrier((sums, rows, reward, previous))
+    sums = lax.all_to_all(sums, "tp", 0, 0, tiled=True)
+    line, sent = weigh(idx, sums, reward, previous, fresh)
+    got = lax.all_to_all(sent, "dom", 0, 0, tiled=True)
 
     def usual(rows, *_):
         return tuple(place(idx, rows))
 
-    def crowded(rows, partner_keys, partner_values, partner_fresh, fresh, idx):
+    def crowded(rows, partner_keys, partner_values, idx):
         even = dom % 2 == 0
-        mine = jnp.concatenate([cache_keys, cache_values, fresh], 1)
-        other = jnp.concatenate([partner_keys, partner_values, partner_fresh], 1)
+        mine = jnp.concatenate([cache_keys, cache_values], 1)
+        other = jnp.concatenate([partner_keys, partner_values], 1)
         chip_rows = jnp.concatenate(
             [jnp.where(even, mine, other), jnp.where(even, other, mine)], 0
         )
@@ -499,18 +518,28 @@
         more = lax.fori_loop(1, NCHIP, turn, start)[1].at[chip].set(chosen[chip])
         return tuple(place(idx, jnp.concatenate([rows, more[:, None]], 1)))
 
-    new_keys, new_values = lax.cond(
+    old_keys, old_values = lax.cond(
         idx[0, 127] > SLOTS * NDOM,
         crowded,
         usual,
         rows,
         partner_keys,
         partner_values,
-        partner_fresh,
-        fresh,
         idx,
     )
-    return (attn.reshape(STEPS, NP, DB), new_keys, new_values, out_logw)
+
+    def by_position(old):
+        return jnp.pad(jnp.transpose(old, (1, 0, 2)), ((0, STEPS), (0, 0), (0, 0)))
+
+    out_logw, new_keys, new_values = finish(
+        idx, line, got, by_position(old_keys), by_position(old_values)
+    )
+    return (
+        attn.reshape(STEPS, NP, DB),
+        jnp.transpose(new_keys, (1, 0, 2)),
+        jnp.transpose(new_values, (1, 0, 2)),
+        out_logw.reshape(NP),
+    )
 
 
 def solution(mesh):

time: 111 us -> 118 us (1.063)
  blocking collectives: 0 us -> 16.6 us
  starting transfers between devices: 61.6 us -> 52.3 us
  waiting for transfers between devices: 20.8 us -> 17.8 us
  Pallas kernels: 18.6 us -> 20.7 us
    all_to_all x0 -> x1, blocking collectives: none -> 16.6 us  [local(): sums = lax.all_to_all(sums, 'tp', 0, 0, tiled=True)]
    ppermute x6 -> x0, starting transfers between devices: 9.98 us -> none  [moved(): return lax.ppermute(value, 'dom', [(i, to(i)) for i in range(NDOM)])]
    ppermute x14, waiting for transfers between devices: 10.8 us -> 15.3 us  [shifted(): return lax.ppermute(value, 'tp', [(i, (i + shift) % TP) for i in range(TP)])]
    all_to_all x1, waiting for transfers between devices: 3.06 us -> 0.01 us  [exchanged(): lax.all_to_all(rows, 'dom', 0, 0, tiled=True, axis_index_groups=SAME_CORE)]
    ppermute x6 -> x0, waiting for transfers between devices: 2.63 us -> none  [moved(): return lax.ppermute(value, 'dom', [(i, to(i)) for i in range(NDOM)])]
    pad x0 -> x3, local copies, waits for them, and re-layouts: none -> 2.44 us  [the longest x2 1.78 us: by_position(): return jnp.pad(jnp.transpose(old, (1, 0, 2)), ((0, STEPS), (0, 0), (0, 0)))]
    ppermute x4 -> x2, starting transfers between devices: 2.94 us -> 3.43 us  [swapped(): return lax.ppermute(value, 'dom', [(i, i ^ 1) for i in range(NDOM)])]
  transfers between devices with their start and end apart: 27 -> 19, of which waited for: 11 -> 8; matrix products, arithmetic and copies ran while one was open for 4% -> 6% of each run, Pallas kernels for 8% -> 12%
where the time goes in v3:
time: 118 us; the launch traced here: 117 us
  starting transfers between devices  52.3 us (44%)
  Pallas kernels  20.7 us (18%)
  waiting for transfers between devices  17.8 us (15%)
  blocking collectives  16.6 us (14%)
  local copies, waits for them, and re-layouts  7.51 us (6%)
  between operations  1.75 us (1%)
    ppermute x14, starting transfers between devices, shifted(): return lax.ppermute(value, 'tp', [(i, (i + shift) % TP) for i in range(TP)])  27.9 us
    all_to_all x1, blocking collectives, local(): sums = lax.all_to_all(sums, 'tp', 0, 0, tiled=True)  16.6 us
    ppermute x14, waiting for transfers between devices, shifted(): return lax.ppermute(value, 'tp', [(i, (i + shift) % TP) for i in range(TP)])  15.3 us
    all_to_all x1, starting transfers between devices, counts_of_all(): return lax.all_to_all(sent, 'dom', 0, 0, tiled=True)  7.77 us
    all_to_all x1, starting transfers between devices, local(): got = lax.all_to_all(sent, 'dom', 0, 0, tiled=True)  7.32 us
    all_to_all x1, starting transfers between devices, exchanged(): lax.all_to_all(rows, 'dom', 0, 0, tiled=True, axis_index_groups=SAME_CORE)  5.89 us
    pallas_call x1, Pallas kernels, project(): pl.pallas_call(project_body, in_specs=[spec(SM)] + [spec(VM)] * (TP + 1)...  5.41 us
    pallas_call x1, Pallas kernels, attend(): pl.pallas_call(attend_body, in_specs=[spec(SM)] + [spec(VM)] * 5 + [spec(...  5.05 us
  transfers between devices with their start and end apart: 19, of which 8 were waited for; matrix products, arithmetic and copies ran while one was open for 6% of the time, Pallas kernels for 12%

profile of v3, /device:TPU:1, one launch (start us, length us, event | category | flops | bytes accessed | tf_op | source)
XLA Modules:
  0.0 117.3 jit_solution(13028373328323691170)
XLA Ops:
  0.6 3.3 %collective-permute-start.5 = (bf16[16,128,128]{2,1,0:T(8,128)(2,1)}, bf16[16,128,128]{2,1,0:T(8,128)(2,1)S(1)}, u32[]{:S(2)}, u32[]{:S(2)}) collective-permute-start(bf16[16,128,128]{2,1,0:T(8,128)(2,1)} %kc.1), channel_id=1, source_target_pairs={{0,8},{8,0},{16,24},{24,16},{32,40},{40,32},{48,56},{56,48},{64,72... | collective-permute-start | bytes 1572872 | tf_op jit(solution)/shard_map/ppermute | solution.py:425
  6.7 7.8 %all-to-all-start = ((s32[32,8,128]{2,1,0:T(8,128)}), s32[32,8,128]{2,1,0:T(8,128)S(1)}, u32[]{:S(2)}, u32[]{:S(2)}) async-start(s32[32,8,128]{2,1,0:T(8,128)} %broadcast_in_dim.9), calls=%async_computation | async-start | bytes 262144 | tf_op jit(solution)/shard_map/all_to_all | solution.py:442
  14.4 4.7 %collective-permute-start.2 = (bf16[64,512]{1,0:T(8,128)(2,1)}, bf16[64,512]{1,0:T(8,128)(2,1)S(1)}, u32[]{:S(2)}, u32[]{:S(2)}) collective-permute-start(bf16[64,512]{1,0:T(8,128)(2,1)} %bitcast.33), channel_id=1, source_target_pairs={{0,3},{1,4},{2,5},{3,6},{4,7},{5,0},{6,1},{7,2},{8,11},{9,12},{10,... | collective-permute-start | bytes 196616 | tf_op jit(solution)/shard_map/ppermute | solution.py:421
  19.8 4.3 %collective-permute-start.4 = (bf16[64,512]{1,0:T(8,128)(2,1)}, bf16[64,512]{1,0:T(8,128)(2,1)S(1)}, u32[]{:S(2)}, u32[]{:S(2)}) collective-permute-start(bf16[64,512]{1,0:T(8,128)(2,1)} %bitcast.35), channel_id=1, source_target_pairs={{0,5},{1,6},{2,7},{3,0},{4,1},{5,2},{6,3},{7,4},{8,13},{9,14},{10,... | collective-permute-start | bytes 196616 | tf_op jit(solution)/shard_map/ppermute | solution.py:421
  24.5 2.0 %collective-permute-done.3.refs_4_ = bf16[64,512]{1,0:T(8,128)(2,1)S(1)} collective-permute-done((bf16[64,512]{1,0:T(8,128)(2,1)}, bf16[64,512]{1,0:T(8,128)(2,1)S(1)}, u32[]{:S(2)}, u32[]{:S(2)}) %collective-permute-start.3) | collective-permute-done | bytes 65568 | tf_op jit(solution)/shard_map/ppermute | solution.py:421
  26.5 3.2 %collective-permute-done.4.refs_5_ = bf16[64,512]{1,0:T(8,128)(2,1)S(1)} collective-permute-done((bf16[64,512]{1,0:T(8,128)(2,1)}, bf16[64,512]{1,0:T(8,128)(2,1)S(1)}, u32[]{:S(2)}, u32[]{:S(2)}) %collective-permute-start.4) | collective-permute-done | bytes 65568 | tf_op jit(solution)/shard_map/ppermute | solution.py:421
  30.1 3.5 %pack.1 = bf16[16,3,256,128]{3,2,1,0:T(8,128)(2,1)} custom-call(s32[1]{0:T(128)} %bitcast.6.me_ref, s32[8,128]{1,0:T(8,128)S(1)} %plan.1.idx, bf16[16,128,128]{2,1,0:T(8,128)(2,1)} %kc.1, bf16[16,128,128]{2,1,0:T(8,128)(2,1)} %vc.1, bf16[16,128,128]{2,1,0:T(8,128)(2,1)S(1)} %collective-permute-done.5.refs_2_, ...), custom_call_target="tpu_custom_call" | custom-call | tf_op jit(solution)/shard_map/pack/pallas_call | solution.py:379
  33.7 5.9 %all-to-all-start.1 = ((bf16[16,3,256,128]{3,2,1,0:T(8,128)(2,1)}), bf16[16,3,256,128]{3,2,1,0:T(8,128)(2,1)S(1)}, u32[]{:S(2)}, u32[]{:S(2)}) async-start(bf16[16,3,256,128]{3,2,1,0:T(8,128)(2,1)} %pack.1), calls=%async_computation.1 | async-start | bytes 6291456 | tf_op jit(solution)/shard_map/all_to_all | solution.py:436
  39.6 2.6 %collective-permute-start.7 = (bf16[64,512]{1,0:T(8,128)(2,1)S(1)}, bf16[64,512]{1,0:T(8,128)(2,1)S(1)}, u32[]{:S(2)}, u32[]{:S(2)}) collective-permute-start(bf16[64,512]{1,0:T(8,128)(2,1)S(1)} %bitcast.37), channel_id=1, source_target_pairs={{0,1},{1,2},{2,3},{3,4},{4,5},{5,6},{6,7},{7,0},{8,9},{9,10},{10,1... | collective-permute-start | bytes 196616 | tf_op jit(solution)/shard_map/ppermute | solution.py:421
  42.3 3.5 %collective-permute-start.8 = (bf16[64,512]{1,0:T(8,128)(2,1)S(1)}, bf16[64,512]{1,0:T(8,128)(2,1)}, u32[]{:S(2)}, u32[]{:S(2)}) collective-permute-start(bf16[64,512]{1,0:T(8,128)(2,1)S(1)} %bitcast.38), channel_id=1, source_target_pairs={{0,6},{1,7},{2,0},{3,1},{4,2},{5,3},{6,4},{7,5},{8,14},{9,15},{10,... | collective-permute-start | bytes 196616 | tf_op jit(solution)/shard_map/ppermute | solution.py:421
  50.0 5.4 %project.1 = (bf16[256,128]{1,0:T(8,128)(2,1)}, bf16[64,128]{1,0:T(8,128)(2,1)}, bf16[64,128]{1,0:T(8,128)(2,1)}, bf16[16,8,128]{2,1,0:T(8,128)(2,1)}) custom-call(s32[16]{0:T(128)} %and_select_fusion.blk, bf16[64,512]{1,0:T(8,128)(2,1)} %bitcast.36, bf16[64,512]{1,0:T(8,128)(2,1)} %copy-done.15, bf16[64,512]{1,0:T(8,128)(2,1)} %copy-done.11, ...), custom_call_target="tpu_custom_call" | custom-call | flops 402653184 | bytes 7340032 | tf_op jit(solution)/shard_map/project/pallas_call | solution.py:101
  55.5 5.0 %attend.1 = (bf16[64,512]{1,0:T(8,128)(2,1)}, bf16[64,512]{1,0:T(8,128)(2,1)}, bf16[64,512]{1,0:T(8,128)(2,1)}, bf16[64,512]{1,0:T(8,128)(2,1)}, bf16[64,512]{1,...) custom-call(s32[16]{0:T(128)} %and_select_fusion.blk, ...), custom_call_target="tpu_custom_call" | custom-call | flops 335544320 | bytes 6291456 | tf_op jit(solution)/shard_map/attend/pallas_call | solution.py:166
  61.3 3.6 %collective-permute-start.12 = (bf16[64,512]{1,0:T(8,128)(2,1)}, bf16[64,512]{1,0:T(8,128)(2,1)S(1)}, u32[]{:S(2)}, u32[]{:S(2)}) collective-permute-start(bf16[64,512]{1,0:T(8,128)(2,1)} %get-tuple-element.241), channel_id=1, source_target_pairs={{0,3},{1,4},{2,5},{3,6},{4,7},{5,0},{6,1},{7,2},{8,11},{9,12},{10,... | collective-permute-start | bytes 196616 | tf_op jit(solution)/shard_map/ppermute | solution.py:421
  64.9 1.9 %collective-permute-start.13 = (bf16[64,512]{1,0:T(8,128)(2,1)}, bf16[64,512]{1,0:T(8,128)(2,1)S(1)}, u32[]{:S(2)}, u32[]{:S(2)}) collective-permute-start(bf16[64,512]{1,0:T(8,128)(2,1)} %get-tuple-element.242), channel_id=1, source_target_pairs={{0,4},{1,5},{2,6},{3,7},{4,0},{5,1},{6,2},{7,3},{8,12},{9,13},{10,... | collective-permute-start | bytes 196616 | tf_op jit(solution)/shard_map/ppermute | solution.py:421
  66.8 3.4 %collective-permute-start.14 = (bf16[64,512]{1,0:T(8,128)(2,1)}, bf16[64,512]{1,0:T(8,128)(2,1)S(1)}, u32[]{:S(2)}, u32[]{:S(2)}) collective-permute-start(bf16[64,512]{1,0:T(8,128)(2,1)} %get-tuple-element.243), channel_id=1, source_target_pairs={{0,5},{1,6},{2,7},{3,0},{4,1},{5,2},{6,3},{7,4},{8,13},{9,14},{10,... | collective-permute-start | bytes 196616 | tf_op jit(solution)/shard_map/ppermute | solution.py:421
  71.3 3.6 %collective-permute-done.13.refs_4_ = bf16[64,512]{1,0:T(8,128)(2,1)S(1)} collective-permute-done((bf16[64,512]{1,0:T(8,128)(2,1)}, bf16[64,512]{1,0:T(8,128)(2,1)S(1)}, u32[]{:S(2)}, u32[]{:S(2)}) %collective-permute-start.13) | collective-permute-done | bytes 65568 | tf_op jit(solution)/shard_map/ppermute | solution.py:421
  75.0 3.9 %collective-permute-done.15.refs_6_ = bf16[64,512]{1,0:T(8,128)(2,1)S(1)} collective-permute-done((bf16[64,512]{1,0:T(8,128)(2,1)}, bf16[64,512]{1,0:T(8,128)(2,1)S(1)}, u32[]{:S(2)}, u32[]{:S(2)}) %collective-permute-start.15) | collective-permute-done | bytes 65568 | tf_op jit(solution)/shard_map/ppermute | solution.py:421
  81.4 16.6 %all_to_all.20.sums = f32[8,1,128]{2,1,0:T(1,128)S(1)} all-to-all(f32[8,1,128]{2,1,0:T(1,128)S(1)} %get-tuple-element.248), channel_id=1, replica_groups=mesh['dom'=32,'tp'=8] {'tp'}, dimensions={0} | all-to-all | bytes 8192 | tf_op jit(solution)/shard_map/all_to_all | solution.py:495
  98.0 1.5 %weigh.1 = (f32[1,128]{1,0:T(1,128)S(1)}, bf16[32,3,8,128]{3,2,1,0:T(8,128)(2,1)}) custom-call(s32[8,128]{1,0:T(8,128)S(1)} %plan.1.idx, f32[8,1,128]{2,1,0:T(1,128)S(1)} %all_to_all.20.sums, f32[1,128]{1,0:T(1,128)S(1)} %bitcast_convert_fusion.reward, f32[1,128]{1,0:T(1,128)S(1)} %pad_bitcast_fusion.previous, bf16[16,8,128]{2,1,0:T(8,128)(2,1)S(1)} %copy-done.4), custom_call_target="tpu_custom_call" | custom-call | tf_op jit(solution)/shard_map/weigh/pallas_call | solution.py:238
  99.5 7.3 %all-to-all-start.3 = ((bf16[32,3,8,128]{3,2,1,0:T(8,128)(2,1)}), bf16[32,3,8,128]{3,2,1,0:T(8,128)(2,1)S(1)}, u32[]{:S(2)}, u32[]{:S(2)}) async-start(bf16[32,3,8,128]{3,2,1,0:T(8,128)(2,1)} %get-tuple-element.253), calls=%async_computation.3 | async-start | bytes 393216 | tf_op jit(solution)/shard_map/all_to_all | solution.py:497
  108.1 2.1 %conditional.1 = ((bf16[16,128,128]{2,1,0:T(8,128)(2,1)S(1)}, bf16[16,128,128]{2,1,0:T(8,128)(2,1)S(1)})) conditional(s32[]{:T(128)} %bitcast.13, (s32[8,128]{1,0:T(8,128)S(1)}, bf16[16,3,256,128]{3,2,1,0:T(8,128)(2,1)}) %tuple.75, (s32[]{:T(128)}, bf16[16,128,128]{2,1,0:T(8,128)(2,1)}, bf16[16,128,128]{2,1,0:T(8,128)(2,1)}, ...), branch_computations={%region_0.1_spmd, %region_1.6_spmd} | conditional | flops 4260986 | bytes 36051572 | solution.py:521
  108.1 2.1 %place.2 = (bf16[16,128,128]{2,1,0:T(8,128)(2,1)S(1)}, bf16[16,128,128]{2,1,0:T(8,128)(2,1)S(1)}) custom-call(s32[8,128]{1,0:T(8,128)S(1)} %get-tuple-element.164.refs_0_, bf16[16,3,256,128]{3,2,1,0:T(8,128)(2,1)} %get-tuple-element.165.refs_1_), custom_call_target="tpu_custom_call" | custom-call | tf_op jit(solution)/shard_map/cond/branch_0_fun/place/pallas_call | solution.py:409
  112.7 2.4 %all-to-all-done.3.got = bf16[32,3,8,128]{3,2,1,0:T(8,128)(2,1)S(1)} async-done(((bf16[32,3,8,128]{3,2,1,0:T(8,128)(2,1)}), bf16[32,3,8,128]{3,2,1,0:T(8,128)(2,1)S(1)}, u32[]{:S(2)}, u32[]{:S(2)}) %all-to-all-start.3) | async-done | bytes 196640 | tf_op jit(solution)/shard_map/all_to_all | solution.py:497
  115.1 2.0 %finish.1 = (f32[1,16]{1,0:T(1,128)}, bf16[132,16,128]{2,1,0:T(8,128)(2,1)}, bf16[132,16,128]{2,1,0:T(8,128)(2,1)}) custom-call(s32[8,128]{1,0:T(8,128)S(1)} %plan.1.idx, f32[1,128]{1,0:T(1,128)S(1)} %get-tuple-element.252.line, bf16[32,3,8,128]{3,2,1,0:T(8,128)(2,1)S(1)} %all-to-all-done.3.got, ...), custom_call_target="tpu_custom_call", output_to_operand_aliasing={{1}: (3, {}), {2}: (4, {})} | custom-call | tf_op jit(solution)/shard_map/finish/pallas_call | solution.py:275
  (76 shorter events, 15.9 us)
Async XLA Ops:
  0.6 46.6 %copy-start = (bf16[128256]{0:T(1024)(128)(2,1)S(1)}, bf16[128256]{0:T(1024)(128)(2,1)}, u32[]{:S(2)}) copy-start(bf16[128256]{0:T(1024)(128)(2,1)} %param.32) | copy-start | bytes 769540
  0.6 29.4 %collective-permute-start.5 = (bf16[16,128,128]{2,1,0:T(8,128)(2,1)}, bf16[16,128,128]{2,1,0:T(8,128)(2,1)S(1)}, u32[]{:S(2)}, u32[]{:S(2)}) collective-permute-start(bf16[16,128,128]{2,1,0:T(8,128)(2,1)} %kc.1), channel_id=1, source_target_pairs={{0,8},{8,0},{16,24},{24,16},{32,40},{40,32},{48,56},{56,48},{64,72... | collective-permute-start | bytes 1572872 | tf_op jit(solution)/shard_map/ppermute | solution.py:425
  4.0 26.1 %collective-permute-start.6 = (bf16[16,128,128]{2,1,0:T(8,128)(2,1)}, bf16[16,128,128]{2,1,0:T(8,128)(2,1)S(1)}, u32[]{:S(2)}, u32[]{:S(2)}) collective-permute-start(bf16[16,128,128]{2,1,0:T(8,128)(2,1)} %vc.1), channel_id=1, source_target_pairs={{0,8},{8,0},{16,24},{24,16},{32,40},{40,32},{48,56},{56,48},{64,72... | collective-permute-start | bytes 1572872 | tf_op jit(solution)/shard_map/ppermute | solution.py:425
  4.1 15.7 %collective-permute-start.1 = (bf16[64,512]{1,0:T(8,128)(2,1)}, bf16[64,512]{1,0:T(8,128)(2,1)S(1)}, u32[]{:S(2)}, u32[]{:S(2)}) collective-permute-start(bf16[64,512]{1,0:T(8,128)(2,1)} %bitcast.32), channel_id=1, source_target_pairs={{0,2},{1,3},{2,4},{3,5},{4,6},{5,7},{6,0},{7,1},{8,10},{9,11},{10,... | collective-permute-start | bytes 196616 | tf_op jit(solution)/shard_map/ppermute | solution.py:421
  6.7 23.0 %all-to-all-start = ((s32[32,8,128]{2,1,0:T(8,128)}), s32[32,8,128]{2,1,0:T(8,128)S(1)}, u32[]{:S(2)}, u32[]{:S(2)}) async-start(s32[32,8,128]{2,1,0:T(8,128)} %broadcast_in_dim.9), calls=%async_computation | async-start | bytes 262144 | tf_op jit(solution)/shard_map/all_to_all | solution.py:442
  14.4 10.0 %collective-permute-start.2 = (bf16[64,512]{1,0:T(8,128)(2,1)}, bf16[64,512]{1,0:T(8,128)(2,1)S(1)}, u32[]{:S(2)}, u32[]{:S(2)}) collective-permute-start(bf16[64,512]{1,0:T(8,128)(2,1)} %bitcast.33), channel_id=1, source_target_pairs={{0,3},{1,4},{2,5},{3,6},{4,7},{5,0},{6,1},{7,2},{8,11},{9,12},{10,... | collective-permute-start | bytes 196616 | tf_op jit(solution)/shard_map/ppermute | solution.py:421
  19.2 7.3 %collective-permute-start.3 = (bf16[64,512]{1,0:T(8,128)(2,1)}, bf16[64,512]{1,0:T(8,128)(2,1)S(1)}, u32[]{:S(2)}, u32[]{:S(2)}) collective-permute-start(bf16[64,512]{1,0:T(8,128)(2,1)} %bitcast.34), channel_id=1, source_target_pairs={{0,4},{1,5},{2,6},{3,7},{4,0},{5,1},{6,2},{7,3},{8,12},{9,13},{10,... | collective-permute-start | bytes 196616 | tf_op jit(solution)/shard_map/ppermute | solution.py:421
  19.8 9.8 %collective-permute-start.4 = (bf16[64,512]{1,0:T(8,128)(2,1)}, bf16[64,512]{1,0:T(8,128)(2,1)S(1)}, u32[]{:S(2)}, u32[]{:S(2)}) collective-permute-start(bf16[64,512]{1,0:T(8,128)(2,1)} %bitcast.35), channel_id=1, source_target_pairs={{0,5},{1,6},{2,7},{3,0},{4,1},{5,2},{6,3},{7,4},{8,13},{9,14},{10,... | collective-permute-start | bytes 196616 | tf_op jit(solution)/shard_map/ppermute | solution.py:421
  33.7 47.7 %all-to-all-start.1 = ((bf16[16,3,256,128]{3,2,1,0:T(8,128)(2,1)}), bf16[16,3,256,128]{3,2,1,0:T(8,128)(2,1)S(1)}, u32[]{:S(2)}, u32[]{:S(2)}) async-start(bf16[16,3,256,128]{3,2,1,0:T(8,128)(2,1)} %pack.1), calls=%async_computation.1 | async-start | bytes 6291456 | tf_op jit(solution)/shard_map/all_to_all | solution.py:436
  39.6 9.0 %collective-permute-start.7 = (bf16[64,512]{1,0:T(8,128)(2,1)S(1)}, bf16[64,512]{1,0:T(8,128)(2,1)S(1)}, u32[]{:S(2)}, u32[]{:S(2)}) collective-permute-start(bf16[64,512]{1,0:T(8,128)(2,1)S(1)} %bitcast.37), channel_id=1, source_target_pairs={{0,1},{1,2},{2,3},{3,4},{4,5},{5,6},{6,7},{7,0},{8,9},{9,10},{10,1... | collective-permute-start | bytes 196616 | tf_op jit(solution)/shard_map/ppermute | solution.py:421
  42.3 6.4 %collective-permute-start.8 = (bf16[64,512]{1,0:T(8,128)(2,1)S(1)}, bf16[64,512]{1,0:T(8,128)(2,1)}, u32[]{:S(2)}, u32[]{:S(2)}) collective-permute-start(bf16[64,512]{1,0:T(8,128)(2,1)S(1)} %bitcast.38), channel_id=1, source_target_pairs={{0,6},{1,7},{2,0},{3,1},{4,2},{5,3},{6,4},{7,5},{8,14},{9,15},{10,... | collective-permute-start | bytes 196616 | tf_op jit(solution)/shard_map/ppermute | solution.py:421
  45.8 4.2 %collective-permute-start.9 = (bf16[64,512]{1,0:T(8,128)(2,1)S(1)}, bf16[64,512]{1,0:T(8,128)(2,1)}, u32[]{:S(2)}, u32[]{:S(2)}) collective-permute-start(bf16[64,512]{1,0:T(8,128)(2,1)S(1)} %bitcast.39), channel_id=1, source_target_pairs={{0,7},{1,0},{2,1},{3,2},{4,3},{5,4},{6,5},{7,6},{8,15},{9,8},{10,9... | collective-permute-start | bytes 196616 | tf_op jit(solution)/shard_map/ppermute | solution.py:421
  55.4 24.5 %copy-start.2 = (bf16[4,16,512]{2,1,0:T(8,128)(2,1)S(1)}, bf16[4,16,512]{2,1,0:T(8,128)(2,1)}, u32[]{:S(2)}) copy-start(bf16[4,16,512]{2,1,0:T(8,128)(2,1)} %param.23) | copy-start | bytes 196612
  55.4 24.4 %copy-start.5 = (f32[512]{0:T(512)S(1)}, f32[512]{0:T(512)}, u32[]{:S(2)}) copy-start(f32[512]{0:T(512)} %param.33) | copy-start | bytes 6148
  55.4 42.6 %copy-start.4 = (bf16[16,8,128]{2,1,0:T(8,128)(2,1)S(1)}, bf16[16,8,128]{2,1,0:T(8,128)(2,1)}, u32[]{:S(2)}) copy-start(bf16[16,8,128]{2,1,0:T(8,128)(2,1)} %get-tuple-element.251.fresh) | copy-start | bytes 98308
  60.5 9.7 %collective-permute-start.10 = (bf16[64,512]{1,0:T(8,128)(2,1)}, bf16[64,512]{1,0:T(8,128)(2,1)S(1)}, u32[]{:S(2)}, u32[]{:S(2)}) collective-permute-start(bf16[64,512]{1,0:T(8,128)(2,1)} %get-tuple-element.239), channel_id=1, source_target_pairs={{0,1},{1,2},{2,3},{3,4},{4,5},{5,6},{6,7},{7,0},{8,9},{9,10},{10,1... | collective-permute-start | bytes 196616 | tf_op jit(solution)/shard_map/ppermute | solution.py:421
  61.3 10.0 %collective-permute-start.11 = (bf16[64,512]{1,0:T(8,128)(2,1)}, bf16[64,512]{1,0:T(8,128)(2,1)S(1)}, u32[]{:S(2)}, u32[]{:S(2)}) collective-permute-start(bf16[64,512]{1,0:T(8,128)(2,1)} %get-tuple-element.240), channel_id=1, source_target_pairs={{0,2},{1,3},{2,4},{3,5},{4,6},{5,7},{6,0},{7,1},{8,10},{9,11},{10,... | collective-permute-start | bytes 196616 | tf_op jit(solution)/shard_map/ppermute | solution.py:421
  61.3 10.0 %collective-permute-start.12 = (bf16[64,512]{1,0:T(8,128)(2,1)}, bf16[64,512]{1,0:T(8,128)(2,1)S(1)}, u32[]{:S(2)}, u32[]{:S(2)}) collective-permute-start(bf16[64,512]{1,0:T(8,128)(2,1)} %get-tuple-element.241), channel_id=1, source_target_pairs={{0,3},{1,4},{2,5},{3,6},{4,7},{5,0},{6,1},{7,2},{8,11},{9,12},{10,... | collective-permute-start | bytes 196616 | tf_op jit(solution)/shard_map/ppermute | solution.py:421
  64.9 10.0 %collective-permute-start.13 = (bf16[64,512]{1,0:T(8,128)(2,1)}, bf16[64,512]{1,0:T(8,128)(2,1)S(1)}, u32[]{:S(2)}, u32[]{:S(2)}) collective-permute-start(bf16[64,512]{1,0:T(8,128)(2,1)} %get-tuple-element.242), channel_id=1, source_target_pairs={{0,4},{1,5},{2,6},{3,7},{4,0},{5,1},{6,2},{7,3},{8,12},{9,13},{10,... | collective-permute-start | bytes 196616 | tf_op jit(solution)/shard_map/ppermute | solution.py:421
  66.8 8.2 %collective-permute-start.14 = (bf16[64,512]{1,0:T(8,128)(2,1)}, bf16[64,512]{1,0:T(8,128)(2,1)S(1)}, u32[]{:S(2)}, u32[]{:S(2)}) collective-permute-start(bf16[64,512]{1,0:T(8,128)(2,1)} %get-tuple-element.243), channel_id=1, source_target_pairs={{0,5},{1,6},{2,7},{3,0},{4,1},{5,2},{6,3},{7,4},{8,13},{9,14},{10,... | collective-permute-start | bytes 196616 | tf_op jit(solution)/shard_map/ppermute | solution.py:421
  70.2 8.7 %collective-permute-start.15 = (bf16[64,512]{1,0:T(8,128)(2,1)}, bf16[64,512]{1,0:T(8,128)(2,1)S(1)}, u32[]{:S(2)}, u32[]{:S(2)}) collective-permute-start(bf16[64,512]{1,0:T(8,128)(2,1)} %get-tuple-element.244), channel_id=1, source_target_pairs={{0,6},{1,7},{2,0},{3,1},{4,2},{5,3},{6,4},{7,5},{8,14},{9,15},{10,... | collective-permute-start | bytes 196616 | tf_op jit(solution)/shard_map/ppermute | solution.py:421
  71.3 8.5 %collective-permute-start.16 = (bf16[64,512]{1,0:T(8,128)(2,1)}, bf16[64,512]{1,0:T(8,128)(2,1)S(1)}, u32[]{:S(2)}, u32[]{:S(2)}) collective-permute-start(bf16[64,512]{1,0:T(8,128)(2,1)} %get-tuple-element.245), channel_id=1, source_target_pairs={{0,7},{1,0},{2,1},{3,2},{4,3},{5,4},{6,5},{7,6},{8,15},{9,8},{10,9... | collective-permute-start | bytes 196616 | tf_op jit(solution)/shard_map/ppermute | solution.py:421
  81.4 18.1 %copy-start.6 = (bf16[16,3,256,128]{3,2,1,0:T(8,128)(2,1)}, bf16[16,3,256,128]{3,2,1,0:T(8,128)(2,1)S(1)}, u32[]{:S(2)}) copy-start(bf16[16,3,256,128]{3,2,1,0:T(8,128)(2,1)S(1)} %all-to-all-done.1) | copy-start | bytes 9437188
  99.5 15.6 %all-to-all-start.3 = ((bf16[32,3,8,128]{3,2,1,0:T(8,128)(2,1)}), bf16[32,3,8,128]{3,2,1,0:T(8,128)(2,1)S(1)}, u32[]{:S(2)}, u32[]{:S(2)}) async-start(bf16[32,3,8,128]{3,2,1,0:T(8,128)(2,1)} %get-tuple-element.253), calls=%async_computation.3 | async-start | bytes 393216 | tf_op jit(solution)/shard_map/all_to_all | solution.py:497
  (13 other events, 92.8 us)

commit v4 on v2

--- a/solution.py
+++ b/solution.py
@@ -182,7 +182,7 @@
 
 def mix_body(*refs):
     parts = refs[:TP]
-    act, twist, attn, sums = refs[TP:]
+    act, twist, base, attn, message = refs[TP:]
     mix = parts[0][...].astype(F32)
     for s in range(1, TP):
         mix = mix + parts[s][...].astype(F32)
@@ -190,67 +190,54 @@
     summed = act[...].astype(F32) + mix
     aligned = jnp.sum(summed * twist[...], -1, keepdims=True)
     energy = jnp.sum(summed * summed, -1, keepdims=True)
+    row = lax.broadcasted_iota(jnp.int32, (ROWS, HD), 0)
     lane = lax.broadcasted_iota(jnp.int32, (ROWS, HD), 1)
-    sums[...] = jnp.where(lane == 0, aligned, energy)
-
-
-def mix(parts, act, twist):
+    both = jnp.where(lane == row, aligned, 0.0) + jnp.where(lane == row + ROWS, energy, 0.0)
+    line = jnp.concatenate([jnp.sum(both, 0, keepdims=True), base[...]], 0)
+    message[...] = jnp.broadcast_to(line[None], (NDOM * TP, 2, HD))
+
+
+def mix(parts, act, twist, base):
     sd = jax.ShapeDtypeStruct
     return pl.pallas_call(
         mix_body,
-        in_specs=[spec(VM)] * (TP + 2),
+        in_specs=[spec(VM)] * (TP + 3),
         out_specs=[spec(VM)] * 2,
-        out_shape=[sd((ROWS, DB), BF), sd((ROWS, HD), F32)],
+        out_shape=[sd((ROWS, DB), BF), sd((NDOM * TP, 2, HD), F32)],
         compiler_params=limit(8),
         name="mix",
-    )(*parts, act, twist)
-
-
-def weigh_body(*refs):
-    parts = refs[:TP]
-    reward, previous, out = refs[TP:]
-    sums = parts[0][...]
-    for s in range(1, TP):
-        sums = sums + parts[s][...]
-    score = sums[:, 0:1] / jnp.sqrt(sums[:, 1:2] / D + 1e-06) + reward[...]
-    gain = score[0:NP]
+    )(*parts, act, twist, base)
+
+
+def finish_body(me_ref, got, out, logw_s):
+    total = got[:, 0]
+    for t in range(1, TP):
+        total = total + got[:, t]
+    sums = total[:, 0, :]
+    energy = pltpu.roll(sums, ROWS, 1)
+    score = sums / jnp.sqrt(energy / D + 1e-06)
+    logw = total[:, 1, :] + score
     for t in range(1, STEPS):
-        gain = gain + score[t * NP : (t + 1) * NP]
-    column = jnp.broadcast_to(previous[...] + gain, (NP, HD))
-    row = lax.broadcasted_iota(jnp.int32, (NP, HD), 0)
-    lane = lax.broadcasted_iota(jnp.int32, (NP, HD), 1)
-    line = jnp.sum(jnp.where(row == lane, column, 0.0), 0, keepdims=True)
-    out[...] = jnp.broadcast_to(line[None], (NDOM, 1, HD))
-
-
-def weigh(parts, reward, previous):
-    return pl.pallas_call(
-        weigh_body,
-        in_specs=[spec(VM)] * (TP + 2),
-        out_specs=spec(VM),
-        out_shape=jax.ShapeDtypeStruct((NDOM, 1, HD), F32),
-        compiler_params=limit(8),
-        name="weigh",
-    )(*parts, reward, previous)
-
-
-def finish_body(mine, every, out):
+        logw = logw + pltpu.roll(score, HD - NP * t, 1)
     lane = lax.broadcasted_iota(jnp.int32, (NDOM, HD), 1)
-    all_w = jnp.where(lane < NP, every[:, 0, :], -jnp.inf)
-    largest = jnp.max(all_w, keepdims=True)
-    mass = jnp.sum(jnp.exp(all_w - largest), keepdims=True)
-    out[...] = (mine[0] - (largest + jnp.log(mass)))[:, 0:NP]
-
-
-def finish(mine, every):
+    logw = jnp.where(lane < NP, logw, -jnp.inf)
+    logw_s[...] = logw
+    largest = jnp.max(logw, keepdims=True)
+    mass = jnp.sum(jnp.exp(logw - largest), keepdims=True)
+    mine = logw_s[pl.ds(me_ref[0], 1), :]
+    out[...] = (mine - (largest + jnp.log(mass)))[:, 0:NP]
+
+
+def finish(me, got):
     return pl.pallas_call(
         finish_body,
-        in_specs=[spec(VM)] * 2,
+        in_specs=[spec(SM), spec(VM)],
         out_specs=spec(VM),
         out_shape=jax.ShapeDtypeStruct((1, NP), F32),
+        scratch_shapes=[VM((NDOM, HD), F32)],
         compiler_params=limit(8),
         name="finish",
-    )(mine, every)
+    )(me, got)
 
 
 def plan_body(me_ref, *refs):
@@ -293,7 +280,13 @@
     pair = lax.broadcasted_iota(jnp.int32, (NDOM, HD), 1)
     most = jnp.max(jnp.sum(jnp.where(pair == device // 2, owned, 0), 0, keepdims=True))
     line = jnp.where(lane < 64, particle, jnp.where(lane < 80, arrived, most))
-    out[...] = jnp.broadcast_to(line, (8, HD))
+
+    found = jnp.zeros((NDOM, HD), jnp.int32)
+    for j in range(NP):
+        found = found + (ends[:, j : j + 1] <= kept).astype(jnp.int32)
+    owner = jnp.clip(jnp.sum(found, 0, keepdims=True), 0, NDOM * NP - 1)
+    row = lax.broadcasted_iota(jnp.int32, (8, HD), 0)
+    out[...] = jnp.where(row == 0, line, owner)
 
 
 def plan(me, blocks):
@@ -345,40 +338,45 @@
     )(me, idx, *own, *partner)
 
 
-def place_body(slots, idx, rows, keys, values, r_s, sems):
+def place_body(slots, idx, rows, fresh, keys, values, r_s, f_s, sems):
     copies = []
     for k in range(NP):
         code = idx[0, 64 + k]
         slot = jnp.minimum(code % 4, slots - 1)
         copies.append(
-            pltpu.make_async_copy(rows.at[code // 4, slot], r_s.at[k], sems.at[k])
+            pltpu.make_async_copy(rows.at[code // 4, slot], r_s.at[k], sems.at[0, k])
+        )
+        copies.append(
+            pltpu.make_async_copy(fresh.at[idx[1, 64 + k]], f_s.at[k], sems.at[1, k])
         )
     for c in copies:
         c.start()
     for k in range(NP):
-        copies[k].wait()
+        copies[2 * k].wait()
+        copies[2 * k + 1].wait()
         keys[k, 0:SPAN, :] = r_s[k, 0:SPAN, :]
         values[k, 0:SPAN, :] = r_s[k, SPAN : 2 * SPAN, :]
-        tail = r_s[k, 2 * SPAN : 2 * SPAN + 2 * STEPS, :].astype(F32)
+        tail = f_s[k].astype(F32)
         keys[k, SPAN : SPAN + STEPS, :] = tail[0:STEPS].astype(BF)
         values[k, SPAN : SPAN + STEPS, :] = tail[STEPS : 2 * STEPS].astype(BF)
 
 
-def place(idx, rows):
+def place(idx, rows, fresh):
     out = jax.ShapeDtypeStruct((NP, SPAN + STEPS, HD), BF)
     slots = rows.shape[1]
     return pl.pallas_call(
         lambda *refs: place_body(slots, *refs),
-        in_specs=[spec(SM), spec(ANY)],
+        in_specs=[spec(SM), spec(ANY), spec(ANY)],
         out_specs=[spec(VM)] * 2,
         out_shape=[out] * 2,
         scratch_shapes=[
-            VM((NP, 2 * SPAN + 2 * STEPS, HD), BF),
-            pltpu.SemaphoreType.DMA((NP,)),
+            VM((NP, 2 * SPAN, HD), BF),
+            VM((NP, 2 * STEPS, HD), BF),
+            pltpu.SemaphoreType.DMA((2, NP)),
         ],
         compiler_params=limit(16),
         name="place",
-    )(idx, rows)
+    )(idx, rows, fresh)
 
 
 def shifted(value, shift):
@@ -450,40 +448,31 @@
     idx = plan(me, spread_counts(copy_counts))
     partner_keys = swapped(cache_keys)
     partner_values = swapped(cache_values)
-    reward = twisting_table[tokens.reshape(ROWS)].astype(F32).reshape(ROWS, 1)
-
-    gathered, idx, partner_keys, partner_values, reward = lax.optimization_barrier(
-        (gathered, idx, partner_keys, partner_values, reward)
-    )
+    packed = pack(me, idx, [cache_keys, cache_values], [partner_keys, partner_values])
+    rows = exchanged(packed)
+
+    packed, gathered = lax.optimization_barrier((packed, gathered))
     qa, kf, vf, fresh = project(
         gathered, norm_gain.reshape(TP, DB), w_query, w_key, value_weight, rotation_table()
     )
-    partner_fresh = swapped(fresh)
-    packed = pack(
-        me,
-        idx,
-        [cache_keys, cache_values, fresh],
-        [partner_keys, partner_values, partner_fresh],
-    )
-    packed, qa = lax.optimization_barrier((packed, qa))
-    rows = exchanged(packed)
+    fresh = lax.all_gather(fresh, "dom", axis=0, tiled=True)
     partials = attend(blk, qa, kf, vf, cache_keys, cache_values, w_output)
-
     parts = [partials[0]] + [shifted(partials[s], s) for s in range(1, TP)]
-    attn, sums = mix(parts, act, twist_vec.reshape(1, DB))
-    all_sums = [sums] + [shifted(sums, s) for s in range(1, TP)]
-    logw = weigh(all_sums, reward, previous_log_weights.reshape(NP, 1))
-    logw, rows = lax.optimization_barrier((logw, rows))
-    every = lax.all_to_all(logw, "dom", 0, 0, tiled=True)
-    out_logw = finish(logw, every).reshape(NP)
-
-    def usual(rows, *_):
-        return tuple(place(idx, rows))
-
-    def crowded(rows, partner_keys, partner_values, partner_fresh, fresh, idx):
+    reward = jnp.sum(twisting_table[tokens].astype(F32), 0)
+    base = jnp.where(tp == 0, previous_log_weights + reward, 0.0)
+    base = jnp.pad(base, (0, HD - NP)).reshape(1, HD)
+    attn, message = mix(parts, act, twist_vec.reshape(1, DB), base)
+    message, rows = lax.optimization_barrier((message, rows))
+    got = lax.all_to_all(message, ("dom", "tp"), 0, 0, tiled=True)
+    out_logw = finish(me, got.reshape(NDOM, TP, 2, HD))
+
+    def usual(rows, fresh, *_):
+        return tuple(place(idx, rows, fresh))
+
+    def crowded(rows, fresh, partner_keys, partner_values, idx):
         even = dom % 2 == 0
-        mine = jnp.concatenate([cache_keys, cache_values, fresh], 1)
-        other = jnp.concatenate([partner_keys, partner_values, partner_fresh], 1)
+        mine = jnp.concatenate([cache_keys, cache_values], 1)
+        other = jnp.concatenate([partner_keys, partner_values], 1)
         chip_rows = jnp.concatenate(
             [jnp.where(even, mine, other), jnp.where(even, other, mine)], 0
         )
@@ -497,20 +486,19 @@
 
         start = (chosen, chosen)
         more = lax.fori_loop(1, NCHIP, turn, start)[1].at[chip].set(chosen[chip])
-        return tuple(place(idx, jnp.concatenate([rows, more[:, None]], 1)))
+        return tuple(place(idx, jnp.concatenate([rows, more[:, None]], 1), fresh))
 
     new_keys, new_values = lax.cond(
         idx[0, 127] > SLOTS * NDOM,
         crowded,
         usual,
         rows,
+        fresh,
         partner_keys,
         partner_values,
-        partner_fresh,
-        fresh,
         idx,
     )
-    return (attn.reshape(STEPS, NP, DB), new_keys, new_values, out_logw)
+    return (attn.reshape(STEPS, NP, DB), new_keys, new_values, out_logw.reshape(NP))
 
 
 def solution(mesh):

time: 111 us -> 127 us (1.14)
  between operations: 1.47 us -> 14.9 us
  waiting for transfers between devices: 20.8 us -> 31.7 us
  starting transfers between devices: 61.6 us -> 52 us
    all_gather x0 -> x1, waiting for transfers between devices: none -> 14.5 us  [local(): fresh = lax.all_gather(fresh, 'dom', axis=0, tiled=True)]
    ppermute x14 -> x7, starting transfers between devices: 27.1 us -> 14.9 us  [shifted(): return lax.ppermute(value, 'tp', [(i, (i + shift) % TP) for i in range(TP)])]
    all_to_all x1, starting transfers between devices: 6.53 us -> 15.1 us  [local(): got = lax.all_to_all(message, ('dom', 'tp'), 0, 0, tiled=True)]
    ppermute x14 -> x7, waiting for transfers between devices: 10.8 us -> 5.53 us  [shifted(): return lax.ppermute(value, 'tp', [(i, (i + shift) % TP) for i in range(TP)])]
    ppermute x6, waiting for transfers between devices: 2.63 us -> 6.29 us  [moved(): return lax.ppermute(value, 'dom', [(i, to(i)) for i in range(NDOM)])]
    ppermute x6, starting transfers between devices: 9.98 us -> 7.45 us  [moved(): return lax.ppermute(value, 'dom', [(i, to(i)) for i in range(NDOM)])]
    all_to_all x1, starting transfers between devices: 5.99 us -> 4.04 us  [exchanged(): lax.all_to_all(rows, 'dom', 0, 0, tiled=True, axis_index_groups=SAME_CORE)]
    all_to_all x1, waiting for transfers between devices: 1.87 us -> 0.01 us  [local(): got = lax.all_to_all(message, ('dom', 'tp'), 0, 0, tiled=True)]
  transfers between devices with their start and end apart: 27 -> 20, of which waited for: 11 -> 10; matrix products, arithmetic and copies ran while one was open for 4% -> 3% of each run, Pallas kernels for 8% -> 14%
where the time goes in v4:
time: 127 us; the launch traced here: 126 us
  starting transfers between devices  52 us (41%)
  waiting for transfers between devices  31.7 us (25%)
  Pallas kernels  18.3 us (14%)
  between operations  14.9 us (12%)
  local copies, waits for them, and re-layouts  8 us (6%)
    all_to_all x1, starting transfers between devices, local(): got = lax.all_to_all(message, ('dom', 'tp'), 0, 0, tiled=True)  15.1 us
    ppermute x7, starting transfers between devices, shifted(): return lax.ppermute(value, 'tp', [(i, (i + shift) % TP) for i in range(TP)])  14.9 us
    all_gather x1, waiting for transfers between devices, local(): fresh = lax.all_gather(fresh, 'dom', axis=0, tiled=True)  14.5 us
    all_to_all x1, starting transfers between devices, local(): lax.all_to_all(jnp.broadcast_to(act[None], (TP, ROWS, DB)), 'tp', 0, 0, t...  9.01 us
    ppermute x6, starting transfers between devices, moved(): return lax.ppermute(value, 'dom', [(i, to(i)) for i in range(NDOM)])  7.45 us
    ppermute x6, waiting for transfers between devices, moved(): return lax.ppermute(value, 'dom', [(i, to(i)) for i in range(NDOM)])  6.29 us
    ppermute x7, waiting for transfers between devices, shifted(): return lax.ppermute(value, 'tp', [(i, (i + shift) % TP) for i in range(TP)])  5.53 us
    pallas_call x1, Pallas kernels, project(): pl.pallas_call(project_body, in_specs=[spec(VM)] * 2 + [spec(ANY)] * 3 +...  5.37 us
  transfers between devices with their start and end apart: 20, of which 10 were waited for; matrix products, arithmetic and copies ran while one was open for 3% of the time, Pallas kernels for 14%

profile of v4, /device:TPU:1, one launch (start us, length us, event | category | flops | bytes accessed | tf_op | source)
XLA Modules:
  0.0 126.2 jit_solution(12978571433457892685)
XLA Ops:
  7.2 1.7 %broadcast_in_dim.25 = bf16[8,64,512]{2,1,0:T(8,128)(2,1)} broadcast(bf16[64,512]{1,0:T(8,128)(2,1)} %bitcast.22), dimensions={1,2} | broadcast | bytes 589824 | tf_op jit(solution)/shard_map/broadcast_in_dim | solution.py:446
  8.9 9.0 %all-to-all-start = ((bf16[8,64,512]{2,1,0:T(8,128)(2,1)}), bf16[8,64,512]{2,1,0:T(8,128)(2,1)S(1)}, u32[]{:S(2)}, u32[]{:S(2)}) async-start(bf16[8,64,512]{2,1,0:T(8,128)(2,1)} %broadcast_in_dim.25), calls=%async_computation | async-start | bytes 1048576 | tf_op jit(solution)/shard_map/all_to_all | solution.py:445
  19.4 2.0 %collective-permute-done.1 = s32[1,16]{1,0:T(1,128)S(1)} collective-permute-done((s32[1,16]{1,0:T(1,128)}, s32[1,16]{1,0:T(1,128)S(1)}, u32[]{:S(2)}, u32[]{:S(2)}) %collective-permute-start.1) | collective-permute-done | bytes 96 | tf_op jit(solution)/shard_map/ppermute | solution.py:387
  22.0 2.5 %collective-permute-start.4 = (s32[2,16]{1,0:T(2,128)S(1)}, s32[2,16]{1,0:T(2,128)S(1)}, u32[]{:S(2)}, u32[]{:S(2)}) collective-permute-start(s32[2,16]{1,0:T(2,128)S(1)} %pad_add_fusion), channel_id=1, source_target_pairs={{0,48},{8,56},{16,0},{24,8},{32,16},{40,24},{48,32},{56,40},{64,11... | collective-permute-start | bytes 392 | tf_op jit(solution)/shard_map/ppermute | solution.py:406
  25.6 3.1 %collective-permute-done.3 = s32[2,16]{1,0:T(2,128)S(1)} collective-permute-done((s32[2,16]{1,0:T(2,128)S(1)}, s32[2,16]{1,0:T(2,128)S(1)}, u32[]{:S(2)}, u32[]{:S(2)}) %collective-permute-start.3) | collective-permute-done | bytes 160 | tf_op jit(solution)/shard_map/ppermute | solution.py:406
  29.6 2.8 %collective-permute-start.7 = (s32[8,16]{1,0:T(8,128)S(1)}, s32[8,16]{1,0:T(8,128)S(1)}, u32[]{:S(2)}, u32[]{:S(2)}) collective-permute-start(s32[8,16]{1,0:T(8,128)S(1)} %concatenate.35.refs_0_), channel_id=1, source_target_pairs={{0,192},{8,200},{16,208},{24,216},{32,224},{40,232},{48,240},{56,2... | collective-permute-start | bytes 1544 | tf_op jit(solution)/shard_map/ppermute | solution.py:406
  33.5 2.9 %collective-permute-done.6.refs_2_ = s32[8,16]{1,0:T(8,128)S(1)} collective-permute-done((s32[8,16]{1,0:T(8,128)S(1)}, s32[8,16]{1,0:T(8,128)S(1)}, u32[]{:S(2)}, u32[]{:S(2)}) %collective-permute-start.6) | collective-permute-done | bytes 544 | tf_op jit(solution)/shard_map/ppermute | solution.py:406
  37.1 3.5 %pack.1 = bf16[16,3,256,128]{3,2,1,0:T(8,128)(2,1)} custom-call(s32[1]{0:T(128)} %bitcast.6.me_ref, s32[8,128]{1,0:T(8,128)S(1)} %plan.1.idx, bf16[16,128,128]{2,1,0:T(8,128)(2,1)} %kc.1, bf16[16,128,128]{2,1,0:T(8,128)(2,1)} %vc.1, bf16[16,128,128]{2,1,0:T(8,128)(2,1)S(1)} %collective-permute-done.8.refs_2_, ...), custom_call_target="tpu_custom_call" | custom-call | tf_op jit(solution)/shard_map/pack/pallas_call | solution.py:327
  41.4 4.0 %all-to-all-start.1 = ((bf16[16,3,256,128]{3,2,1,0:T(8,128)(2,1)}), bf16[16,3,256,128]{3,2,1,0:T(8,128)(2,1)S(1)}, u32[]{:S(2)}, u32[]{:S(2)}) async-start(bf16[16,3,256,128]{3,2,1,0:T(8,128)(2,1)} %pack.1), calls=%async_computation.1 | async-start | bytes 6291456 | tf_op jit(solution)/shard_map/all_to_all | solution.py:398
  46.2 5.4 %project.1 = (bf16[256,128]{1,0:T(8,128)(2,1)}, bf16[64,128]{1,0:T(8,128)(2,1)}, bf16[64,128]{1,0:T(8,128)(2,1)}, bf16[16,8,128]{2,1,0:T(8,128)(2,1)}) custom-call(bf16[8,64,512]{2,1,0:T(8,128)(2,1)} %copy-done.8, f32[8,512]{1,0:T(8,128)} %reshape.161.gain, bf16[4096,512]{1,0:T(8,128)(2,1)} %wq.1, bf16[4096,128]{1,0:T(8,128)(2,1)} %wk.1, ...), custom_call_target="tpu_custom_call" | custom-call | flops 402653184 | bytes 7340032 | tf_op jit(solution)/shard_map/project/pallas_call | solution.py:99
  53.1 4.7 %attend.1 = (bf16[64,512]{1,0:T(8,128)(2,1)}, bf16[64,512]{1,0:T(8,128)(2,1)}, bf16[64,512]{1,0:T(8,128)(2,1)}, bf16[64,512]{1,0:T(8,128)(2,1)}, bf16[64,512]{1,...) custom-call(s32[8]{0:T(128)} %and_select_fusion.blk, ...), custom_call_target="tpu_custom_call" | custom-call | flops 335544320 | bytes 6291456 | tf_op jit(solution)/shard_map/attend/pallas_call | solution.py:164
  57.8 1.8 %collective-permute-start.10 = (bf16[64,512]{1,0:T(8,128)(2,1)}, bf16[64,512]{1,0:T(8,128)(2,1)S(1)}, u32[]{:S(2)}, u32[]{:S(2)}) collective-permute-start(bf16[64,512]{1,0:T(8,128)(2,1)} %get-tuple-element.214), channel_id=1, source_target_pairs={{0,1},{1,2},{2,3},{3,4},{4,5},{5,6},{6,7},{7,0},{8,9},{9,10},{10,1... | collective-permute-start | bytes 196616 | tf_op jit(solution)/shard_map/ppermute | solution.py:383
  59.6 1.8 %collective-permute-start.11 = (bf16[64,512]{1,0:T(8,128)(2,1)}, bf16[64,512]{1,0:T(8,128)(2,1)S(1)}, u32[]{:S(2)}, u32[]{:S(2)}) collective-permute-start(bf16[64,512]{1,0:T(8,128)(2,1)} %get-tuple-element.215), channel_id=1, source_target_pairs={{0,2},{1,3},{2,4},{3,5},{4,6},{5,7},{6,0},{7,1},{8,10},{9,11},{10,... | collective-permute-start | bytes 196616 | tf_op jit(solution)/shard_map/ppermute | solution.py:383
  61.4 2.4 %collective-permute-start.12 = (bf16[64,512]{1,0:T(8,128)(2,1)}, bf16[64,512]{1,0:T(8,128)(2,1)S(1)}, u32[]{:S(2)}, u32[]{:S(2)}) collective-permute-start(bf16[64,512]{1,0:T(8,128)(2,1)} %get-tuple-element.216), channel_id=1, source_target_pairs={{0,3},{1,4},{2,5},{3,6},{4,7},{5,0},{6,1},{7,2},{8,11},{9,12},{10,... | collective-permute-start | bytes 196616 | tf_op jit(solution)/shard_map/ppermute | solution.py:383
  63.8 2.1 %collective-permute-start.13 = (bf16[64,512]{1,0:T(8,128)(2,1)}, bf16[64,512]{1,0:T(8,128)(2,1)S(1)}, u32[]{:S(2)}, u32[]{:S(2)}) collective-permute-start(bf16[64,512]{1,0:T(8,128)(2,1)} %get-tuple-element.217), channel_id=1, source_target_pairs={{0,4},{1,5},{2,6},{3,7},{4,0},{5,1},{6,2},{7,3},{8,12},{9,13},{10,... | collective-permute-start | bytes 196616 | tf_op jit(solution)/shard_map/ppermute | solution.py:383
  65.9 2.4 %collective-permute-start.14 = (bf16[64,512]{1,0:T(8,128)(2,1)}, bf16[64,512]{1,0:T(8,128)(2,1)S(1)}, u32[]{:S(2)}, u32[]{:S(2)}) collective-permute-start(bf16[64,512]{1,0:T(8,128)(2,1)} %get-tuple-element.218), channel_id=1, source_target_pairs={{0,5},{1,6},{2,7},{3,0},{4,1},{5,2},{6,3},{7,4},{8,13},{9,14},{10,... | collective-permute-start | bytes 196616 | tf_op jit(solution)/shard_map/ppermute | solution.py:383
  68.3 3.3 %collective-permute-start.15 = (bf16[64,512]{1,0:T(8,128)(2,1)}, bf16[64,512]{1,0:T(8,128)(2,1)S(1)}, u32[]{:S(2)}, u32[]{:S(2)}) collective-permute-start(bf16[64,512]{1,0:T(8,128)(2,1)} %get-tuple-element.219), channel_id=1, source_target_pairs={{0,6},{1,7},{2,0},{3,1},{4,2},{5,3},{6,4},{7,5},{8,14},{9,15},{10,... | collective-permute-start | bytes 196616 | tf_op jit(solution)/shard_map/ppermute | solution.py:383
  72.8 2.7 %collective-permute-done.15.refs_6_ = bf16[64,512]{1,0:T(8,128)(2,1)S(1)} collective-permute-done((bf16[64,512]{1,0:T(8,128)(2,1)}, bf16[64,512]{1,0:T(8,128)(2,1)S(1)}, u32[]{:S(2)}, u32[]{:S(2)}) %collective-permute-start.15) | collective-permute-done | bytes 65568 | tf_op jit(solution)/shard_map/ppermute | solution.py:383
  75.6 2.7 %collective-permute-done.16.refs_7_ = bf16[64,512]{1,0:T(8,128)(2,1)S(1)} collective-permute-done((bf16[64,512]{1,0:T(8,128)(2,1)}, bf16[64,512]{1,0:T(8,128)(2,1)S(1)}, u32[]{:S(2)}, u32[]{:S(2)}) %collective-permute-start.16) | collective-permute-done | bytes 65568 | tf_op jit(solution)/shard_map/ppermute | solution.py:383
  80.1 3.4 %all-to-all-done.1 = bf16[16,3,256,128]{3,2,1,0:T(8,128)(2,1)S(1)} async-done(((bf16[16,3,256,128]{3,2,1,0:T(8,128)(2,1)}), bf16[16,3,256,128]{3,2,1,0:T(8,128)(2,1)S(1)}, u32[]{:S(2)}, u32[]{:S(2)}) %all-to-all-start.1) | async-done | bytes 3145760 | tf_op jit(solution)/shard_map/all_to_all | solution.py:398
  85.2 15.1 %all-to-all-start.2 = ((f32[256,2,128]{2,1,0:T(2,128)}), f32[256,2,128]{2,1,0:T(2,128)S(1)}, u32[]{:S(2)}, u32[]{:S(2)}) async-start(f32[256,2,128]{2,1,0:T(2,128)} %get-tuple-element.227), calls=%async_computation.2 | async-start | bytes 524288 | tf_op jit(solution)/shard_map/all_to_all | solution.py:466
  101.4 14.5 %all-gather.2.cloned.1.call-done = bf16[512,8,128]{2,1,0:T(8,128)(2,1)} async-done(((bf16[16,8,128]{2,1,0:T(8,128)(2,1)}), bf16[512,8,128]{2,1,0:T(8,128)(2,1)}) %all-gather.2.cloned.1.call-update) | async-done | bytes 1048592 | tf_op jit(solution)/shard_map/all_gather | solution.py:458
  115.9 2.4 %conditional.1 = (bf16[16,132,128]{2,0,1:T(8,128)(2,1)S(1)}, bf16[16,132,128]{2,0,1:T(8,128)(2,1)S(1)}) conditional(s32[]{:T(128)} %bitcast.12, (s32[8,128]{1,0:T(8,128)S(1)}, bf16[16,3,256,128]{3,2,1,0:T(8,128)(2,1)}, bf16[512,8,128]{2,1,0:T(8,128)(2,1)}) %tuple.79, (s32[]{:T(128)}, bf16[16,128,128]{2,1,0:T(8,128)(2,1)}, ...), branch_computations={%region_1.2_spmd, %region_2.7_spmd} | conditional | flops 4260986 | bytes 42408600 | solution.py:491
  115.9 2.2 %place.2 = (bf16[16,132,128]{2,1,0:T(8,128)(2,1)S(1)}, bf16[16,132,128]{2,1,0:T(8,128)(2,1)S(1)}) custom-call(s32[8,128]{1,0:T(8,128)S(1)} %get-tuple-element.168.refs_0_, bf16[16,3,256,128]{3,2,1,0:T(8,128)(2,1)} %get-tuple-element.169.refs_1_, bf16[512,8,128]{2,1,0:T(8,128)(2,1)} %get-tuple-element.170.refs_2_), custom_call_target="tpu_custom_call" | custom-call | tf_op jit(solution)/shard_map/cond/branch_0_fun/place/pallas_call | solution.py:367
  (67 shorter events, 15.2 us)
Async XLA Ops:
  7.2 44.5 %copy-start = (bf16[128256]{0:T(1024)(128)(2,1)S(1)}, bf16[128256]{0:T(1024)(128)(2,1)}, u32[]{:S(2)}) copy-start(bf16[128256]{0:T(1024)(128)(2,1)} %param.32) | copy-start | bytes 769540
  8.9 31.7 %all-to-all-start = ((bf16[8,64,512]{2,1,0:T(8,128)(2,1)}), bf16[8,64,512]{2,1,0:T(8,128)(2,1)S(1)}, u32[]{:S(2)}, u32[]{:S(2)}) async-start(bf16[8,64,512]{2,1,0:T(8,128)(2,1)} %broadcast_in_dim.25), calls=%async_computation | async-start | bytes 1048576 | tf_op jit(solution)/shard_map/all_to_all | solution.py:445
  17.9 19.1 %collective-permute-start.8 = (bf16[16,128,128]{2,1,0:T(8,128)(2,1)}, bf16[16,128,128]{2,1,0:T(8,128)(2,1)S(1)}, u32[]{:S(2)}, u32[]{:S(2)}) collective-permute-start(bf16[16,128,128]{2,1,0:T(8,128)(2,1)} %kc.1), channel_id=1, source_target_pairs={{0,8},{8,0},{16,24},{24,16},{32,40},{40,32},{48,56},{56,48},{64,72... | collective-permute-start | bytes 1572872 | tf_op jit(solution)/shard_map/ppermute | solution.py:387
  18.9 18.2 %collective-permute-start.9 = (bf16[16,128,128]{2,1,0:T(8,128)(2,1)}, bf16[16,128,128]{2,1,0:T(8,128)(2,1)S(1)}, u32[]{:S(2)}, u32[]{:S(2)}) collective-permute-start(bf16[16,128,128]{2,1,0:T(8,128)(2,1)} %vc.1), channel_id=1, source_target_pairs={{0,8},{8,0},{16,24},{24,16},{32,40},{40,32},{48,56},{56,48},{64,72... | collective-permute-start | bytes 1572872 | tf_op jit(solution)/shard_map/ppermute | solution.py:387
  19.0 2.4 %collective-permute-start.1 = (s32[1,16]{1,0:T(1,128)}, s32[1,16]{1,0:T(1,128)S(1)}, u32[]{:S(2)}, u32[]{:S(2)}) collective-permute-start(s32[1,16]{1,0:T(1,128)} %bitcast.26), channel_id=1, source_target_pairs={{0,8},{8,0},{16,24},{24,16},{32,40},{40,32},{48,56},{56,48},{64,72... | collective-permute-start | bytes 200 | tf_op jit(solution)/shard_map/ppermute | solution.py:387
  22.0 3.6 %collective-permute-start.4 = (s32[2,16]{1,0:T(2,128)S(1)}, s32[2,16]{1,0:T(2,128)S(1)}, u32[]{:S(2)}, u32[]{:S(2)}) collective-permute-start(s32[2,16]{1,0:T(2,128)S(1)} %pad_add_fusion), channel_id=1, source_target_pairs={{0,48},{8,56},{16,0},{24,8},{32,16},{40,24},{48,32},{56,40},{64,11... | collective-permute-start | bytes 392 | tf_op jit(solution)/shard_map/ppermute | solution.py:406
  24.5 4.2 %collective-permute-start.3 = (s32[2,16]{1,0:T(2,128)S(1)}, s32[2,16]{1,0:T(2,128)S(1)}, u32[]{:S(2)}, u32[]{:S(2)}) collective-permute-start(s32[2,16]{1,0:T(2,128)S(1)} %pad_add_fusion), channel_id=1, source_target_pairs={{0,32},{8,40},{16,48},{24,56},{32,0},{40,8},{48,16},{56,24},{64,96... | collective-permute-start | bytes 392 | tf_op jit(solution)/shard_map/ppermute | solution.py:406
  25.0 3.9 %collective-permute-start.2 = (s32[2,16]{1,0:T(2,128)S(1)}, s32[2,16]{1,0:T(2,128)S(1)}, u32[]{:S(2)}, u32[]{:S(2)}) collective-permute-start(s32[2,16]{1,0:T(2,128)S(1)} %pad_add_fusion), channel_id=1, source_target_pairs={{0,16},{8,24},{16,32},{24,40},{32,48},{40,56},{48,0},{56,8},{64,80... | collective-permute-start | bytes 392 | tf_op jit(solution)/shard_map/ppermute | solution.py:406
  29.6 3.9 %collective-permute-start.7 = (s32[8,16]{1,0:T(8,128)S(1)}, s32[8,16]{1,0:T(8,128)S(1)}, u32[]{:S(2)}, u32[]{:S(2)}) collective-permute-start(s32[8,16]{1,0:T(8,128)S(1)} %concatenate.35.refs_0_), channel_id=1, source_target_pairs={{0,192},{8,200},{16,208},{24,216},{32,224},{40,232},{48,240},{56,2... | collective-permute-start | bytes 1544 | tf_op jit(solution)/shard_map/ppermute | solution.py:406
  32.4 4.0 %collective-permute-start.6 = (s32[8,16]{1,0:T(8,128)S(1)}, s32[8,16]{1,0:T(8,128)S(1)}, u32[]{:S(2)}, u32[]{:S(2)}) collective-permute-start(s32[8,16]{1,0:T(8,128)S(1)} %concatenate.35.refs_0_), channel_id=1, source_target_pairs={{0,128},{8,136},{16,144},{24,152},{32,160},{40,168},{48,176},{56,1... | collective-permute-start | bytes 1544 | tf_op jit(solution)/shard_map/ppermute | solution.py:406
  32.8 3.7 %collective-permute-start.5 = (s32[8,16]{1,0:T(8,128)S(1)}, s32[8,16]{1,0:T(8,128)S(1)}, u32[]{:S(2)}, u32[]{:S(2)}) collective-permute-start(s32[8,16]{1,0:T(8,128)S(1)} %concatenate.35.refs_0_), channel_id=1, source_target_pairs={{0,64},{8,72},{16,80},{24,88},{32,96},{40,104},{48,112},{56,120},{... | collective-permute-start | bytes 1544 | tf_op jit(solution)/shard_map/ppermute | solution.py:406
  41.4 42.1 %all-to-all-start.1 = ((bf16[16,3,256,128]{3,2,1,0:T(8,128)(2,1)}), bf16[16,3,256,128]{3,2,1,0:T(8,128)(2,1)S(1)}, u32[]{:S(2)}, u32[]{:S(2)}) async-start(bf16[16,3,256,128]{3,2,1,0:T(8,128)(2,1)} %pack.1), calls=%async_computation.1 | async-start | bytes 6291456 | tf_op jit(solution)/shard_map/all_to_all | solution.py:398
  45.5 70.4 %all-gather.2.cloned.1.call-start = ((), (), s32[]{:S(2)}) async-start(), calls=%async_computation.3 | async-start | bytes 1081344 | tf_op jit(solution)/shard_map/all_gather | solution.py:458
  51.7 9.8 %copy-start.14 = (f32[16]{0:T(128)S(1)}, f32[16]{0:T(128)}, u32[]{:S(2)}) copy-start(f32[16]{0:T(128)} %param.34) | copy-start | bytes 196
  51.7 26.6 %copy-start.1 = (bf16[4,16,512]{2,1,0:T(8,128)(2,1)S(1)}, bf16[4,16,512]{2,1,0:T(8,128)(2,1)}, u32[]{:S(2)}) copy-start(bf16[4,16,512]{2,1,0:T(8,128)(2,1)} %param.23) | copy-start | bytes 196612
  51.7 26.6 %copy-start.3 = (f32[512]{0:T(512)S(1)}, f32[512]{0:T(512)}, u32[]{:S(2)}) copy-start(f32[512]{0:T(512)} %param.33) | copy-start | bytes 6148
  57.8 10.5 %collective-permute-start.10 = (bf16[64,512]{1,0:T(8,128)(2,1)}, bf16[64,512]{1,0:T(8,128)(2,1)S(1)}, u32[]{:S(2)}, u32[]{:S(2)}) collective-permute-start(bf16[64,512]{1,0:T(8,128)(2,1)} %get-tuple-element.214), channel_id=1, source_target_pairs={{0,1},{1,2},{2,3},{3,4},{4,5},{5,6},{6,7},{7,0},{8,9},{9,10},{10,1... | collective-permute-start | bytes 196616 | tf_op jit(solution)/shard_map/ppermute | solution.py:383
  59.6 12.0 %collective-permute-start.11 = (bf16[64,512]{1,0:T(8,128)(2,1)}, bf16[64,512]{1,0:T(8,128)(2,1)S(1)}, u32[]{:S(2)}, u32[]{:S(2)}) collective-permute-start(bf16[64,512]{1,0:T(8,128)(2,1)} %get-tuple-element.215), channel_id=1, source_target_pairs={{0,2},{1,3},{2,4},{3,5},{4,6},{5,7},{6,0},{7,1},{8,10},{9,11},{10,... | collective-permute-start | bytes 196616 | tf_op jit(solution)/shard_map/ppermute | solution.py:383
  61.4 11.4 %collective-permute-start.12 = (bf16[64,512]{1,0:T(8,128)(2,1)}, bf16[64,512]{1,0:T(8,128)(2,1)S(1)}, u32[]{:S(2)}, u32[]{:S(2)}) collective-permute-start(bf16[64,512]{1,0:T(8,128)(2,1)} %get-tuple-element.216), channel_id=1, source_target_pairs={{0,3},{1,4},{2,5},{3,6},{4,7},{5,0},{6,1},{7,2},{8,11},{9,12},{10,... | collective-permute-start | bytes 196616 | tf_op jit(solution)/shard_map/ppermute | solution.py:383
  63.8 9.0 %collective-permute-start.13 = (bf16[64,512]{1,0:T(8,128)(2,1)}, bf16[64,512]{1,0:T(8,128)(2,1)S(1)}, u32[]{:S(2)}, u32[]{:S(2)}) collective-permute-start(bf16[64,512]{1,0:T(8,128)(2,1)} %get-tuple-element.217), channel_id=1, source_target_pairs={{0,4},{1,5},{2,6},{3,7},{4,0},{5,1},{6,2},{7,3},{8,12},{9,13},{10,... | collective-permute-start | bytes 196616 | tf_op jit(solution)/shard_map/ppermute | solution.py:383
  65.9 6.9 %collective-permute-start.14 = (bf16[64,512]{1,0:T(8,128)(2,1)}, bf16[64,512]{1,0:T(8,128)(2,1)S(1)}, u32[]{:S(2)}, u32[]{:S(2)}) collective-permute-start(bf16[64,512]{1,0:T(8,128)(2,1)} %get-tuple-element.218), channel_id=1, source_target_pairs={{0,5},{1,6},{2,7},{3,0},{4,1},{5,2},{6,3},{7,4},{8,13},{9,14},{10,... | collective-permute-start | bytes 196616 | tf_op jit(solution)/shard_map/ppermute | solution.py:383
  68.3 7.3 %collective-permute-start.15 = (bf16[64,512]{1,0:T(8,128)(2,1)}, bf16[64,512]{1,0:T(8,128)(2,1)S(1)}, u32[]{:S(2)}, u32[]{:S(2)}) collective-permute-start(bf16[64,512]{1,0:T(8,128)(2,1)} %get-tuple-element.219), channel_id=1, source_target_pairs={{0,6},{1,7},{2,0},{3,1},{4,2},{5,3},{6,4},{7,5},{8,14},{9,15},{10,... | collective-permute-start | bytes 196616 | tf_op jit(solution)/shard_map/ppermute | solution.py:383
  71.6 6.7 %collective-permute-start.16 = (bf16[64,512]{1,0:T(8,128)(2,1)}, bf16[64,512]{1,0:T(8,128)(2,1)S(1)}, u32[]{:S(2)}, u32[]{:S(2)}) collective-permute-start(bf16[64,512]{1,0:T(8,128)(2,1)} %get-tuple-element.220), channel_id=1, source_target_pairs={{0,7},{1,0},{2,1},{3,2},{4,3},{5,4},{6,5},{7,6},{8,15},{9,8},{10,9... | collective-permute-start | bytes 196616 | tf_op jit(solution)/shard_map/ppermute | solution.py:383
  85.2 33.2 %all-to-all-start.2 = ((f32[256,2,128]{2,1,0:T(2,128)}), f32[256,2,128]{2,1,0:T(2,128)S(1)}, u32[]{:S(2)}, u32[]{:S(2)}) async-start(f32[256,2,128]{2,1,0:T(2,128)} %get-tuple-element.227), calls=%async_computation.2 | async-start | bytes 524288 | tf_op jit(solution)/shard_map/all_to_all | solution.py:466
  (9 other events, 22.8 us)
Sparse Core Ops, SparseCore 0:
  51.7 64.1 all-gather.1

commit v5 on v3

--- a/solution.py
+++ b/solution.py
@@ -42,13 +42,11 @@
     return jnp.dot(a, b, preferred_element_type=F32)
 
 
-def project_body(blk, *refs):
-    acts = refs[:TP]
-    gain, wq, wk, wv, table, qa, kf, vf, fresh = refs[TP : TP + 9]
-    wq_s, wk_s, wv_s, q_s, kf_s, vf_s, sems = refs[TP + 9 :]
+def project_body(acts, gain, wq, wk, wv, table, qa, kf, vf, fresh, *scratch):
+    wq_s, wk_s, wv_s, q_s, kf_s, vf_s, sems = scratch
     copies = []
     for s in range(TP):
-        part = pl.ds(pl.multiple_of(blk[s] * DB, DB), DB)
+        part = pl.ds(s * DB, DB)
         copies.append(
             [
                 pltpu.make_async_copy(w.at[part, :], w_s.at[s], sems.at[n, s])
@@ -60,15 +58,15 @@
             c.start()
     square = jnp.zeros((ROWS, 1), F32)
     for s in range(TP):
-        x = acts[s][...].astype(F32)
+        x = acts[s].astype(F32)
         square = square + jnp.sum(x * x, -1, keepdims=True)
     inv = lax.rsqrt(square / D + 1e-05)
     q = jnp.zeros((ROWS, DB), F32)
     k = jnp.zeros((ROWS, HD), F32)
     v = jnp.zeros((ROWS, HD), F32)
     for s in range(TP):
-        x = acts[s][...].astype(F32)
-        normed = (x * inv * gain[pl.ds(blk[s], 1), :]).astype(BF)
+        x = acts[s].astype(F32)
+        normed = (x * inv * gain[s : s + 1, :]).astype(BF)
         for c in copies[s]:
             c.wait()
         q = q + mm(normed, wq_s[s])
@@ -96,11 +94,11 @@
         ).astype(BF)
 
 
-def project(blk, acts, gain, wq, wk, wv, table):
+def project(acts, gain, wq, wk, wv, table):
     sd = jax.ShapeDtypeStruct
     return pl.pallas_call(
         project_body,
-        in_specs=[spec(SM)] + [spec(VM)] * (TP + 1) + [spec(ANY)] * 3 + [spec(VM)],
+        in_specs=[spec(VM)] * 2 + [spec(ANY)] * 3 + [spec(VM)],
         out_specs=[spec(VM)] * 4,
         out_shape=[
             sd((NP * GROUP, HD), BF),
@@ -122,7 +120,7 @@
             flops=2 * ROWS * D * 768, bytes_accessed=7 * 2**20, transcendentals=0
         ),
         name="project",
-    )(blk, *acts, gain, wq, wk, wv, table)
+    )(acts, gain, wq, wk, wv, table)
 
 
 def attend_body(blk, qa, kf, vf, kc, vc, wo, *refs):
@@ -130,7 +128,7 @@
     s1_s, ctx_s, wo_s, sems = refs[TP:]
     copies = []
     for s in range(TP):
-        there = pl.ds(pl.multiple_of(blk[TP + s] * DB, DB), DB)
+        there = pl.ds(pl.multiple_of(blk[s] * DB, DB), DB)
         copies.append(pltpu.make_async_copy(wo.at[:, there], wo_s.at[s], sems.at[s]))
     for c in copies:
         c.start()
@@ -292,7 +290,7 @@
 
 def plan_body(me_ref, counts_ref, out):
     me = me_ref[0]
-    counts = counts_ref[:, 0, 0:NP].astype(F32)
+    counts = counts_ref[:, 0, :].astype(F32)
     r16 = lax.broadcasted_iota(jnp.int32, (NP, NP), 0)
     c16 = lax.broadcasted_iota(jnp.int32, (NP, NP), 1)
     within = mm(counts, (r16 <= c16).astype(F32))
@@ -437,8 +435,7 @@
 
 
 def counts_of_all(counts):
-    line = jnp.pad(counts, (0, HD - NP))
-    sent = jnp.broadcast_to(line[None, None], (NDOM, 8, HD))
+    sent = jnp.broadcast_to(counts[None, None], (NDOM, 1, NP))
     return lax.all_to_all(sent, "dom", 0, 0, tiled=True)
 
 
@@ -468,30 +465,32 @@
     dom = lax.axis_index("dom")
     tp = lax.axis_index("tp")
     me = dom.reshape(1)
-    ring = np.arange(TP)
-    blk = (jnp.concatenate([tp - ring, tp + ring]) % TP).astype(jnp.int32)
+    blk = ((tp + np.arange(TP)) % TP).astype(jnp.int32)
     act = activations.reshape(ROWS, DB)
-
-    counts = counts_of_all(copy_counts)
-    acts = [act] + [shifted(act, s) for s in range(1, TP)]
-    counts, *acts[2:6] = lax.optimization_barrier((counts, *acts[2:6]))
-    partner_keys = swapped(cache_keys)
-    partner_values = swapped(cache_values)
-    idx = plan(me, counts)
-    packed = pack(me, idx, [cache_keys, cache_values], [partner_keys, partner_values])
-    rows = exchanged(packed)
     reward = twisting_table[tokens.reshape(ROWS)].astype(F32)
     reward = jnp.pad(reward, (0, HD - ROWS)).reshape(1, HD)
     previous = jnp.pad(previous_log_weights, (0, HD - NP)).reshape(1, HD)
-
-    packed, *acts = lax.optimization_barrier((packed, *acts))
+    partner_keys = swapped(cache_keys)
+    partner_values = swapped(cache_values)
+
+    counts = counts_of_all(copy_counts)
+    sent = jnp.broadcast_to(act[None], (TP, ROWS, DB))
+    sent, counts, partner_keys, partner_values, reward, previous = lax.optimization_barrier(
+        (sent, counts, partner_keys, partner_values, reward, previous)
+    )
+    gathered = lax.all_to_all(sent, "tp", 0, 0, tiled=True)
+    idx = plan(me, counts)
+    packed = pack(me, idx, [cache_keys, cache_values], [partner_keys, partner_values])
+    packed, gathered = lax.optimization_barrier((packed, gathered))
+    rows = exchanged(packed)
+
     qa, kf, vf, fresh = project(
-        blk, acts, norm_gain.reshape(TP, DB), w_query, w_key, value_weight, rotation_table()
+        gathered, norm_gain.reshape(TP, DB), w_query, w_key, value_weight, rotation_table()
     )
     partials = attend(blk, qa, kf, vf, cache_keys, cache_values, w_output)
     parts = [partials[0]] + [shifted(partials[s], s) for s in range(1, TP)]
     attn, sums = mix(parts, act, twist_vec.reshape(1, DB))
-    sums, rows, reward, previous = lax.optimization_barrier((sums, rows, reward, previous))
+    sums, rows = lax.optimization_barrier((sums, rows))
     sums = lax.all_to_all(sums, "tp", 0, 0, tiled=True)
     line, sent = weigh(idx, sums, reward, previous, fresh)
     got = lax.all_to_all(sent, "dom", 0, 0, tiled=True)

time: 118 us -> 128 us (1.085)
  waiting for transfers between devices: 17.8 us -> 49.7 us
  blocking collectives: 16.6 us -> 0 us
  starting transfers between devices: 52.3 us -> 41 us
  local copies, waits for them, and re-layouts: 7.51 us -> 11.8 us
  Pallas kernels: 20.7 us -> 22.1 us
    ppermute x14 -> x7, starting transfers between devices: 27.9 us -> 9.58 us  [shifted(): return lax.ppermute(value, 'tp', [(i, (i + shift) % TP) for i in range(TP)])]
    all_to_all x1 -> x0, blocking collectives: 16.6 us -> none  [local(): sums = lax.all_to_all(sums, 'tp', 0, 0, tiled=True)]
    all_to_all x0 -> x2, waiting for transfers between devices: none -> 15.5 us  [the longest x1 14 us: local(): gathered = lax.all_to_all(sent, 'tp', 0, 0, tiled=True)]
    all_to_all x1, waiting for transfers between devices: 0.01 us -> 15.3 us  [exchanged(): lax.all_to_all(rows, 'dom', 0, 0, tiled=True, axis_index_groups=SAME_CORE)]
    all_to_all x0 -> x2, starting transfers between devices: none -> 11.5 us  [the longest x1 8.19 us: local(): gathered = lax.all_to_all(sent, 'tp', 0, 0, tiled=True)]
    ppermute x14 -> x7, waiting for transfers between devices: 15.3 us -> 9.59 us  [shifted(): return lax.ppermute(value, 'tp', [(i, (i + shift) % TP) for i in range(TP)])]
    all_to_all x1, waiting for transfers between devices: 0.01 us -> 4.61 us  [counts_of_all(): return lax.all_to_all(sent, 'dom', 0, 0, tiled=True)]
    broadcast_in_dim x1 -> x2, local copies, waits for them, and re-layouts: 0.67 us -> 3.04 us  [the longest x1 1.77 us: local(): sent = jnp.broadcast_to(act[None], (TP, ROWS, DB))]
  transfers between devices with their start and end apart: 19 -> 14, of which waited for: 8 -> 9; matrix products, arithmetic and copies ran while one was open for 6% -> 7% of each run, Pallas kernels for 12% -> 15%
where the time goes in v5:
time: 128 us; the launch traced here: 127 us
  waiting for transfers between devices  49.7 us (39%)
  starting transfers between devices  41 us (32%)
  Pallas kernels  22.1 us (17%)
  local copies, waits for them, and re-layouts  11.8 us (9%)
  between operations  1.65 us (1%)
    all_to_all x1, waiting for transfers between devices, exchanged(): lax.all_to_all(rows, 'dom', 0, 0, tiled=True, axis_index_groups=SAME_CORE)  15.3 us
    all_to_all x1, waiting for transfers between devices, local(): gathered = lax.all_to_all(sent, 'tp', 0, 0, tiled=True)  14 us
    ppermute x7, waiting for transfers between devices, shifted(): return lax.ppermute(value, 'tp', [(i, (i + shift) % TP) for i in range(TP)])  9.59 us
    ppermute x7, starting transfers between devices, shifted(): return lax.ppermute(value, 'tp', [(i, (i + shift) % TP) for i in range(TP)])  9.58 us
    all_to_all x1, starting transfers between devices, local(): gathered = lax.all_to_all(sent, 'tp', 0, 0, tiled=True)  8.19 us
    all_to_all x1, starting transfers between devices, local(): got = lax.all_to_all(sent, 'dom', 0, 0, tiled=True)  6.95 us
    all_to_all x1, starting transfers between devices, counts_of_all(): return lax.all_to_all(sent, 'dom', 0, 0, tiled=True)  5.76 us
    pallas_call x1, Pallas kernels, project(): pl.pallas_call(project_body, in_specs=[spec(VM)] * 2 + [spec(ANY)] * 3 +...  5.44 us
  transfers between devices with their start and end apart: 14, of which 9 were waited for; matrix products, arithmetic and copies ran while one was open for 7% of the time, Pallas kernels for 15%

profile of v5, /device:TPU:1, one launch (start us, length us, event | category | flops | bytes accessed | tf_op | source)
XLA Modules:
  0.0 126.9 jit_solution(18286545172622962143)
XLA Ops:
  0.6 3.3 %collective-permute-start.1 = (bf16[16,128,128]{2,1,0:T(8,128)(2,1)}, bf16[16,128,128]{2,1,0:T(8,128)(2,1)S(1)}, u32[]{:S(2)}, u32[]{:S(2)}) collective-permute-start(bf16[16,128,128]{2,1,0:T(8,128)(2,1)} %kc.1), channel_id=1, source_target_pairs={{0,8},{8,0},{16,24},{24,16},{32,40},{40,32},{48,56},{56,48},{64,72... | collective-permute-start | bytes 1572872 | tf_op jit(solution)/shard_map/ppermute | solution.py:423
  5.3 5.8 %all-to-all-start = ((s32[32,1,16]{2,1,0:T(1,128)}), s32[32,1,16]{2,1,0:T(1,128)S(1)}, u32[]{:S(2)}, u32[]{:S(2)}) async-start(s32[32,1,16]{2,1,0:T(1,128)} %broadcast_in_dim.26), calls=%async_computation | async-start | bytes 32768 | tf_op jit(solution)/shard_map/all_to_all | solution.py:439
  13.4 4.6 %all-to-all-done.counts_ref = s32[32,1,16]{2,1,0:T(1,128)S(1)} async-done(((s32[32,1,16]{2,1,0:T(1,128)}), s32[32,1,16]{2,1,0:T(1,128)S(1)}, u32[]{:S(2)}, u32[]{:S(2)}) %all-to-all-start) | async-done | bytes 2080 | tf_op jit(solution)/shard_map/all_to_all | solution.py:439
  18.0 1.8 %broadcast_in_dim.25 = bf16[8,64,512]{2,1,0:T(8,128)(2,1)} broadcast(bf16[64,512]{1,0:T(8,128)(2,1)} %bitcast.30), dimensions={1,2} | broadcast | bytes 589824 | tf_op jit(solution)/shard_map/broadcast_in_dim | solution.py:477
  19.8 8.2 %all-to-all-start.1 = ((bf16[8,64,512]{2,1,0:T(8,128)(2,1)}), bf16[8,64,512]{2,1,0:T(8,128)(2,1)S(1)}, u32[]{:S(2)}, u32[]{:S(2)}) async-start(bf16[8,64,512]{2,1,0:T(8,128)(2,1)} %broadcast_in_dim.25), calls=%async_computation.1 | async-start | bytes 1048576 | tf_op jit(solution)/shard_map/all_to_all | solution.py:481
  28.4 3.5 %pack.1 = bf16[16,3,256,128]{3,2,1,0:T(8,128)(2,1)} custom-call(s32[1]{0:T(128)} %bitcast.6.me_ref, s32[8,128]{1,0:T(8,128)S(1)} %plan.1.idx, bf16[16,128,128]{2,1,0:T(8,128)(2,1)} %kc.1, bf16[16,128,128]{2,1,0:T(8,128)(2,1)} %vc.1, bf16[16,128,128]{2,1,0:T(8,128)(2,1)S(1)} %collective-permute-done.1.refs_2_, ...), custom_call_target="tpu_custom_call" | custom-call | tf_op jit(solution)/shard_map/pack/pallas_call | solution.py:377
  31.9 14.0 %all-to-all-done.1.acts = bf16[8,64,512]{2,1,0:T(8,128)(2,1)S(1)} async-done(((bf16[8,64,512]{2,1,0:T(8,128)(2,1)}), bf16[8,64,512]{2,1,0:T(8,128)(2,1)S(1)}, u32[]{:S(2)}, u32[]{:S(2)}) %all-to-all-start.1) | async-done | bytes 524320 | tf_op jit(solution)/shard_map/all_to_all | solution.py:481
  46.7 3.7 %all-to-all-start.2 = ((bf16[16,3,256,128]{3,2,1,0:T(8,128)(2,1)}), bf16[16,3,256,128]{3,2,1,0:T(8,128)(2,1)S(1)}, u32[]{:S(2)}, u32[]{:S(2)}) async-start(bf16[16,3,256,128]{3,2,1,0:T(8,128)(2,1)} %pack.1), calls=%async_computation.2 | async-start | bytes 6291456 | tf_op jit(solution)/shard_map/all_to_all | solution.py:434
  51.6 5.4 %project.1 = (bf16[256,128]{1,0:T(8,128)(2,1)}, bf16[64,128]{1,0:T(8,128)(2,1)}, bf16[64,128]{1,0:T(8,128)(2,1)}, bf16[16,8,128]{2,1,0:T(8,128)(2,1)}) custom-call(bf16[8,64,512]{2,1,0:T(8,128)(2,1)} %copy-done.10, f32[8,512]{1,0:T(8,128)} %reshape.198.gain, bf16[4096,512]{1,0:T(8,128)(2,1)} %wq.1, bf16[4096,128]{1,0:T(8,128)(2,1)} %wk.1, ...), custom_call_target="tpu_custom_call" | custom-call | flops 402653184 | bytes 7340032 | tf_op jit(solution)/shard_map/project/pallas_call | solution.py:99
  57.1 5.1 %attend.1 = (bf16[64,512]{1,0:T(8,128)(2,1)}, bf16[64,512]{1,0:T(8,128)(2,1)}, bf16[64,512]{1,0:T(8,128)(2,1)}, bf16[64,512]{1,0:T(8,128)(2,1)}, bf16[64,512]{1,...) custom-call(s32[8]{0:T(128)} %and_select_fusion.blk, ...), custom_call_target="tpu_custom_call" | custom-call | flops 335544320 | bytes 6291456 | tf_op jit(solution)/shard_map/attend/pallas_call | solution.py:164
  63.7 4.2 %collective-permute-start.6 = (bf16[64,512]{1,0:T(8,128)(2,1)}, bf16[64,512]{1,0:T(8,128)(2,1)S(1)}, u32[]{:S(2)}, u32[]{:S(2)}) collective-permute-start(bf16[64,512]{1,0:T(8,128)(2,1)} %get-tuple-element.227), channel_id=1, source_target_pairs={{0,4},{1,5},{2,6},{3,7},{4,0},{5,1},{6,2},{7,3},{8,12},{9,13},{10,... | collective-permute-start | bytes 196616 | tf_op jit(solution)/shard_map/ppermute | solution.py:419
  68.0 3.5 %collective-permute-start.8 = (bf16[64,512]{1,0:T(8,128)(2,1)}, bf16[64,512]{1,0:T(8,128)(2,1)S(1)}, u32[]{:S(2)}, u32[]{:S(2)}) collective-permute-start(bf16[64,512]{1,0:T(8,128)(2,1)} %get-tuple-element.229), channel_id=1, source_target_pairs={{0,6},{1,7},{2,0},{3,1},{4,2},{5,3},{6,4},{7,5},{8,14},{9,15},{10,... | collective-permute-start | bytes 196616 | tf_op jit(solution)/shard_map/ppermute | solution.py:419
  72.8 3.7 %collective-permute-done.7.refs_5_ = bf16[64,512]{1,0:T(8,128)(2,1)S(1)} collective-permute-done((bf16[64,512]{1,0:T(8,128)(2,1)}, bf16[64,512]{1,0:T(8,128)(2,1)S(1)}, u32[]{:S(2)}, u32[]{:S(2)}) %collective-permute-start.7) | collective-permute-done | bytes 65568 | tf_op jit(solution)/shard_map/ppermute | solution.py:419
  76.5 3.3 %collective-permute-done.8.refs_6_ = bf16[64,512]{1,0:T(8,128)(2,1)S(1)} collective-permute-done((bf16[64,512]{1,0:T(8,128)(2,1)}, bf16[64,512]{1,0:T(8,128)(2,1)S(1)}, u32[]{:S(2)}, u32[]{:S(2)}) %collective-permute-start.8) | collective-permute-done | bytes 65568 | tf_op jit(solution)/shard_map/ppermute | solution.py:419
  79.7 1.6 %collective-permute-done.9.refs_7_ = bf16[64,512]{1,0:T(8,128)(2,1)S(1)} collective-permute-done((bf16[64,512]{1,0:T(8,128)(2,1)}, bf16[64,512]{1,0:T(8,128)(2,1)S(1)}, u32[]{:S(2)}, u32[]{:S(2)}) %collective-permute-start.9) | collective-permute-done | bytes 65568 | tf_op jit(solution)/shard_map/ppermute | solution.py:419
  83.0 15.3 %all-to-all-done.2 = bf16[16,3,256,128]{3,2,1,0:T(8,128)(2,1)S(1)} async-done(((bf16[16,3,256,128]{3,2,1,0:T(8,128)(2,1)}), bf16[16,3,256,128]{3,2,1,0:T(8,128)(2,1)S(1)}, u32[]{:S(2)}, u32[]{:S(2)}) %all-to-all-start.2) | async-done | bytes 3145760 | tf_op jit(solution)/shard_map/all_to_all | solution.py:434
  98.3 3.3 %all-to-all-start.3 = ((f32[8,1,128]{2,1,0:T(1,128)}), f32[8,1,128]{2,1,0:T(1,128)S(1)}, u32[]{:S(2)}, u32[]{:S(2)}) async-start(f32[8,1,128]{2,1,0:T(1,128)} %get-tuple-element.234), calls=%async_computation.3 | async-start | bytes 8192 | tf_op jit(solution)/shard_map/all_to_all | solution.py:494
  102.9 3.6 %conditional.1 = ((bf16[16,128,128]{2,1,0:T(8,128)(2,1)}, bf16[16,128,128]{2,1,0:T(8,128)(2,1)})) conditional(s32[]{:T(128)} %bitcast.13, (s32[8,128]{1,0:T(8,128)S(1)}, bf16[16,3,256,128]{3,2,1,0:T(8,128)(2,1)S(1)}) %tuple.54, (s32[]{:T(128)}, bf16[16,128,128]{2,1,0:T(8,128)(2,1)}, bf16[16,128,128]{2,1,0:T(8,128)(2,1)}, ...), branch_computations={%region_0.1_spmd, %region_1.6_spmd} | conditional | flops 4260986 | bytes 48632988 | solution.py:520
  102.9 3.4 %place.2 = (bf16[16,128,128]{2,1,0:T(8,128)(2,1)}, bf16[16,128,128]{2,1,0:T(8,128)(2,1)}) custom-call(s32[8,128]{1,0:T(8,128)S(1)} %get-tuple-element.164.refs_0_, bf16[16,3,256,128]{3,2,1,0:T(8,128)(2,1)S(1)} %get-tuple-element.165.refs_1_), custom_call_target="tpu_custom_call" | custom-call | tf_op jit(solution)/shard_map/cond/branch_0_fun/place/pallas_call | solution.py:407
  106.5 1.6 %all-to-all-done.3.sums = f32[8,1,128]{2,1,0:T(1,128)S(1)} async-done(((f32[8,1,128]{2,1,0:T(1,128)}), f32[8,1,128]{2,1,0:T(1,128)S(1)}, u32[]{:S(2)}, u32[]{:S(2)}) %all-to-all-start.3) | async-done | bytes 4128 | tf_op jit(solution)/shard_map/all_to_all | solution.py:494
  109.5 6.9 %all-to-all-start.4 = ((bf16[32,3,8,128]{3,2,1,0:T(8,128)(2,1)}), bf16[32,3,8,128]{3,2,1,0:T(8,128)(2,1)S(1)}, u32[]{:S(2)}, u32[]{:S(2)}) async-start(bf16[32,3,8,128]{3,2,1,0:T(8,128)(2,1)} %get-tuple-element.239), calls=%async_computation.4 | async-start | bytes 393216 | tf_op jit(solution)/shard_map/all_to_all | solution.py:496
  116.5 1.9 %copy_bitcast_fusion = (bf16[128,16,128]{2,1,0:T(8,128)(2,1)S(1)}, bf16[128,16,128]{2,1,0:T(8,128)(2,1)S(1)}) fusion(bf16[16,128,128]{2,1,0:T(8,128)(2,1)} %get-tuple-element.242, bf16[16,128,128]{2,1,0:T(8,128)(2,1)} %get-tuple-element.241), kind=kLoop, calls=%fused_computation.17 | loop fusion | bytes 2097152 | tf_op jit(solution)/shard_map/transpose | solution.py:531
  120.1 4.6 %all-to-all-done.4.got = bf16[32,3,8,128]{3,2,1,0:T(8,128)(2,1)S(1)} async-done(((bf16[32,3,8,128]{3,2,1,0:T(8,128)(2,1)}), bf16[32,3,8,128]{3,2,1,0:T(8,128)(2,1)S(1)}, u32[]{:S(2)}, u32[]{:S(2)}) %all-to-all-start.4) | async-done | bytes 196640 | tf_op jit(solution)/shard_map/all_to_all | solution.py:496
  124.7 2.0 %finish.1 = (f32[1,16]{1,0:T(1,128)}, bf16[132,16,128]{2,1,0:T(8,128)(2,1)}, bf16[132,16,128]{2,1,0:T(8,128)(2,1)}) custom-call(s32[8,128]{1,0:T(8,128)S(1)} %plan.1.idx, f32[1,128]{1,0:T(1,128)S(1)} %get-tuple-element.238.line, bf16[32,3,8,128]{3,2,1,0:T(8,128)(2,1)S(1)} %all-to-all-done.4.got, ...), custom_call_target="tpu_custom_call", output_to_operand_aliasing={{1}: (3, {}), {2}: (4, {})} | custom-call | tf_op jit(solution)/shard_map/finish/pallas_call | solution.py:273
  (49 shorter events, 14.4 us)
Async XLA Ops:
  0.6 11.3 %copy-start = (bf16[128256]{0:T(1024)(128)(2,1)S(1)}, bf16[128256]{0:T(1024)(128)(2,1)}, u32[]{:S(2)}) copy-start(bf16[128256]{0:T(1024)(128)(2,1)} %param.32) | copy-start | bytes 769540
  0.6 17.3 %collective-permute-start.1 = (bf16[16,128,128]{2,1,0:T(8,128)(2,1)}, bf16[16,128,128]{2,1,0:T(8,128)(2,1)S(1)}, u32[]{:S(2)}, u32[]{:S(2)}) collective-permute-start(bf16[16,128,128]{2,1,0:T(8,128)(2,1)} %kc.1), channel_id=1, source_target_pairs={{0,8},{8,0},{16,24},{24,16},{32,40},{40,32},{48,56},{56,48},{64,72... | collective-permute-start | bytes 1572872 | tf_op jit(solution)/shard_map/ppermute | solution.py:423
  4.0 14.0 %collective-permute-start.2 = (bf16[16,128,128]{2,1,0:T(8,128)(2,1)}, bf16[16,128,128]{2,1,0:T(8,128)(2,1)S(1)}, u32[]{:S(2)}, u32[]{:S(2)}) collective-permute-start(bf16[16,128,128]{2,1,0:T(8,128)(2,1)} %vc.1), channel_id=1, source_target_pairs={{0,8},{8,0},{16,24},{24,16},{32,40},{40,32},{48,56},{56,48},{64,72... | collective-permute-start | bytes 1572872 | tf_op jit(solution)/shard_map/ppermute | solution.py:423
  5.3 12.6 %all-to-all-start = ((s32[32,1,16]{2,1,0:T(1,128)}), s32[32,1,16]{2,1,0:T(1,128)S(1)}, u32[]{:S(2)}, u32[]{:S(2)}) async-start(s32[32,1,16]{2,1,0:T(1,128)} %broadcast_in_dim.26), calls=%async_computation | async-start | bytes 32768 | tf_op jit(solution)/shard_map/all_to_all | solution.py:439
  18.0 13.9 %copy-start.8 = (bf16[16,128,128]{2,1,0:T(8,128)(2,1)}, bf16[16,128,128]{2,1,0:T(8,128)(2,1)S(1)}, u32[]{:S(2)}) copy-start(bf16[16,128,128]{2,1,0:T(8,128)(2,1)S(1)} %collective-permute-done.1.refs_2_) | copy-start | bytes 1572868
  18.0 13.9 %copy-start.9 = (bf16[16,128,128]{2,1,0:T(8,128)(2,1)}, bf16[16,128,128]{2,1,0:T(8,128)(2,1)S(1)}, u32[]{:S(2)}) copy-start(bf16[16,128,128]{2,1,0:T(8,128)(2,1)S(1)} %collective-permute-done.2.refs_3_) | copy-start | bytes 1572868
  19.8 26.1 %all-to-all-start.1 = ((bf16[8,64,512]{2,1,0:T(8,128)(2,1)}), bf16[8,64,512]{2,1,0:T(8,128)(2,1)S(1)}, u32[]{:S(2)}, u32[]{:S(2)}) async-start(bf16[8,64,512]{2,1,0:T(8,128)(2,1)} %broadcast_in_dim.25), calls=%async_computation.1 | async-start | bytes 1048576 | tf_op jit(solution)/shard_map/all_to_all | solution.py:481
  31.9 18.5 %copy-start.12 = (f32[4096]{0:T(1024)S(1)}, f32[4096]{0:T(1024)}, u32[]{:S(2)}) copy-start(f32[4096]{0:T(1024)} %param.24) | copy-start | bytes 49156
  46.7 51.6 %all-to-all-start.2 = ((bf16[16,3,256,128]{3,2,1,0:T(8,128)(2,1)}), bf16[16,3,256,128]{3,2,1,0:T(8,128)(2,1)S(1)}, u32[]{:S(2)}, u32[]{:S(2)}) async-start(bf16[16,3,256,128]{3,2,1,0:T(8,128)(2,1)} %pack.1), calls=%async_computation.2 | async-start | bytes 6291456 | tf_op jit(solution)/shard_map/all_to_all | solution.py:434
  51.6 5.5 %copy-start.6 = (bf16[16,128,128]{2,1,0:T(8,128)(2,1)S(1)}, bf16[16,128,128]{2,1,0:T(8,128)(2,1)}, u32[]{:S(2)}) copy-start(bf16[16,128,128]{2,1,0:T(8,128)(2,1)} %kc.1) | copy-start | bytes 1572868
  51.6 5.5 %copy-start.7 = (bf16[16,128,128]{2,1,0:T(8,128)(2,1)S(1)}, bf16[16,128,128]{2,1,0:T(8,128)(2,1)}, u32[]{:S(2)}) copy-start(bf16[16,128,128]{2,1,0:T(8,128)(2,1)} %vc.1) | copy-start | bytes 1572868
  57.0 24.3 %copy-start.1 = (bf16[4,16,512]{2,1,0:T(8,128)(2,1)S(1)}, bf16[4,16,512]{2,1,0:T(8,128)(2,1)}, u32[]{:S(2)}) copy-start(bf16[4,16,512]{2,1,0:T(8,128)(2,1)} %param.23) | copy-start | bytes 196612
  57.1 24.3 %copy-start.4 = (f32[512]{0:T(512)S(1)}, f32[512]{0:T(512)}, u32[]{:S(2)}) copy-start(f32[512]{0:T(512)} %param.33) | copy-start | bytes 6148
  62.2 5.8 %collective-permute-start.3 = (bf16[64,512]{1,0:T(8,128)(2,1)}, bf16[64,512]{1,0:T(8,128)(2,1)S(1)}, u32[]{:S(2)}, u32[]{:S(2)}) collective-permute-start(bf16[64,512]{1,0:T(8,128)(2,1)} %get-tuple-element.224), channel_id=1, source_target_pairs={{0,1},{1,2},{2,3},{3,4},{4,5},{5,6},{6,7},{7,0},{8,9},{9,10},{10,1... | collective-permute-start | bytes 196616 | tf_op jit(solution)/shard_map/ppermute | solution.py:419
  62.3 9.2 %collective-permute-start.4 = (bf16[64,512]{1,0:T(8,128)(2,1)}, bf16[64,512]{1,0:T(8,128)(2,1)S(1)}, u32[]{:S(2)}, u32[]{:S(2)}) collective-permute-start(bf16[64,512]{1,0:T(8,128)(2,1)} %get-tuple-element.225), channel_id=1, source_target_pairs={{0,2},{1,3},{2,4},{3,5},{4,6},{5,7},{6,0},{7,1},{8,10},{9,11},{10,... | collective-permute-start | bytes 196616 | tf_op jit(solution)/shard_map/ppermute | solution.py:419
  62.3 9.4 %collective-permute-start.5 = (bf16[64,512]{1,0:T(8,128)(2,1)}, bf16[64,512]{1,0:T(8,128)(2,1)S(1)}, u32[]{:S(2)}, u32[]{:S(2)}) collective-permute-start(bf16[64,512]{1,0:T(8,128)(2,1)} %get-tuple-element.226), channel_id=1, source_target_pairs={{0,3},{1,4},{2,5},{3,6},{4,7},{5,0},{6,1},{7,2},{8,11},{9,12},{10,... | collective-permute-start | bytes 196616 | tf_op jit(solution)/shard_map/ppermute | solution.py:419
  63.7 9.1 %collective-permute-start.6 = (bf16[64,512]{1,0:T(8,128)(2,1)}, bf16[64,512]{1,0:T(8,128)(2,1)S(1)}, u32[]{:S(2)}, u32[]{:S(2)}) collective-permute-start(bf16[64,512]{1,0:T(8,128)(2,1)} %get-tuple-element.227), channel_id=1, source_target_pairs={{0,4},{1,5},{2,6},{3,7},{4,0},{5,1},{6,2},{7,3},{8,12},{9,13},{10,... | collective-permute-start | bytes 196616 | tf_op jit(solution)/shard_map/ppermute | solution.py:419
  67.9 8.6 %collective-permute-start.7 = (bf16[64,512]{1,0:T(8,128)(2,1)}, bf16[64,512]{1,0:T(8,128)(2,1)S(1)}, u32[]{:S(2)}, u32[]{:S(2)}) collective-permute-start(bf16[64,512]{1,0:T(8,128)(2,1)} %get-tuple-element.228), channel_id=1, source_target_pairs={{0,5},{1,6},{2,7},{3,0},{4,1},{5,2},{6,3},{7,4},{8,13},{9,14},{10,... | collective-permute-start | bytes 196616 | tf_op jit(solution)/shard_map/ppermute | solution.py:419
  68.0 11.7 %collective-permute-start.8 = (bf16[64,512]{1,0:T(8,128)(2,1)}, bf16[64,512]{1,0:T(8,128)(2,1)S(1)}, u32[]{:S(2)}, u32[]{:S(2)}) collective-permute-start(bf16[64,512]{1,0:T(8,128)(2,1)} %get-tuple-element.229), channel_id=1, source_target_pairs={{0,6},{1,7},{2,0},{3,1},{4,2},{5,3},{6,4},{7,5},{8,14},{9,15},{10,... | collective-permute-start | bytes 196616 | tf_op jit(solution)/shard_map/ppermute | solution.py:419
  71.5 9.9 %collective-permute-start.9 = (bf16[64,512]{1,0:T(8,128)(2,1)}, bf16[64,512]{1,0:T(8,128)(2,1)S(1)}, u32[]{:S(2)}, u32[]{:S(2)}) collective-permute-start(bf16[64,512]{1,0:T(8,128)(2,1)} %get-tuple-element.230), channel_id=1, source_target_pairs={{0,7},{1,0},{2,1},{3,2},{4,3},{5,4},{6,5},{7,6},{8,15},{9,8},{10,9... | collective-permute-start | bytes 196616 | tf_op jit(solution)/shard_map/ppermute | solution.py:419
  81.4 0.8 copy-start.2
  98.3 9.8 %all-to-all-start.3 = ((f32[8,1,128]{2,1,0:T(1,128)}), f32[8,1,128]{2,1,0:T(1,128)S(1)}, u32[]{:S(2)}, u32[]{:S(2)}) async-start(f32[8,1,128]{2,1,0:T(1,128)} %get-tuple-element.234), calls=%async_computation.3 | async-start | bytes 8192 | tf_op jit(solution)/shard_map/all_to_all | solution.py:494
  102.9 5.2 %copy-start.3 = (bf16[16,8,128]{2,1,0:T(8,128)(2,1)S(1)}, bf16[16,8,128]{2,1,0:T(8,128)(2,1)}, u32[]{:S(2)}) copy-start(bf16[16,8,128]{2,1,0:T(8,128)(2,1)} %get-tuple-element.237.fresh) | copy-start | bytes 98308
  109.5 15.2 %all-to-all-start.4 = ((bf16[32,3,8,128]{3,2,1,0:T(8,128)(2,1)}), bf16[32,3,8,128]{3,2,1,0:T(8,128)(2,1)S(1)}, u32[]{:S(2)}, u32[]{:S(2)}) async-start(bf16[32,3,8,128]{3,2,1,0:T(8,128)(2,1)} %get-tuple-element.239), calls=%async_computation.4 | async-start | bytes 393216 | tf_op jit(solution)/shard_map/all_to_all | solution.py:496
  (1 other events, 0.8 us)

commit v6 on v2

--- a/solution.py
+++ b/solution.py
@@ -13,6 +13,7 @@
 ROWS = STEPS * NP
 SPAN = 128
 TP = 8
+PAIRS = TP // 2
 DB = D // TP
 HEADS = DB // HD
 GROUP = HEADS * STEPS
@@ -172,7 +173,7 @@
             VM((TP, DB, DB), BF),
             pltpu.SemaphoreType.DMA((TP,)),
         ],
-        compiler_params=limit(55),
+        compiler_params=limit(50),
         cost_estimate=pl.CostEstimate(
             flops=2 * ROWS * D * 640, bytes_accessed=6 * 2**20, transcendentals=NP * 16 * 192
         ),
@@ -190,8 +191,10 @@
     summed = act[...].astype(F32) + mix
     aligned = jnp.sum(summed * twist[...], -1, keepdims=True)
     energy = jnp.sum(summed * summed, -1, keepdims=True)
+    row = lax.broadcasted_iota(jnp.int32, (ROWS, HD), 0)
     lane = lax.broadcasted_iota(jnp.int32, (ROWS, HD), 1)
-    sums[...] = jnp.where(lane == 0, aligned, energy)
+    both = jnp.where(lane == row, aligned, 0.0) + jnp.where(lane == row + ROWS, energy, 0.0)
+    sums[...] = jnp.sum(both, 0, keepdims=True)
 
 
 def mix(parts, act, twist):
@@ -200,33 +203,30 @@
         mix_body,
         in_specs=[spec(VM)] * (TP + 2),
         out_specs=[spec(VM)] * 2,
-        out_shape=[sd((ROWS, DB), BF), sd((ROWS, HD), F32)],
+        out_shape=[sd((ROWS, DB), BF), sd((1, HD), F32)],
         compiler_params=limit(8),
         name="mix",
     )(*parts, act, twist)
 
 
 def weigh_body(*refs):
-    parts = refs[:TP]
-    reward, previous, out = refs[TP:]
+    parts = refs[:PAIRS]
+    reward, previous, out = refs[PAIRS:]
     sums = parts[0][...]
-    for s in range(1, TP):
+    for s in range(1, PAIRS):
         sums = sums + parts[s][...]
-    score = sums[:, 0:1] / jnp.sqrt(sums[:, 1:2] / D + 1e-06) + reward[...]
-    gain = score[0:NP]
+    energy = pltpu.roll(sums, ROWS, 1)
+    score = sums / jnp.sqrt(energy / D + 1e-06) + reward[...]
+    gain = score
     for t in range(1, STEPS):
-        gain = gain + score[t * NP : (t + 1) * NP]
-    column = jnp.broadcast_to(previous[...] + gain, (NP, HD))
-    row = lax.broadcasted_iota(jnp.int32, (NP, HD), 0)
-    lane = lax.broadcasted_iota(jnp.int32, (NP, HD), 1)
-    line = jnp.sum(jnp.where(row == lane, column, 0.0), 0, keepdims=True)
-    out[...] = jnp.broadcast_to(line[None], (NDOM, 1, HD))
+        gain = gain + pltpu.roll(score, HD - NP * t, 1)
+    out[...] = jnp.broadcast_to((previous[...] + gain)[None], (NDOM, 1, HD))
 
 
 def weigh(parts, reward, previous):
     return pl.pallas_call(
         weigh_body,
-        in_specs=[spec(VM)] * (TP + 2),
+        in_specs=[spec(VM)] * (PAIRS + 2),
         out_specs=spec(VM),
         out_shape=jax.ShapeDtypeStruct((NDOM, 1, HD), F32),
         compiler_params=limit(8),
@@ -385,6 +385,10 @@
     return lax.ppermute(value, "tp", [(i, (i + shift) % TP) for i in range(TP)])
 
 
+def z_swapped(value):
+    return lax.ppermute(value, "tp", [(i, i ^ 1) for i in range(TP)])
+
+
 def swapped(value):
     return lax.ppermute(value, "dom", [(i, i ^ 1) for i in range(NDOM)])
 
@@ -450,10 +454,8 @@
     idx = plan(me, spread_counts(copy_counts))
     partner_keys = swapped(cache_keys)
     partner_values = swapped(cache_values)
-    reward = twisting_table[tokens.reshape(ROWS)].astype(F32).reshape(ROWS, 1)
-
-    gathered, idx, partner_keys, partner_values, reward = lax.optimization_barrier(
-        (gathered, idx, partner_keys, partner_values, reward)
+    gathered, idx, partner_keys, partner_values = lax.optimization_barrier(
+        (gathered, idx, partner_keys, partner_values)
     )
     qa, kf, vf, fresh = project(
         gathered, norm_gain.reshape(TP, DB), w_query, w_key, value_weight, rotation_table()
@@ -469,10 +471,15 @@
     rows = exchanged(packed)
     partials = attend(blk, qa, kf, vf, cache_keys, cache_values, w_output)
 
+    tokens, *partials = lax.optimization_barrier((tokens, *partials))
+    reward = twisting_table[tokens.reshape(ROWS)].astype(F32)
+    reward = jnp.pad(reward, (0, HD - ROWS)).reshape(1, HD)
+    previous = jnp.pad(previous_log_weights, (0, HD - NP)).reshape(1, HD)
     parts = [partials[0]] + [shifted(partials[s], s) for s in range(1, TP)]
     attn, sums = mix(parts, act, twist_vec.reshape(1, DB))
-    all_sums = [sums] + [shifted(sums, s) for s in range(1, TP)]
-    logw = weigh(all_sums, reward, previous_log_weights.reshape(NP, 1))
+    sums = sums + z_swapped(sums)
+    all_sums = [sums] + [shifted(sums, 2 * s) for s in range(1, PAIRS)]
+    logw = weigh(all_sums, reward, previous)
     logw, rows = lax.optimization_barrier((logw, rows))
     every = lax.all_to_all(logw, "dom", 0, 0, tiled=True)
     out_logw = finish(logw, every).reshape(NP)

time: 111 us -> 111 us (level)
  waiting for transfers between devices: 20.8 us -> 27.9 us
  starting transfers between devices: 61.6 us -> 57.4 us
    all_to_all x1, waiting for transfers between devices: 3.06 us -> 10 us  [exchanged(): lax.all_to_all(rows, 'dom', 0, 0, tiled=True, axis_index_groups=SAME_CORE)]
    ppermute x14 -> x10, starting transfers between devices: 27.1 us -> 20.4 us  [shifted(): return lax.ppermute(value, 'tp', [(i, (i + shift) % TP) for i in range(TP)])]
    ppermute x0 -> x1, starting transfers between devices: none -> 2.24 us  [z_swapped(): return lax.ppermute(value, 'tp', [(i, i ^ 1) for i in range(TP)])]
    ppermute x4, waiting for transfers between devices: 0.87 us -> 2.64 us  [swapped(): return lax.ppermute(value, 'dom', [(i, i ^ 1) for i in range(NDOM)])]
    ppermute x14 -> x10, waiting for transfers between devices: 10.8 us -> 9.4 us  [shifted(): return lax.ppermute(value, 'tp', [(i, (i + shift) % TP) for i in range(TP)])]
    ppermute x4, starting transfers between devices: 2.94 us -> 4.06 us  [swapped(): return lax.ppermute(value, 'dom', [(i, i ^ 1) for i in range(NDOM)])]
  transfers between devices with their start and end apart: 27 -> 24, of which waited for: 11 -> 14; matrix products, arithmetic and copies ran while one was open for 4% -> 3% of each run, Pallas kernels for 8% -> 7%
where the time goes in v6:
time: 111 us
  starting transfers between devices  57.4 us (52%)
  waiting for transfers between devices  27.9 us (25%)
  Pallas kernels  17.6 us (16%)
  local copies, waits for them, and re-layouts  6.47 us (6%)
  between operations  1.52 us (1%)
    ppermute x10, starting transfers between devices, shifted(): return lax.ppermute(value, 'tp', [(i, (i + shift) % TP) for i in range(TP)])  20.4 us
    all_to_all x1, waiting for transfers between devices, exchanged(): lax.all_to_all(rows, 'dom', 0, 0, tiled=True, axis_index_groups=SAME_CORE)  10 us
    ppermute x6, starting transfers between devices, moved(): return lax.ppermute(value, 'dom', [(i, to(i)) for i in range(NDOM)])  9.87 us
    ppermute x10, waiting for transfers between devices, shifted(): return lax.ppermute(value, 'tp', [(i, (i + shift) % TP) for i in range(TP)])  9.4 us
    all_to_all x1, starting transfers between devices, local(): lax.all_to_all(jnp.broadcast_to(act[None], (TP, ROWS, DB)), 'tp', 0, 0, t...  9.01 us
    all_to_all x1, starting transfers between devices, exchanged(): lax.all_to_all(rows, 'dom', 0, 0, tiled=True, axis_index_groups=SAME_CORE)  5.93 us
    all_to_all x1, starting transfers between devices, local(): every = lax.all_to_all(logw, 'dom', 0, 0, tiled=True)  5.91 us
    pallas_call x1, Pallas kernels, project(): pl.pallas_call(project_body, in_specs=[spec(VM)] * 2 + [spec(ANY)] * 3 +...  5.35 us
  transfers between devices with their start and end apart: 24, of which 14 were waited for; matrix products, arithmetic and copies ran while one was open for 3% of the time, Pallas kernels for 7%

profile of v6, /device:TPU:1, one launch (start us, length us, event | category | flops | bytes accessed | tf_op | source)
XLA Modules:
  0.0 110.9 jit_solution(13106495386259898965)
XLA Ops:
  0.7 1.8 %broadcast_in_dim.19 = bf16[8,64,512]{2,1,0:T(8,128)(2,1)} broadcast(bf16[64,512]{1,0:T(8,128)(2,1)} %bitcast.25), dimensions={1,2} | broadcast | bytes 589824 | tf_op jit(solution)/shard_map/broadcast_in_dim | solution.py:452
  2.5 9.0 %all-to-all-start = ((bf16[8,64,512]{2,1,0:T(8,128)(2,1)}), bf16[8,64,512]{2,1,0:T(8,128)(2,1)S(1)}, u32[]{:S(2)}, u32[]{:S(2)}) async-start(bf16[8,64,512]{2,1,0:T(8,128)(2,1)} %broadcast_in_dim.19), calls=%async_computation | async-start | bytes 1048576 | tf_op jit(solution)/shard_map/all_to_all | solution.py:451
  13.0 1.8 %collective-permute-done.1 = s32[1,16]{1,0:T(1,128)S(1)} collective-permute-done((s32[1,16]{1,0:T(1,128)S(1)}, s32[1,16]{1,0:T(1,128)S(1)}, u32[]{:S(2)}, u32[]{:S(2)}) %collective-permute-start.1) | collective-permute-done | bytes 96 | tf_op jit(solution)/shard_map/ppermute | solution.py:393
  16.0 2.5 %collective-permute-start.3 = (s32[2,16]{1,0:T(2,128)S(1)}, s32[2,16]{1,0:T(2,128)S(1)}, u32[]{:S(2)}, u32[]{:S(2)}) collective-permute-start(s32[2,16]{1,0:T(2,128)S(1)} %pad_add_fusion), channel_id=1, source_target_pairs={{0,32},{8,40},{16,48},{24,56},{32,0},{40,8},{48,16},{56,24},{64,96... | collective-permute-start | bytes 392 | tf_op jit(solution)/shard_map/ppermute | solution.py:412
  22.6 2.6 %collective-permute-start.6 = (s32[8,16]{1,0:T(8,128)S(1)}, s32[8,16]{1,0:T(8,128)S(1)}, u32[]{:S(2)}, u32[]{:S(2)}) collective-permute-start(s32[8,16]{1,0:T(8,128)S(1)} %concatenate.35.refs_0_), channel_id=1, source_target_pairs={{0,128},{8,136},{16,144},{24,152},{32,160},{40,168},{48,176},{56,1... | collective-permute-start | bytes 1544 | tf_op jit(solution)/shard_map/ppermute | solution.py:412
  30.2 5.3 %project.1 = (bf16[256,128]{1,0:T(8,128)(2,1)}, bf16[64,128]{1,0:T(8,128)(2,1)}, bf16[64,128]{1,0:T(8,128)(2,1)}, bf16[16,8,128]{2,1,0:T(8,128)(2,1)S(1)}) custom-call(bf16[8,64,512]{2,1,0:T(8,128)(2,1)} %copy-done.8, f32[8,512]{1,0:T(8,128)} %reshape.194.gain, bf16[4096,512]{1,0:T(8,128)(2,1)} %wq.1, bf16[4096,128]{1,0:T(8,128)(2,1)} %wk.1, ...), custom_call_target="tpu_custom_call" | custom-call | flops 402653184 | bytes 7340032 | tf_op jit(solution)/shard_map/project/pallas_call | solution.py:100
  35.6 2.5 %collective-permute-start.10 = (bf16[16,8,128]{2,1,0:T(8,128)(2,1)S(1)}, bf16[16,8,128]{2,1,0:T(8,128)(2,1)S(1)}, u32[]{:S(2)}, u32[]{:S(2)}) collective-permute-start(bf16[16,8,128]{2,1,0:T(8,128)(2,1)S(1)} %get-tuple-element.225.refs_2_), channel_id=1, source_target_pairs={{0,8},{8,0},{16,24},{24,16},{32,40},{40,32},{48,56},{56,48},{64,72... | collective-permute-start | bytes 98312 | tf_op jit(solution)/shard_map/ppermute | solution.py:393
  38.9 2.5 %pack.1 = bf16[16,3,264,128]{3,2,1,0:T(8,128)(2,1)} custom-call(s32[1]{0:T(128)} %bitcast.6.me_ref, s32[8,128]{1,0:T(8,128)S(1)} %plan.1.idx, bf16[16,128,128]{2,1,0:T(8,128)(2,1)S(1)} %copy-done.6, bf16[16,128,128]{2,1,0:T(8,128)(2,1)S(1)} %copy-done.7, bf16[16,8,128]{2,1,0:T(8,128)(2,1)S(1)} %get-tuple-element.225.refs_2_, ...), custom_call_target="tpu_custom_call" | custom-call | tf_op jit(solution)/shard_map/pack/pallas_call | solution.py:334
  41.5 5.9 %all-to-all-start.1 = ((bf16[16,3,264,128]{3,2,1,0:T(8,128)(2,1)}), bf16[16,3,264,128]{3,2,1,0:T(8,128)(2,1)}, u32[]{:S(2)}, u32[]{:S(2)}) async-start(bf16[16,3,264,128]{3,2,1,0:T(8,128)(2,1)} %pack.1), calls=%async_computation.1 | async-start | bytes 6488064 | tf_op jit(solution)/shard_map/all_to_all | solution.py:404
  47.5 4.1 %attend.1 = (bf16[64,512]{1,0:T(8,128)(2,1)S(1)}, bf16[64,512]{1,0:T(8,128)(2,1)S(1)}, bf16[64,512]{1,0:T(8,128)(2,1)S(1)}, bf16[64,512]{1,0:T(8,128)(2,1)S(1)},...) custom-call(s32[8]{0:T(128)S(1)} %and_select_fusion.blk, ...), custom_call_target="tpu_custom_call" | custom-call | flops 335544320 | bytes 6291456 | tf_op jit(solution)/shard_map/attend/pallas_call | solution.py:165
  53.4 2.1 %collective-permute-start.12 = (bf16[64,512]{1,0:T(8,128)(2,1)S(1)}, bf16[64,512]{1,0:T(8,128)(2,1)S(1)}, u32[]{:S(2)}, u32[]{:S(2)}) collective-permute-start(bf16[64,512]{1,0:T(8,128)(2,1)S(1)} %get-tuple-element.242), channel_id=1, source_target_pairs={{0,2},{1,3},{2,4},{3,5},{4,6},{5,7},{6,0},{7,1},{8,10},{9,11},{10,... | collective-permute-start | bytes 196616 | tf_op jit(solution)/shard_map/ppermute | solution.py:385
  55.5 2.4 %collective-permute-start.13 = (bf16[64,512]{1,0:T(8,128)(2,1)S(1)}, bf16[64,512]{1,0:T(8,128)(2,1)S(1)}, u32[]{:S(2)}, u32[]{:S(2)}) collective-permute-start(bf16[64,512]{1,0:T(8,128)(2,1)S(1)} %get-tuple-element.243), channel_id=1, source_target_pairs={{0,3},{1,4},{2,5},{3,6},{4,7},{5,0},{6,1},{7,2},{8,11},{9,12},{10,... | collective-permute-start | bytes 196616 | tf_op jit(solution)/shard_map/ppermute | solution.py:385
  57.9 2.0 %collective-permute-start.14 = (bf16[64,512]{1,0:T(8,128)(2,1)S(1)}, bf16[64,512]{1,0:T(8,128)(2,1)S(1)}, u32[]{:S(2)}, u32[]{:S(2)}) collective-permute-start(bf16[64,512]{1,0:T(8,128)(2,1)S(1)} %get-tuple-element.244), channel_id=1, source_target_pairs={{0,4},{1,5},{2,6},{3,7},{4,0},{5,1},{6,2},{7,3},{8,12},{9,13},{10,... | collective-permute-start | bytes 196616 | tf_op jit(solution)/shard_map/ppermute | solution.py:385
  59.9 2.4 %collective-permute-start.15 = (bf16[64,512]{1,0:T(8,128)(2,1)S(1)}, bf16[64,512]{1,0:T(8,128)(2,1)S(1)}, u32[]{:S(2)}, u32[]{:S(2)}) collective-permute-start(bf16[64,512]{1,0:T(8,128)(2,1)S(1)} %get-tuple-element.245), channel_id=1, source_target_pairs={{0,5},{1,6},{2,7},{3,0},{4,1},{5,2},{6,3},{7,4},{8,13},{9,14},{10,... | collective-permute-start | bytes 196616 | tf_op jit(solution)/shard_map/ppermute | solution.py:385
  62.5 3.3 %collective-permute-start.16 = (bf16[64,512]{1,0:T(8,128)(2,1)S(1)}, bf16[64,512]{1,0:T(8,128)(2,1)S(1)}, u32[]{:S(2)}, u32[]{:S(2)}) collective-permute-start(bf16[64,512]{1,0:T(8,128)(2,1)S(1)} %get-tuple-element.246), channel_id=1, source_target_pairs={{0,6},{1,7},{2,0},{3,1},{4,2},{5,3},{6,4},{7,5},{8,14},{9,15},{10,... | collective-permute-start | bytes 196616 | tf_op jit(solution)/shard_map/ppermute | solution.py:385
  66.9 2.1 %collective-permute-done.15.refs_5_ = bf16[64,512]{1,0:T(8,128)(2,1)S(1)} collective-permute-done((bf16[64,512]{1,0:T(8,128)(2,1)S(1)}, bf16[64,512]{1,0:T(8,128)(2,1)S(1)}, u32[]{:S(2)}, u32[]{:S(2)}) %collective-permute-start.15) | collective-permute-done | bytes 65568 | tf_op jit(solution)/shard_map/ppermute | solution.py:385
  69.0 4.6 %collective-permute-done.16.refs_6_ = bf16[64,512]{1,0:T(8,128)(2,1)S(1)} collective-permute-done((bf16[64,512]{1,0:T(8,128)(2,1)S(1)}, bf16[64,512]{1,0:T(8,128)(2,1)S(1)}, u32[]{:S(2)}, u32[]{:S(2)}) %collective-permute-start.16) | collective-permute-done | bytes 65568 | tf_op jit(solution)/shard_map/ppermute | solution.py:385
  74.5 2.2 %collective-permute-start.18 = (f32[1,128]{1,0:T(1,128)S(1)}, f32[1,128]{1,0:T(1,128)S(1)}, u32[]{:S(2)}, u32[]{:S(2)}) collective-permute-start(f32[1,128]{1,0:T(1,128)S(1)} %get-tuple-element.249), channel_id=1, source_target_pairs={{0,1},{1,0},{2,3},{3,2},{4,5},{5,4},{6,7},{7,6},{8,9},{9,8},{10,11... | collective-permute-start | bytes 1544 | tf_op jit(solution)/shard_map/ppermute | solution.py:389
  78.4 3.7 %collective-permute-start.20 = (f32[1,128]{1,0:T(1,128)S(1)}, f32[1,128]{1,0:T(1,128)S(1)}, u32[]{:S(2)}, u32[]{:S(2)}) collective-permute-start(f32[1,128]{1,0:T(1,128)S(1)} %add.107.refs_0_), channel_id=1, source_target_pairs={{0,4},{1,5},{2,6},{3,7},{4,0},{5,1},{6,2},{7,3},{8,12},{9,13},{10,... | collective-permute-start | bytes 1544 | tf_op jit(solution)/shard_map/ppermute | solution.py:385
  86.6 10.0 %all-to-all-done.1 = bf16[16,3,264,128]{3,2,1,0:T(8,128)(2,1)} async-done(((bf16[16,3,264,128]{3,2,1,0:T(8,128)(2,1)}), bf16[16,3,264,128]{3,2,1,0:T(8,128)(2,1)}, u32[]{:S(2)}, u32[]{:S(2)}) %all-to-all-start.1) | async-done | bytes 3244064 | tf_op jit(solution)/shard_map/all_to_all | solution.py:404
  96.6 5.9 %all-to-all-start.2 = ((f32[32,1,128]{2,1,0:T(1,128)}), f32[32,1,128]{2,1,0:T(1,128)S(1)}, u32[]{:S(2)}, u32[]{:S(2)}) async-start(f32[32,1,128]{2,1,0:T(1,128)} %weigh.1.mine), calls=%async_computation.2 | async-start | bytes 32768 | tf_op jit(solution)/shard_map/all_to_all | solution.py:484
  103.7 3.8 %conditional.1 = (bf16[16,132,128]{2,0,1:T(8,128)(2,1)}, bf16[16,132,128]{2,0,1:T(8,128)(2,1)}) conditional(s32[]{:T(128)} %bitcast.11, (s32[8,128]{1,0:T(8,128)S(1)}, bf16[16,3,264,128]{3,2,1,0:T(8,128)(2,1)}) %tuple.56, (s32[]{:T(128)}, bf16[16,128,128]{2,1,0:T(8,128)(2,1)S(1)}, bf16[16,128,128]{2,1,0:T(8,128)(2,1)S(1)}, ...), branch_computations={%region_0.1_spmd, %region_1.6_spmd} | conditional | flops 4394106 | bytes 39339144 | solution.py:509
  103.7 2.1 %place.2 = (bf16[16,132,128]{2,1,0:T(8,128)(2,1)S(1)}, bf16[16,132,128]{2,1,0:T(8,128)(2,1)S(1)}) custom-call(s32[8,128]{1,0:T(8,128)S(1)} %get-tuple-element.168.refs_0_, bf16[16,3,264,128]{3,2,1,0:T(8,128)(2,1)} %get-tuple-element.169.refs_1_), custom_call_target="tpu_custom_call" | custom-call | tf_op jit(solution)/shard_map/cond/branch_0_fun/place/pallas_call | solution.py:370
  107.6 1.9 %all-to-all-done.2.every = f32[32,1,128]{2,1,0:T(1,128)S(1)} async-done(((f32[32,1,128]{2,1,0:T(1,128)}), f32[32,1,128]{2,1,0:T(1,128)S(1)}, u32[]{:S(2)}, u32[]{:S(2)}) %all-to-all-start.2) | async-done | bytes 16416 | tf_op jit(solution)/shard_map/all_to_all | solution.py:484
  (74 shorter events, 26.6 us)
Async XLA Ops:
  2.5 27.0 %all-to-all-start = ((bf16[8,64,512]{2,1,0:T(8,128)(2,1)}), bf16[8,64,512]{2,1,0:T(8,128)(2,1)S(1)}, u32[]{:S(2)}, u32[]{:S(2)}) async-start(bf16[8,64,512]{2,1,0:T(8,128)(2,1)} %broadcast_in_dim.19), calls=%async_computation | async-start | bytes 1048576 | tf_op jit(solution)/shard_map/all_to_all | solution.py:451
  11.5 17.1 %collective-permute-start.8 = (bf16[16,128,128]{2,1,0:T(8,128)(2,1)S(1)}, bf16[16,128,128]{2,1,0:T(8,128)(2,1)S(1)}, u32[]{:S(2)}, u32[]{:S(2)}) collective-permute-start(bf16[16,128,128]{2,1,0:T(8,128)(2,1)S(1)} %copy-done.6), channel_id=1, source_target_pairs={{0,8},{8,0},{16,24},{24,16},{32,40},{40,32},{48,56},{56,48},{64,72... | collective-permute-start | bytes 1572872 | tf_op jit(solution)/shard_map/ppermute | solution.py:393
  12.5 16.0 %collective-permute-start.9 = (bf16[16,128,128]{2,1,0:T(8,128)(2,1)S(1)}, bf16[16,128,128]{2,1,0:T(8,128)(2,1)S(1)}, u32[]{:S(2)}, u32[]{:S(2)}) collective-permute-start(bf16[16,128,128]{2,1,0:T(8,128)(2,1)S(1)} %copy-done.7), channel_id=1, source_target_pairs={{0,8},{8,0},{16,24},{24,16},{32,40},{40,32},{48,56},{56,48},{64,72... | collective-permute-start | bytes 1572872 | tf_op jit(solution)/shard_map/ppermute | solution.py:393
  12.6 2.2 %collective-permute-start.1 = (s32[1,16]{1,0:T(1,128)S(1)}, s32[1,16]{1,0:T(1,128)S(1)}, u32[]{:S(2)}, u32[]{:S(2)}) collective-permute-start(s32[1,16]{1,0:T(1,128)S(1)} %bitcast.29), channel_id=1, source_target_pairs={{0,8},{8,0},{16,24},{24,16},{32,40},{40,32},{48,56},{56,48},{64,72... | collective-permute-start | bytes 200 | tf_op jit(solution)/shard_map/ppermute | solution.py:393
  14.8 4.8 %collective-permute-start.2 = (s32[2,16]{1,0:T(2,128)S(1)}, s32[2,16]{1,0:T(2,128)S(1)}, u32[]{:S(2)}, u32[]{:S(2)}) collective-permute-start(s32[2,16]{1,0:T(2,128)S(1)} %pad_add_fusion), channel_id=1, source_target_pairs={{0,16},{8,24},{16,32},{24,40},{32,48},{40,56},{48,0},{56,8},{64,80... | collective-permute-start | bytes 392 | tf_op jit(solution)/shard_map/ppermute | solution.py:412
  16.0 4.2 %collective-permute-start.3 = (s32[2,16]{1,0:T(2,128)S(1)}, s32[2,16]{1,0:T(2,128)S(1)}, u32[]{:S(2)}, u32[]{:S(2)}) collective-permute-start(s32[2,16]{1,0:T(2,128)S(1)} %pad_add_fusion), channel_id=1, source_target_pairs={{0,32},{8,40},{16,48},{24,56},{32,0},{40,8},{48,16},{56,24},{64,96... | collective-permute-start | bytes 392 | tf_op jit(solution)/shard_map/ppermute | solution.py:412
  18.5 2.7 %collective-permute-start.4 = (s32[2,16]{1,0:T(2,128)S(1)}, s32[2,16]{1,0:T(2,128)S(1)}, u32[]{:S(2)}, u32[]{:S(2)}) collective-permute-start(s32[2,16]{1,0:T(2,128)S(1)} %pad_add_fusion), channel_id=1, source_target_pairs={{0,48},{8,56},{16,0},{24,8},{32,16},{40,24},{48,32},{56,40},{64,11... | collective-permute-start | bytes 392 | tf_op jit(solution)/shard_map/ppermute | solution.py:412
  21.2 5.7 %collective-permute-start.5 = (s32[8,16]{1,0:T(8,128)S(1)}, s32[8,16]{1,0:T(8,128)S(1)}, u32[]{:S(2)}, u32[]{:S(2)}) collective-permute-start(s32[8,16]{1,0:T(8,128)S(1)} %concatenate.35.refs_0_), channel_id=1, source_target_pairs={{0,64},{8,72},{16,80},{24,88},{32,96},{40,104},{48,112},{56,120},{... | collective-permute-start | bytes 1544 | tf_op jit(solution)/shard_map/ppermute | solution.py:412
  22.6 4.3 %collective-permute-start.6 = (s32[8,16]{1,0:T(8,128)S(1)}, s32[8,16]{1,0:T(8,128)S(1)}, u32[]{:S(2)}, u32[]{:S(2)}) collective-permute-start(s32[8,16]{1,0:T(8,128)S(1)} %concatenate.35.refs_0_), channel_id=1, source_target_pairs={{0,128},{8,136},{16,144},{24,152},{32,160},{40,168},{48,176},{56,1... | collective-permute-start | bytes 1544 | tf_op jit(solution)/shard_map/ppermute | solution.py:412
  25.2 2.8 %collective-permute-start.7 = (s32[8,16]{1,0:T(8,128)S(1)}, s32[8,16]{1,0:T(8,128)S(1)}, u32[]{:S(2)}, u32[]{:S(2)}) collective-permute-start(s32[8,16]{1,0:T(8,128)S(1)} %concatenate.35.refs_0_), channel_id=1, source_target_pairs={{0,192},{8,200},{16,208},{24,216},{32,224},{40,232},{48,240},{56,2... | collective-permute-start | bytes 1544 | tf_op jit(solution)/shard_map/ppermute | solution.py:412
  35.6 3.4 %collective-permute-start.10 = (bf16[16,8,128]{2,1,0:T(8,128)(2,1)S(1)}, bf16[16,8,128]{2,1,0:T(8,128)(2,1)S(1)}, u32[]{:S(2)}, u32[]{:S(2)}) collective-permute-start(bf16[16,8,128]{2,1,0:T(8,128)(2,1)S(1)} %get-tuple-element.225.refs_2_), channel_id=1, source_target_pairs={{0,8},{8,0},{16,24},{24,16},{32,40},{40,32},{48,56},{56,48},{64,72... | collective-permute-start | bytes 98312 | tf_op jit(solution)/shard_map/ppermute | solution.py:393
  41.5 55.1 %all-to-all-start.1 = ((bf16[16,3,264,128]{3,2,1,0:T(8,128)(2,1)}), bf16[16,3,264,128]{3,2,1,0:T(8,128)(2,1)}, u32[]{:S(2)}, u32[]{:S(2)}) async-start(bf16[16,3,264,128]{3,2,1,0:T(8,128)(2,1)} %pack.1), calls=%async_computation.1 | async-start | bytes 6488064 | tf_op jit(solution)/shard_map/all_to_all | solution.py:404
  51.7 10.8 %collective-permute-start.11 = (bf16[64,512]{1,0:T(8,128)(2,1)S(1)}, bf16[64,512]{1,0:T(8,128)(2,1)S(1)}, u32[]{:S(2)}, u32[]{:S(2)}) collective-permute-start(bf16[64,512]{1,0:T(8,128)(2,1)S(1)} %get-tuple-element.241), channel_id=1, source_target_pairs={{0,1},{1,2},{2,3},{3,4},{4,5},{5,6},{6,7},{7,0},{8,9},{9,10},{10,1... | collective-permute-start | bytes 196616 | tf_op jit(solution)/shard_map/ppermute | solution.py:385
  53.4 12.4 %collective-permute-start.12 = (bf16[64,512]{1,0:T(8,128)(2,1)S(1)}, bf16[64,512]{1,0:T(8,128)(2,1)S(1)}, u32[]{:S(2)}, u32[]{:S(2)}) collective-permute-start(bf16[64,512]{1,0:T(8,128)(2,1)S(1)} %get-tuple-element.242), channel_id=1, source_target_pairs={{0,2},{1,3},{2,4},{3,5},{4,6},{5,7},{6,0},{7,1},{8,10},{9,11},{10,... | collective-permute-start | bytes 196616 | tf_op jit(solution)/shard_map/ppermute | solution.py:385
  55.5 11.5 %collective-permute-start.13 = (bf16[64,512]{1,0:T(8,128)(2,1)S(1)}, bf16[64,512]{1,0:T(8,128)(2,1)S(1)}, u32[]{:S(2)}, u32[]{:S(2)}) collective-permute-start(bf16[64,512]{1,0:T(8,128)(2,1)S(1)} %get-tuple-element.243), channel_id=1, source_target_pairs={{0,3},{1,4},{2,5},{3,6},{4,7},{5,0},{6,1},{7,2},{8,11},{9,12},{10,... | collective-permute-start | bytes 196616 | tf_op jit(solution)/shard_map/ppermute | solution.py:385
  57.9 9.0 %collective-permute-start.14 = (bf16[64,512]{1,0:T(8,128)(2,1)S(1)}, bf16[64,512]{1,0:T(8,128)(2,1)S(1)}, u32[]{:S(2)}, u32[]{:S(2)}) collective-permute-start(bf16[64,512]{1,0:T(8,128)(2,1)S(1)} %get-tuple-element.244), channel_id=1, source_target_pairs={{0,4},{1,5},{2,6},{3,7},{4,0},{5,1},{6,2},{7,3},{8,12},{9,13},{10,... | collective-permute-start | bytes 196616 | tf_op jit(solution)/shard_map/ppermute | solution.py:385
  59.9 9.1 %collective-permute-start.15 = (bf16[64,512]{1,0:T(8,128)(2,1)S(1)}, bf16[64,512]{1,0:T(8,128)(2,1)S(1)}, u32[]{:S(2)}, u32[]{:S(2)}) collective-permute-start(bf16[64,512]{1,0:T(8,128)(2,1)S(1)} %get-tuple-element.245), channel_id=1, source_target_pairs={{0,5},{1,6},{2,7},{3,0},{4,1},{5,2},{6,3},{7,4},{8,13},{9,14},{10,... | collective-permute-start | bytes 196616 | tf_op jit(solution)/shard_map/ppermute | solution.py:385
  62.5 11.2 %collective-permute-start.16 = (bf16[64,512]{1,0:T(8,128)(2,1)S(1)}, bf16[64,512]{1,0:T(8,128)(2,1)S(1)}, u32[]{:S(2)}, u32[]{:S(2)}) collective-permute-start(bf16[64,512]{1,0:T(8,128)(2,1)S(1)} %get-tuple-element.246), channel_id=1, source_target_pairs={{0,6},{1,7},{2,0},{3,1},{4,2},{5,3},{6,4},{7,5},{8,14},{9,15},{10,... | collective-permute-start | bytes 196616 | tf_op jit(solution)/shard_map/ppermute | solution.py:385
  65.7 8.0 %collective-permute-start.17 = (bf16[64,512]{1,0:T(8,128)(2,1)S(1)}, bf16[64,512]{1,0:T(8,128)(2,1)S(1)}, u32[]{:S(2)}, u32[]{:S(2)}) collective-permute-start(bf16[64,512]{1,0:T(8,128)(2,1)S(1)} %get-tuple-element.247), channel_id=1, source_target_pairs={{0,7},{1,0},{2,1},{3,2},{4,3},{5,4},{6,5},{7,6},{8,15},{9,8},{10,9... | collective-permute-start | bytes 196616 | tf_op jit(solution)/shard_map/ppermute | solution.py:385
  74.5 3.6 %collective-permute-start.18 = (f32[1,128]{1,0:T(1,128)S(1)}, f32[1,128]{1,0:T(1,128)S(1)}, u32[]{:S(2)}, u32[]{:S(2)}) collective-permute-start(f32[1,128]{1,0:T(1,128)S(1)} %get-tuple-element.249), channel_id=1, source_target_pairs={{0,1},{1,0},{2,3},{3,2},{4,5},{5,4},{6,7},{7,6},{8,9},{9,8},{10,11... | collective-permute-start | bytes 1544 | tf_op jit(solution)/shard_map/ppermute | solution.py:389
  78.1 5.2 %collective-permute-start.19 = (f32[1,128]{1,0:T(1,128)S(1)}, f32[1,128]{1,0:T(1,128)S(1)}, u32[]{:S(2)}, u32[]{:S(2)}) collective-permute-start(f32[1,128]{1,0:T(1,128)S(1)} %add.107.refs_0_), channel_id=1, source_target_pairs={{0,2},{1,3},{2,4},{3,5},{4,6},{5,7},{6,0},{7,1},{8,10},{9,11},{10,... | collective-permute-start | bytes 1544 | tf_op jit(solution)/shard_map/ppermute | solution.py:385
  78.4 6.3 %collective-permute-start.20 = (f32[1,128]{1,0:T(1,128)S(1)}, f32[1,128]{1,0:T(1,128)S(1)}, u32[]{:S(2)}, u32[]{:S(2)}) collective-permute-start(f32[1,128]{1,0:T(1,128)S(1)} %add.107.refs_0_), channel_id=1, source_target_pairs={{0,4},{1,5},{2,6},{3,7},{4,0},{5,1},{6,2},{7,3},{8,12},{9,13},{10,... | collective-permute-start | bytes 1544 | tf_op jit(solution)/shard_map/ppermute | solution.py:385
  82.1 3.7 %collective-permute-start.21 = (f32[1,128]{1,0:T(1,128)S(1)}, f32[1,128]{1,0:T(1,128)S(1)}, u32[]{:S(2)}, u32[]{:S(2)}) collective-permute-start(f32[1,128]{1,0:T(1,128)S(1)} %add.107.refs_0_), channel_id=1, source_target_pairs={{0,6},{1,7},{2,0},{3,1},{4,2},{5,3},{6,4},{7,5},{8,14},{9,15},{10,... | collective-permute-start | bytes 1544 | tf_op jit(solution)/shard_map/ppermute | solution.py:385
  96.6 12.8 %all-to-all-start.2 = ((f32[32,1,128]{2,1,0:T(1,128)}), f32[32,1,128]{2,1,0:T(1,128)S(1)}, u32[]{:S(2)}, u32[]{:S(2)}) async-start(f32[32,1,128]{2,1,0:T(1,128)} %weigh.1.mine), calls=%async_computation.2 | async-start | bytes 32768 | tf_op jit(solution)/shard_map/all_to_all | solution.py:484
  (13 other events, 230.5 us)

commit v7 on v5

--- a/solution.py
+++ b/solution.py
@@ -13,6 +13,7 @@
 ROWS = STEPS * NP
 SPAN = 128
 TP = 8
+PAIRS = TP // 2
 DB = D // TP
 HEADS = DB // HD
 GROUP = HEADS * STEPS
@@ -115,7 +116,7 @@
             VM((ROWS, HD), F32),
             pltpu.SemaphoreType.DMA((3, TP)),
         ],
-        compiler_params=limit(55),
+        compiler_params=limit(53),
         cost_estimate=pl.CostEstimate(
             flops=2 * ROWS * D * 768, bytes_accessed=7 * 2**20, transcendentals=0
         ),
@@ -172,7 +173,7 @@
             VM((TP, DB, DB), BF),
             pltpu.SemaphoreType.DMA((TP,)),
         ],
-        compiler_params=limit(55),
+        compiler_params=limit(53),
         cost_estimate=pl.CostEstimate(
             flops=2 * ROWS * D * 640, bytes_accessed=6 * 2**20, transcendentals=NP * 16 * 192
         ),
@@ -193,7 +194,7 @@
     row = lax.broadcasted_iota(jnp.int32, (ROWS, HD), 0)
     lane = lax.broadcasted_iota(jnp.int32, (ROWS, HD), 1)
     both = jnp.where(lane == row, aligned, 0.0) + jnp.where(lane == row + ROWS, energy, 0.0)
-    sums[...] = jnp.broadcast_to(jnp.sum(both, 0, keepdims=True)[None], (TP, 1, HD))
+    sums[...] = jnp.sum(both, 0, keepdims=True)
 
 
 def mix(parts, act, twist):
@@ -202,16 +203,18 @@
         mix_body,
         in_specs=[spec(VM)] * (TP + 2),
         out_specs=[spec(VM)] * 2,
-        out_shape=[sd((ROWS, DB), BF), sd((TP, 1, HD), F32)],
+        out_shape=[sd((ROWS, DB), BF), sd((1, HD), F32)],
         compiler_params=limit(8),
         name="mix",
     )(*parts, act, twist)
 
 
-def weigh_body(idx, sums, reward, previous, fresh, line, sent):
-    total = sums[0]
-    for t in range(1, TP):
-        total = total + sums[t]
+def weigh_body(idx, *refs):
+    parts = refs[:PAIRS]
+    reward, previous, fresh, line, sent = refs[PAIRS:]
+    total = parts[0][...]
+    for s in range(1, PAIRS):
+        total = total + parts[s][...]
     energy = pltpu.roll(total, ROWS, 1)
     score = total / jnp.sqrt(energy / D + 1e-06) + reward[...]
     gain = score
@@ -231,16 +234,16 @@
         sent[d, 2] = parts
 
 
-def weigh(idx, sums, reward, previous, fresh):
+def weigh(idx, parts, reward, previous, fresh):
     sd = jax.ShapeDtypeStruct
     return pl.pallas_call(
         weigh_body,
-        in_specs=[spec(SM)] + [spec(VM)] * 4,
+        in_specs=[spec(SM)] + [spec(VM)] * (PAIRS + 3),
         out_specs=[spec(VM)] * 2,
         out_shape=[sd((1, HD), F32), sd((NDOM, 3, 8, HD), BF)],
         compiler_params=limit(8),
         name="weigh",
-    )(idx, sums, reward, previous, fresh)
+    )(idx, *parts, reward, previous, fresh)
 
 
 def finish_body(idx, line, got, keys_in, values_in, logw, keys, values, all_s, f_s, k_s, v_s, sems):
@@ -288,9 +291,16 @@
     )(idx, line, got, keys, values)
 
 
-def plan_body(me_ref, counts_ref, out):
+def plan_body(me_ref, *refs):
+    out = refs[-1]
     me = me_ref[0]
-    counts = counts_ref[:, 0, :].astype(F32)
+    blocks = jnp.concatenate([r[...] for r in refs[:-1]], 0).astype(F32)
+    rel = lax.broadcasted_iota(jnp.int32, (NDOM, NDOM), 1)
+    back_y = (me // 8 - rel // 8) & 3
+    back_x = (me // 2 - rel // 2) & 3
+    holder = 8 * back_y + 2 * back_x + ((me + rel) & 1)
+    sorted_rows = lax.broadcasted_iota(jnp.int32, (NDOM, NDOM), 0) == holder
+    counts = mm(sorted_rows.astype(F32), blocks)
     r16 = lax.broadcasted_iota(jnp.int32, (NP, NP), 0)
     c16 = lax.broadcasted_iota(jnp.int32, (NP, NP), 1)
     within = mm(counts, (r16 <= c16).astype(F32))
@@ -339,15 +349,15 @@
     out[...] = jnp.where(row == 0, line, second)
 
 
-def plan(me, counts):
+def plan(me, blocks):
     return pl.pallas_call(
         plan_body,
-        in_specs=[spec(SM), spec(VM)],
+        in_specs=[spec(SM)] + [spec(VM)] * len(blocks),
         out_specs=spec(VM),
         out_shape=jax.ShapeDtypeStruct((8, HD), jnp.int32),
         compiler_params=limit(8),
         name="plan",
-    )(me, counts)
+    )(me, *blocks)
 
 
 def pack_body(me_ref, idx, *refs):
@@ -419,6 +429,10 @@
     return lax.ppermute(value, "tp", [(i, (i + shift) % TP) for i in range(TP)])
 
 
+def z_swapped(value):
+    return lax.ppermute(value, "tp", [(i, i ^ 1) for i in range(TP)])
+
+
 def swapped(value):
     return lax.ppermute(value, "dom", [(i, i ^ 1) for i in range(NDOM)])
 
@@ -434,9 +448,19 @@
     return lax.all_to_all(rows, "dom", 0, 0, tiled=True, axis_index_groups=SAME_CORE)
 
 
-def counts_of_all(counts):
-    sent = jnp.broadcast_to(counts[None, None], (NDOM, 1, NP))
-    return lax.all_to_all(sent, "dom", 0, 0, tiled=True)
+def moved(value, axis_stride, shift):
+    def to(i):
+        at = i // axis_stride % 4
+        return i + ((at + shift) % 4 - at) * axis_stride
+
+    return lax.ppermute(value, "dom", [(i, to(i)) for i in range(NDOM)])
+
+
+def spread_counts(copy_counts):
+    own = copy_counts.reshape(1, NP)
+    chip = jnp.concatenate([own, swapped(own)], 0)
+    row = jnp.concatenate([chip] + [moved(chip, 2, s) for s in range(1, 4)], 0)
+    return [row] + [moved(row, 8, s) for s in range(1, 4)]
 
 
 def rotation_table():
@@ -467,32 +491,31 @@
     me = dom.reshape(1)
     blk = ((tp + np.arange(TP)) % TP).astype(jnp.int32)
     act = activations.reshape(ROWS, DB)
-    reward = twisting_table[tokens.reshape(ROWS)].astype(F32)
-    reward = jnp.pad(reward, (0, HD - ROWS)).reshape(1, HD)
-    previous = jnp.pad(previous_log_weights, (0, HD - NP)).reshape(1, HD)
+
+    gathered = lax.all_to_all(
+        jnp.broadcast_to(act[None], (TP, ROWS, DB)), "tp", 0, 0, tiled=True
+    )
+    idx = plan(me, spread_counts(copy_counts))
     partner_keys = swapped(cache_keys)
     partner_values = swapped(cache_values)
-
-    counts = counts_of_all(copy_counts)
-    sent = jnp.broadcast_to(act[None], (TP, ROWS, DB))
-    sent, counts, partner_keys, partner_values, reward, previous = lax.optimization_barrier(
-        (sent, counts, partner_keys, partner_values, reward, previous)
-    )
-    gathered = lax.all_to_all(sent, "tp", 0, 0, tiled=True)
-    idx = plan(me, counts)
     packed = pack(me, idx, [cache_keys, cache_values], [partner_keys, partner_values])
+    rows = exchanged(packed)
+
     packed, gathered = lax.optimization_barrier((packed, gathered))
-    rows = exchanged(packed)
-
     qa, kf, vf, fresh = project(
         gathered, norm_gain.reshape(TP, DB), w_query, w_key, value_weight, rotation_table()
     )
     partials = attend(blk, qa, kf, vf, cache_keys, cache_values, w_output)
+    tokens, *partials = lax.optimization_barrier((tokens, *partials))
+    reward = twisting_table[tokens.reshape(ROWS)].astype(F32)
+    reward = jnp.pad(reward, (0, HD - ROWS)).reshape(1, HD)
+    previous = jnp.pad(previous_log_weights, (0, HD - NP)).reshape(1, HD)
     parts = [partials[0]] + [shifted(partials[s], s) for s in range(1, TP)]
     attn, sums = mix(parts, act, twist_vec.reshape(1, DB))
-    sums, rows = lax.optimization_barrier((sums, rows))
-    sums = lax.all_to_all(sums, "tp", 0, 0, tiled=True)
-    line, sent = weigh(idx, sums, reward, previous, fresh)
+    sums = sums + z_swapped(sums)
+    all_sums = [sums] + [shifted(sums, 2 * s) for s in range(1, PAIRS)]
+    line, sent = weigh(idx, all_sums, reward, previous, fresh)
+    sent, rows = lax.optimization_barrier((sent, rows))
     got = lax.all_to_all(sent, "dom", 0, 0, tiled=True)
 
     def usual(rows, *_):

time: 128 us -> 106 us (0.83)
  waiting for transfers between devices: 49.7 us -> 15.1 us
  starting transfers between devices: 41 us -> 61 us
  local copies, waits for them, and re-layouts: 11.8 us -> 7.59 us
  Pallas kernels: 22.1 us -> 19.2 us
    all_to_all x3 -> x1, waiting for transfers between devices: 20.1 us -> 0.01 us  [local(): lax.all_to_all(jnp.broadcast_to(act[None], (TP, ROWS, DB)), 'tp', 0, 0, t...]
    all_to_all x1, waiting for transfers between devices: 15.3 us -> 0.01 us  [exchanged(): lax.all_to_all(rows, 'dom', 0, 0, tiled=True, axis_index_groups=SAME_CORE)]
    ppermute x0 -> x7, starting transfers between devices: none -> 11.2 us  [the longest x6 9.87 us: moved(): return lax.ppermute(value, 'dom', [(i, to(i)) for i in range(NDOM)])]
    ppermute x7 -> x10, starting transfers between devices: 9.58 us -> 20.4 us  [shifted(): return lax.ppermute(value, 'tp', [(i, (i + shift) % TP) for i in range(TP)])]
    all_to_all x3 -> x1, starting transfers between devices: 17.3 us -> 9.01 us  [local(): lax.all_to_all(jnp.broadcast_to(act[None], (TP, ROWS, DB)), 'tp', 0, 0, t...]
    all_to_all x1, starting transfers between devices: 6.95 us -> 13.2 us  [local(): got = lax.all_to_all(sent, 'dom', 0, 0, tiled=True)]
    ppermute x0 -> x7, waiting for transfers between devices: none -> 3.87 us  [the longest x6 3.24 us: moved(): return lax.ppermute(value, 'dom', [(i, to(i)) for i in range(NDOM)])]
    all_to_all x1, waiting for transfers between devices: 4.6 us -> 1.53 us  [local(): got = lax.all_to_all(sent, 'dom', 0, 0, tiled=True)]
  transfers between devices with their start and end apart: 14 -> 23, of which waited for: 9 -> 11; matrix products, arithmetic and copies ran while one was open for 7% -> 6% of each run, Pallas kernels for 15% -> 16%
where the time goes in v7:
time: 106 us; the launch traced here: 105 us
  starting transfers between devices  61 us (58%)
  Pallas kernels  19.2 us (18%)
  waiting for transfers between devices  15.1 us (14%)
  local copies, waits for them, and re-layouts  7.59 us (7%)
  between operations  1.7 us (2%)
    ppermute x10, starting transfers between devices, shifted(): return lax.ppermute(value, 'tp', [(i, (i + shift) % TP) for i in range(TP)])  20.4 us
    all_to_all x1, starting transfers between devices, local(): got = lax.all_to_all(sent, 'dom', 0, 0, tiled=True)  13.2 us
    ppermute x6, starting transfers between devices, moved(): return lax.ppermute(value, 'dom', [(i, to(i)) for i in range(NDOM)])  9.87 us
    all_to_all x1, starting transfers between devices, local(): lax.all_to_all(jnp.broadcast_to(act[None], (TP, ROWS, DB)), 'tp', 0, 0, t...  9.01 us
    ppermute x10, waiting for transfers between devices, shifted(): return lax.ppermute(value, 'tp', [(i, (i + shift) % TP) for i in range(TP)])  7.68 us
    all_to_all x1, starting transfers between devices, exchanged(): lax.all_to_all(rows, 'dom', 0, 0, tiled=True, axis_index_groups=SAME_CORE)  5.8 us
    pallas_call x1, Pallas kernels, attend(): pl.pallas_call(attend_body, in_specs=[spec(SM)] + [spec(VM)] * 5 + [spec(...  4.1 us
    pallas_call x1, Pallas kernels, project(): pl.pallas_call(project_body, in_specs=[spec(VM)] * 2 + [spec(ANY)] * 3 +...  3.76 us
  transfers between devices with their start and end apart: 23, of which 11 were waited for; matrix products, arithmetic and copies ran while one was open for 6% of the time, Pallas kernels for 16%

profile of v7, /device:TPU:1, one launch (start us, length us, event | category | flops | bytes accessed | tf_op | source)
XLA Modules:
  0.0 105.4 jit_solution(12304996284617728142)
XLA Ops:
  0.6 1.7 %broadcast_in_dim.19 = bf16[8,64,512]{2,1,0:T(8,128)(2,1)} broadcast(bf16[64,512]{1,0:T(8,128)(2,1)} %bitcast.31), dimensions={1,2} | broadcast | bytes 589824 | tf_op jit(solution)/shard_map/broadcast_in_dim | solution.py:496
  2.4 9.0 %all-to-all-start = ((bf16[8,64,512]{2,1,0:T(8,128)(2,1)}), bf16[8,64,512]{2,1,0:T(8,128)(2,1)S(1)}, u32[]{:S(2)}, u32[]{:S(2)}) async-start(bf16[8,64,512]{2,1,0:T(8,128)(2,1)} %broadcast_in_dim.19), calls=%async_computation | async-start | bytes 1048576 | tf_op jit(solution)/shard_map/all_to_all | solution.py:495
  12.8 2.0 %collective-permute-done.1 = s32[1,16]{1,0:T(1,128)S(1)} collective-permute-done((s32[1,16]{1,0:T(1,128)}, s32[1,16]{1,0:T(1,128)S(1)}, u32[]{:S(2)}, u32[]{:S(2)}) %collective-permute-start.1) | collective-permute-done | bytes 96 | tf_op jit(solution)/shard_map/ppermute | solution.py:437
  16.7 2.5 %collective-permute-start.3 = (s32[2,16]{1,0:T(2,128)S(1)}, s32[2,16]{1,0:T(2,128)S(1)}, u32[]{:S(2)}, u32[]{:S(2)}) collective-permute-start(s32[2,16]{1,0:T(2,128)S(1)} %pad_add_fusion), channel_id=1, source_target_pairs={{0,32},{8,40},{16,48},{24,56},{32,0},{40,8},{48,16},{56,24},{64,96... | collective-permute-start | bytes 392 | tf_op jit(solution)/shard_map/ppermute | solution.py:456
  23.9 2.6 %collective-permute-start.6 = (s32[8,16]{1,0:T(8,128)S(1)}, s32[8,16]{1,0:T(8,128)S(1)}, u32[]{:S(2)}, u32[]{:S(2)}) collective-permute-start(s32[8,16]{1,0:T(8,128)S(1)} %concatenate.35.refs_0_), channel_id=1, source_target_pairs={{0,128},{8,136},{16,144},{24,152},{32,160},{40,168},{48,176},{56,1... | collective-permute-start | bytes 1544 | tf_op jit(solution)/shard_map/ppermute | solution.py:456
  29.9 3.6 %pack.1 = bf16[16,3,256,128]{3,2,1,0:T(8,128)(2,1)} custom-call(s32[1]{0:T(128)} %bitcast.6.me_ref, s32[8,128]{1,0:T(8,128)S(1)} %plan.1.idx, bf16[16,128,128]{2,1,0:T(8,128)(2,1)} %kc.1, bf16[16,128,128]{2,1,0:T(8,128)(2,1)} %vc.1, bf16[16,128,128]{2,1,0:T(8,128)(2,1)S(1)} %collective-permute-done.8.refs_2_, ...), custom_call_target="tpu_custom_call" | custom-call | tf_op jit(solution)/shard_map/pack/pallas_call | solution.py:387
  33.5 5.8 %all-to-all-start.1 = ((bf16[16,3,256,128]{3,2,1,0:T(8,128)(2,1)}), bf16[16,3,256,128]{3,2,1,0:T(8,128)(2,1)}, u32[]{:S(2)}, u32[]{:S(2)}) async-start(bf16[16,3,256,128]{3,2,1,0:T(8,128)(2,1)} %pack.1), calls=%async_computation.1 | async-start | bytes 6291456 | tf_op jit(solution)/shard_map/all_to_all | solution.py:448
  39.4 3.8 %project.1 = (bf16[256,128]{1,0:T(8,128)(2,1)S(1)}, bf16[64,128]{1,0:T(8,128)(2,1)S(1)}, bf16[64,128]{1,0:T(8,128)(2,1)S(1)}, bf16[16,8,128]{2,1,0:T(8,128)(2,1)S(1)}) custom-call(bf16[8,64,512]{2,1,0:T(8,128)(2,1)S(1)} %all-to-all-done.acts, f32[8,512]{1,0:T(8,128)S(1)} %reshape.194.gain, bf16[4096,512]{1,0:T(8,128)(2,1)} %wq.1, bf16[4096,128]{1,0:T(8,128)(2,1)} %wk.1, ...), custom_call_target="tpu_custom_call" | custom-call | flops 402653184 | bytes 7340032 | tf_op jit(solution)/shard_map/project/pallas_call | solution.py:100
  43.2 4.1 %attend.1 = (bf16[64,512]{1,0:T(8,128)(2,1)S(1)}, bf16[64,512]{1,0:T(8,128)(2,1)S(1)}, bf16[64,512]{1,0:T(8,128)(2,1)S(1)}, bf16[64,512]{1,0:T(8,128)(2,1)S(1)},...) custom-call(s32[8]{0:T(128)S(1)} %and_select_fusion.blk, ...), custom_call_target="tpu_custom_call" | custom-call | flops 335544320 | bytes 6291456 | tf_op jit(solution)/shard_map/attend/pallas_call | solution.py:165
  47.3 1.5 %collective-permute-start.10 = (bf16[64,512]{1,0:T(8,128)(2,1)S(1)}, bf16[64,512]{1,0:T(8,128)(2,1)S(1)}, u32[]{:S(2)}, u32[]{:S(2)}) collective-permute-start(bf16[64,512]{1,0:T(8,128)(2,1)S(1)} %get-tuple-element.230), channel_id=1, source_target_pairs={{0,1},{1,2},{2,3},{3,4},{4,5},{5,6},{6,7},{7,0},{8,9},{9,10},{10,1... | collective-permute-start | bytes 196616 | tf_op jit(solution)/shard_map/ppermute | solution.py:429
  48.8 2.1 %collective-permute-start.11 = (bf16[64,512]{1,0:T(8,128)(2,1)S(1)}, bf16[64,512]{1,0:T(8,128)(2,1)S(1)}, u32[]{:S(2)}, u32[]{:S(2)}) collective-permute-start(bf16[64,512]{1,0:T(8,128)(2,1)S(1)} %get-tuple-element.231), channel_id=1, source_target_pairs={{0,2},{1,3},{2,4},{3,5},{4,6},{5,7},{6,0},{7,1},{8,10},{9,11},{10,... | collective-permute-start | bytes 196616 | tf_op jit(solution)/shard_map/ppermute | solution.py:429
  52.2 2.3 %collective-permute-start.12 = (bf16[64,512]{1,0:T(8,128)(2,1)S(1)}, bf16[64,512]{1,0:T(8,128)(2,1)S(1)}, u32[]{:S(2)}, u32[]{:S(2)}) collective-permute-start(bf16[64,512]{1,0:T(8,128)(2,1)S(1)} %get-tuple-element.232), channel_id=1, source_target_pairs={{0,3},{1,4},{2,5},{3,6},{4,7},{5,0},{6,1},{7,2},{8,11},{9,12},{10,... | collective-permute-start | bytes 196616 | tf_op jit(solution)/shard_map/ppermute | solution.py:429
  54.5 2.3 %collective-permute-start.13 = (bf16[64,512]{1,0:T(8,128)(2,1)S(1)}, bf16[64,512]{1,0:T(8,128)(2,1)S(1)}, u32[]{:S(2)}, u32[]{:S(2)}) collective-permute-start(bf16[64,512]{1,0:T(8,128)(2,1)S(1)} %get-tuple-element.233), channel_id=1, source_target_pairs={{0,4},{1,5},{2,6},{3,7},{4,0},{5,1},{6,2},{7,3},{8,12},{9,13},{10,... | collective-permute-start | bytes 196616 | tf_op jit(solution)/shard_map/ppermute | solution.py:429
  56.7 2.4 %collective-permute-start.14 = (bf16[64,512]{1,0:T(8,128)(2,1)S(1)}, bf16[64,512]{1,0:T(8,128)(2,1)S(1)}, u32[]{:S(2)}, u32[]{:S(2)}) collective-permute-start(bf16[64,512]{1,0:T(8,128)(2,1)S(1)} %get-tuple-element.234), channel_id=1, source_target_pairs={{0,5},{1,6},{2,7},{3,0},{4,1},{5,2},{6,3},{7,4},{8,13},{9,14},{10,... | collective-permute-start | bytes 196616 | tf_op jit(solution)/shard_map/ppermute | solution.py:429
  59.2 3.3 %collective-permute-start.15 = (bf16[64,512]{1,0:T(8,128)(2,1)S(1)}, bf16[64,512]{1,0:T(8,128)(2,1)S(1)}, u32[]{:S(2)}, u32[]{:S(2)}) collective-permute-start(bf16[64,512]{1,0:T(8,128)(2,1)S(1)} %get-tuple-element.235), channel_id=1, source_target_pairs={{0,6},{1,7},{2,0},{3,1},{4,2},{5,3},{6,4},{7,5},{8,14},{9,15},{10,... | collective-permute-start | bytes 196616 | tf_op jit(solution)/shard_map/ppermute | solution.py:429
  63.7 2.6 %collective-permute-done.15.refs_6_ = bf16[64,512]{1,0:T(8,128)(2,1)S(1)} collective-permute-done((bf16[64,512]{1,0:T(8,128)(2,1)S(1)}, bf16[64,512]{1,0:T(8,128)(2,1)S(1)}, u32[]{:S(2)}, u32[]{:S(2)}) %collective-permute-start.15) | collective-permute-done | bytes 65568 | tf_op jit(solution)/shard_map/ppermute | solution.py:429
  66.3 3.0 %collective-permute-done.16.refs_7_ = bf16[64,512]{1,0:T(8,128)(2,1)S(1)} collective-permute-done((bf16[64,512]{1,0:T(8,128)(2,1)S(1)}, bf16[64,512]{1,0:T(8,128)(2,1)S(1)}, u32[]{:S(2)}, u32[]{:S(2)}) %collective-permute-start.16) | collective-permute-done | bytes 65568 | tf_op jit(solution)/shard_map/ppermute | solution.py:429
  72.9 4.1 %collective-permute-start.19 = (f32[1,128]{1,0:T(1,128)S(1)}, f32[1,128]{1,0:T(1,128)S(1)}, u32[]{:S(2)}, u32[]{:S(2)}) collective-permute-start(f32[1,128]{1,0:T(1,128)S(1)} %add.111.refs_0_), channel_id=1, source_target_pairs={{0,4},{1,5},{2,6},{3,7},{4,0},{5,1},{6,2},{7,3},{8,12},{9,13},{10,... | collective-permute-start | bytes 1544 | tf_op jit(solution)/shard_map/ppermute | solution.py:429
  81.7 13.2 %all-to-all-start.2 = ((bf16[32,3,8,128]{3,2,1,0:T(8,128)(2,1)}), bf16[32,3,8,128]{3,2,1,0:T(8,128)(2,1)S(1)}, u32[]{:S(2)}, u32[]{:S(2)}) async-start(bf16[32,3,8,128]{3,2,1,0:T(8,128)(2,1)} %get-tuple-element.243), calls=%async_computation.2 | async-start | bytes 393216 | tf_op jit(solution)/shard_map/all_to_all | solution.py:519
  94.9 3.1 %conditional.1 = ((bf16[16,128,128]{2,1,0:T(8,128)(2,1)}, bf16[16,128,128]{2,1,0:T(8,128)(2,1)})) conditional(s32[]{:T(128)} %bitcast.14, (s32[8,128]{1,0:T(8,128)S(1)}, bf16[16,3,256,128]{3,2,1,0:T(8,128)(2,1)}) %tuple.54, (s32[]{:T(128)}, bf16[16,128,128]{2,1,0:T(8,128)(2,1)S(1)}, bf16[16,128,128]{2,1,0:T(8,128)(2,1)S(1)}, ...), branch_computations={%region_0.1_spmd, %region_1.6_spmd} | conditional | flops 4260986 | bytes 40245904 | solution.py:543
  94.9 3.0 %place.2 = (bf16[16,128,128]{2,1,0:T(8,128)(2,1)}, bf16[16,128,128]{2,1,0:T(8,128)(2,1)}) custom-call(s32[8,128]{1,0:T(8,128)S(1)} %get-tuple-element.164.refs_0_, bf16[16,3,256,128]{3,2,1,0:T(8,128)(2,1)} %get-tuple-element.165.refs_1_), custom_call_target="tpu_custom_call" | custom-call | tf_op jit(solution)/shard_map/cond/branch_0_fun/place/pallas_call | solution.py:417
  98.0 1.9 %copy_bitcast_fusion = (bf16[128,16,128]{2,1,0:T(8,128)(2,1)S(1)}, bf16[128,16,128]{2,1,0:T(8,128)(2,1)S(1)}) fusion(bf16[16,128,128]{2,1,0:T(8,128)(2,1)} %get-tuple-element.246, bf16[16,128,128]{2,1,0:T(8,128)(2,1)} %get-tuple-element.245), kind=kLoop, calls=%fused_computation.17 | loop fusion | bytes 2097152 | tf_op jit(solution)/shard_map/transpose | solution.py:554
  101.6 1.5 %all-to-all-done.2.got = bf16[32,3,8,128]{3,2,1,0:T(8,128)(2,1)S(1)} async-done(((bf16[32,3,8,128]{3,2,1,0:T(8,128)(2,1)}), bf16[32,3,8,128]{3,2,1,0:T(8,128)(2,1)S(1)}, u32[]{:S(2)}, u32[]{:S(2)}) %all-to-all-start.2) | async-done | bytes 196640 | tf_op jit(solution)/shard_map/all_to_all | solution.py:519
  103.2 2.0 %finish.1 = (f32[1,16]{1,0:T(1,128)}, bf16[132,16,128]{2,1,0:T(8,128)(2,1)}, bf16[132,16,128]{2,1,0:T(8,128)(2,1)}) custom-call(s32[8,128]{1,0:T(8,128)S(1)} %plan.1.idx, f32[1,128]{1,0:T(1,128)S(1)} %get-tuple-element.241.line, bf16[32,3,8,128]{3,2,1,0:T(8,128)(2,1)S(1)} %all-to-all-done.2.got, ...), custom_call_target="tpu_custom_call", output_to_operand_aliasing={{1}: (3, {}), {2}: (4, {})} | custom-call | tf_op jit(solution)/shard_map/finish/pallas_call | solution.py:276
  (67 shorter events, 23.4 us)
Async XLA Ops:
  0.6 70.8 %copy-start = (bf16[128256]{0:T(1024)(128)(2,1)S(1)}, bf16[128256]{0:T(1024)(128)(2,1)}, u32[]{:S(2)}) copy-start(bf16[128256]{0:T(1024)(128)(2,1)} %param.32) | copy-start | bytes 769540
  2.4 31.1 %all-to-all-start = ((bf16[8,64,512]{2,1,0:T(8,128)(2,1)}), bf16[8,64,512]{2,1,0:T(8,128)(2,1)S(1)}, u32[]{:S(2)}, u32[]{:S(2)}) async-start(bf16[8,64,512]{2,1,0:T(8,128)(2,1)} %broadcast_in_dim.19), calls=%async_computation | async-start | bytes 1048576 | tf_op jit(solution)/shard_map/all_to_all | solution.py:495
  11.4 18.5 %collective-permute-start.8 = (bf16[16,128,128]{2,1,0:T(8,128)(2,1)}, bf16[16,128,128]{2,1,0:T(8,128)(2,1)S(1)}, u32[]{:S(2)}, u32[]{:S(2)}) collective-permute-start(bf16[16,128,128]{2,1,0:T(8,128)(2,1)} %kc.1), channel_id=1, source_target_pairs={{0,8},{8,0},{16,24},{24,16},{32,40},{40,32},{48,56},{56,48},{64,72... | collective-permute-start | bytes 1572872 | tf_op jit(solution)/shard_map/ppermute | solution.py:437
  12.3 17.5 %collective-permute-start.9 = (bf16[16,128,128]{2,1,0:T(8,128)(2,1)}, bf16[16,128,128]{2,1,0:T(8,128)(2,1)S(1)}, u32[]{:S(2)}, u32[]{:S(2)}) collective-permute-start(bf16[16,128,128]{2,1,0:T(8,128)(2,1)} %vc.1), channel_id=1, source_target_pairs={{0,8},{8,0},{16,24},{24,16},{32,40},{40,32},{48,56},{56,48},{64,72... | collective-permute-start | bytes 1572872 | tf_op jit(solution)/shard_map/ppermute | solution.py:437
  12.4 2.4 %collective-permute-start.1 = (s32[1,16]{1,0:T(1,128)}, s32[1,16]{1,0:T(1,128)S(1)}, u32[]{:S(2)}, u32[]{:S(2)}) collective-permute-start(s32[1,16]{1,0:T(1,128)} %bitcast.37), channel_id=1, source_target_pairs={{0,8},{8,0},{16,24},{24,16},{32,40},{40,32},{48,56},{56,48},{64,72... | collective-permute-start | bytes 200 | tf_op jit(solution)/shard_map/ppermute | solution.py:437
  15.5 4.8 %collective-permute-start.2 = (s32[2,16]{1,0:T(2,128)S(1)}, s32[2,16]{1,0:T(2,128)S(1)}, u32[]{:S(2)}, u32[]{:S(2)}) collective-permute-start(s32[2,16]{1,0:T(2,128)S(1)} %pad_add_fusion), channel_id=1, source_target_pairs={{0,16},{8,24},{16,32},{24,40},{32,48},{40,56},{48,0},{56,8},{64,80... | collective-permute-start | bytes 392 | tf_op jit(solution)/shard_map/ppermute | solution.py:456
  16.7 4.2 %collective-permute-start.3 = (s32[2,16]{1,0:T(2,128)S(1)}, s32[2,16]{1,0:T(2,128)S(1)}, u32[]{:S(2)}, u32[]{:S(2)}) collective-permute-start(s32[2,16]{1,0:T(2,128)S(1)} %pad_add_fusion), channel_id=1, source_target_pairs={{0,32},{8,40},{16,48},{24,56},{32,0},{40,8},{48,16},{56,24},{64,96... | collective-permute-start | bytes 392 | tf_op jit(solution)/shard_map/ppermute | solution.py:456
  19.2 2.7 %collective-permute-start.4 = (s32[2,16]{1,0:T(2,128)S(1)}, s32[2,16]{1,0:T(2,128)S(1)}, u32[]{:S(2)}, u32[]{:S(2)}) collective-permute-start(s32[2,16]{1,0:T(2,128)S(1)} %pad_add_fusion), channel_id=1, source_target_pairs={{0,48},{8,56},{16,0},{24,8},{32,16},{40,24},{48,32},{56,40},{64,11... | collective-permute-start | bytes 392 | tf_op jit(solution)/shard_map/ppermute | solution.py:456
  22.5 5.1 %collective-permute-start.5 = (s32[8,16]{1,0:T(8,128)S(1)}, s32[8,16]{1,0:T(8,128)S(1)}, u32[]{:S(2)}, u32[]{:S(2)}) collective-permute-start(s32[8,16]{1,0:T(8,128)S(1)} %concatenate.35.refs_0_), channel_id=1, source_target_pairs={{0,64},{8,72},{16,80},{24,88},{32,96},{40,104},{48,112},{56,120},{... | collective-permute-start | bytes 1544 | tf_op jit(solution)/shard_map/ppermute | solution.py:456
  23.9 4.3 %collective-permute-start.6 = (s32[8,16]{1,0:T(8,128)S(1)}, s32[8,16]{1,0:T(8,128)S(1)}, u32[]{:S(2)}, u32[]{:S(2)}) collective-permute-start(s32[8,16]{1,0:T(8,128)S(1)} %concatenate.35.refs_0_), channel_id=1, source_target_pairs={{0,128},{8,136},{16,144},{24,152},{32,160},{40,168},{48,176},{56,1... | collective-permute-start | bytes 1544 | tf_op jit(solution)/shard_map/ppermute | solution.py:456
  26.5 2.8 %collective-permute-start.7 = (s32[8,16]{1,0:T(8,128)S(1)}, s32[8,16]{1,0:T(8,128)S(1)}, u32[]{:S(2)}, u32[]{:S(2)}) collective-permute-start(s32[8,16]{1,0:T(8,128)S(1)} %concatenate.35.refs_0_), channel_id=1, source_target_pairs={{0,192},{8,200},{16,208},{24,216},{32,224},{40,232},{48,240},{56,2... | collective-permute-start | bytes 1544 | tf_op jit(solution)/shard_map/ppermute | solution.py:456
  33.5 48.2 %all-to-all-start.1 = ((bf16[16,3,256,128]{3,2,1,0:T(8,128)(2,1)}), bf16[16,3,256,128]{3,2,1,0:T(8,128)(2,1)}, u32[]{:S(2)}, u32[]{:S(2)}) async-start(bf16[16,3,256,128]{3,2,1,0:T(8,128)(2,1)} %pack.1), calls=%async_computation.1 | async-start | bytes 6291456 | tf_op jit(solution)/shard_map/all_to_all | solution.py:448
  47.3 11.9 %collective-permute-start.10 = (bf16[64,512]{1,0:T(8,128)(2,1)S(1)}, bf16[64,512]{1,0:T(8,128)(2,1)S(1)}, u32[]{:S(2)}, u32[]{:S(2)}) collective-permute-start(bf16[64,512]{1,0:T(8,128)(2,1)S(1)} %get-tuple-element.230), channel_id=1, source_target_pairs={{0,1},{1,2},{2,3},{3,4},{4,5},{5,6},{6,7},{7,0},{8,9},{9,10},{10,1... | collective-permute-start | bytes 196616 | tf_op jit(solution)/shard_map/ppermute | solution.py:429
  48.8 13.7 %collective-permute-start.11 = (bf16[64,512]{1,0:T(8,128)(2,1)S(1)}, bf16[64,512]{1,0:T(8,128)(2,1)S(1)}, u32[]{:S(2)}, u32[]{:S(2)}) collective-permute-start(bf16[64,512]{1,0:T(8,128)(2,1)S(1)} %get-tuple-element.231), channel_id=1, source_target_pairs={{0,2},{1,3},{2,4},{3,5},{4,6},{5,7},{6,0},{7,1},{8,10},{9,11},{10,... | collective-permute-start | bytes 196616 | tf_op jit(solution)/shard_map/ppermute | solution.py:429
  52.2 11.5 %collective-permute-start.12 = (bf16[64,512]{1,0:T(8,128)(2,1)S(1)}, bf16[64,512]{1,0:T(8,128)(2,1)S(1)}, u32[]{:S(2)}, u32[]{:S(2)}) collective-permute-start(bf16[64,512]{1,0:T(8,128)(2,1)S(1)} %get-tuple-element.232), channel_id=1, source_target_pairs={{0,3},{1,4},{2,5},{3,6},{4,7},{5,0},{6,1},{7,2},{8,11},{9,12},{10,... | collective-permute-start | bytes 196616 | tf_op jit(solution)/shard_map/ppermute | solution.py:429
  54.5 9.3 %collective-permute-start.13 = (bf16[64,512]{1,0:T(8,128)(2,1)S(1)}, bf16[64,512]{1,0:T(8,128)(2,1)S(1)}, u32[]{:S(2)}, u32[]{:S(2)}) collective-permute-start(bf16[64,512]{1,0:T(8,128)(2,1)S(1)} %get-tuple-element.233), channel_id=1, source_target_pairs={{0,4},{1,5},{2,6},{3,7},{4,0},{5,1},{6,2},{7,3},{8,12},{9,13},{10,... | collective-permute-start | bytes 196616 | tf_op jit(solution)/shard_map/ppermute | solution.py:429
  56.7 7.0 %collective-permute-start.14 = (bf16[64,512]{1,0:T(8,128)(2,1)S(1)}, bf16[64,512]{1,0:T(8,128)(2,1)S(1)}, u32[]{:S(2)}, u32[]{:S(2)}) collective-permute-start(bf16[64,512]{1,0:T(8,128)(2,1)S(1)} %get-tuple-element.234), channel_id=1, source_target_pairs={{0,5},{1,6},{2,7},{3,0},{4,1},{5,2},{6,3},{7,4},{8,13},{9,14},{10,... | collective-permute-start | bytes 196616 | tf_op jit(solution)/shard_map/ppermute | solution.py:429
  59.2 7.1 %collective-permute-start.15 = (bf16[64,512]{1,0:T(8,128)(2,1)S(1)}, bf16[64,512]{1,0:T(8,128)(2,1)S(1)}, u32[]{:S(2)}, u32[]{:S(2)}) collective-permute-start(bf16[64,512]{1,0:T(8,128)(2,1)S(1)} %get-tuple-element.235), channel_id=1, source_target_pairs={{0,6},{1,7},{2,0},{3,1},{4,2},{5,3},{6,4},{7,5},{8,14},{9,15},{10,... | collective-permute-start | bytes 196616 | tf_op jit(solution)/shard_map/ppermute | solution.py:429
  62.5 6.8 %collective-permute-start.16 = (bf16[64,512]{1,0:T(8,128)(2,1)S(1)}, bf16[64,512]{1,0:T(8,128)(2,1)S(1)}, u32[]{:S(2)}, u32[]{:S(2)}) collective-permute-start(bf16[64,512]{1,0:T(8,128)(2,1)S(1)} %get-tuple-element.236), channel_id=1, source_target_pairs={{0,7},{1,0},{2,1},{3,2},{4,3},{5,4},{6,5},{7,6},{8,15},{9,8},{10,9... | collective-permute-start | bytes 196616 | tf_op jit(solution)/shard_map/ppermute | solution.py:429
  70.0 2.8 %collective-permute-start.17 = (f32[1,128]{1,0:T(1,128)S(1)}, f32[1,128]{1,0:T(1,128)S(1)}, u32[]{:S(2)}, u32[]{:S(2)}) collective-permute-start(f32[1,128]{1,0:T(1,128)S(1)} %get-tuple-element.238), channel_id=1, source_target_pairs={{0,1},{1,0},{2,3},{3,2},{4,5},{5,4},{6,7},{7,6},{8,9},{9,8},{10,11... | collective-permute-start | bytes 1544 | tf_op jit(solution)/shard_map/ppermute | solution.py:433
  72.8 5.3 %collective-permute-start.18 = (f32[1,128]{1,0:T(1,128)S(1)}, f32[1,128]{1,0:T(1,128)S(1)}, u32[]{:S(2)}, u32[]{:S(2)}) collective-permute-start(f32[1,128]{1,0:T(1,128)S(1)} %add.111.refs_0_), channel_id=1, source_target_pairs={{0,2},{1,3},{2,4},{3,5},{4,6},{5,7},{6,0},{7,1},{8,10},{9,11},{10,... | collective-permute-start | bytes 1544 | tf_op jit(solution)/shard_map/ppermute | solution.py:429
  72.9 6.3 %collective-permute-start.19 = (f32[1,128]{1,0:T(1,128)S(1)}, f32[1,128]{1,0:T(1,128)S(1)}, u32[]{:S(2)}, u32[]{:S(2)}) collective-permute-start(f32[1,128]{1,0:T(1,128)S(1)} %add.111.refs_0_), channel_id=1, source_target_pairs={{0,4},{1,5},{2,6},{3,7},{4,0},{5,1},{6,2},{7,3},{8,12},{9,13},{10,... | collective-permute-start | bytes 1544 | tf_op jit(solution)/shard_map/ppermute | solution.py:429
  77.0 3.3 %collective-permute-start.20 = (f32[1,128]{1,0:T(1,128)S(1)}, f32[1,128]{1,0:T(1,128)S(1)}, u32[]{:S(2)}, u32[]{:S(2)}) collective-permute-start(f32[1,128]{1,0:T(1,128)S(1)} %add.111.refs_0_), channel_id=1, source_target_pairs={{0,6},{1,7},{2,0},{3,1},{4,2},{5,3},{6,4},{7,5},{8,14},{9,15},{10,... | collective-permute-start | bytes 1544 | tf_op jit(solution)/shard_map/ppermute | solution.py:429
  81.7 21.4 %all-to-all-start.2 = ((bf16[32,3,8,128]{3,2,1,0:T(8,128)(2,1)}), bf16[32,3,8,128]{3,2,1,0:T(8,128)(2,1)S(1)}, u32[]{:S(2)}, u32[]{:S(2)}) async-start(bf16[32,3,8,128]{3,2,1,0:T(8,128)(2,1)} %get-tuple-element.243), calls=%async_computation.2 | async-start | bytes 393216 | tf_op jit(solution)/shard_map/all_to_all | solution.py:519
  (9 other events, 99.0 us)

commit v8 on v7

--- a/solution.py
+++ b/solution.py
@@ -296,9 +296,7 @@
     me = me_ref[0]
     blocks = jnp.concatenate([r[...] for r in refs[:-1]], 0).astype(F32)
     rel = lax.broadcasted_iota(jnp.int32, (NDOM, NDOM), 1)
-    back_y = (me // 8 - rel // 8) & 3
-    back_x = (me // 2 - rel // 2) & 3
-    holder = 8 * back_y + 2 * back_x + ((me + rel) & 1)
+    holder = me ^ rel
     sorted_rows = lax.broadcasted_iota(jnp.int32, (NDOM, NDOM), 0) == holder
     counts = mm(sorted_rows.astype(F32), blocks)
     r16 = lax.broadcasted_iota(jnp.int32, (NP, NP), 0)
@@ -425,16 +423,13 @@
     )(idx, rows)
 
 
-def shifted(value, shift):
-    return lax.ppermute(value, "tp", [(i, (i + shift) % TP) for i in range(TP)])
-
-
-def z_swapped(value):
-    return lax.ppermute(value, "tp", [(i, i ^ 1) for i in range(TP)])
+def met(value, axis, step):
+    length = lax.axis_size(axis)
+    return lax.ppermute(value, axis, [(i, i ^ step) for i in range(length)])
 
 
 def swapped(value):
-    return lax.ppermute(value, "dom", [(i, i ^ 1) for i in range(NDOM)])
+    return met(value, "dom", 1)
 
 
 def next_chip(value):
@@ -446,21 +441,13 @@
 
 def exchanged(rows):
     return lax.all_to_all(rows, "dom", 0, 0, tiled=True, axis_index_groups=SAME_CORE)
-
-
-def moved(value, axis_stride, shift):
-    def to(i):
-        at = i // axis_stride % 4
-        return i + ((at + shift) % 4 - at) * axis_stride
-
-    return lax.ppermute(value, "dom", [(i, to(i)) for i in range(NDOM)])
 
 
 def spread_counts(copy_counts):
     own = copy_counts.reshape(1, NP)
     chip = jnp.concatenate([own, swapped(own)], 0)
-    row = jnp.concatenate([chip] + [moved(chip, 2, s) for s in range(1, 4)], 0)
-    return [row] + [moved(row, 8, s) for s in range(1, 4)]
+    row = jnp.concatenate([chip] + [met(chip, "dom", 2 * s) for s in range(1, 4)], 0)
+    return [row] + [met(row, "dom", 8 * s) for s in range(1, 4)]
 
 
 def rotation_table():
@@ -489,7 +476,7 @@
     dom = lax.axis_index("dom")
     tp = lax.axis_index("tp")
     me = dom.reshape(1)
-    blk = ((tp + np.arange(TP)) % TP).astype(jnp.int32)
+    blk = (tp ^ np.arange(TP)).astype(jnp.int32)
     act = activations.reshape(ROWS, DB)
 
     gathered = lax.all_to_all(
@@ -510,10 +497,10 @@
     reward = twisting_table[tokens.reshape(ROWS)].astype(F32)
     reward = jnp.pad(reward, (0, HD - ROWS)).reshape(1, HD)
     previous = jnp.pad(previous_log_weights, (0, HD - NP)).reshape(1, HD)
-    parts = [partials[0]] + [shifted(partials[s], s) for s in range(1, TP)]
+    parts = [partials[0]] + [met(partials[s], "tp", s) for s in range(1, TP)]
     attn, sums = mix(parts, act, twist_vec.reshape(1, DB))
-    sums = sums + z_swapped(sums)
-    all_sums = [sums] + [shifted(sums, 2 * s) for s in range(1, PAIRS)]
+    sums = sums + met(sums, "tp", 1)
+    all_sums = [sums] + [met(sums, "tp", 2 * s) for s in range(1, PAIRS)]
     line, sent = weigh(idx, all_sums, reward, previous, fresh)
     sent, rows = lax.optimization_barrier((sent, rows))
     got = lax.all_to_all(sent, "dom", 0, 0, tiled=True)

time: 106 us -> 107 us (level)
  waiting for transfers between devices: 15.1 us -> 26.4 us
  starting transfers between devices: 61 us -> 51.1 us
    ppermute x20, waiting for transfers between devices: 13.5 us -> 24.8 us  [met(): return lax.ppermute(value, axis, [(i, i ^ step) for i in range(length)])]
    ppermute x20, starting transfers between devices: 33.1 us -> 27.1 us  [met(): return lax.ppermute(value, axis, [(i, i ^ step) for i in range(length)])]
    all_to_all x1, starting transfers between devices: 13.2 us -> 10.5 us  [local(): got = lax.all_to_all(sent, 'dom', 0, 0, tiled=True)]
    all_to_all x1, starting transfers between devices: 5.8 us -> 4.49 us  [exchanged(): lax.all_to_all(rows, 'dom', 0, 0, tiled=True, axis_index_groups=SAME_CORE)]
  transfers between devices with their start and end apart: 23 -> 23, of which waited for: 11 -> 13; matrix products, arithmetic and copies ran while one was open for 6% -> 6% of each run, Pallas kernels for 16% -> 16%
where the time goes in v8:
time: 107 us
  starting transfers between devices  51.1 us (48%)
  waiting for transfers between devices  26.4 us (25%)
  Pallas kernels  19.3 us (18%)
  local copies, waits for them, and re-layouts  7.59 us (7%)
  between operations  1.7 us (2%)
    ppermute x20, starting transfers between devices, met(): return lax.ppermute(value, axis, [(i, i ^ step) for i in range(length)])  27.1 us
    ppermute x20, waiting for transfers between devices, met(): return lax.ppermute(value, axis, [(i, i ^ step) for i in range(length)])  24.8 us
    all_to_all x1, starting transfers between devices, local(): got = lax.all_to_all(sent, 'dom', 0, 0, tiled=True)  10.5 us
    all_to_all x1, starting transfers between devices, local(): lax.all_to_all(jnp.broadcast_to(act[None], (TP, ROWS, DB)), 'tp', 0, 0, t...  9.01 us
    all_to_all x1, starting transfers between devices, exchanged(): lax.all_to_all(rows, 'dom', 0, 0, tiled=True, axis_index_groups=SAME_CORE)  4.49 us
    pallas_call x1, Pallas kernels, attend(): pl.pallas_call(attend_body, in_specs=[spec(SM)] + [spec(VM)] * 5 + [spec(...  4.1 us
    pallas_call x1, Pallas kernels, project(): pl.pallas_call(project_body, in_specs=[spec(VM)] * 2 + [spec(ANY)] * 3 +...  3.76 us
    pallas_call x1, Pallas kernels, pack(): pl.pallas_call(pack_body, in_specs=[spec(SM), spec(SM)] + [spec(ANY)] * (...  3.58 us
  transfers between devices with their start and end apart: 23, of which 13 were waited for; matrix products, arithmetic and copies ran while one was open for 6% of the time, Pallas kernels for 16%

profile of v8, /device:TPU:1, one launch (start us, length us, event | category | flops | bytes accessed | tf_op | source)
XLA Modules:
  0.0 106.8 jit_solution(7178258854162200804)
XLA Ops:
  2.4 9.0 %all-to-all-start = ((bf16[8,64,512]{2,1,0:T(8,128)(2,1)}), bf16[8,64,512]{2,1,0:T(8,128)(2,1)S(1)}, u32[]{:S(2)}, u32[]{:S(2)}) async-start(bf16[8,64,512]{2,1,0:T(8,128)(2,1)} %broadcast_in_dim.19), calls=%async_computation | async-start | bytes 1048576 | tf_op jit(solution)/shard_map/all_to_all | solution.py:482
  12.8 2.0 %collective-permute-done.1 = s32[1,16]{1,0:T(1,128)S(1)} collective-permute-done((s32[1,16]{1,0:T(1,128)}, s32[1,16]{1,0:T(1,128)S(1)}, u32[]{:S(2)}, u32[]{:S(2)}) %collective-permute-start.1) | collective-permute-done | bytes 96 | tf_op jit(solution)/shard_map/ppermute | solution.py:428
  16.7 2.5 %collective-permute-start.3 = (s32[2,16]{1,0:T(2,128)S(1)}, s32[2,16]{1,0:T(2,128)S(1)}, u32[]{:S(2)}, u32[]{:S(2)}) collective-permute-start(s32[2,16]{1,0:T(2,128)S(1)} %pad_add_fusion), channel_id=1, source_target_pairs={{0,32},{8,40},{16,48},{24,56},{32,0},{40,8},{48,16},{56,24},{64,96... | collective-permute-start | bytes 392 | tf_op jit(solution)/shard_map/ppermute | solution.py:428
  20.9 2.2 %collective-permute-done.4 = s32[2,16]{1,0:T(2,128)S(1)} collective-permute-done((s32[2,16]{1,0:T(2,128)S(1)}, s32[2,16]{1,0:T(2,128)S(1)}, u32[]{:S(2)}, u32[]{:S(2)}) %collective-permute-start.4) | collective-permute-done | bytes 160 | tf_op jit(solution)/shard_map/ppermute | solution.py:428
  25.1 2.6 %collective-permute-start.6 = (s32[8,16]{1,0:T(8,128)S(1)}, s32[8,16]{1,0:T(8,128)S(1)}, u32[]{:S(2)}, u32[]{:S(2)}) collective-permute-start(s32[8,16]{1,0:T(8,128)S(1)} %concatenate.35.refs_0_), channel_id=1, source_target_pairs={{0,128},{8,136},{16,144},{24,152},{32,160},{40,168},{48,176},{56,1... | collective-permute-start | bytes 1544 | tf_op jit(solution)/shard_map/ppermute | solution.py:428
  29.4 2.3 %collective-permute-done.7.refs_3_ = s32[8,16]{1,0:T(8,128)S(1)} collective-permute-done((s32[8,16]{1,0:T(8,128)S(1)}, s32[8,16]{1,0:T(8,128)S(1)}, u32[]{:S(2)}, u32[]{:S(2)}) %collective-permute-start.7) | collective-permute-done | bytes 544 | tf_op jit(solution)/shard_map/ppermute | solution.py:428
  32.3 3.6 %pack.1 = bf16[16,3,256,128]{3,2,1,0:T(8,128)(2,1)} custom-call(s32[1]{0:T(128)} %bitcast.6.me_ref, s32[8,128]{1,0:T(8,128)S(1)} %plan.1.idx, bf16[16,128,128]{2,1,0:T(8,128)(2,1)} %kc.1, bf16[16,128,128]{2,1,0:T(8,128)(2,1)} %vc.1, bf16[16,128,128]{2,1,0:T(8,128)(2,1)S(1)} %collective-permute-done.8.refs_2_, ...), custom_call_target="tpu_custom_call" | custom-call | tf_op jit(solution)/shard_map/pack/pallas_call | solution.py:385
  36.0 4.5 %all-to-all-start.1 = ((bf16[16,3,256,128]{3,2,1,0:T(8,128)(2,1)}), bf16[16,3,256,128]{3,2,1,0:T(8,128)(2,1)}, u32[]{:S(2)}, u32[]{:S(2)}) async-start(bf16[16,3,256,128]{3,2,1,0:T(8,128)(2,1)} %pack.1), calls=%async_computation.1 | async-start | bytes 6291456 | tf_op jit(solution)/shard_map/all_to_all | solution.py:443
  40.5 3.8 %project.1 = (bf16[256,128]{1,0:T(8,128)(2,1)S(1)}, bf16[64,128]{1,0:T(8,128)(2,1)S(1)}, bf16[64,128]{1,0:T(8,128)(2,1)S(1)}, bf16[16,8,128]{2,1,0:T(8,128)(2,1)S(1)}) custom-call(bf16[8,64,512]{2,1,0:T(8,128)(2,1)S(1)} %all-to-all-done.acts, f32[8,512]{1,0:T(8,128)S(1)} %reshape.194.gain, bf16[4096,512]{1,0:T(8,128)(2,1)} %wq.1, bf16[4096,128]{1,0:T(8,128)(2,1)} %wk.1, ...), custom_call_target="tpu_custom_call" | custom-call | flops 402653184 | bytes 7340032 | tf_op jit(solution)/shard_map/project/pallas_call | solution.py:100
  44.4 4.1 %attend.1 = (bf16[64,512]{1,0:T(8,128)(2,1)S(1)}, bf16[64,512]{1,0:T(8,128)(2,1)S(1)}, bf16[64,512]{1,0:T(8,128)(2,1)S(1)}, bf16[64,512]{1,0:T(8,128)(2,1)S(1)},...) custom-call(s32[8]{0:T(128)S(1)} %iota_xor_fusion.blk, ...), custom_call_target="tpu_custom_call" | custom-call | flops 335544320 | bytes 6291456 | tf_op jit(solution)/shard_map/attend/pallas_call | solution.py:165
  49.7 2.7 %collective-permute-start.11 = (bf16[64,512]{1,0:T(8,128)(2,1)S(1)}, bf16[64,512]{1,0:T(8,128)(2,1)S(1)}, u32[]{:S(2)}, u32[]{:S(2)}) collective-permute-start(bf16[64,512]{1,0:T(8,128)(2,1)S(1)} %get-tuple-element.231), channel_id=1, source_target_pairs={{0,2},{1,3},{2,0},{3,1},{4,6},{5,7},{6,4},{7,5},{8,10},{9,11},{10,... | collective-permute-start | bytes 196616 | tf_op jit(solution)/shard_map/ppermute | solution.py:428
  53.7 5.4 %collective-permute-start.13 = (bf16[64,512]{1,0:T(8,128)(2,1)S(1)}, bf16[64,512]{1,0:T(8,128)(2,1)S(1)}, u32[]{:S(2)}, u32[]{:S(2)}) collective-permute-start(bf16[64,512]{1,0:T(8,128)(2,1)S(1)} %get-tuple-element.233), channel_id=1, source_target_pairs={{0,4},{1,5},{2,6},{3,7},{4,0},{5,1},{6,2},{7,3},{8,12},{9,13},{10,... | collective-permute-start | bytes 196616 | tf_op jit(solution)/shard_map/ppermute | solution.py:428
  59.2 2.7 %collective-permute-start.15 = (bf16[64,512]{1,0:T(8,128)(2,1)S(1)}, bf16[64,512]{1,0:T(8,128)(2,1)S(1)}, u32[]{:S(2)}, u32[]{:S(2)}) collective-permute-start(bf16[64,512]{1,0:T(8,128)(2,1)S(1)} %get-tuple-element.235), channel_id=1, source_target_pairs={{0,6},{1,7},{2,4},{3,5},{4,2},{5,3},{6,0},{7,1},{8,14},{9,15},{10,... | collective-permute-start | bytes 196616 | tf_op jit(solution)/shard_map/ppermute | solution.py:428
  62.1 5.0 %collective-permute-done.14.refs_5_ = bf16[64,512]{1,0:T(8,128)(2,1)S(1)} collective-permute-done((bf16[64,512]{1,0:T(8,128)(2,1)S(1)}, bf16[64,512]{1,0:T(8,128)(2,1)S(1)}, u32[]{:S(2)}, u32[]{:S(2)}) %collective-permute-start.14) | collective-permute-done | bytes 65568 | tf_op jit(solution)/shard_map/ppermute | solution.py:428
  67.6 3.4 %collective-permute-done.16.refs_7_ = bf16[64,512]{1,0:T(8,128)(2,1)S(1)} collective-permute-done((bf16[64,512]{1,0:T(8,128)(2,1)S(1)}, bf16[64,512]{1,0:T(8,128)(2,1)S(1)}, u32[]{:S(2)}, u32[]{:S(2)}) %collective-permute-start.16) | collective-permute-done | bytes 65568 | tf_op jit(solution)/shard_map/ppermute | solution.py:428
  72.6 2.0 %collective-permute-done.17 = f32[1,128]{1,0:T(1,128)S(1)} collective-permute-done((f32[1,128]{1,0:T(1,128)S(1)}, f32[1,128]{1,0:T(1,128)S(1)}, u32[]{:S(2)}, u32[]{:S(2)}) %collective-permute-start.17) | collective-permute-done | bytes 544 | tf_op jit(solution)/shard_map/ppermute | solution.py:428
  75.6 3.8 %collective-permute-start.19 = (f32[1,128]{1,0:T(1,128)S(1)}, f32[1,128]{1,0:T(1,128)S(1)}, u32[]{:S(2)}, u32[]{:S(2)}) collective-permute-start(f32[1,128]{1,0:T(1,128)S(1)} %add.96.refs_0_), channel_id=1, source_target_pairs={{0,4},{1,5},{2,6},{3,7},{4,0},{5,1},{6,2},{7,3},{8,12},{9,13},{10,... | collective-permute-start | bytes 1544 | tf_op jit(solution)/shard_map/ppermute | solution.py:428
  80.2 2.1 %collective-permute-done.19.refs_2_ = f32[1,128]{1,0:T(1,128)S(1)} collective-permute-done((f32[1,128]{1,0:T(1,128)S(1)}, f32[1,128]{1,0:T(1,128)S(1)}, u32[]{:S(2)}, u32[]{:S(2)}) %collective-permute-start.19) | collective-permute-done | bytes 544 | tf_op jit(solution)/shard_map/ppermute | solution.py:428
  82.3 2.0 %collective-permute-done.20.refs_3_ = f32[1,128]{1,0:T(1,128)S(1)} collective-permute-done((f32[1,128]{1,0:T(1,128)S(1)}, f32[1,128]{1,0:T(1,128)S(1)}, u32[]{:S(2)}, u32[]{:S(2)}) %collective-permute-start.20) | collective-permute-done | bytes 544 | tf_op jit(solution)/shard_map/ppermute | solution.py:428
  85.8 10.5 %all-to-all-start.2 = ((bf16[32,3,8,128]{3,2,1,0:T(8,128)(2,1)}), bf16[32,3,8,128]{3,2,1,0:T(8,128)(2,1)S(1)}, u32[]{:S(2)}, u32[]{:S(2)}) async-start(bf16[32,3,8,128]{3,2,1,0:T(8,128)(2,1)} %get-tuple-element.243), calls=%async_computation.2 | async-start | bytes 393216 | tf_op jit(solution)/shard_map/all_to_all | solution.py:506
  96.3 3.1 %conditional.1 = ((bf16[16,128,128]{2,1,0:T(8,128)(2,1)}, bf16[16,128,128]{2,1,0:T(8,128)(2,1)})) conditional(s32[]{:T(128)} %bitcast.14, (s32[8,128]{1,0:T(8,128)S(1)}, bf16[16,3,256,128]{3,2,1,0:T(8,128)(2,1)}) %tuple.54, (s32[]{:T(128)}, bf16[16,128,128]{2,1,0:T(8,128)(2,1)S(1)}, bf16[16,128,128]{2,1,0:T(8,128)(2,1)S(1)}, ...), branch_computations={%region_0.1_spmd, %region_1.6_spmd} | conditional | flops 4260986 | bytes 40245904 | solution.py:530
  96.3 3.0 %place.2 = (bf16[16,128,128]{2,1,0:T(8,128)(2,1)}, bf16[16,128,128]{2,1,0:T(8,128)(2,1)}) custom-call(s32[8,128]{1,0:T(8,128)S(1)} %get-tuple-element.164.refs_0_, bf16[16,3,256,128]{3,2,1,0:T(8,128)(2,1)} %get-tuple-element.165.refs_1_), custom_call_target="tpu_custom_call" | custom-call | tf_op jit(solution)/shard_map/cond/branch_0_fun/place/pallas_call | solution.py:415
  99.4 1.9 %copy_bitcast_fusion = (bf16[128,16,128]{2,1,0:T(8,128)(2,1)S(1)}, bf16[128,16,128]{2,1,0:T(8,128)(2,1)S(1)}) fusion(bf16[16,128,128]{2,1,0:T(8,128)(2,1)} %get-tuple-element.246, bf16[16,128,128]{2,1,0:T(8,128)(2,1)} %get-tuple-element.245), kind=kLoop, calls=%fused_computation.17 | loop fusion | bytes 2097152 | tf_op jit(solution)/shard_map/transpose | solution.py:541
  104.6 2.0 %finish.1 = (f32[1,16]{1,0:T(1,128)}, bf16[132,16,128]{2,1,0:T(8,128)(2,1)}, bf16[132,16,128]{2,1,0:T(8,128)(2,1)}) custom-call(s32[8,128]{1,0:T(8,128)S(1)} %plan.1.idx, f32[1,128]{1,0:T(1,128)S(1)} %get-tuple-element.241.line, bf16[32,3,8,128]{3,2,1,0:T(8,128)(2,1)S(1)} %all-to-all-done.2.got, ...), custom_call_target="tpu_custom_call", output_to_operand_aliasing={{1}: (3, {}), {2}: (4, {})} | custom-call | tf_op jit(solution)/shard_map/finish/pallas_call | solution.py:276
  (67 shorter events, 22.1 us)
Async XLA Ops:
  0.6 71.2 %copy-start = (bf16[128256]{0:T(1024)(128)(2,1)S(1)}, bf16[128256]{0:T(1024)(128)(2,1)}, u32[]{:S(2)}) copy-start(bf16[128256]{0:T(1024)(128)(2,1)} %param.32) | copy-start | bytes 769540
  2.4 33.6 %all-to-all-start = ((bf16[8,64,512]{2,1,0:T(8,128)(2,1)}), bf16[8,64,512]{2,1,0:T(8,128)(2,1)S(1)}, u32[]{:S(2)}, u32[]{:S(2)}) async-start(bf16[8,64,512]{2,1,0:T(8,128)(2,1)} %broadcast_in_dim.19), calls=%async_computation | async-start | bytes 1048576 | tf_op jit(solution)/shard_map/all_to_all | solution.py:482
  11.4 20.9 %collective-permute-start.8 = (bf16[16,128,128]{2,1,0:T(8,128)(2,1)}, bf16[16,128,128]{2,1,0:T(8,128)(2,1)S(1)}, u32[]{:S(2)}, u32[]{:S(2)}) collective-permute-start(bf16[16,128,128]{2,1,0:T(8,128)(2,1)} %kc.1), channel_id=1, source_target_pairs={{0,8},{8,0},{16,24},{24,16},{32,40},{40,32},{48,56},{56,48},{64,72... | collective-permute-start | bytes 1572872 | tf_op jit(solution)/shard_map/ppermute | solution.py:428
  12.3 20.0 %collective-permute-start.9 = (bf16[16,128,128]{2,1,0:T(8,128)(2,1)}, bf16[16,128,128]{2,1,0:T(8,128)(2,1)S(1)}, u32[]{:S(2)}, u32[]{:S(2)}) collective-permute-start(bf16[16,128,128]{2,1,0:T(8,128)(2,1)} %vc.1), channel_id=1, source_target_pairs={{0,8},{8,0},{16,24},{24,16},{32,40},{40,32},{48,56},{56,48},{64,72... | collective-permute-start | bytes 1572872 | tf_op jit(solution)/shard_map/ppermute | solution.py:428
  12.4 2.4 %collective-permute-start.1 = (s32[1,16]{1,0:T(1,128)}, s32[1,16]{1,0:T(1,128)S(1)}, u32[]{:S(2)}, u32[]{:S(2)}) collective-permute-start(s32[1,16]{1,0:T(1,128)} %bitcast.37), channel_id=1, source_target_pairs={{0,8},{8,0},{16,24},{24,16},{32,40},{40,32},{48,56},{56,48},{64,72... | collective-permute-start | bytes 200 | tf_op jit(solution)/shard_map/ppermute | solution.py:428
  15.5 3.9 %collective-permute-start.2 = (s32[2,16]{1,0:T(2,128)S(1)}, s32[2,16]{1,0:T(2,128)S(1)}, u32[]{:S(2)}, u32[]{:S(2)}) collective-permute-start(s32[2,16]{1,0:T(2,128)S(1)} %pad_add_fusion), channel_id=1, source_target_pairs={{0,16},{8,24},{16,0},{24,8},{32,48},{40,56},{48,32},{56,40},{64,80... | collective-permute-start | bytes 392 | tf_op jit(solution)/shard_map/ppermute | solution.py:428
  16.7 4.2 %collective-permute-start.3 = (s32[2,16]{1,0:T(2,128)S(1)}, s32[2,16]{1,0:T(2,128)S(1)}, u32[]{:S(2)}, u32[]{:S(2)}) collective-permute-start(s32[2,16]{1,0:T(2,128)S(1)} %pad_add_fusion), channel_id=1, source_target_pairs={{0,32},{8,40},{16,48},{24,56},{32,0},{40,8},{48,16},{56,24},{64,96... | collective-permute-start | bytes 392 | tf_op jit(solution)/shard_map/ppermute | solution.py:428
  19.2 3.9 %collective-permute-start.4 = (s32[2,16]{1,0:T(2,128)S(1)}, s32[2,16]{1,0:T(2,128)S(1)}, u32[]{:S(2)}, u32[]{:S(2)}) collective-permute-start(s32[2,16]{1,0:T(2,128)S(1)} %pad_add_fusion), channel_id=1, source_target_pairs={{0,48},{8,56},{16,32},{24,40},{32,16},{40,24},{48,0},{56,8},{64,11... | collective-permute-start | bytes 392 | tf_op jit(solution)/shard_map/ppermute | solution.py:428
  23.8 4.0 %collective-permute-start.5 = (s32[8,16]{1,0:T(8,128)S(1)}, s32[8,16]{1,0:T(8,128)S(1)}, u32[]{:S(2)}, u32[]{:S(2)}) collective-permute-start(s32[8,16]{1,0:T(8,128)S(1)} %concatenate.35.refs_0_), channel_id=1, source_target_pairs={{0,64},{8,72},{16,80},{24,88},{32,96},{40,104},{48,112},{56,120},{... | collective-permute-start | bytes 1544 | tf_op jit(solution)/shard_map/ppermute | solution.py:428
  25.1 4.3 %collective-permute-start.6 = (s32[8,16]{1,0:T(8,128)S(1)}, s32[8,16]{1,0:T(8,128)S(1)}, u32[]{:S(2)}, u32[]{:S(2)}) collective-permute-start(s32[8,16]{1,0:T(8,128)S(1)} %concatenate.35.refs_0_), channel_id=1, source_target_pairs={{0,128},{8,136},{16,144},{24,152},{32,160},{40,168},{48,176},{56,1... | collective-permute-start | bytes 1544 | tf_op jit(solution)/shard_map/ppermute | solution.py:428
  27.8 4.0 %collective-permute-start.7 = (s32[8,16]{1,0:T(8,128)S(1)}, s32[8,16]{1,0:T(8,128)S(1)}, u32[]{:S(2)}, u32[]{:S(2)}) collective-permute-start(s32[8,16]{1,0:T(8,128)S(1)} %concatenate.35.refs_0_), channel_id=1, source_target_pairs={{0,192},{8,200},{16,208},{24,216},{32,224},{40,232},{48,240},{56,2... | collective-permute-start | bytes 1544 | tf_op jit(solution)/shard_map/ppermute | solution.py:428
  36.0 49.8 %all-to-all-start.1 = ((bf16[16,3,256,128]{3,2,1,0:T(8,128)(2,1)}), bf16[16,3,256,128]{3,2,1,0:T(8,128)(2,1)}, u32[]{:S(2)}, u32[]{:S(2)}) async-start(bf16[16,3,256,128]{3,2,1,0:T(8,128)(2,1)} %pack.1), calls=%async_computation.1 | async-start | bytes 6291456 | tf_op jit(solution)/shard_map/all_to_all | solution.py:443
  48.5 10.7 %collective-permute-start.10 = (bf16[64,512]{1,0:T(8,128)(2,1)S(1)}, bf16[64,512]{1,0:T(8,128)(2,1)S(1)}, u32[]{:S(2)}, u32[]{:S(2)}) collective-permute-start(bf16[64,512]{1,0:T(8,128)(2,1)S(1)} %get-tuple-element.230), channel_id=1, source_target_pairs={{0,1},{1,0},{2,3},{3,2},{4,5},{5,4},{6,7},{7,6},{8,9},{9,8},{10,11... | collective-permute-start | bytes 196616 | tf_op jit(solution)/shard_map/ppermute | solution.py:428
  49.7 12.2 %collective-permute-start.11 = (bf16[64,512]{1,0:T(8,128)(2,1)S(1)}, bf16[64,512]{1,0:T(8,128)(2,1)S(1)}, u32[]{:S(2)}, u32[]{:S(2)}) collective-permute-start(bf16[64,512]{1,0:T(8,128)(2,1)S(1)} %get-tuple-element.231), channel_id=1, source_target_pairs={{0,2},{1,3},{2,0},{3,1},{4,6},{5,7},{6,4},{7,5},{8,10},{9,11},{10,... | collective-permute-start | bytes 196616 | tf_op jit(solution)/shard_map/ppermute | solution.py:428
  53.6 8.4 %collective-permute-start.12 = (bf16[64,512]{1,0:T(8,128)(2,1)S(1)}, bf16[64,512]{1,0:T(8,128)(2,1)S(1)}, u32[]{:S(2)}, u32[]{:S(2)}) collective-permute-start(bf16[64,512]{1,0:T(8,128)(2,1)S(1)} %get-tuple-element.232), channel_id=1, source_target_pairs={{0,3},{1,2},{2,1},{3,0},{4,7},{5,6},{6,5},{7,4},{8,11},{9,10},{10,... | collective-permute-start | bytes 196616 | tf_op jit(solution)/shard_map/ppermute | solution.py:428
  53.7 8.3 %collective-permute-start.13 = (bf16[64,512]{1,0:T(8,128)(2,1)S(1)}, bf16[64,512]{1,0:T(8,128)(2,1)S(1)}, u32[]{:S(2)}, u32[]{:S(2)}) collective-permute-start(bf16[64,512]{1,0:T(8,128)(2,1)S(1)} %get-tuple-element.233), channel_id=1, source_target_pairs={{0,4},{1,5},{2,6},{3,7},{4,0},{5,1},{6,2},{7,3},{8,12},{9,13},{10,... | collective-permute-start | bytes 196616 | tf_op jit(solution)/shard_map/ppermute | solution.py:428
  59.1 8.0 %collective-permute-start.14 = (bf16[64,512]{1,0:T(8,128)(2,1)S(1)}, bf16[64,512]{1,0:T(8,128)(2,1)S(1)}, u32[]{:S(2)}, u32[]{:S(2)}) collective-permute-start(bf16[64,512]{1,0:T(8,128)(2,1)S(1)} %get-tuple-element.234), channel_id=1, source_target_pairs={{0,5},{1,4},{2,7},{3,6},{4,1},{5,0},{6,3},{7,2},{8,13},{9,12},{10,... | collective-permute-start | bytes 196616 | tf_op jit(solution)/shard_map/ppermute | solution.py:428
  59.2 8.5 %collective-permute-start.15 = (bf16[64,512]{1,0:T(8,128)(2,1)S(1)}, bf16[64,512]{1,0:T(8,128)(2,1)S(1)}, u32[]{:S(2)}, u32[]{:S(2)}) collective-permute-start(bf16[64,512]{1,0:T(8,128)(2,1)S(1)} %get-tuple-element.235), channel_id=1, source_target_pairs={{0,6},{1,7},{2,4},{3,5},{4,2},{5,3},{6,0},{7,1},{8,14},{9,15},{10,... | collective-permute-start | bytes 196616 | tf_op jit(solution)/shard_map/ppermute | solution.py:428
  61.9 9.2 %collective-permute-start.16 = (bf16[64,512]{1,0:T(8,128)(2,1)S(1)}, bf16[64,512]{1,0:T(8,128)(2,1)S(1)}, u32[]{:S(2)}, u32[]{:S(2)}) collective-permute-start(bf16[64,512]{1,0:T(8,128)(2,1)S(1)} %get-tuple-element.236), channel_id=1, source_target_pairs={{0,7},{1,6},{2,5},{3,4},{4,3},{5,2},{6,1},{7,0},{8,15},{9,14},{10,... | collective-permute-start | bytes 196616 | tf_op jit(solution)/shard_map/ppermute | solution.py:428
  71.8 2.8 %collective-permute-start.17 = (f32[1,128]{1,0:T(1,128)S(1)}, f32[1,128]{1,0:T(1,128)S(1)}, u32[]{:S(2)}, u32[]{:S(2)}) collective-permute-start(f32[1,128]{1,0:T(1,128)S(1)} %get-tuple-element.238), channel_id=1, source_target_pairs={{0,1},{1,0},{2,3},{3,2},{4,5},{5,4},{6,7},{7,6},{8,9},{9,8},{10,11... | collective-permute-start | bytes 1544 | tf_op jit(solution)/shard_map/ppermute | solution.py:428
  74.6 5.7 %collective-permute-start.18 = (f32[1,128]{1,0:T(1,128)S(1)}, f32[1,128]{1,0:T(1,128)S(1)}, u32[]{:S(2)}, u32[]{:S(2)}) collective-permute-start(f32[1,128]{1,0:T(1,128)S(1)} %add.96.refs_0_), channel_id=1, source_target_pairs={{0,2},{1,3},{2,0},{3,1},{4,6},{5,7},{6,4},{7,5},{8,10},{9,11},{10,... | collective-permute-start | bytes 1544 | tf_op jit(solution)/shard_map/ppermute | solution.py:428
  75.6 6.7 %collective-permute-start.19 = (f32[1,128]{1,0:T(1,128)S(1)}, f32[1,128]{1,0:T(1,128)S(1)}, u32[]{:S(2)}, u32[]{:S(2)}) collective-permute-start(f32[1,128]{1,0:T(1,128)S(1)} %add.96.refs_0_), channel_id=1, source_target_pairs={{0,4},{1,5},{2,6},{3,7},{4,0},{5,1},{6,2},{7,3},{8,12},{9,13},{10,... | collective-permute-start | bytes 1544 | tf_op jit(solution)/shard_map/ppermute | solution.py:428
  79.4 4.9 %collective-permute-start.20 = (f32[1,128]{1,0:T(1,128)S(1)}, f32[1,128]{1,0:T(1,128)S(1)}, u32[]{:S(2)}, u32[]{:S(2)}) collective-permute-start(f32[1,128]{1,0:T(1,128)S(1)} %add.96.refs_0_), channel_id=1, source_target_pairs={{0,6},{1,7},{2,4},{3,5},{4,2},{5,3},{6,0},{7,1},{8,14},{9,15},{10,... | collective-permute-start | bytes 1544 | tf_op jit(solution)/shard_map/ppermute | solution.py:428
  85.8 18.8 %all-to-all-start.2 = ((bf16[32,3,8,128]{3,2,1,0:T(8,128)(2,1)}), bf16[32,3,8,128]{3,2,1,0:T(8,128)(2,1)S(1)}, u32[]{:S(2)}, u32[]{:S(2)}) async-start(bf16[32,3,8,128]{3,2,1,0:T(8,128)(2,1)} %get-tuple-element.243), calls=%async_computation.2 | async-start | bytes 393216 | tf_op jit(solution)/shard_map/all_to_all | solution.py:506
  (9 other events, 96.8 us)

commit v9 on v7

--- a/solution.py
+++ b/solution.py
@@ -292,9 +292,9 @@
 
 
 def plan_body(me_ref, *refs):
-    out = refs[-1]
+    out, crowd = refs[-2:]
     me = me_ref[0]
-    blocks = jnp.concatenate([r[...] for r in refs[:-1]], 0).astype(F32)
+    blocks = jnp.concatenate([r[...] for r in refs[:-2]], 0).astype(F32)
     rel = lax.broadcasted_iota(jnp.int32, (NDOM, NDOM), 1)
     back_y = (me // 8 - rel // 8) & 3
     back_x = (me // 2 - rel // 2) & 3
@@ -347,14 +347,18 @@
     second = jnp.where(lane < 64, particle, arrived)
     row = lax.broadcasted_iota(jnp.int32, (8, HD), 0)
     out[...] = jnp.where(row == 0, line, second)
+    crowd[0] = most
 
 
 def plan(me, blocks):
     return pl.pallas_call(
         plan_body,
         in_specs=[spec(SM)] + [spec(VM)] * len(blocks),
-        out_specs=spec(VM),
-        out_shape=jax.ShapeDtypeStruct((8, HD), jnp.int32),
+        out_specs=[spec(VM), spec(SM)],
+        out_shape=[
+            jax.ShapeDtypeStruct((8, HD), jnp.int32),
+            jax.ShapeDtypeStruct((1,), jnp.int32),
+        ],
         compiler_params=limit(8),
         name="plan",
     )(me, *blocks)
@@ -405,9 +409,13 @@
         slot = jnp.minimum(code % 4, slots - 1)
         for n, out in enumerate((keys, values)):
             part = rows.at[code // 4, slot, pl.ds(n * SPAN, SPAN), :]
-            copies.append(pltpu.make_async_copy(part, out.at[k], sems.at[n, k]))
+            there = out.at[k, pl.ds(0, SPAN), :]
+            copies.append(pltpu.make_async_copy(part, there, sems.at[n, k]))
     for c in copies:
         c.start()
+    blank = jnp.zeros((NP, STEPS, HD), BF)
+    for out in (keys, values):
+        out[:, SPAN : SPAN + STEPS, :] = blank
     for c in copies:
         c.wait()
 
@@ -418,7 +426,7 @@
         lambda *refs: place_body(slots, *refs),
         in_specs=[spec(SM), spec(ANY)],
         out_specs=[spec(VM)] * 2,
-        out_shape=[jax.ShapeDtypeStruct((NP, SPAN, HD), BF)] * 2,
+        out_shape=[jax.ShapeDtypeStruct((NP, SPAN + STEPS, HD), BF)] * 2,
         scratch_shapes=[pltpu.SemaphoreType.DMA((2, NP))],
         compiler_params=limit(16),
         name="place",
@@ -495,7 +503,7 @@
     gathered = lax.all_to_all(
         jnp.broadcast_to(act[None], (TP, ROWS, DB)), "tp", 0, 0, tiled=True
     )
-    idx = plan(me, spread_counts(copy_counts))
+    idx, crowd = plan(me, spread_counts(copy_counts))
     partner_keys = swapped(cache_keys)
     partner_values = swapped(cache_values)
     packed = pack(me, idx, [cache_keys, cache_values], [partner_keys, partner_values])
@@ -541,7 +549,7 @@
         return tuple(place(idx, jnp.concatenate([rows, more[:, None]], 1)))
 
     old_keys, old_values = lax.cond(
-        idx[0, 127] > SLOTS * NDOM,
+        crowd[0] > SLOTS * NDOM,
         crowded,
         usual,
         rows,
@@ -551,7 +559,7 @@
     )
 
     def by_position(old):
-        return jnp.pad(jnp.transpose(old, (1, 0, 2)), ((0, STEPS), (0, 0), (0, 0)))
+        return jnp.transpose(old, (1, 0, 2))
 
     out_logw, new_keys, new_values = finish(
         idx, line, got, by_position(old_keys), by_position(old_values)

time: 106 us -> 107 us (level)
  waiting for transfers between devices: 15.1 us -> 23 us
  starting transfers between devices: 61 us -> 57.6 us
  local copies, waits for them, and re-layouts: 7.59 us -> 4.46 us
    all_to_all x1, waiting for transfers between devices: 1.53 us -> 5.03 us  [local(): got = lax.all_to_all(sent, 'dom', 0, 0, tiled=True)]
    ppermute x6, waiting for transfers between devices: 3.24 us -> 6.29 us  [moved(): return lax.ppermute(value, 'dom', [(i, to(i)) for i in range(NDOM)])]
    ppermute x6, starting transfers between devices: 9.87 us -> 7.45 us  [moved(): return lax.ppermute(value, 'dom', [(i, to(i)) for i in range(NDOM)])]
    pad x2 -> x0, local copies, waits for them, and re-layouts: 1.78 us -> none  [by_position(): return jnp.pad(jnp.transpose(old, (1, 0, 2)), ((0, STEPS), (0, 0), (0, 0)))]
    ppermute x10, waiting for transfers between devices: 7.68 us -> 9.15 us  [shifted(): return lax.ppermute(value, 'tp', [(i, (i + shift) % TP) for i in range(TP)])]
    all_to_all x1, starting transfers between devices: 5.8 us -> 4.63 us  [exchanged(): lax.all_to_all(rows, 'dom', 0, 0, tiled=True, axis_index_groups=SAME_CORE)]
  transfers between devices with their start and end apart: 23 -> 23, of which waited for: 11 -> 10; matrix products, arithmetic and copies ran while one was open for 6% -> 3% of each run, Pallas kernels for 16% -> 16%
where the time goes in v9:
time: 107 us; the launch traced here: 106 us
  starting transfers between devices  57.6 us (54%)
  waiting for transfers between devices  23 us (21%)
  Pallas kernels  18.7 us (17%)
  local copies, waits for them, and re-layouts  4.46 us (4%)
  between operations  1.69 us (2%)
    ppermute x10, starting transfers between devices, shifted(): return lax.ppermute(value, 'tp', [(i, (i + shift) % TP) for i in range(TP)])  19.9 us
    all_to_all x1, starting transfers between devices, local(): got = lax.all_to_all(sent, 'dom', 0, 0, tiled=True)  12.9 us
    ppermute x10, waiting for transfers between devices, shifted(): return lax.ppermute(value, 'tp', [(i, (i + shift) % TP) for i in range(TP)])  9.15 us
    all_to_all x1, starting transfers between devices, local(): lax.all_to_all(jnp.broadcast_to(act[None], (TP, ROWS, DB)), 'tp', 0, 0, t...  9.01 us
    ppermute x6, starting transfers between devices, moved(): return lax.ppermute(value, 'dom', [(i, to(i)) for i in range(NDOM)])  7.45 us
    ppermute x6, waiting for transfers between devices, moved(): return lax.ppermute(value, 'dom', [(i, to(i)) for i in range(NDOM)])  6.29 us
    all_to_all x1, waiting for transfers between devices, local(): got = lax.all_to_all(sent, 'dom', 0, 0, tiled=True)  5.03 us
    all_to_all x1, starting transfers between devices, exchanged(): lax.all_to_all(rows, 'dom', 0, 0, tiled=True, axis_index_groups=SAME_CORE)  4.63 us
  transfers between devices with their start and end apart: 23, of which 10 were waited for; matrix products, arithmetic and copies ran while one was open for 3% of the time, Pallas kernels for 16%

profile of v9, /device:TPU:1, one launch (start us, length us, event | category | flops | bytes accessed | tf_op | source)
XLA Modules:
  0.0 106.1 jit_solution(9550290119055168812)
XLA Ops:
  2.4 9.0 %all-to-all-start = ((bf16[8,64,512]{2,1,0:T(8,128)(2,1)}), bf16[8,64,512]{2,1,0:T(8,128)(2,1)S(1)}, u32[]{:S(2)}, u32[]{:S(2)}) async-start(bf16[8,64,512]{2,1,0:T(8,128)(2,1)} %broadcast_in_dim.19), calls=%async_computation | async-start | bytes 1048576 | tf_op jit(solution)/shard_map/all_to_all | solution.py:503
  12.8 2.0 %collective-permute-done.1 = s32[1,16]{1,0:T(1,128)S(1)} collective-permute-done((s32[1,16]{1,0:T(1,128)}, s32[1,16]{1,0:T(1,128)S(1)}, u32[]{:S(2)}, u32[]{:S(2)}) %collective-permute-start.1) | collective-permute-done | bytes 96 | tf_op jit(solution)/shard_map/ppermute | solution.py:445
  15.5 2.5 %collective-permute-start.4 = (s32[2,16]{1,0:T(2,128)S(1)}, s32[2,16]{1,0:T(2,128)S(1)}, u32[]{:S(2)}, u32[]{:S(2)}) collective-permute-start(s32[2,16]{1,0:T(2,128)S(1)} %pad_add_fusion), channel_id=1, source_target_pairs={{0,48},{8,56},{16,0},{24,8},{32,16},{40,24},{48,32},{56,40},{64,11... | collective-permute-start | bytes 392 | tf_op jit(solution)/shard_map/ppermute | solution.py:464
  19.1 3.1 %collective-permute-done.3 = s32[2,16]{1,0:T(2,128)S(1)} collective-permute-done((s32[2,16]{1,0:T(2,128)S(1)}, s32[2,16]{1,0:T(2,128)S(1)}, u32[]{:S(2)}, u32[]{:S(2)}) %collective-permute-start.3) | collective-permute-done | bytes 160 | tf_op jit(solution)/shard_map/ppermute | solution.py:464
  23.1 2.8 %collective-permute-start.7 = (s32[8,16]{1,0:T(8,128)S(1)}, s32[8,16]{1,0:T(8,128)S(1)}, u32[]{:S(2)}, u32[]{:S(2)}) collective-permute-start(s32[8,16]{1,0:T(8,128)S(1)} %concatenate.35.refs_0_), channel_id=1, source_target_pairs={{0,192},{8,200},{16,208},{24,216},{32,224},{40,232},{48,240},{56,2... | collective-permute-start | bytes 1544 | tf_op jit(solution)/shard_map/ppermute | solution.py:464
  26.9 2.9 %collective-permute-done.6.refs_2_ = s32[8,16]{1,0:T(8,128)S(1)} collective-permute-done((s32[8,16]{1,0:T(8,128)S(1)}, s32[8,16]{1,0:T(8,128)S(1)}, u32[]{:S(2)}, u32[]{:S(2)}) %collective-permute-start.6) | collective-permute-done | bytes 544 | tf_op jit(solution)/shard_map/ppermute | solution.py:464
  30.9 3.6 %pack.1 = bf16[16,3,256,128]{3,2,1,0:T(8,128)(2,1)} custom-call(s32[1]{0:T(128)} %bitcast.6.me_ref, s32[8,128]{1,0:T(8,128)S(1)} %get-tuple-element.219.idx, bf16[16,128,128]{2,1,0:T(8,128)(2,1)} %kc.1, bf16[16,128,128]{2,1,0:T(8,128)(2,1)} %vc.1, bf16[16,128,128]{2,1,0:T(8,128)(2,1)S(1)} %collective-permute-done.8.refs_2_, ...), custom_call_target="tpu_custom_call" | custom-call | tf_op jit(solution)/shard_map/pack/pallas_call | solution.py:391
  34.5 4.6 %all-to-all-start.1 = ((bf16[16,3,256,128]{3,2,1,0:T(8,128)(2,1)}), bf16[16,3,256,128]{3,2,1,0:T(8,128)(2,1)}, u32[]{:S(2)}, u32[]{:S(2)}) async-start(bf16[16,3,256,128]{3,2,1,0:T(8,128)(2,1)} %pack.1), calls=%async_computation.1 | async-start | bytes 6291456 | tf_op jit(solution)/shard_map/all_to_all | solution.py:456
  39.2 3.8 %project.1 = (bf16[256,128]{1,0:T(8,128)(2,1)S(1)}, bf16[64,128]{1,0:T(8,128)(2,1)S(1)}, bf16[64,128]{1,0:T(8,128)(2,1)S(1)}, bf16[16,8,128]{2,1,0:T(8,128)(2,1)S(1)}) custom-call(bf16[8,64,512]{2,1,0:T(8,128)(2,1)S(1)} %all-to-all-done.acts, f32[8,512]{1,0:T(8,128)S(1)} %reshape.194.gain, bf16[4096,512]{1,0:T(8,128)(2,1)} %wq.1, bf16[4096,128]{1,0:T(8,128)(2,1)} %wk.1, ...), custom_call_target="tpu_custom_call" | custom-call | flops 402653184 | bytes 7340032 | tf_op jit(solution)/shard_map/project/pallas_call | solution.py:100
  43.1 4.1 %attend.1 = (bf16[64,512]{1,0:T(8,128)(2,1)S(1)}, bf16[64,512]{1,0:T(8,128)(2,1)S(1)}, bf16[64,512]{1,0:T(8,128)(2,1)S(1)}, bf16[64,512]{1,0:T(8,128)(2,1)S(1)},...) custom-call(s32[8]{0:T(128)S(1)} %and_select_fusion.blk, ...), custom_call_target="tpu_custom_call" | custom-call | flops 335544320 | bytes 6291456 | tf_op jit(solution)/shard_map/attend/pallas_call | solution.py:165
  48.7 2.4 %collective-permute-start.11 = (bf16[64,512]{1,0:T(8,128)(2,1)S(1)}, bf16[64,512]{1,0:T(8,128)(2,1)S(1)}, u32[]{:S(2)}, u32[]{:S(2)}) collective-permute-start(bf16[64,512]{1,0:T(8,128)(2,1)S(1)} %get-tuple-element.234), channel_id=1, source_target_pairs={{0,2},{1,3},{2,4},{3,5},{4,6},{5,7},{6,0},{7,1},{8,10},{9,11},{10,... | collective-permute-start | bytes 196616 | tf_op jit(solution)/shard_map/ppermute | solution.py:437
  51.8 2.4 %collective-permute-start.12 = (bf16[64,512]{1,0:T(8,128)(2,1)S(1)}, bf16[64,512]{1,0:T(8,128)(2,1)S(1)}, u32[]{:S(2)}, u32[]{:S(2)}) collective-permute-start(bf16[64,512]{1,0:T(8,128)(2,1)S(1)} %get-tuple-element.235), channel_id=1, source_target_pairs={{0,3},{1,4},{2,5},{3,6},{4,7},{5,0},{6,1},{7,2},{8,11},{9,12},{10,... | collective-permute-start | bytes 196616 | tf_op jit(solution)/shard_map/ppermute | solution.py:437
  54.2 2.1 %collective-permute-start.13 = (bf16[64,512]{1,0:T(8,128)(2,1)S(1)}, bf16[64,512]{1,0:T(8,128)(2,1)S(1)}, u32[]{:S(2)}, u32[]{:S(2)}) collective-permute-start(bf16[64,512]{1,0:T(8,128)(2,1)S(1)} %get-tuple-element.236), channel_id=1, source_target_pairs={{0,4},{1,5},{2,6},{3,7},{4,0},{5,1},{6,2},{7,3},{8,12},{9,13},{10,... | collective-permute-start | bytes 196616 | tf_op jit(solution)/shard_map/ppermute | solution.py:437
  56.3 2.4 %collective-permute-start.14 = (bf16[64,512]{1,0:T(8,128)(2,1)S(1)}, bf16[64,512]{1,0:T(8,128)(2,1)S(1)}, u32[]{:S(2)}, u32[]{:S(2)}) collective-permute-start(bf16[64,512]{1,0:T(8,128)(2,1)S(1)} %get-tuple-element.237), channel_id=1, source_target_pairs={{0,5},{1,6},{2,7},{3,0},{4,1},{5,2},{6,3},{7,4},{8,13},{9,14},{10,... | collective-permute-start | bytes 196616 | tf_op jit(solution)/shard_map/ppermute | solution.py:437
  58.7 3.3 %collective-permute-start.15 = (bf16[64,512]{1,0:T(8,128)(2,1)S(1)}, bf16[64,512]{1,0:T(8,128)(2,1)S(1)}, u32[]{:S(2)}, u32[]{:S(2)}) collective-permute-start(bf16[64,512]{1,0:T(8,128)(2,1)S(1)} %get-tuple-element.238), channel_id=1, source_target_pairs={{0,6},{1,7},{2,0},{3,1},{4,2},{5,3},{6,4},{7,5},{8,14},{9,15},{10,... | collective-permute-start | bytes 196616 | tf_op jit(solution)/shard_map/ppermute | solution.py:437
  63.2 2.7 %collective-permute-done.15.refs_6_ = bf16[64,512]{1,0:T(8,128)(2,1)S(1)} collective-permute-done((bf16[64,512]{1,0:T(8,128)(2,1)S(1)}, bf16[64,512]{1,0:T(8,128)(2,1)S(1)}, u32[]{:S(2)}, u32[]{:S(2)}) %collective-permute-start.15) | collective-permute-done | bytes 65568 | tf_op jit(solution)/shard_map/ppermute | solution.py:437
  65.9 2.6 %collective-permute-done.16.refs_7_ = bf16[64,512]{1,0:T(8,128)(2,1)S(1)} collective-permute-done((bf16[64,512]{1,0:T(8,128)(2,1)S(1)}, bf16[64,512]{1,0:T(8,128)(2,1)S(1)}, u32[]{:S(2)}, u32[]{:S(2)}) %collective-permute-start.16) | collective-permute-done | bytes 65568 | tf_op jit(solution)/shard_map/ppermute | solution.py:437
  69.2 2.2 %collective-permute-start.17 = (f32[1,128]{1,0:T(1,128)S(1)}, f32[1,128]{1,0:T(1,128)S(1)}, u32[]{:S(2)}, u32[]{:S(2)}) collective-permute-start(f32[1,128]{1,0:T(1,128)S(1)} %get-tuple-element.241), channel_id=1, source_target_pairs={{0,1},{1,0},{2,3},{3,2},{4,5},{5,4},{6,7},{7,6},{8,9},{9,8},{10,11... | collective-permute-start | bytes 1544 | tf_op jit(solution)/shard_map/ppermute | solution.py:441
  77.4 3.9 %collective-permute-done.19.refs_2_ = f32[1,128]{1,0:T(1,128)S(1)} collective-permute-done((f32[1,128]{1,0:T(1,128)S(1)}, f32[1,128]{1,0:T(1,128)S(1)}, u32[]{:S(2)}, u32[]{:S(2)}) %collective-permute-start.19) | collective-permute-done | bytes 544 | tf_op jit(solution)/shard_map/ppermute | solution.py:437
  82.7 12.9 %all-to-all-start.2 = ((bf16[32,3,8,128]{3,2,1,0:T(8,128)(2,1)}), bf16[32,3,8,128]{3,2,1,0:T(8,128)(2,1)S(1)}, u32[]{:S(2)}, u32[]{:S(2)}) async-start(bf16[32,3,8,128]{3,2,1,0:T(8,128)(2,1)} %get-tuple-element.246), calls=%async_computation.2 | async-start | bytes 393216 | tf_op jit(solution)/shard_map/all_to_all | solution.py:527
  95.6 2.1 %conditional.1 = ((bf16[16,132,128]{2,1,0:T(8,128)(2,1)S(1)}, bf16[16,132,128]{2,1,0:T(8,128)(2,1)S(1)})) conditional(s32[]{:T(128)} %bitcast.14, (s32[8,128]{1,0:T(8,128)S(1)}, bf16[16,3,256,128]{3,2,1,0:T(8,128)(2,1)}) %tuple.54, (s32[]{:T(128)}, bf16[16,128,128]{2,1,0:T(8,128)(2,1)S(1)}, bf16[16,128,128]{2,1,0:T(8,128)(2,1)S(1)}, ...), branch_computations={%region_0.1_spmd, %region_1.6_spmd} | conditional | flops 4260986 | bytes 36051572 | solution.py:551
  95.6 2.1 %place.2 = (bf16[16,132,128]{2,1,0:T(8,128)(2,1)S(1)}, bf16[16,132,128]{2,1,0:T(8,128)(2,1)S(1)}) custom-call(s32[8,128]{1,0:T(8,128)S(1)} %get-tuple-element.164.refs_0_, bf16[16,3,256,128]{3,2,1,0:T(8,128)(2,1)} %get-tuple-element.165.refs_1_), custom_call_target="tpu_custom_call" | custom-call | tf_op jit(solution)/shard_map/cond/branch_0_fun/place/pallas_call | solution.py:425
  98.9 5.0 %all-to-all-done.2.got = bf16[32,3,8,128]{3,2,1,0:T(8,128)(2,1)S(1)} async-done(((bf16[32,3,8,128]{3,2,1,0:T(8,128)(2,1)}), bf16[32,3,8,128]{3,2,1,0:T(8,128)(2,1)S(1)}, u32[]{:S(2)}, u32[]{:S(2)}) %all-to-all-start.2) | async-done | bytes 196640 | tf_op jit(solution)/shard_map/all_to_all | solution.py:527
  103.9 2.0 %finish.1 = (f32[1,16]{1,0:T(1,128)}, bf16[132,16,128]{2,1,0:T(8,128)(2,1)}, bf16[132,16,128]{2,1,0:T(8,128)(2,1)}) custom-call(s32[8,128]{1,0:T(8,128)S(1)} %get-tuple-element.219.idx, f32[1,128]{1,0:T(1,128)S(1)} %get-tuple-element.244.line, bf16[32,3,8,128]{3,2,1,0:T(8,128)(2,1)S(1)} %all-to-all-done.2.got, ...), custom_call_target="tpu_custom_call", output_to_operand_aliasing={{1}: (3, {}), {2}: (4, {})} | custom-call | tf_op jit(solution)/shard_map/finish/pallas_call | solution.py:276
  (62 shorter events, 20.1 us)
Async XLA Ops:
  0.6 70.8 %copy-start = (bf16[128256]{0:T(1024)(128)(2,1)S(1)}, bf16[128256]{0:T(1024)(128)(2,1)}, u32[]{:S(2)}) copy-start(bf16[128256]{0:T(1024)(128)(2,1)} %param.32) | copy-start | bytes 769540
  2.4 32.1 %all-to-all-start = ((bf16[8,64,512]{2,1,0:T(8,128)(2,1)}), bf16[8,64,512]{2,1,0:T(8,128)(2,1)S(1)}, u32[]{:S(2)}, u32[]{:S(2)}) async-start(bf16[8,64,512]{2,1,0:T(8,128)(2,1)} %broadcast_in_dim.19), calls=%async_computation | async-start | bytes 1048576 | tf_op jit(solution)/shard_map/all_to_all | solution.py:503
  11.4 19.5 %collective-permute-start.8 = (bf16[16,128,128]{2,1,0:T(8,128)(2,1)}, bf16[16,128,128]{2,1,0:T(8,128)(2,1)S(1)}, u32[]{:S(2)}, u32[]{:S(2)}) collective-permute-start(bf16[16,128,128]{2,1,0:T(8,128)(2,1)} %kc.1), channel_id=1, source_target_pairs={{0,8},{8,0},{16,24},{24,16},{32,40},{40,32},{48,56},{56,48},{64,72... | collective-permute-start | bytes 1572872 | tf_op jit(solution)/shard_map/ppermute | solution.py:445
  12.3 18.5 %collective-permute-start.9 = (bf16[16,128,128]{2,1,0:T(8,128)(2,1)}, bf16[16,128,128]{2,1,0:T(8,128)(2,1)S(1)}, u32[]{:S(2)}, u32[]{:S(2)}) collective-permute-start(bf16[16,128,128]{2,1,0:T(8,128)(2,1)} %vc.1), channel_id=1, source_target_pairs={{0,8},{8,0},{16,24},{24,16},{32,40},{40,32},{48,56},{56,48},{64,72... | collective-permute-start | bytes 1572872 | tf_op jit(solution)/shard_map/ppermute | solution.py:445
  12.4 2.4 %collective-permute-start.1 = (s32[1,16]{1,0:T(1,128)}, s32[1,16]{1,0:T(1,128)S(1)}, u32[]{:S(2)}, u32[]{:S(2)}) collective-permute-start(s32[1,16]{1,0:T(1,128)} %bitcast.37), channel_id=1, source_target_pairs={{0,8},{8,0},{16,24},{24,16},{32,40},{40,32},{48,56},{56,48},{64,72... | collective-permute-start | bytes 200 | tf_op jit(solution)/shard_map/ppermute | solution.py:445
  15.5 3.6 %collective-permute-start.4 = (s32[2,16]{1,0:T(2,128)S(1)}, s32[2,16]{1,0:T(2,128)S(1)}, u32[]{:S(2)}, u32[]{:S(2)}) collective-permute-start(s32[2,16]{1,0:T(2,128)S(1)} %pad_add_fusion), channel_id=1, source_target_pairs={{0,48},{8,56},{16,0},{24,8},{32,16},{40,24},{48,32},{56,40},{64,11... | collective-permute-start | bytes 392 | tf_op jit(solution)/shard_map/ppermute | solution.py:464
  18.0 4.2 %collective-permute-start.3 = (s32[2,16]{1,0:T(2,128)S(1)}, s32[2,16]{1,0:T(2,128)S(1)}, u32[]{:S(2)}, u32[]{:S(2)}) collective-permute-start(s32[2,16]{1,0:T(2,128)S(1)} %pad_add_fusion), channel_id=1, source_target_pairs={{0,32},{8,40},{16,48},{24,56},{32,0},{40,8},{48,16},{56,24},{64,96... | collective-permute-start | bytes 392 | tf_op jit(solution)/shard_map/ppermute | solution.py:464
  18.5 3.9 %collective-permute-start.2 = (s32[2,16]{1,0:T(2,128)S(1)}, s32[2,16]{1,0:T(2,128)S(1)}, u32[]{:S(2)}, u32[]{:S(2)}) collective-permute-start(s32[2,16]{1,0:T(2,128)S(1)} %pad_add_fusion), channel_id=1, source_target_pairs={{0,16},{8,24},{16,32},{24,40},{32,48},{40,56},{48,0},{56,8},{64,80... | collective-permute-start | bytes 392 | tf_op jit(solution)/shard_map/ppermute | solution.py:464
  23.1 3.9 %collective-permute-start.7 = (s32[8,16]{1,0:T(8,128)S(1)}, s32[8,16]{1,0:T(8,128)S(1)}, u32[]{:S(2)}, u32[]{:S(2)}) collective-permute-start(s32[8,16]{1,0:T(8,128)S(1)} %concatenate.35.refs_0_), channel_id=1, source_target_pairs={{0,192},{8,200},{16,208},{24,216},{32,224},{40,232},{48,240},{56,2... | collective-permute-start | bytes 1544 | tf_op jit(solution)/shard_map/ppermute | solution.py:464
  25.9 4.0 %collective-permute-start.6 = (s32[8,16]{1,0:T(8,128)S(1)}, s32[8,16]{1,0:T(8,128)S(1)}, u32[]{:S(2)}, u32[]{:S(2)}) collective-permute-start(s32[8,16]{1,0:T(8,128)S(1)} %concatenate.35.refs_0_), channel_id=1, source_target_pairs={{0,128},{8,136},{16,144},{24,152},{32,160},{40,168},{48,176},{56,1... | collective-permute-start | bytes 1544 | tf_op jit(solution)/shard_map/ppermute | solution.py:464
  26.3 3.7 %collective-permute-start.5 = (s32[8,16]{1,0:T(8,128)S(1)}, s32[8,16]{1,0:T(8,128)S(1)}, u32[]{:S(2)}, u32[]{:S(2)}) collective-permute-start(s32[8,16]{1,0:T(8,128)S(1)} %concatenate.35.refs_0_), channel_id=1, source_target_pairs={{0,64},{8,72},{16,80},{24,88},{32,96},{40,104},{48,112},{56,120},{... | collective-permute-start | bytes 1544 | tf_op jit(solution)/shard_map/ppermute | solution.py:464
  34.5 48.2 %all-to-all-start.1 = ((bf16[16,3,256,128]{3,2,1,0:T(8,128)(2,1)}), bf16[16,3,256,128]{3,2,1,0:T(8,128)(2,1)}, u32[]{:S(2)}, u32[]{:S(2)}) async-start(bf16[16,3,256,128]{3,2,1,0:T(8,128)(2,1)} %pack.1), calls=%async_computation.1 | async-start | bytes 6291456 | tf_op jit(solution)/shard_map/all_to_all | solution.py:456
  47.2 11.5 %collective-permute-start.10 = (bf16[64,512]{1,0:T(8,128)(2,1)S(1)}, bf16[64,512]{1,0:T(8,128)(2,1)S(1)}, u32[]{:S(2)}, u32[]{:S(2)}) collective-permute-start(bf16[64,512]{1,0:T(8,128)(2,1)S(1)} %get-tuple-element.233), channel_id=1, source_target_pairs={{0,1},{1,2},{2,3},{3,4},{4,5},{5,6},{6,7},{7,0},{8,9},{9,10},{10,1... | collective-permute-start | bytes 196616 | tf_op jit(solution)/shard_map/ppermute | solution.py:437
  48.7 13.3 %collective-permute-start.11 = (bf16[64,512]{1,0:T(8,128)(2,1)S(1)}, bf16[64,512]{1,0:T(8,128)(2,1)S(1)}, u32[]{:S(2)}, u32[]{:S(2)}) collective-permute-start(bf16[64,512]{1,0:T(8,128)(2,1)S(1)} %get-tuple-element.234), channel_id=1, source_target_pairs={{0,2},{1,3},{2,4},{3,5},{4,6},{5,7},{6,0},{7,1},{8,10},{9,11},{10,... | collective-permute-start | bytes 196616 | tf_op jit(solution)/shard_map/ppermute | solution.py:437
  51.8 11.4 %collective-permute-start.12 = (bf16[64,512]{1,0:T(8,128)(2,1)S(1)}, bf16[64,512]{1,0:T(8,128)(2,1)S(1)}, u32[]{:S(2)}, u32[]{:S(2)}) collective-permute-start(bf16[64,512]{1,0:T(8,128)(2,1)S(1)} %get-tuple-element.235), channel_id=1, source_target_pairs={{0,3},{1,4},{2,5},{3,6},{4,7},{5,0},{6,1},{7,2},{8,11},{9,12},{10,... | collective-permute-start | bytes 196616 | tf_op jit(solution)/shard_map/ppermute | solution.py:437
  54.2 9.0 %collective-permute-start.13 = (bf16[64,512]{1,0:T(8,128)(2,1)S(1)}, bf16[64,512]{1,0:T(8,128)(2,1)S(1)}, u32[]{:S(2)}, u32[]{:S(2)}) collective-permute-start(bf16[64,512]{1,0:T(8,128)(2,1)S(1)} %get-tuple-element.236), channel_id=1, source_target_pairs={{0,4},{1,5},{2,6},{3,7},{4,0},{5,1},{6,2},{7,3},{8,12},{9,13},{10,... | collective-permute-start | bytes 196616 | tf_op jit(solution)/shard_map/ppermute | solution.py:437
  56.3 6.9 %collective-permute-start.14 = (bf16[64,512]{1,0:T(8,128)(2,1)S(1)}, bf16[64,512]{1,0:T(8,128)(2,1)S(1)}, u32[]{:S(2)}, u32[]{:S(2)}) collective-permute-start(bf16[64,512]{1,0:T(8,128)(2,1)S(1)} %get-tuple-element.237), channel_id=1, source_target_pairs={{0,5},{1,6},{2,7},{3,0},{4,1},{5,2},{6,3},{7,4},{8,13},{9,14},{10,... | collective-permute-start | bytes 196616 | tf_op jit(solution)/shard_map/ppermute | solution.py:437
  58.7 7.2 %collective-permute-start.15 = (bf16[64,512]{1,0:T(8,128)(2,1)S(1)}, bf16[64,512]{1,0:T(8,128)(2,1)S(1)}, u32[]{:S(2)}, u32[]{:S(2)}) collective-permute-start(bf16[64,512]{1,0:T(8,128)(2,1)S(1)} %get-tuple-element.238), channel_id=1, source_target_pairs={{0,6},{1,7},{2,0},{3,1},{4,2},{5,3},{6,4},{7,5},{8,14},{9,15},{10,... | collective-permute-start | bytes 196616 | tf_op jit(solution)/shard_map/ppermute | solution.py:437
  62.0 6.5 %collective-permute-start.16 = (bf16[64,512]{1,0:T(8,128)(2,1)S(1)}, bf16[64,512]{1,0:T(8,128)(2,1)S(1)}, u32[]{:S(2)}, u32[]{:S(2)}) collective-permute-start(bf16[64,512]{1,0:T(8,128)(2,1)S(1)} %get-tuple-element.239), channel_id=1, source_target_pairs={{0,7},{1,0},{2,1},{3,2},{4,3},{5,4},{6,5},{7,6},{8,15},{9,8},{10,9... | collective-permute-start | bytes 196616 | tf_op jit(solution)/shard_map/ppermute | solution.py:437
  69.2 3.5 %collective-permute-start.17 = (f32[1,128]{1,0:T(1,128)S(1)}, f32[1,128]{1,0:T(1,128)S(1)}, u32[]{:S(2)}, u32[]{:S(2)}) collective-permute-start(f32[1,128]{1,0:T(1,128)S(1)} %get-tuple-element.241), channel_id=1, source_target_pairs={{0,1},{1,0},{2,3},{3,2},{4,5},{5,4},{6,7},{7,6},{8,9},{9,8},{10,11... | collective-permute-start | bytes 1544 | tf_op jit(solution)/shard_map/ppermute | solution.py:441
  72.7 4.7 %collective-permute-start.20 = (f32[1,128]{1,0:T(1,128)S(1)}, f32[1,128]{1,0:T(1,128)S(1)}, u32[]{:S(2)}, u32[]{:S(2)}) collective-permute-start(f32[1,128]{1,0:T(1,128)S(1)} %add.107.refs_0_), channel_id=1, source_target_pairs={{0,6},{1,7},{2,0},{3,1},{4,2},{5,3},{6,4},{7,5},{8,14},{9,15},{10,... | collective-permute-start | bytes 1544 | tf_op jit(solution)/shard_map/ppermute | solution.py:437
  74.6 6.7 %collective-permute-start.19 = (f32[1,128]{1,0:T(1,128)S(1)}, f32[1,128]{1,0:T(1,128)S(1)}, u32[]{:S(2)}, u32[]{:S(2)}) collective-permute-start(f32[1,128]{1,0:T(1,128)S(1)} %add.107.refs_0_), channel_id=1, source_target_pairs={{0,4},{1,5},{2,6},{3,7},{4,0},{5,1},{6,2},{7,3},{8,12},{9,13},{10,... | collective-permute-start | bytes 1544 | tf_op jit(solution)/shard_map/ppermute | solution.py:437
  76.2 5.1 %collective-permute-start.18 = (f32[1,128]{1,0:T(1,128)S(1)}, f32[1,128]{1,0:T(1,128)S(1)}, u32[]{:S(2)}, u32[]{:S(2)}) collective-permute-start(f32[1,128]{1,0:T(1,128)S(1)} %add.107.refs_0_), channel_id=1, source_target_pairs={{0,2},{1,3},{2,4},{3,5},{4,6},{5,7},{6,0},{7,1},{8,10},{9,11},{10,... | collective-permute-start | bytes 1544 | tf_op jit(solution)/shard_map/ppermute | solution.py:437
  82.7 21.2 %all-to-all-start.2 = ((bf16[32,3,8,128]{3,2,1,0:T(8,128)(2,1)}), bf16[32,3,8,128]{3,2,1,0:T(8,128)(2,1)S(1)}, u32[]{:S(2)}, u32[]{:S(2)}) async-start(bf16[32,3,8,128]{3,2,1,0:T(8,128)(2,1)} %get-tuple-element.246), calls=%async_computation.2 | async-start | bytes 393216 | tf_op jit(solution)/shard_map/all_to_all | solution.py:527
  (8 other events, 84.8 us)

commit v10 on v9

--- a/solution.py
+++ b/solution.py
@@ -14,6 +14,7 @@
 SPAN = 128
 TP = 8
 PAIRS = TP // 2
+FAR_FIRST = (4, 3, 5, 2, 6, 1, 7)
 DB = D // TP
 HEADS = DB // HD
 GROUP = HEADS * STEPS
@@ -467,8 +468,10 @@
 def spread_counts(copy_counts):
     own = copy_counts.reshape(1, NP)
     chip = jnp.concatenate([own, swapped(own)], 0)
-    row = jnp.concatenate([chip] + [moved(chip, 2, s) for s in range(1, 4)], 0)
-    return [row] + [moved(row, 8, s) for s in range(1, 4)]
+    far, near, back = [moved(chip, 2, s) for s in (2, 1, 3)]
+    row = jnp.concatenate([chip, near, far, back], 0)
+    far, near, back = [moved(row, 8, s) for s in (2, 1, 3)]
+    return [row, near, far, back]
 
 
 def rotation_table():
@@ -518,10 +521,10 @@
     reward = twisting_table[tokens.reshape(ROWS)].astype(F32)
     reward = jnp.pad(reward, (0, HD - ROWS)).reshape(1, HD)
     previous = jnp.pad(previous_log_weights, (0, HD - NP)).reshape(1, HD)
-    parts = [partials[0]] + [shifted(partials[s], s) for s in range(1, TP)]
+    parts = [partials[0]] + [shifted(partials[s], s) for s in FAR_FIRST]
     attn, sums = mix(parts, act, twist_vec.reshape(1, DB))
     sums = sums + z_swapped(sums)
-    all_sums = [sums] + [shifted(sums, 2 * s) for s in range(1, PAIRS)]
+    all_sums = [sums] + [shifted(sums, s) for s in (4, 2, 6)]
     line, sent = weigh(idx, all_sums, reward, previous, fresh)
     sent, rows = lax.optimization_barrier((sent, rows))
     got = lax.all_to_all(sent, "dom", 0, 0, tiled=True)

time: 107 us -> 106 us (level)
    ppermute x10, waiting for transfers between devices: 9.15 us -> 6.72 us  [shifted(): return lax.ppermute(value, 'tp', [(i, (i + shift) % TP) for i in range(TP)])]
    ppermute x1, starting transfers between devices: 2.17 us -> 0.01 us  [z_swapped(): return lax.ppermute(value, 'tp', [(i, i ^ 1) for i in range(TP)])]
    all_to_all x1, starting transfers between devices: 12.9 us -> 14.4 us  [local(): got = lax.all_to_all(sent, 'dom', 0, 0, tiled=True)]
    ppermute x1, waiting for transfers between devices: 0.52 us -> 1.97 us  [z_swapped(): return lax.ppermute(value, 'tp', [(i, i ^ 1) for i in range(TP)])]
    ppermute x10, starting transfers between devices: 19.9 us -> 21.3 us  [shifted(): return lax.ppermute(value, 'tp', [(i, (i + shift) % TP) for i in range(TP)])]
  transfers between devices with their start and end apart: 23 -> 23, of which waited for: 10 -> 12; matrix products, arithmetic and copies ran while one was open for 3% -> 3% of each run, Pallas kernels for 16% -> 16%
where the time goes in v10:
time: 106 us
  starting transfers between devices  58.3 us (55%)
  waiting for transfers between devices  22 us (21%)
  Pallas kernels  18.7 us (18%)
  local copies, waits for them, and re-layouts  4.46 us (4%)
  between operations  1.69 us (2%)
    ppermute x10, starting transfers between devices, shifted(): return lax.ppermute(value, 'tp', [(i, (i + shift) % TP) for i in range(TP)])  21.3 us
    all_to_all x1, starting transfers between devices, local(): got = lax.all_to_all(sent, 'dom', 0, 0, tiled=True)  14.4 us
    all_to_all x1, starting transfers between devices, local(): lax.all_to_all(jnp.broadcast_to(act[None], (TP, ROWS, DB)), 'tp', 0, 0, t...  9.01 us
    ppermute x6, starting transfers between devices, moved(): return lax.ppermute(value, 'dom', [(i, to(i)) for i in range(NDOM)])  7.45 us
    ppermute x10, waiting for transfers between devices, shifted(): return lax.ppermute(value, 'tp', [(i, (i + shift) % TP) for i in range(TP)])  6.72 us
    ppermute x6, waiting for transfers between devices, moved(): return lax.ppermute(value, 'dom', [(i, to(i)) for i in range(NDOM)])  6.29 us
    all_to_all x1, waiting for transfers between devices, local(): got = lax.all_to_all(sent, 'dom', 0, 0, tiled=True)  5.03 us
    all_to_all x1, starting transfers between devices, exchanged(): lax.all_to_all(rows, 'dom', 0, 0, tiled=True, axis_index_groups=SAME_CORE)  4.63 us
  transfers between devices with their start and end apart: 23, of which 12 were waited for; matrix products, arithmetic and copies ran while one was open for 3% of the time, Pallas kernels for 16%

profile of v10, /device:TPU:1, one launch (start us, length us, event | category | flops | bytes accessed | tf_op | source)
XLA Modules:
  0.0 105.8 jit_solution(9552151581877391393)
XLA Ops:
  2.4 9.0 %all-to-all-start = ((bf16[8,64,512]{2,1,0:T(8,128)(2,1)}), bf16[8,64,512]{2,1,0:T(8,128)(2,1)S(1)}, u32[]{:S(2)}, u32[]{:S(2)}) async-start(bf16[8,64,512]{2,1,0:T(8,128)(2,1)} %broadcast_in_dim.19), calls=%async_computation | async-start | bytes 1048576 | tf_op jit(solution)/shard_map/all_to_all | solution.py:506
  12.8 2.0 %collective-permute-done.1 = s32[1,16]{1,0:T(1,128)S(1)} collective-permute-done((s32[1,16]{1,0:T(1,128)}, s32[1,16]{1,0:T(1,128)S(1)}, u32[]{:S(2)}, u32[]{:S(2)}) %collective-permute-start.1) | collective-permute-done | bytes 96 | tf_op jit(solution)/shard_map/ppermute | solution.py:446
  15.5 2.5 %collective-permute-start.4 = (s32[2,16]{1,0:T(2,128)S(1)}, s32[2,16]{1,0:T(2,128)S(1)}, u32[]{:S(2)}, u32[]{:S(2)}) collective-permute-start(s32[2,16]{1,0:T(2,128)S(1)} %pad_add_fusion), channel_id=1, source_target_pairs={{0,48},{8,56},{16,0},{24,8},{32,16},{40,24},{48,32},{56,40},{64,11... | collective-permute-start | bytes 392 | tf_op jit(solution)/shard_map/ppermute | solution.py:465
  19.1 3.1 %collective-permute-done.3 = s32[2,16]{1,0:T(2,128)S(1)} collective-permute-done((s32[2,16]{1,0:T(2,128)S(1)}, s32[2,16]{1,0:T(2,128)S(1)}, u32[]{:S(2)}, u32[]{:S(2)}) %collective-permute-start.3) | collective-permute-done | bytes 160 | tf_op jit(solution)/shard_map/ppermute | solution.py:465
  23.1 2.8 %collective-permute-start.7 = (s32[8,16]{1,0:T(8,128)S(1)}, s32[8,16]{1,0:T(8,128)S(1)}, u32[]{:S(2)}, u32[]{:S(2)}) collective-permute-start(s32[8,16]{1,0:T(8,128)S(1)} %concatenate.35.refs_0_), channel_id=1, source_target_pairs={{0,192},{8,200},{16,208},{24,216},{32,224},{40,232},{48,240},{56,2... | collective-permute-start | bytes 1544 | tf_op jit(solution)/shard_map/ppermute | solution.py:465
  26.9 2.9 %collective-permute-done.6.refs_2_ = s32[8,16]{1,0:T(8,128)S(1)} collective-permute-done((s32[8,16]{1,0:T(8,128)S(1)}, s32[8,16]{1,0:T(8,128)S(1)}, u32[]{:S(2)}, u32[]{:S(2)}) %collective-permute-start.6) | collective-permute-done | bytes 544 | tf_op jit(solution)/shard_map/ppermute | solution.py:465
  30.9 3.6 %pack.1 = bf16[16,3,256,128]{3,2,1,0:T(8,128)(2,1)} custom-call(s32[1]{0:T(128)} %bitcast.6.me_ref, s32[8,128]{1,0:T(8,128)S(1)} %get-tuple-element.219.idx, bf16[16,128,128]{2,1,0:T(8,128)(2,1)} %kc.1, bf16[16,128,128]{2,1,0:T(8,128)(2,1)} %vc.1, bf16[16,128,128]{2,1,0:T(8,128)(2,1)S(1)} %collective-permute-done.8.refs_2_, ...), custom_call_target="tpu_custom_call" | custom-call | tf_op jit(solution)/shard_map/pack/pallas_call | solution.py:392
  34.5 4.6 %all-to-all-start.1 = ((bf16[16,3,256,128]{3,2,1,0:T(8,128)(2,1)}), bf16[16,3,256,128]{3,2,1,0:T(8,128)(2,1)}, u32[]{:S(2)}, u32[]{:S(2)}) async-start(bf16[16,3,256,128]{3,2,1,0:T(8,128)(2,1)} %pack.1), calls=%async_computation.1 | async-start | bytes 6291456 | tf_op jit(solution)/shard_map/all_to_all | solution.py:457
  39.2 3.8 %project.1 = (bf16[256,128]{1,0:T(8,128)(2,1)S(1)}, bf16[64,128]{1,0:T(8,128)(2,1)S(1)}, bf16[64,128]{1,0:T(8,128)(2,1)S(1)}, bf16[16,8,128]{2,1,0:T(8,128)(2,1)S(1)}) custom-call(bf16[8,64,512]{2,1,0:T(8,128)(2,1)S(1)} %all-to-all-done.acts, f32[8,512]{1,0:T(8,128)S(1)} %reshape.194.gain, bf16[4096,512]{1,0:T(8,128)(2,1)} %wq.1, bf16[4096,128]{1,0:T(8,128)(2,1)} %wk.1, ...), custom_call_target="tpu_custom_call" | custom-call | flops 402653184 | bytes 7340032 | tf_op jit(solution)/shard_map/project/pallas_call | solution.py:101
  43.1 4.1 %attend.1 = (bf16[64,512]{1,0:T(8,128)(2,1)S(1)}, bf16[64,512]{1,0:T(8,128)(2,1)S(1)}, bf16[64,512]{1,0:T(8,128)(2,1)S(1)}, bf16[64,512]{1,0:T(8,128)(2,1)S(1)},...) custom-call(s32[8]{0:T(128)S(1)} %and_select_fusion.blk, ...), custom_call_target="tpu_custom_call" | custom-call | flops 335544320 | bytes 6291456 | tf_op jit(solution)/shard_map/attend/pallas_call | solution.py:166
  47.2 5.7 %collective-permute-start.10 = (bf16[64,512]{1,0:T(8,128)(2,1)S(1)}, bf16[64,512]{1,0:T(8,128)(2,1)S(1)}, u32[]{:S(2)}, u32[]{:S(2)}) collective-permute-start(bf16[64,512]{1,0:T(8,128)(2,1)S(1)} %get-tuple-element.233), channel_id=1, source_target_pairs={{0,4},{1,5},{2,6},{3,7},{4,0},{5,1},{6,2},{7,3},{8,12},{9,13},{10,... | collective-permute-start | bytes 196616 | tf_op jit(solution)/shard_map/ppermute | solution.py:438
  53.9 4.2 %collective-permute-start.12 = (bf16[64,512]{1,0:T(8,128)(2,1)S(1)}, bf16[64,512]{1,0:T(8,128)(2,1)S(1)}, u32[]{:S(2)}, u32[]{:S(2)}) collective-permute-start(bf16[64,512]{1,0:T(8,128)(2,1)S(1)} %get-tuple-element.235), channel_id=1, source_target_pairs={{0,5},{1,6},{2,7},{3,0},{4,1},{5,2},{6,3},{7,4},{8,13},{9,14},{10,... | collective-permute-start | bytes 196616 | tf_op jit(solution)/shard_map/ppermute | solution.py:438
  58.4 3.3 %collective-permute-start.14 = (bf16[64,512]{1,0:T(8,128)(2,1)S(1)}, bf16[64,512]{1,0:T(8,128)(2,1)S(1)}, u32[]{:S(2)}, u32[]{:S(2)}) collective-permute-start(bf16[64,512]{1,0:T(8,128)(2,1)S(1)} %get-tuple-element.237), channel_id=1, source_target_pairs={{0,6},{1,7},{2,0},{3,1},{4,2},{5,3},{6,4},{7,5},{8,14},{9,15},{10,... | collective-permute-start | bytes 196616 | tf_op jit(solution)/shard_map/ppermute | solution.py:438
  62.0 2.4 %collective-permute-start.16 = (bf16[64,512]{1,0:T(8,128)(2,1)S(1)}, bf16[64,512]{1,0:T(8,128)(2,1)S(1)}, u32[]{:S(2)}, u32[]{:S(2)}) collective-permute-start(bf16[64,512]{1,0:T(8,128)(2,1)S(1)} %get-tuple-element.239), channel_id=1, source_target_pairs={{0,7},{1,0},{2,1},{3,2},{4,3},{5,4},{6,5},{7,6},{8,15},{9,8},{10,9... | collective-permute-start | bytes 196616 | tf_op jit(solution)/shard_map/ppermute | solution.py:438
  68.5 2.0 %collective-permute-done.17 = f32[1,128]{1,0:T(1,128)S(1)} collective-permute-done((f32[1,128]{1,0:T(1,128)S(1)}, f32[1,128]{1,0:T(1,128)S(1)}, u32[]{:S(2)}, u32[]{:S(2)}) %collective-permute-start.17) | collective-permute-done | bytes 544 | tf_op jit(solution)/shard_map/ppermute | solution.py:442
  70.4 2.8 %collective-permute-start.20 = (f32[1,128]{1,0:T(1,128)S(1)}, f32[1,128]{1,0:T(1,128)S(1)}, u32[]{:S(2)}, u32[]{:S(2)}) collective-permute-start(f32[1,128]{1,0:T(1,128)S(1)} %add.107.refs_0_), channel_id=1, source_target_pairs={{0,6},{1,7},{2,0},{3,1},{4,2},{5,3},{6,4},{7,5},{8,14},{9,15},{10,... | collective-permute-start | bytes 1544 | tf_op jit(solution)/shard_map/ppermute | solution.py:438
  73.2 2.1 %collective-permute-start.18 = (f32[1,128]{1,0:T(1,128)S(1)}, f32[1,128]{1,0:T(1,128)S(1)}, u32[]{:S(2)}, u32[]{:S(2)}) collective-permute-start(f32[1,128]{1,0:T(1,128)S(1)} %add.107.refs_0_), channel_id=1, source_target_pairs={{0,4},{1,5},{2,6},{3,7},{4,0},{5,1},{6,2},{7,3},{8,12},{9,13},{10,... | collective-permute-start | bytes 1544 | tf_op jit(solution)/shard_map/ppermute | solution.py:438
  75.3 2.4 %collective-permute-done.19.refs_2_ = f32[1,128]{1,0:T(1,128)S(1)} collective-permute-done((f32[1,128]{1,0:T(1,128)S(1)}, f32[1,128]{1,0:T(1,128)S(1)}, u32[]{:S(2)}, u32[]{:S(2)}) %collective-permute-start.19) | collective-permute-done | bytes 544 | tf_op jit(solution)/shard_map/ppermute | solution.py:438
  77.7 1.8 %collective-permute-done.18.refs_1_ = f32[1,128]{1,0:T(1,128)S(1)} collective-permute-done((f32[1,128]{1,0:T(1,128)S(1)}, f32[1,128]{1,0:T(1,128)S(1)}, u32[]{:S(2)}, u32[]{:S(2)}) %collective-permute-start.18) | collective-permute-done | bytes 544 | tf_op jit(solution)/shard_map/ppermute | solution.py:438
  81.0 14.4 %all-to-all-start.2 = ((bf16[32,3,8,128]{3,2,1,0:T(8,128)(2,1)}), bf16[32,3,8,128]{3,2,1,0:T(8,128)(2,1)S(1)}, u32[]{:S(2)}, u32[]{:S(2)}) async-start(bf16[32,3,8,128]{3,2,1,0:T(8,128)(2,1)} %get-tuple-element.246), calls=%async_computation.2 | async-start | bytes 393216 | tf_op jit(solution)/shard_map/all_to_all | solution.py:530
  95.4 2.1 %conditional.1 = ((bf16[16,132,128]{2,1,0:T(8,128)(2,1)S(1)}, bf16[16,132,128]{2,1,0:T(8,128)(2,1)S(1)})) conditional(s32[]{:T(128)} %bitcast.14, (s32[8,128]{1,0:T(8,128)S(1)}, bf16[16,3,256,128]{3,2,1,0:T(8,128)(2,1)}) %tuple.54, (s32[]{:T(128)}, bf16[16,128,128]{2,1,0:T(8,128)(2,1)S(1)}, bf16[16,128,128]{2,1,0:T(8,128)(2,1)S(1)}, ...), branch_computations={%region_0.1_spmd, %region_1.6_spmd} | conditional | flops 4260986 | bytes 36051572 | solution.py:554
  95.4 2.1 %place.2 = (bf16[16,132,128]{2,1,0:T(8,128)(2,1)S(1)}, bf16[16,132,128]{2,1,0:T(8,128)(2,1)S(1)}) custom-call(s32[8,128]{1,0:T(8,128)S(1)} %get-tuple-element.164.refs_0_, bf16[16,3,256,128]{3,2,1,0:T(8,128)(2,1)} %get-tuple-element.165.refs_1_), custom_call_target="tpu_custom_call" | custom-call | tf_op jit(solution)/shard_map/cond/branch_0_fun/place/pallas_call | solution.py:426
  98.6 5.0 %all-to-all-done.2.got = bf16[32,3,8,128]{3,2,1,0:T(8,128)(2,1)S(1)} async-done(((bf16[32,3,8,128]{3,2,1,0:T(8,128)(2,1)}), bf16[32,3,8,128]{3,2,1,0:T(8,128)(2,1)S(1)}, u32[]{:S(2)}, u32[]{:S(2)}) %all-to-all-start.2) | async-done | bytes 196640 | tf_op jit(solution)/shard_map/all_to_all | solution.py:530
  103.6 2.0 %finish.1 = (f32[1,16]{1,0:T(1,128)}, bf16[132,16,128]{2,1,0:T(8,128)(2,1)}, bf16[132,16,128]{2,1,0:T(8,128)(2,1)}) custom-call(s32[8,128]{1,0:T(8,128)S(1)} %get-tuple-element.219.idx, f32[1,128]{1,0:T(1,128)S(1)} %get-tuple-element.244.line, bf16[32,3,8,128]{3,2,1,0:T(8,128)(2,1)S(1)} %all-to-all-done.2.got, ...), custom_call_target="tpu_custom_call", output_to_operand_aliasing={{1}: (3, {}), {2}: (4, {})} | custom-call | tf_op jit(solution)/shard_map/finish/pallas_call | solution.py:277
  (62 shorter events, 15.6 us)
Async XLA Ops:
  0.6 67.0 %copy-start = (bf16[128256]{0:T(1024)(128)(2,1)S(1)}, bf16[128256]{0:T(1024)(128)(2,1)}, u32[]{:S(2)}) copy-start(bf16[128256]{0:T(1024)(128)(2,1)} %param.32) | copy-start | bytes 769540
  2.4 32.1 %all-to-all-start = ((bf16[8,64,512]{2,1,0:T(8,128)(2,1)}), bf16[8,64,512]{2,1,0:T(8,128)(2,1)S(1)}, u32[]{:S(2)}, u32[]{:S(2)}) async-start(bf16[8,64,512]{2,1,0:T(8,128)(2,1)} %broadcast_in_dim.19), calls=%async_computation | async-start | bytes 1048576 | tf_op jit(solution)/shard_map/all_to_all | solution.py:506
  11.4 19.5 %collective-permute-start.8 = (bf16[16,128,128]{2,1,0:T(8,128)(2,1)}, bf16[16,128,128]{2,1,0:T(8,128)(2,1)S(1)}, u32[]{:S(2)}, u32[]{:S(2)}) collective-permute-start(bf16[16,128,128]{2,1,0:T(8,128)(2,1)} %kc.1), channel_id=1, source_target_pairs={{0,8},{8,0},{16,24},{24,16},{32,40},{40,32},{48,56},{56,48},{64,72... | collective-permute-start | bytes 1572872 | tf_op jit(solution)/shard_map/ppermute | solution.py:446
  12.3 18.5 %collective-permute-start.9 = (bf16[16,128,128]{2,1,0:T(8,128)(2,1)}, bf16[16,128,128]{2,1,0:T(8,128)(2,1)S(1)}, u32[]{:S(2)}, u32[]{:S(2)}) collective-permute-start(bf16[16,128,128]{2,1,0:T(8,128)(2,1)} %vc.1), channel_id=1, source_target_pairs={{0,8},{8,0},{16,24},{24,16},{32,40},{40,32},{48,56},{56,48},{64,72... | collective-permute-start | bytes 1572872 | tf_op jit(solution)/shard_map/ppermute | solution.py:446
  12.4 2.4 %collective-permute-start.1 = (s32[1,16]{1,0:T(1,128)}, s32[1,16]{1,0:T(1,128)S(1)}, u32[]{:S(2)}, u32[]{:S(2)}) collective-permute-start(s32[1,16]{1,0:T(1,128)} %bitcast.37), channel_id=1, source_target_pairs={{0,8},{8,0},{16,24},{24,16},{32,40},{40,32},{48,56},{56,48},{64,72... | collective-permute-start | bytes 200 | tf_op jit(solution)/shard_map/ppermute | solution.py:446
  15.5 3.6 %collective-permute-start.4 = (s32[2,16]{1,0:T(2,128)S(1)}, s32[2,16]{1,0:T(2,128)S(1)}, u32[]{:S(2)}, u32[]{:S(2)}) collective-permute-start(s32[2,16]{1,0:T(2,128)S(1)} %pad_add_fusion), channel_id=1, source_target_pairs={{0,48},{8,56},{16,0},{24,8},{32,16},{40,24},{48,32},{56,40},{64,11... | collective-permute-start | bytes 392 | tf_op jit(solution)/shard_map/ppermute | solution.py:465
  18.0 4.2 %collective-permute-start.3 = (s32[2,16]{1,0:T(2,128)S(1)}, s32[2,16]{1,0:T(2,128)S(1)}, u32[]{:S(2)}, u32[]{:S(2)}) collective-permute-start(s32[2,16]{1,0:T(2,128)S(1)} %pad_add_fusion), channel_id=1, source_target_pairs={{0,32},{8,40},{16,48},{24,56},{32,0},{40,8},{48,16},{56,24},{64,96... | collective-permute-start | bytes 392 | tf_op jit(solution)/shard_map/ppermute | solution.py:465
  18.5 3.9 %collective-permute-start.2 = (s32[2,16]{1,0:T(2,128)S(1)}, s32[2,16]{1,0:T(2,128)S(1)}, u32[]{:S(2)}, u32[]{:S(2)}) collective-permute-start(s32[2,16]{1,0:T(2,128)S(1)} %pad_add_fusion), channel_id=1, source_target_pairs={{0,16},{8,24},{16,32},{24,40},{32,48},{40,56},{48,0},{56,8},{64,80... | collective-permute-start | bytes 392 | tf_op jit(solution)/shard_map/ppermute | solution.py:465
  23.1 3.9 %collective-permute-start.7 = (s32[8,16]{1,0:T(8,128)S(1)}, s32[8,16]{1,0:T(8,128)S(1)}, u32[]{:S(2)}, u32[]{:S(2)}) collective-permute-start(s32[8,16]{1,0:T(8,128)S(1)} %concatenate.35.refs_0_), channel_id=1, source_target_pairs={{0,192},{8,200},{16,208},{24,216},{32,224},{40,232},{48,240},{56,2... | collective-permute-start | bytes 1544 | tf_op jit(solution)/shard_map/ppermute | solution.py:465
  25.9 4.0 %collective-permute-start.6 = (s32[8,16]{1,0:T(8,128)S(1)}, s32[8,16]{1,0:T(8,128)S(1)}, u32[]{:S(2)}, u32[]{:S(2)}) collective-permute-start(s32[8,16]{1,0:T(8,128)S(1)} %concatenate.35.refs_0_), channel_id=1, source_target_pairs={{0,128},{8,136},{16,144},{24,152},{32,160},{40,168},{48,176},{56,1... | collective-permute-start | bytes 1544 | tf_op jit(solution)/shard_map/ppermute | solution.py:465
  26.3 3.7 %collective-permute-start.5 = (s32[8,16]{1,0:T(8,128)S(1)}, s32[8,16]{1,0:T(8,128)S(1)}, u32[]{:S(2)}, u32[]{:S(2)}) collective-permute-start(s32[8,16]{1,0:T(8,128)S(1)} %concatenate.35.refs_0_), channel_id=1, source_target_pairs={{0,64},{8,72},{16,80},{24,88},{32,96},{40,104},{48,112},{56,120},{... | collective-permute-start | bytes 1544 | tf_op jit(solution)/shard_map/ppermute | solution.py:465
  34.5 46.4 %all-to-all-start.1 = ((bf16[16,3,256,128]{3,2,1,0:T(8,128)(2,1)}), bf16[16,3,256,128]{3,2,1,0:T(8,128)(2,1)}, u32[]{:S(2)}, u32[]{:S(2)}) async-start(bf16[16,3,256,128]{3,2,1,0:T(8,128)(2,1)} %pack.1), calls=%async_computation.1 | async-start | bytes 6291456 | tf_op jit(solution)/shard_map/all_to_all | solution.py:457
  47.2 14.6 %collective-permute-start.10 = (bf16[64,512]{1,0:T(8,128)(2,1)S(1)}, bf16[64,512]{1,0:T(8,128)(2,1)S(1)}, u32[]{:S(2)}, u32[]{:S(2)}) collective-permute-start(bf16[64,512]{1,0:T(8,128)(2,1)S(1)} %get-tuple-element.233), channel_id=1, source_target_pairs={{0,4},{1,5},{2,6},{3,7},{4,0},{5,1},{6,2},{7,3},{8,12},{9,13},{10,... | collective-permute-start | bytes 196616 | tf_op jit(solution)/shard_map/ppermute | solution.py:438
  52.9 9.1 %collective-permute-start.11 = (bf16[64,512]{1,0:T(8,128)(2,1)S(1)}, bf16[64,512]{1,0:T(8,128)(2,1)S(1)}, u32[]{:S(2)}, u32[]{:S(2)}) collective-permute-start(bf16[64,512]{1,0:T(8,128)(2,1)S(1)} %get-tuple-element.234), channel_id=1, source_target_pairs={{0,3},{1,4},{2,5},{3,6},{4,7},{5,0},{6,1},{7,2},{8,11},{9,12},{10,... | collective-permute-start | bytes 196616 | tf_op jit(solution)/shard_map/ppermute | solution.py:438
  53.9 10.5 %collective-permute-start.12 = (bf16[64,512]{1,0:T(8,128)(2,1)S(1)}, bf16[64,512]{1,0:T(8,128)(2,1)S(1)}, u32[]{:S(2)}, u32[]{:S(2)}) collective-permute-start(bf16[64,512]{1,0:T(8,128)(2,1)S(1)} %get-tuple-element.235), channel_id=1, source_target_pairs={{0,5},{1,6},{2,7},{3,0},{4,1},{5,2},{6,3},{7,4},{8,13},{9,14},{10,... | collective-permute-start | bytes 196616 | tf_op jit(solution)/shard_map/ppermute | solution.py:438
  58.1 7.0 %collective-permute-start.13 = (bf16[64,512]{1,0:T(8,128)(2,1)S(1)}, bf16[64,512]{1,0:T(8,128)(2,1)S(1)}, u32[]{:S(2)}, u32[]{:S(2)}) collective-permute-start(bf16[64,512]{1,0:T(8,128)(2,1)S(1)} %get-tuple-element.236), channel_id=1, source_target_pairs={{0,2},{1,3},{2,4},{3,5},{4,6},{5,7},{6,0},{7,1},{8,10},{9,11},{10,... | collective-permute-start | bytes 196616 | tf_op jit(solution)/shard_map/ppermute | solution.py:438
  58.4 6.7 %collective-permute-start.14 = (bf16[64,512]{1,0:T(8,128)(2,1)S(1)}, bf16[64,512]{1,0:T(8,128)(2,1)S(1)}, u32[]{:S(2)}, u32[]{:S(2)}) collective-permute-start(bf16[64,512]{1,0:T(8,128)(2,1)S(1)} %get-tuple-element.237), channel_id=1, source_target_pairs={{0,6},{1,7},{2,0},{3,1},{4,2},{5,3},{6,4},{7,5},{8,14},{9,15},{10,... | collective-permute-start | bytes 196616 | tf_op jit(solution)/shard_map/ppermute | solution.py:438
  61.7 4.7 %collective-permute-start.15 = (bf16[64,512]{1,0:T(8,128)(2,1)S(1)}, bf16[64,512]{1,0:T(8,128)(2,1)S(1)}, u32[]{:S(2)}, u32[]{:S(2)}) collective-permute-start(bf16[64,512]{1,0:T(8,128)(2,1)S(1)} %get-tuple-element.238), channel_id=1, source_target_pairs={{0,1},{1,2},{2,3},{3,4},{4,5},{5,6},{6,7},{7,0},{8,9},{9,10},{10,1... | collective-permute-start | bytes 196616 | tf_op jit(solution)/shard_map/ppermute | solution.py:438
  62.0 4.9 %collective-permute-start.16 = (bf16[64,512]{1,0:T(8,128)(2,1)S(1)}, bf16[64,512]{1,0:T(8,128)(2,1)S(1)}, u32[]{:S(2)}, u32[]{:S(2)}) collective-permute-start(bf16[64,512]{1,0:T(8,128)(2,1)S(1)} %get-tuple-element.239), channel_id=1, source_target_pairs={{0,7},{1,0},{2,1},{3,2},{4,3},{5,4},{6,5},{7,6},{8,15},{9,8},{10,9... | collective-permute-start | bytes 196616 | tf_op jit(solution)/shard_map/ppermute | solution.py:438
  67.6 2.8 %collective-permute-start.17 = (f32[1,128]{1,0:T(1,128)S(1)}, f32[1,128]{1,0:T(1,128)S(1)}, u32[]{:S(2)}, u32[]{:S(2)}) collective-permute-start(f32[1,128]{1,0:T(1,128)S(1)} %get-tuple-element.241), channel_id=1, source_target_pairs={{0,1},{1,0},{2,3},{3,2},{4,5},{5,4},{6,7},{7,6},{8,9},{9,8},{10,11... | collective-permute-start | bytes 1544 | tf_op jit(solution)/shard_map/ppermute | solution.py:442
  70.4 4.9 %collective-permute-start.20 = (f32[1,128]{1,0:T(1,128)S(1)}, f32[1,128]{1,0:T(1,128)S(1)}, u32[]{:S(2)}, u32[]{:S(2)}) collective-permute-start(f32[1,128]{1,0:T(1,128)S(1)} %add.107.refs_0_), channel_id=1, source_target_pairs={{0,6},{1,7},{2,0},{3,1},{4,2},{5,3},{6,4},{7,5},{8,14},{9,15},{10,... | collective-permute-start | bytes 1544 | tf_op jit(solution)/shard_map/ppermute | solution.py:438
  73.2 4.5 %collective-permute-start.19 = (f32[1,128]{1,0:T(1,128)S(1)}, f32[1,128]{1,0:T(1,128)S(1)}, u32[]{:S(2)}, u32[]{:S(2)}) collective-permute-start(f32[1,128]{1,0:T(1,128)S(1)} %add.107.refs_0_), channel_id=1, source_target_pairs={{0,2},{1,3},{2,4},{3,5},{4,6},{5,7},{6,0},{7,1},{8,10},{9,11},{10,... | collective-permute-start | bytes 1544 | tf_op jit(solution)/shard_map/ppermute | solution.py:438
  73.2 6.3 %collective-permute-start.18 = (f32[1,128]{1,0:T(1,128)S(1)}, f32[1,128]{1,0:T(1,128)S(1)}, u32[]{:S(2)}, u32[]{:S(2)}) collective-permute-start(f32[1,128]{1,0:T(1,128)S(1)} %add.107.refs_0_), channel_id=1, source_target_pairs={{0,4},{1,5},{2,6},{3,7},{4,0},{5,1},{6,2},{7,3},{8,12},{9,13},{10,... | collective-permute-start | bytes 1544 | tf_op jit(solution)/shard_map/ppermute | solution.py:438
  81.0 22.7 %all-to-all-start.2 = ((bf16[32,3,8,128]{3,2,1,0:T(8,128)(2,1)}), bf16[32,3,8,128]{3,2,1,0:T(8,128)(2,1)S(1)}, u32[]{:S(2)}, u32[]{:S(2)}) async-start(bf16[32,3,8,128]{3,2,1,0:T(8,128)(2,1)} %get-tuple-element.246), calls=%async_computation.2 | async-start | bytes 393216 | tf_op jit(solution)/shard_map/all_to_all | solution.py:530
  (8 other events, 85.9 us)
